TPU v7x, 128 devices: a whole 4x4x4 slice. The times are simulated.
128 devices in a mesh: heads: 2 (over y_lo), seq: 64 (over y_hi, z, x, core).
Axes of the slice: x: 4, y: 4 (y_hi: 2, y_lo: 2; y = y_hi * 2 + y_lo), z: 4, core: 2. Of those that a mesh axis runs over, the one named last changes fastest.
Arguments:
- queries: bfloat16 [2, 24576, 4096], P(None, 'seq', 'heads'), may hold values from -72 to 72, as said below
- key_rows: bfloat16 [2, 24576, 4096], P(None, 'seq', 'heads'), may hold values from -6.06 to 6.06, as said below
- value_rows: bfloat16 [2, 24576, 4096], P(None, 'seq', 'heads'), may hold values from -6 to 6
- step_rates: float32 [8, 2, 24576], P('heads', None, 'seq'), may hold values from 0.0001 to 0.001
- w_gate: float32 [8, 512, 512], P('heads', 'seq'), may hold values from -0.25 to 0.25
- w_up: float32 [8, 512, 512], P('heads', 'seq'), may hold values from -0.25 to 0.25
- w_down: float32 [8, 512, 512], P('heads', 'seq'), may hold values from -0.25 to 0.25
- out_gain: float32 [4096], P('heads'), may hold values from 0.5 to 1.5
Outputs:
- layer_out: bfloat16 [2, 24576, 4096], P(None, 'seq', 'heads')
- new_gate: float32 [8, 512, 512], P('heads', 'seq')
- new_up: float32 [8, 512, 512], P('heads', 'seq')
- new_down: float32 [8, 512, 512], P('heads', 'seq')
Inputs may be any that keep to these rules, and one draw needn't show every extreme that they name: `queries`: entries of order one with a few larger ones. `key_rows`: entries of order one.
All inputs are finite; a program needn't handle non-finite values.
Results may differ from a plain program's by a relative error of at most 0.0069.
The roundings to bfloat16 on the way count: a program that leaves them out, or rounds other values in their place, can miss the bound.
Values may be sent and summed in bfloat16 or wider, within the bound.
No kernel may reach another device: no remote copies, remote signals or barrier semaphores. Data moves between devices by JAX's collectives and lax.ppermute only.
A program may use at most 192 MiB of HBM per device.

v0:
```python
import functools

import jax
import jax.numpy as jnp
from jax import lax
from jax.experimental import pallas as pl
from jax.experimental.pallas import tpu as pltpu
from jax.sharding import Mesh, PartitionSpec as P

NORM_EPS = 1e-05
MASKED = -1e30
SIZES = {"heads": 2, "yh": 2, "z": 4, "x": 4, "core": 2}
SEQ = ("yh", "z", "x", "core")
TOK = 384
DH = 512
SCALE = DH ** -0.5

f32 = jnp.float32
bf16 = jnp.bfloat16


def shift(value, axis, steps):
    count = SIZES[axis]
    return lax.ppermute(value, axis, [(i, (i + steps) % count) for i in range(count)])


def dot(a, b, dims):
    return lax.dot_general(a, b, (dims, ((), ())), preferred_element_type=f32)


NN = ((1,), (0,))
NT = ((1,), (1,))
TN = ((0,), (0,))


def cparams(**kw):
    return pltpu.CompilerParams(vmem_limit_bytes=56 * 1024 * 1024, **kw)


def piece_rows(kind, part, idx, item):
    yh, z, x = idx
    a, k = item % 2, item // 2
    y = lax.rem(yh + a, 2)
    if kind == 0:
        zz, xx = lax.rem(z + k, 4), lax.rem(x + part, 4)
    else:
        zz, xx = lax.rem(z + part, 4), lax.rem(x + k, 4)
    return pl.multiple_of(y * 256 + zz * 64 + xx * 16, 16)


def weight_copies(head, pieces, w_vmem, sem, idx):
    for part in range(4):
        for item in range(8):
            row = piece_rows(head, part, idx, item)
            yield pltpu.make_async_copy(
                pieces[head * 4 + part].at[item],
                w_vmem.at[head, :, pl.ds(row, 16), :],
                sem.at[head],
            )


def load_weights(pieces, w_vmem, sem, idx, head_now):
    @pl.when(head_now == 0)
    def _():
        for head in range(2):
            for copy in weight_copies(head, pieces, w_vmem, sem, idx):
                copy.start()

    for head in range(2):

        @pl.when(head_now == head)
        def _(head=head):
            pltpu.make_async_copy(w_vmem.at[head], w_vmem.at[head], sem.at[head]).wait()


def grads_kernel(s_ref, *refs):
    pieces = refs[:8]
    k_own, v_own, k_rec, v_rec, r_ref = refs[8:13]
    outs = refs[13:21]
    w_vmem, sums, sem = refs[21:]
    head = pl.program_id(0)
    idx = (s_ref[1], s_ref[2], s_ref[3])
    load_weights(pieces, w_vmem, sem, idx, head)
    gate, up, down = w_vmem[head, 0], w_vmem[head, 1], w_vmem[head, 2]
    for j, (k_ref, v_ref) in enumerate(((k_own, v_own), (k_rec, v_rec))):
        k = k_ref[0]
        rate = r_ref[0, j]
        target = (-(rate * v_ref[0].astype(f32))).astype(bf16)
        g = dot(k, gate, NN)
        u = dot(k, up, NN)
        back = dot(target, down, NT)
        s = jax.nn.sigmoid(g)
        silu = g * s
        active = (silu * u).astype(bf16)
        d_gate = (back * u * s * (1.0 + g * (1.0 - s))).astype(bf16)
        d_up = (back * silu).astype(bf16)
        parts = (dot(k, d_gate, TN), dot(k, d_up, TN), dot(active, target, TN))
        for m in range(3):
            if j == 0:
                sums[m] = parts[m]
            else:
                sums[m] += parts[m]
    yh, z, x = idx
    for kind in range(2):

        @pl.when(head == kind)
        def _(kind=kind):
            for part in range(4):
                for item in range(8):
                    a, k = item % 2, item // 2
                    y = lax.rem(yh + a, 2)
                    zz = lax.rem(z + 4 - (k if kind == 0 else part), 4)
                    xx = lax.rem(x + 4 - (part if kind == 0 else k), 4)
                    row = pl.multiple_of(y * 256 + zz * 64 + xx * 16, 16)
                    for m in range(3):
                        outs[kind * 4 + part][item, m] = sums[m, pl.ds(row, 16), :].astype(bf16)


def own_spec(c):
    return pl.BlockSpec((1, TOK, DH), lambda h, s: (c, 0, s[0] * 2 + h))


def rec_spec(c):
    return pl.BlockSpec((1, TOK, DH), lambda h, s: (c, 0, h))


ANY = pl.BlockSpec(memory_space=pl.ANY)


def compute_grads(scal, pieces, k, v, k_rec, v_rec, rates):
    whole = pl.BlockSpec((8, 3, 16, DH), lambda h, s: (0, 0, 0, 0))
    return pl.pallas_call(
        grads_kernel,
        name="fast_grads",
        out_shape=[jax.ShapeDtypeStruct((8, 3, 16, DH), bf16)] * 8,
        grid_spec=pltpu.PrefetchScalarGridSpec(
            num_scalar_prefetch=1,
            grid=(2,),
            in_specs=[ANY] * 8
            + [own_spec(0), own_spec(0), rec_spec(0), rec_spec(0)]
            + [pl.BlockSpec((1, 2, TOK, 1), lambda h, s: (h, 0, 0, 0))],
            out_specs=[whole] * 8,
            scratch_shapes=[
                pltpu.VMEM((2, 3, DH, DH), bf16),
                pltpu.VMEM((3, DH, DH), f32),
                pltpu.SemaphoreType.DMA((2,)),
            ],
        ),
        compiler_params=cparams(),
    )(scal, *pieces, k, v, k_rec, v_rec, rates)


def apply_kernel(s_ref, *refs):
    pieces = refs[:8]
    q_own, q_rec = refs[8:10]
    out_ref, pow_ref = refs[10:12]
    w_vmem, sem = refs[12:]
    head = pl.program_id(0)
    idx = (s_ref[1], s_ref[2], s_ref[3])
    load_weights(pieces, w_vmem, sem, idx, head)
    gate, up, down = w_vmem[head, 0], w_vmem[head, 1], w_vmem[head, 2]
    for j, q_ref in enumerate((q_own, q_rec)):
        q = q_ref[0]
        g = dot(q, gate, NN)
        u = dot(q, up, NN)
        active = (g * jax.nn.sigmoid(g) * u).astype(bf16)
        out = dot(active, down, NN)
        out_ref[j] = out
        power = jnp.sum(out * out, axis=-1, keepdims=True)
        power = jnp.transpose(jnp.broadcast_to(power, (TOK, 128)))[:8]

        @pl.when(head == 0)
        def _(j=j, power=power):
            pow_ref[j] = power

        @pl.when(head == 1)
        def _(j=j, power=power):
            pow_ref[j] += power


def fast_apply(c, scal, pieces, q, q_rec):
    return pl.pallas_call(
        apply_kernel,
        name="fast_apply",
        out_shape=[
            jax.ShapeDtypeStruct((2, TOK, 2 * DH), f32),
            jax.ShapeDtypeStruct((2, 8, TOK), f32),
        ],
        grid_spec=pltpu.PrefetchScalarGridSpec(
            num_scalar_prefetch=1,
            grid=(2,),
            in_specs=[ANY] * 8 + [own_spec(c), rec_spec(c)],
            out_specs=[
                pl.BlockSpec((2, TOK, DH), lambda h, s: (0, 0, h)),
                pl.BlockSpec((2, 8, TOK), lambda h, s: (0, 0, 0)),
            ],
            scratch_shapes=[
                pltpu.VMEM((2, 3, DH, DH), bf16),
                pltpu.SemaphoreType.DMA((2,)),
            ],
        ),
        compiler_params=cparams(),
    )(scal, *pieces, q, q_rec)


def attention_kernel(c, s_ref, qo, qr, k0, ka, kb, k2, v0, va, vb, v2, out_ref):
    block = pl.program_id(1)
    row = lax.broadcasted_iota(jnp.int32, (TOK, TOK), 0)
    col = lax.broadcasted_iota(jnp.int32, (TOK, TOK), 1)
    q = jnp.where(s_ref[0] == block, qo[0], qr[0])
    keys = (k0[0], jnp.where(block == 0, ka[0], kb[0]), k2[0])
    values = (v0[0], jnp.where(block == 0, va[0], vb[0]), v2[0])
    scores = [dot(q, k, NT) * SCALE for k in keys]
    if c == 0:
        low = jnp.where(s_ref[4] == 1, TOK, row)
        scores[1] = jnp.where(col >= jnp.where((s_ref[4] == 1) & (block == 0), TOK, 0), scores[1], MASKED)
    else:
        low = row
    scores[0] = jnp.where(col > low, scores[0], MASKED)
    scores[2] = jnp.where(col <= row, scores[2], MASKED)
    peak = jnp.max(jnp.maximum(jnp.maximum(scores[0], scores[1]), scores[2]), axis=-1, keepdims=True)
    weights = [jnp.exp(s - peak) for s in scores]
    total = jnp.sum(weights[0] + weights[1] + weights[2], axis=-1, keepdims=True)
    inv = 1.0 / total
    out_ref[0] = sum(
        dot((w * inv).astype(bf16), v, NN) for w, v in zip(weights, values)
    )


def attention(c, scal, q, q_rec, before, mine):
    def block(at):
        return pl.BlockSpec((1, TOK, DH), lambda h, b, s: (at(b), 0, h))

    return pl.pallas_call(
        functools.partial(attention_kernel, c),
        name="window_attention",
        out_shape=jax.ShapeDtypeStruct((2, TOK, 2 * DH), f32),
        grid_spec=pltpu.PrefetchScalarGridSpec(
            num_scalar_prefetch=1,
            grid=(2, 2),
            in_specs=[
                pl.BlockSpec((1, TOK, DH), lambda h, b, s: (c, 0, s[0] * 2 + h)),
                pl.BlockSpec((1, TOK, DH), lambda h, b, s: (c, 0, h)),
            ]
            + [
                block(at)
                for o in (0, 2)
                for at in (lambda b, o=o: o + b, lambda b, o=o: o + 1, lambda b, o=o: o, lambda b, o=o: o + b)
            ],
            out_specs=pl.BlockSpec(
                (1, TOK, DH), lambda h, b, s: (jnp.where(s[0] == b, 0, 1), 0, h)
            ),
        ),
        compiler_params=cparams(),
    )(scal, q, q_rec, *(before, before, mine, mine) * 2)


def finish_kernel(s_ref, fast_ref, p0, p1, p2, p3, gain_ref, att_ref, *refs):
    own_ref, rec_ref = refs[-2:]
    total = p0[...] + p1[...] + p2[...] + p3[...]
    rs = lax.rsqrt(total * (1.0 / 4096.0) + NORM_EPS)
    for j in range(2):
        col = jnp.transpose(rs[j])[:, :1]
        out = (fast_ref[j] * gain_ref[...] * col + att_ref[j]).astype(bf16)
        if j == 0:
            own_ref[0] = out
        else:
            rec_ref[...] = out


ROWS = 128


def finish(c, scal, fast, powers, gain, att, layer):
    both = pl.BlockSpec((2, ROWS, 2 * DH), lambda i, s: (0, i, 0))
    power = pl.BlockSpec((2, 8, ROWS), lambda i, s: (0, 0, i))
    more = [] if layer is None else [layer]
    return pl.pallas_call(
        finish_kernel,
        name="finish",
        out_shape=[
            jax.ShapeDtypeStruct((2, TOK, 4 * DH), bf16),
            jax.ShapeDtypeStruct((TOK, 2 * DH), bf16),
        ],
        grid_spec=pltpu.PrefetchScalarGridSpec(
            num_scalar_prefetch=1,
            grid=(TOK // ROWS,),
            in_specs=[both] + [power] * 4 + [pl.BlockSpec((1, 2 * DH), lambda i, s: (0, 0)), both]
            + [ANY] * len(more),
            out_specs=[
                pl.BlockSpec((1, ROWS, 2 * DH), lambda i, s: (c, i, s[0])),
                pl.BlockSpec((ROWS, 2 * DH), lambda i, s: (i, 0)),
            ],
        ),
        input_output_aliases={8: 0} if more else {},
        compiler_params=cparams(),
    )(scal, fast, *powers, gain, att, *more)


def place_kernel(c, s_ref, arrived_ref, layer_ref, out_ref, sem):
    column = pl.multiple_of((1 - s_ref[0]) * 2 * DH, 2 * DH)
    copy = pltpu.make_async_copy(arrived_ref, out_ref.at[c, :, pl.ds(column, 2 * DH)], sem)
    copy.start()
    copy.wait()


def place(c, scal, arrived, layer):
    return pl.pallas_call(
        functools.partial(place_kernel, c),
        name="place",
        out_shape=jax.ShapeDtypeStruct((2, TOK, 4 * DH), bf16),
        grid_spec=pltpu.PrefetchScalarGridSpec(
            num_scalar_prefetch=1,
            grid=(1,),
            in_specs=[ANY, ANY],
            out_specs=ANY,
            scratch_shapes=[pltpu.SemaphoreType.DMA(())],
        ),
        input_output_aliases={2: 0},
        compiler_params=cparams(),
    )(scal, arrived, layer)


def gather_direct(both):
    out = []
    for head, (first, last) in enumerate((("z", "x"), ("x", "z"))):
        v = both[head]
        v = jnp.concatenate([v] + [shift(v, first, -k) for k in range(1, 4)], axis=0)
        out.append([v] + [shift(v, last, -k) for k in range(1, 4)])
    return out[0] + out[1]


def gather_rings(both):
    axes = (("z", "x"), ("x", "z"))
    now = [both[h] for h in range(2)]
    held = [[n] for n in now]
    for _ in range(3):
        for h in range(2):
            now[h] = shift(now[h], axes[h][0], -1)
            held[h].append(now[h])
    now = [jnp.concatenate(held[h], axis=0) for h in range(2)]
    out = [[n] for n in now]
    for _ in range(3):
        for h in range(2):
            now[h] = shift(now[h], axes[h][1], -1)
            out[h].append(now[h])
    return out[0] + out[1]


def scatter_rings(slabs):
    axes = (("x", "z"), ("z", "x"))
    now = [slabs[3], slabs[7]]
    for k in (2, 1, 0):
        for h in range(2):
            got = shift(now[h], axes[h][0], -1)
            total = got.astype(f32) + slabs[h * 4 + k].astype(f32)
            now[h] = total.astype(bf16) if k else total
    parts = now
    now = [p[6:8].astype(bf16) for p in parts]
    for k in (2, 1, 0):
        for h in range(2):
            got = shift(now[h], axes[h][1], -1)
            now[h] = (got.astype(f32) + parts[h][2 * k : 2 * k + 2]).astype(bf16)
    return jnp.stack(now)


def power_parts(power):
    flat = ("heads", "core")
    swapped = power[::-1]
    return [
        lax.ppermute(swapped, flat, [(0, 1), (1, 0), (2, 3), (3, 2)]),
        lax.ppermute(power, flat, [(0, 2), (2, 0), (1, 3), (3, 1)]),
        lax.ppermute(swapped, flat, [(0, 3), (3, 0), (1, 2), (2, 1)]),
    ]


def on_device(queries, key_rows, value_rows, step_rates, w_gate, w_up, w_down, out_gain):
    core = lax.axis_index("core")
    yh, z, x = lax.axis_index("yh"), lax.axis_index("z"), lax.axis_index("x")
    chip = (yh * 4 + z) * 4 + x
    first = (chip == 0).astype(jnp.int32)
    scal = jnp.stack([core, yh, z, x, first]).astype(jnp.int32)

    masters = jnp.stack([w_gate, w_up, w_down], axis=1)
    mine = lax.dynamic_slice_in_dim(masters, core * 2, 2, 0)
    theirs = lax.dynamic_slice_in_dim(masters, (1 - core) * 2, 2, 0)
    got = shift(theirs, "core", 1)
    m16 = jnp.where(
        core == 0,
        jnp.concatenate([mine, got], axis=2),
        jnp.concatenate([got, mine], axis=2),
    )
    m16_other = shift(m16, "yh", 1)
    m16_other, key_rows, value_rows, queries, step_rates = lax.optimization_barrier(
        (m16_other, key_rows, value_rows, queries, step_rates)
    )
    both = jnp.stack([m16, m16_other], axis=1)
    pieces = gather_direct(both.astype(bf16))

    def split_in(a):
        keep = lax.dynamic_slice_in_dim(a, core * 1024, 1024, 2)
        give = lax.dynamic_slice_in_dim(a, (1 - core) * 1024, 1024, 2)
        return keep, shift(give, "core", 1)

    k_own, k_rec = split_in(key_rows)
    v_own, v_rec = split_in(value_rows)
    q_rec = split_in(queries)[1]
    rates = step_rates[:, 0, :]
    r_own = lax.dynamic_slice_in_dim(rates, core * 2, 2, 0)
    r_rec = shift(lax.dynamic_slice_in_dim(rates, (1 - core) * 2, 2, 0), "core", 1)
    rates = jnp.stack([r_own, r_rec], axis=1)[..., None]

    chips = ("yh", "z", "x")
    row = [(i, (i + 1) % 32) for i in range(32) if i % 16 != 15]
    turn = [(15, 16), (31, 0)]
    pair = [
        jnp.where(
            core == 0,
            jnp.stack([k_own[c], k_rec[c], v_own[c], v_rec[c]]),
            jnp.stack([k_rec[c], k_own[c], v_rec[c], v_own[c]]),
        )
        for c in range(2)
    ]
    pair[0], pair[1], *pieces = lax.optimization_barrier((pair[0], pair[1], *pieces))
    halo = []
    for c in range(2):
        halo.append(lax.ppermute(pair[c], chips, row))
    turned0 = lax.ppermute(pair[0], chips, turn)

    slabs = compute_grads(scal, pieces, key_rows, value_rows, k_rec, v_rec, rates)
    fast0, pow0 = fast_apply(0, scal, pieces, queries, q_rec)
    half_sums = scatter_rings(slabs)
    half_sums, pow0 = lax.optimization_barrier((half_sums, pow0))
    other_sums = shift(half_sums, "yh", 1)
    powers0 = [pow0] + power_parts(pow0)
    grad_both = half_sums.astype(f32) + other_sums[:, ::-1].astype(f32)
    grad_both, pair1, *powers0 = lax.optimization_barrier((grad_both, pair[1], *powers0))
    new_both = both - grad_both
    new16 = new_both[:, 0]
    pieces2 = gather_rings(new_both.astype(bf16))
    turned1 = lax.ppermute(pair1, chips, turn[:1])
    own_rows = lax.dynamic_slice_in_dim(new16, core * 8, 8, 2)
    their_rows = shift(lax.dynamic_slice_in_dim(new16, (1 - core) * 8, 8, 2), "core", 1)
    new_all = jnp.where(
        core == 0,
        jnp.concatenate([own_rows, their_rows], axis=0),
        jnp.concatenate([their_rows, own_rows], axis=0),
    )

    gain = lax.dynamic_slice_in_dim(out_gain, core * 1024, 1024, 0)[None]
    at_turn = (z == 0) & (x == 0)

    def attend(c, before, mine):
        return attention(c, scal, queries, q_rec, before, mine)

    before0 = jnp.where(at_turn, turned0, halo[0])
    att0 = attend(0, before0, pair[0])
    fast1, pow1 = fast_apply(1, scal, pieces2, queries, q_rec)
    powers1 = [pow1] + power_parts(pow1)
    fast1, turned1, halo1, earlier0 = lax.optimization_barrier(
        (fast1, turned1, halo[1], before0)
    )
    before1 = jnp.where(chip == 0, earlier0, jnp.where(at_turn, turned1, halo1))
    att1 = attend(1, before1, pair[1])

    def complete(c, fast, powers, attended, layer):
        layer, out_rec = finish(c, scal, fast, powers, gain, attended, layer)
        arrived = shift(out_rec, "core", 1)
        return place(c, scal, arrived, layer)

    layer_out = complete(0, fast0, powers0, att0, None)
    layer_out = complete(1, fast1, powers1, att1, layer_out)
    return layer_out, new_all[:, 0], new_all[:, 1], new_all[:, 2]


def solution(mesh):
    fine = Mesh(mesh.devices.reshape(2, 2, 4, 4, 2), ("heads",) + SEQ)
    rows = P(None, SEQ, "heads")
    weight = P("heads", SEQ, None)
    return jax.shard_map(
        on_device,
        mesh=fine,
        in_specs=(rows, rows, rows, P("heads", None, SEQ), weight, weight, weight, P("heads")),
        out_specs=(rows, weight, weight, weight),
        check_vma=False,
    )
```

profile of v0, /device:TPU:1, one launch (start us, length us, event | category | flops | bytes accessed | tf_op | source)
XLA Modules:
  0.0 456.1 jit_solution(14369534492787244464)
XLA Ops:
  1.6 1.5 collective-permute-start
  4.7 3.0 collective-permute-start.1
  7.7 4.9 %collective-permute-done.1 = f32[2,3,16,512]{3,2,1,0:T(8,128)S(1)} collective-permute-done((f32[2,3,16,512]{3,2,1,0:T(8,128)}, f32[2,3,16,512]{3,2,1,0:T(8,128)S(1)}, u32[]{:S(2)}, u32[]{:S(2)}) %collective-permute-start.1) | collective-permute-done | bytes 196640 | tf_op jit(solution)/shard_map/ppermute | solution.py:24
  12.6 2.7 constant_dynamic-slice_fusion.7
  16.5 2.7 constant_dynamic-slice_fusion.5
  21.7 1.4 constant_dynamic-slice_fusion.8
  24.4 2.5 collective-permute-start.10
  29.4 1.8 collective-permute-done.10
  31.2 3.8 collective-permute-start.4
  37.1 2.6 collective-permute-start.13
  42.4 4.5 collective-permute-start.7
  46.9 1.5 fusion.14
  48.5 1.5 fusion.15
  50.9 3.4 maximum_select_fusion
  54.3 6.6 %collective-permute-done.15.refs_7_ = bf16[8,3,16,512]{3,2,1,0:T(8,128)(2,1)S(1)} collective-permute-done((bf16[8,3,16,512]{3,2,1,0:T(8,128)(2,1)S(1)}, bf16[8,3,16,512]{3,2,1,0:T(8,128)(2,1)S(1)}, u32[]{:S(2)}, u32[]{:S(2)}) %collective-permute-start.15) | collective-permute-done | bytes 393248 | tf_op jit(solution)/shard_map/ppermute | solution.py:24
  62.2 7.4 %collective-permute-done.9.refs_3_ = bf16[8,3,16,512]{3,2,1,0:T(8,128)(2,1)S(1)} collective-permute-done((bf16[8,3,16,512]{3,2,1,0:T(8,128)(2,1)S(1)}, bf16[8,3,16,512]{3,2,1,0:T(8,128)(2,1)S(1)}, u32[]{:S(2)}, u32[]{:S(2)}) %collective-permute-start.9) | collective-permute-done | bytes 393248 | tf_op jit(solution)/shard_map/ppermute | solution.py:24
  70.3 13.1 %fast_grads.1 = (bf16[8,3,16,512]{3,2,1,0:T(8,128)(2,1)}, bf16[8,3,16,512]{3,2,1,0:T(8,128)(2,1)}, bf16[8,3,16,512]{3,2,1,0:T(8,128)(2,1)}, bf16[8,3,16,512]{3,2...) custom-call(s32[5]{0:T(128)} %stack.74.s_ref, ...), custom_call_target="tpu_custom_call" | custom-call | tf_op jit(solution)/shard_map/fast_grads/pallas_call | solution.py:132
  84.9 3.1 collective-permute-start.29
  88.0 3.6 collective-permute-start.23
  92.1 2.2 collective-permute-start.18
  94.3 5.5 %collective-permute-done.23 = bf16[8,3,16,512]{3,2,1,0:T(8,128)(2,1)S(1)} collective-permute-done((bf16[8,3,16,512]{3,2,1,0:T(8,128)(2,1)S(1)}, bf16[8,3,16,512]{3,2,1,0:T(8,128)(2,1)S(1)}, u32[]{:S(2)}, u32[]{:S(2)}) %collective-permute-start.23) | collective-permute-done | bytes 393248 | tf_op jit(solution)/shard_map/ppermute | solution.py:24
  99.9 3.5 collective-permute-start.24
  104.3 6.5 %collective-permute-done.24 = bf16[8,3,16,512]{3,2,1,0:T(8,128)(2,1)S(1)} collective-permute-done((bf16[8,3,16,512]{3,2,1,0:T(8,128)(2,1)S(1)}, bf16[8,3,16,512]{3,2,1,0:T(8,128)(2,1)S(1)}, u32[]{:S(2)}, u32[]{:S(2)}) %collective-permute-start.24) | collective-permute-done | bytes 393248 | tf_op jit(solution)/shard_map/ppermute | solution.py:24
  110.9 3.5 collective-permute-start.25
  115.7 4.5 collective-permute-start.49
  121.4 8.1 %fast_apply.2 = (f32[2,384,1024]{2,1,0:T(8,128)}, f32[2,8,384]{2,1,0:T(8,128)}) custom-call(s32[5]{0:T(128)} %stack.74.s_ref, bf16[8,3,16,512]{3,2,1,0:T(8,128)(2,1)} %copy-done.7, bf16[8,3,16,512]{3,2,1,0:T(8,128)(2,1)} %copy-done.16, bf16[8,3,16,512]{3,2,1,0:T(8,128)(2,1)} %copy-done.17, bf16[8,3,16,512]{3,2,1,0:T(8,128)(2,1)} %copy-done.18, ...), custom_call_target="tpu_custom_call" | custom-call | tf_op jit(solution)/shard_map/fast_apply/pallas_call | solution.py:182
  131.0 6.7 %collective-permute-start.26 = (bf16[2,3,16,512]{3,2,1,0:T(8,128)(2,1)S(1)}, bf16[2,3,16,512]{3,2,1,0:T(8,128)(2,1)S(1)}, u32[]{:S(2)}, u32[]{:S(2)}) collective-permute-start(bf16[2,3,16,512]{3,2,1,0:T(8,128)(2,1)S(1)} %slice.162), channel_id=1, source_target_pairs={{0,6},{2,0},{4,2},{6,4},{1,7},{3,1},{5,3},{7,5},{8,14},{10,8},{12,... | collective-permute-start | bytes 294920 | tf_op jit(solution)/shard_map/ppermute | solution.py:24
  137.8 1.5 collective-permute-done.26
  139.4 3.1 collective-permute-start.27
  144.1 3.1 collective-permute-start.28
  147.3 2.3 collective-permute-done.28
  149.7 1.3 rev.10
  151.1 6.3 %collective-permute-start.31 = (f32[2,8,384]{2,1,0:T(8,128)}, f32[2,8,384]{2,1,0:T(8,128)S(1)}, u32[]{:S(2)}, u32[]{:S(2)}) collective-permute-start(f32[2,8,384]{2,1,0:T(8,128)} %rev.10), channel_id=1, source_target_pairs={{0,1},{1,0},{64,65},{65,64},{2,3},{3,2},{66,67},{67,66},{4,5},{5,4... | collective-permute-start | bytes 73736 | tf_op jit(solution)/shard_map/ppermute | solution.py:371
  159.8 5.5 %collective-permute-start.47 = (bf16[4,384,1024]{2,1,0:T(8,128)(2,1)S(1)}, bf16[4,384,1024]{2,1,0:T(8,128)(2,1)}, u32[]{:S(2)}, u32[]{:S(2)}) collective-permute-start(bf16[4,384,1024]{2,1,0:T(8,128)(2,1)S(1)} %get-tuple-element.74.kb.k2.vb.v2), channel_id=1, source_target_pairs={{0,2},{2,4},{4,6},{6,8},{8,10},{10,12},{12,14},{14,16},{16,18},{18... | collective-permute-start | bytes 9437192 | tf_op jit(solution)/shard_map/ppermute | solution.py:427
  166.5 2.4 collective-permute-start.46
  168.9 1.8 fusion.12
  170.8 3.9 collective-permute-done.40
  174.6 101.4 %collective-permute-start.34 = (bf16[2,3,16,512]{3,2,1,0:T(8,128)(2,1)S(1)}, bf16[2,3,16,512]{3,2,1,0:T(8,128)(2,1)S(1)}, u32[]{:S(2)}, u32[]{:S(2)}) collective-permute-start(bf16[2,3,16,512]{3,2,1,0:T(8,128)(2,1)S(1)} %get-tuple-element.106), channel_id=1, source_target_pairs={{0,24},{8,0},{16,8},{24,16},{1,25},{9,1},{17,9},{25,17},{2,26},{10... | collective-permute-start | bytes 294920 | tf_op jit(solution)/shard_map/ppermute | solution.py:24
  276.0 1.6 collective-permute-done.34
  278.8 2.4 collective-permute-done.41
  281.1 3.8 collective-permute-start.35
  285.0 1.6 collective-permute-done.35
  286.6 2.2 collective-permute-start.42
  288.8 1.6 collective-permute-done.42
  290.4 3.5 collective-permute-start.36
  294.0 1.6 collective-permute-done.36
  295.6 3.4 collective-permute-start.43
  299.8 4.9 %collective-permute-done.43.refs_5_ = bf16[8,3,16,512]{3,2,1,0:T(8,128)(2,1)} collective-permute-done((bf16[8,3,16,512]{3,2,1,0:T(8,128)(2,1)S(1)}, bf16[8,3,16,512]{3,2,1,0:T(8,128)(2,1)}, u32[]{:S(2)}, u32[]{:S(2)}) %collective-permute-start.43) | collective-permute-done | bytes 393248 | tf_op jit(solution)/shard_map/ppermute | solution.py:24
  304.8 2.6 collective-permute-start.37
  308.0 4.4 collective-permute-done.37.refs_1_
  312.5 3.2 collective-permute-start.44
  315.7 3.1 collective-permute-start.38
  318.8 3.9 broadcast_select_fusion.k0.ka.v0.va
  322.7 11.9 %window_attention.3.att_ref = f32[2,384,1024]{2,1,0:T(8,128)} custom-call(s32[5]{0:T(128)} %stack.74.s_ref, bf16[2,384,2048]{2,1,0:T(8,128)(2,1)} %qo.1, bf16[2,384,1024]{2,1,0:T(8,128)(2,1)} %copy-done.3, bf16[4,384,1024]{2,1,0:T(8,128)(2,1)} %broadcast_select_fusion.k0.ka.v0.va, bf16[4,384,1024]{2,1,0:T(8,128)(2,1)} %broadcast_select_fusion.k0.ka.v0.va, ...), custom_call_target="tpu_custom_call" | custom-call | tf_op jit(solution)/shard_map/window_attention/pallas_call | solution.py:234
  334.6 5.7 %finish.2 = (bf16[2,384,2048]{2,1,0:T(8,128)(2,1)}, bf16[384,1024]{1,0:T(8,128)(2,1)}) custom-call(s32[5]{0:T(128)} %stack.74.s_ref, f32[2,384,1024]{2,1,0:T(8,128)} %get-tuple-element.81.fast_ref, f32[2,8,384]{2,1,0:T(8,128)} %get-tuple-element.82.p0, f32[2,8,384]{2,1,0:T(8,128)} %copy-done.32, f32[2,8,384]{2,1,0:T(8,128)} %copy-done.34, ...), custom_call_target="tpu_custom_call" | custom-call | tf_op jit(solution)/shard_map/finish/pallas_call | solution.py:278
  340.3 13.7 %collective-permute-start.53 = (bf16[384,1024]{1,0:T(8,128)(2,1)}, bf16[384,1024]{1,0:T(8,128)(2,1)}, u32[]{:S(2)}, u32[]{:S(2)}) collective-permute-start(bf16[384,1024]{1,0:T(8,128)(2,1)} %get-tuple-element.86), channel_id=1, source_target_pairs={{0,1},{1,0},{2,3},{3,2},{4,5},{5,4},{6,7},{7,6},{8,9},{9,8},{10,11... | collective-permute-start | bytes 2359304 | tf_op jit(solution)/shard_map/ppermute | solution.py:24
  354.1 10.5 %collective-permute-done.45.refs_7_ = bf16[8,3,16,512]{3,2,1,0:T(8,128)(2,1)S(1)} collective-permute-done((bf16[8,3,16,512]{3,2,1,0:T(8,128)(2,1)S(1)}, bf16[8,3,16,512]{3,2,1,0:T(8,128)(2,1)S(1)}, u32[]{:S(2)}, u32[]{:S(2)}) %collective-permute-start.45) | collective-permute-done | bytes 393248 | tf_op jit(solution)/shard_map/ppermute | solution.py:24
  366.1 8.1 %fast_apply.3 = (f32[2,384,1024]{2,1,0:T(8,128)}, f32[2,8,384]{2,1,0:T(8,128)}) custom-call(s32[5]{0:T(128)} %stack.74.s_ref, bf16[8,3,16,512]{3,2,1,0:T(8,128)(2,1)} %pad_maximum_fusion.3.refs_0_, bf16[8,3,16,512]{3,2,1,0:T(8,128)(2,1)} %collective-permute-done.37.refs_1_, bf16[8,3,16,512]{3,2,1,0:T(8,128)(2,1)} %copy-done.23, ...), custom_call_target="tpu_custom_call" | custom-call | tf_op jit(solution)/shard_map/fast_apply/pallas_call | solution.py:182
  377.3 25.7 %place.2.refs_0_ = bf16[2,384,2048]{2,1,0:T(8,128)(2,1)} custom-call(s32[5]{0:T(128)} %stack.74.s_ref, bf16[384,1024]{1,0:T(8,128)(2,1)} %collective-permute-done.53.arrived_ref, bf16[2,384,2048]{2,1,0:T(8,128)(2,1)} %get-tuple-element.87.layer_ref), custom_call_target="tpu_custom_call", output_to_operand_aliasing={{}: (2, {})} | custom-call | tf_op jit(solution)/shard_map/place/pallas_call | solution.py:308
  403.0 3.9 select_select_fusion.k0.ka.v0.va
  406.9 11.7 %window_attention.2.att_ref = f32[2,384,1024]{2,1,0:T(8,128)} custom-call(s32[5]{0:T(128)} %stack.74.s_ref, bf16[2,384,2048]{2,1,0:T(8,128)(2,1)} %qo.1, bf16[2,384,1024]{2,1,0:T(8,128)(2,1)} %copy-done.3, bf16[4,384,1024]{2,1,0:T(8,128)(2,1)} %select_select_fusion.k0.ka.v0.va, bf16[4,384,1024]{2,1,0:T(8,128)(2,1)} %select_select_fusion.k0.ka.v0.va, ...), custom_call_target="tpu_custom_call" | custom-call | tf_op jit(solution)/shard_map/window_attention/pallas_call | solution.py:234
  419.9 5.7 %finish.3 = (bf16[2,384,2048]{2,1,0:T(8,128)(2,1)}, bf16[384,1024]{1,0:T(8,128)(2,1)}) custom-call(s32[5]{0:T(128)} %stack.74.s_ref, f32[2,384,1024]{2,1,0:T(8,128)} %get-tuple-element.76.fast_ref, f32[2,8,384]{2,1,0:T(8,128)} %get-tuple-element.77.p0, f32[2,8,384]{2,1,0:T(8,128)} %copy-done.35, ...), custom_call_target="tpu_custom_call", output_to_operand_aliasing={{0}: (8, {})} | custom-call | tf_op jit(solution)/shard_map/finish/pallas_call | solution.py:278
  426.6 2.1 collective-permute-done.55
  430.3 25.6 %place.3 = bf16[2,384,2048]{2,1,0:T(8,128)(2,1)} custom-call(s32[5]{0:T(128)} %stack.74.s_ref, bf16[384,1024]{1,0:T(8,128)(2,1)} %copy-done.20, bf16[2,384,2048]{2,1,0:T(8,128)(2,1)} %get-tuple-element.89.layer_ref), custom_call_target="tpu_custom_call", output_to_operand_aliasing={{}: (2, {})} | custom-call | tf_op jit(solution)/shard_map/place/pallas_call | solution.py:308
  (190 shorter events, 41.4 us)
Async XLA Ops:
  1.6 2.4 collective-permute-start
  4.7 7.9 %collective-permute-start.1 = (f32[2,3,16,512]{3,2,1,0:T(8,128)}, f32[2,3,16,512]{3,2,1,0:T(8,128)S(1)}, u32[]{:S(2)}, u32[]{:S(2)}) collective-permute-start(f32[2,3,16,512]{3,2,1,0:T(8,128)} %maximum_select_fusion.3), channel_id=1, source_target_pairs={{0,32},{32,0},{1,33},{33,1},{2,34},{34,2},{3,35},{35,3},{4,36},{36... | collective-permute-start | bytes 589832 | tf_op jit(solution)/shard_map/ppermute | solution.py:24
  15.4 27.0 %collective-permute-start.2 = (bf16[2,384,1024]{2,1,0:T(8,128)(2,1)}, bf16[2,384,1024]{2,1,0:T(8,128)(2,1)}, u32[]{:S(2)}, u32[]{:S(2)}) collective-permute-start(bf16[2,384,1024]{2,1,0:T(8,128)(2,1)} %constant_dynamic-slice_fusion.7), channel_id=1, source_target_pairs={{0,1},{1,0},{2,3},{3,2},{4,5},{5,4},{6,7},{7,6},{8,9},{9,8},{10,11... | collective-permute-start | bytes 4718600 | tf_op jit(solution)/shard_map/ppermute | solution.py:24
  19.2 29.2 %collective-permute-start.3 = (bf16[2,384,1024]{2,1,0:T(8,128)(2,1)}, bf16[2,384,1024]{2,1,0:T(8,128)(2,1)}, u32[]{:S(2)}, u32[]{:S(2)}) collective-permute-start(bf16[2,384,1024]{2,1,0:T(8,128)(2,1)} %constant_dynamic-slice_fusion.5), channel_id=1, source_target_pairs={{0,1},{1,0},{2,3},{3,2},{4,5},{5,4},{6,7},{7,6},{8,9},{9,8},{10,11... | collective-permute-start | bytes 4718600 | tf_op jit(solution)/shard_map/ppermute | solution.py:24
  19.9 7.6 %collective-permute-start.16 = (f32[2,384]{1,0:T(2,128)S(1)}, f32[2,384]{1,0:T(2,128)S(1)}, u32[]{:S(2)}, u32[]{:S(2)}) collective-permute-start(f32[2,384]{1,0:T(2,128)S(1)} %get-tuple-element.112), channel_id=1, source_target_pairs={{0,1},{1,0},{2,3},{3,2},{4,5},{5,4},{6,7},{7,6},{8,9},{9,8},{10,11... | collective-permute-start | bytes 9224 | tf_op jit(solution)/shard_map/ppermute | solution.py:24
  24.4 6.8 %collective-permute-start.10 = (bf16[2,3,16,512]{3,2,1,0:T(8,128)(2,1)S(1)}, bf16[2,3,16,512]{3,2,1,0:T(8,128)(2,1)S(1)}, u32[]{:S(2)}, u32[]{:S(2)}) collective-permute-start(bf16[2,3,16,512]{3,2,1,0:T(8,128)(2,1)S(1)} %get-tuple-element.107), channel_id=1, source_target_pairs={{0,6},{2,0},{4,2},{6,4},{1,7},{3,1},{5,3},{7,5},{8,14},{10,8},{12,... | collective-permute-start | bytes 294920 | tf_op jit(solution)/shard_map/ppermute | solution.py:24
  27.0 8.0 %collective-permute-start.11 = (bf16[2,3,16,512]{3,2,1,0:T(8,128)(2,1)S(1)}, bf16[2,3,16,512]{3,2,1,0:T(8,128)(2,1)S(1)}, u32[]{:S(2)}, u32[]{:S(2)}) collective-permute-start(bf16[2,3,16,512]{3,2,1,0:T(8,128)(2,1)S(1)} %get-tuple-element.107), channel_id=1, source_target_pairs={{0,4},{2,6},{4,0},{6,2},{1,5},{3,7},{5,1},{7,3},{8,12},{10,14},{12... | collective-permute-start | bytes 294920 | tf_op jit(solution)/shard_map/ppermute | solution.py:24
  27.5 8.8 %collective-permute-start.12 = (bf16[2,3,16,512]{3,2,1,0:T(8,128)(2,1)S(1)}, bf16[2,3,16,512]{3,2,1,0:T(8,128)(2,1)S(1)}, u32[]{:S(2)}, u32[]{:S(2)}) collective-permute-start(bf16[2,3,16,512]{3,2,1,0:T(8,128)(2,1)S(1)} %get-tuple-element.107), channel_id=1, source_target_pairs={{0,2},{2,4},{4,6},{6,0},{1,3},{3,5},{5,7},{7,1},{8,10},{10,12},{12... | collective-permute-start | bytes 294920 | tf_op jit(solution)/shard_map/ppermute | solution.py:24
  31.2 5.9 %collective-permute-start.4 = (bf16[2,3,16,512]{3,2,1,0:T(8,128)(2,1)S(1)}, bf16[2,3,16,512]{3,2,1,0:T(8,128)(2,1)S(1)}, u32[]{:S(2)}, u32[]{:S(2)}) collective-permute-start(bf16[2,3,16,512]{3,2,1,0:T(8,128)(2,1)S(1)} %get-tuple-element.108), channel_id=1, source_target_pairs={{0,24},{8,0},{16,8},{24,16},{1,25},{9,1},{17,9},{25,17},{2,26},{10... | collective-permute-start | bytes 294920 | tf_op jit(solution)/shard_map/ppermute | solution.py:24
  34.9 5.0 %collective-permute-start.5 = (bf16[2,3,16,512]{3,2,1,0:T(8,128)(2,1)S(1)}, bf16[2,3,16,512]{3,2,1,0:T(8,128)(2,1)S(1)}, u32[]{:S(2)}, u32[]{:S(2)}) collective-permute-start(bf16[2,3,16,512]{3,2,1,0:T(8,128)(2,1)S(1)} %get-tuple-element.108), channel_id=1, source_target_pairs={{0,16},{8,24},{16,0},{24,8},{1,17},{9,25},{17,1},{25,9},{2,18},{10... | collective-permute-start | bytes 294920 | tf_op jit(solution)/shard_map/ppermute | solution.py:24
  36.2 6.0 %collective-permute-start.6 = (bf16[2,3,16,512]{3,2,1,0:T(8,128)(2,1)S(1)}, bf16[2,3,16,512]{3,2,1,0:T(8,128)(2,1)S(1)}, u32[]{:S(2)}, u32[]{:S(2)}) collective-permute-start(bf16[2,3,16,512]{3,2,1,0:T(8,128)(2,1)S(1)} %get-tuple-element.108), channel_id=1, source_target_pairs={{0,8},{8,16},{16,24},{24,0},{1,9},{9,17},{17,25},{25,1},{2,10},{10... | collective-permute-start | bytes 294920 | tf_op jit(solution)/shard_map/ppermute | solution.py:24
  37.1 12.9 %collective-permute-start.13 = (bf16[8,3,16,512]{3,2,1,0:T(8,128)(2,1)S(1)}, bf16[8,3,16,512]{3,2,1,0:T(8,128)(2,1)S(1)}, u32[]{:S(2)}, u32[]{:S(2)}) collective-permute-start(bf16[8,3,16,512]{3,2,1,0:T(8,128)(2,1)S(1)} %pad_maximum_fusion.2.refs_4_), channel_id=1, source_target_pairs={{0,24},{8,0},{16,8},{24,16},{1,25},{9,1},{17,9},{25,17},{2,26},{10... | collective-permute-start | bytes 1179656 | tf_op jit(solution)/shard_map/ppermute | solution.py:24
  39.9 14.4 %collective-permute-start.14 = (bf16[8,3,16,512]{3,2,1,0:T(8,128)(2,1)S(1)}, bf16[8,3,16,512]{3,2,1,0:T(8,128)(2,1)S(1)}, u32[]{:S(2)}, u32[]{:S(2)}) collective-permute-start(bf16[8,3,16,512]{3,2,1,0:T(8,128)(2,1)S(1)} %pad_maximum_fusion.2.refs_4_), channel_id=1, source_target_pairs={{0,16},{8,24},{16,0},{24,8},{1,17},{9,25},{17,1},{25,9},{2,18},{10... | collective-permute-start | bytes 1179656 | tf_op jit(solution)/shard_map/ppermute | solution.py:24
  42.3 18.6 %collective-permute-start.15 = (bf16[8,3,16,512]{3,2,1,0:T(8,128)(2,1)S(1)}, bf16[8,3,16,512]{3,2,1,0:T(8,128)(2,1)S(1)}, u32[]{:S(2)}, u32[]{:S(2)}) collective-permute-start(bf16[8,3,16,512]{3,2,1,0:T(8,128)(2,1)S(1)} %pad_maximum_fusion.2.refs_4_), channel_id=1, source_target_pairs={{0,8},{8,16},{16,24},{24,0},{1,9},{9,17},{17,25},{25,1},{2,10},{10... | collective-permute-start | bytes 1179656 | tf_op jit(solution)/shard_map/ppermute | solution.py:24
  42.4 19.8 %collective-permute-start.7 = (bf16[8,3,16,512]{3,2,1,0:T(8,128)(2,1)S(1)}, bf16[8,3,16,512]{3,2,1,0:T(8,128)(2,1)S(1)}, u32[]{:S(2)}, u32[]{:S(2)}) collective-permute-start(bf16[8,3,16,512]{3,2,1,0:T(8,128)(2,1)S(1)} %pad_maximum_fusion.1.refs_0_), channel_id=1, source_target_pairs={{0,6},{2,0},{4,2},{6,4},{1,7},{3,1},{5,3},{7,5},{8,14},{10,8},{12,... | collective-permute-start | bytes 1179656 | tf_op jit(solution)/shard_map/ppermute | solution.py:24
  48.4 13.8 %collective-permute-start.8 = (bf16[8,3,16,512]{3,2,1,0:T(8,128)(2,1)S(1)}, bf16[8,3,16,512]{3,2,1,0:T(8,128)(2,1)S(1)}, u32[]{:S(2)}, u32[]{:S(2)}) collective-permute-start(bf16[8,3,16,512]{3,2,1,0:T(8,128)(2,1)S(1)} %pad_maximum_fusion.1.refs_0_), channel_id=1, source_target_pairs={{0,4},{2,6},{4,0},{6,2},{1,5},{3,7},{5,1},{7,3},{8,12},{10,14},{12... | collective-permute-start | bytes 1179656 | tf_op jit(solution)/shard_map/ppermute | solution.py:24
  50.0 19.5 %collective-permute-start.9 = (bf16[8,3,16,512]{3,2,1,0:T(8,128)(2,1)S(1)}, bf16[8,3,16,512]{3,2,1,0:T(8,128)(2,1)S(1)}, u32[]{:S(2)}, u32[]{:S(2)}) collective-permute-start(bf16[8,3,16,512]{3,2,1,0:T(8,128)(2,1)S(1)} %pad_maximum_fusion.1.refs_0_), channel_id=1, source_target_pairs={{0,2},{2,4},{4,6},{6,0},{1,3},{3,5},{5,7},{7,1},{8,10},{10,12},{12... | collective-permute-start | bytes 1179656 | tf_op jit(solution)/shard_map/ppermute | solution.py:24
  54.3 111.0 %copy-start.1 = (bf16[4,384,1024]{2,1,0:T(8,128)(2,1)}, bf16[4,384,1024]{2,1,0:T(8,128)(2,1)S(1)}, u32[]{:S(2)}) copy-start(bf16[4,384,1024]{2,1,0:T(8,128)(2,1)S(1)} %get-tuple-element.74.kb.k2.vb.v2) | copy-start | bytes 9437188
  83.5 20.0 %copy-start.29 = (bf16[8,3,16,512]{3,2,1,0:T(8,128)(2,1)S(1)}, bf16[8,3,16,512]{3,2,1,0:T(8,128)(2,1)}, u32[]{:S(2)}) copy-start(bf16[8,3,16,512]{3,2,1,0:T(8,128)(2,1)} %get-tuple-element.61) | copy-start | bytes 1179652
  83.5 27.3 %copy-start.28 = (bf16[8,3,16,512]{3,2,1,0:T(8,128)(2,1)S(1)}, bf16[8,3,16,512]{3,2,1,0:T(8,128)(2,1)}, u32[]{:S(2)}) copy-start(bf16[8,3,16,512]{3,2,1,0:T(8,128)(2,1)} %get-tuple-element.65) | copy-start | bytes 1179652
  83.5 8.5 %collective-permute-start.17 = (bf16[8,3,16,512]{3,2,1,0:T(8,128)(2,1)}, bf16[8,3,16,512]{3,2,1,0:T(8,128)(2,1)S(1)}, u32[]{:S(2)}, u32[]{:S(2)}) collective-permute-start(bf16[8,3,16,512]{3,2,1,0:T(8,128)(2,1)} %get-tuple-element.59), channel_id=1, source_target_pairs={{0,6},{2,0},{4,2},{6,4},{1,7},{3,1},{5,3},{7,5},{8,14},{10,8},{12,... | collective-permute-start | bytes 1179656 | tf_op jit(solution)/shard_map/ppermute | solution.py:24
  84.9 35.3 %collective-permute-start.29 = (bf16[2,384,1024]{2,1,0:T(8,128)(2,1)S(1)}, bf16[2,384,1024]{2,1,0:T(8,128)(2,1)S(1)}, u32[]{:S(2)}, u32[]{:S(2)}) collective-permute-start(bf16[2,384,1024]{2,1,0:T(8,128)(2,1)S(1)} %constant_dynamic-slice_fusion.2), channel_id=1, source_target_pairs={{0,1},{1,0},{2,3},{3,2},{4,5},{5,4},{6,7},{7,6},{8,9},{9,8},{10,11... | collective-permute-start | bytes 4718600 | tf_op jit(solution)/shard_map/ppermute | solution.py:24
  88.0 11.8 %collective-permute-start.23 = (bf16[8,3,16,512]{3,2,1,0:T(8,128)(2,1)S(1)}, bf16[8,3,16,512]{3,2,1,0:T(8,128)(2,1)S(1)}, u32[]{:S(2)}, u32[]{:S(2)}) collective-permute-start(bf16[8,3,16,512]{3,2,1,0:T(8,128)(2,1)S(1)} %copy-done.40), channel_id=1, source_target_pairs={{0,24},{8,0},{16,8},{24,16},{1,25},{9,1},{17,9},{25,17},{2,26},{10... | collective-permute-start | bytes 1179656 | tf_op jit(solution)/shard_map/ppermute | solution.py:24
  92.1 11.3 %collective-permute-start.18 = (bf16[8,3,16,512]{3,2,1,0:T(8,128)(2,1)S(1)}, bf16[8,3,16,512]{3,2,1,0:T(8,128)(2,1)S(1)}, u32[]{:S(2)}, u32[]{:S(2)}) collective-permute-start(bf16[8,3,16,512]{3,2,1,0:T(8,128)(2,1)S(1)} %add_convert_fusion.3), channel_id=1, source_target_pairs={{0,6},{2,0},{4,2},{6,4},{1,7},{3,1},{5,3},{7,5},{8,14},{10,8},{12,... | collective-permute-start | bytes 1179656 | tf_op jit(solution)/shard_map/ppermute | solution.py:24
  99.9 10.8 %collective-permute-start.24 = (bf16[8,3,16,512]{3,2,1,0:T(8,128)(2,1)S(1)}, bf16[8,3,16,512]{3,2,1,0:T(8,128)(2,1)S(1)}, u32[]{:S(2)}, u32[]{:S(2)}) collective-permute-start(bf16[8,3,16,512]{3,2,1,0:T(8,128)(2,1)S(1)} %add_convert_fusion.1), channel_id=1, source_target_pairs={{0,24},{8,0},{16,8},{24,16},{1,25},{9,1},{17,9},{25,17},{2,26},{10... | collective-permute-start | bytes 1179656 | tf_op jit(solution)/shard_map/ppermute | solution.py:24
  104.3 25.3 %collective-permute-start.19 = (bf16[8,3,16,512]{3,2,1,0:T(8,128)(2,1)}, bf16[8,3,16,512]{3,2,1,0:T(8,128)(2,1)}, u32[]{:S(2)}, u32[]{:S(2)}) collective-permute-start(bf16[8,3,16,512]{3,2,1,0:T(8,128)(2,1)} %add_convert_fusion.2), channel_id=1, source_target_pairs={{0,6},{2,0},{4,2},{6,4},{1,7},{3,1},{5,3},{7,5},{8,14},{10,8},{12,... | collective-permute-start | bytes 1179656 | tf_op jit(solution)/shard_map/ppermute | solution.py:24
  110.9 18.7 %copy-start.27 = (bf16[8,3,16,512]{3,2,1,0:T(8,128)(2,1)S(1)}, bf16[8,3,16,512]{3,2,1,0:T(8,128)(2,1)}, u32[]{:S(2)}) copy-start(bf16[8,3,16,512]{3,2,1,0:T(8,128)(2,1)} %get-tuple-element.62) | copy-start | bytes 1179652
  110.9 19.9 %copy-start.26 = (bf16[8,3,16,512]{3,2,1,0:T(8,128)(2,1)S(1)}, bf16[8,3,16,512]{3,2,1,0:T(8,128)(2,1)}, u32[]{:S(2)}) copy-start(bf16[8,3,16,512]{3,2,1,0:T(8,128)(2,1)} %get-tuple-element.66) | copy-start | bytes 1179652
  110.9 19.9 %collective-permute-start.25 = (bf16[8,3,16,512]{3,2,1,0:T(8,128)(2,1)S(1)}, bf16[8,3,16,512]{3,2,1,0:T(8,128)(2,1)S(1)}, u32[]{:S(2)}, u32[]{:S(2)}) collective-permute-start(bf16[8,3,16,512]{3,2,1,0:T(8,128)(2,1)S(1)} %add_convert_fusion), channel_id=1, source_target_pairs={{0,24},{8,0},{16,8},{24,16},{1,25},{9,1},{17,9},{25,17},{2,26},{10... | collective-permute-start | bytes 1179656 | tf_op jit(solution)/shard_map/ppermute | solution.py:24
  114.4 201.3 %collective-permute-start.48 = (bf16[4,384,1024]{2,1,0:T(8,128)(2,1)}, bf16[4,384,1024]{2,1,0:T(8,128)(2,1)}, u32[]{:S(2)}, u32[]{:S(2)}) collective-permute-start(bf16[4,384,1024]{2,1,0:T(8,128)(2,1)} %get-tuple-element.75.kb.k2.vb.v2), channel_id=1, source_target_pairs={{30,32},{62,0},{31,33},{63,1},{94,96},{126,64},{95,97},{127,65}} | collective-permute-start | bytes 9437192 | tf_op jit(solution)/shard_map/ppermute | solution.py:428
  115.7 203.1 %collective-permute-start.49 = (bf16[4,384,1024]{2,1,0:T(8,128)(2,1)}, bf16[4,384,1024]{2,1,0:T(8,128)(2,1)}, u32[]{:S(2)}, u32[]{:S(2)}) collective-permute-start(bf16[4,384,1024]{2,1,0:T(8,128)(2,1)} %get-tuple-element.75.kb.k2.vb.v2), channel_id=1, source_target_pairs={{0,2},{2,4},{4,6},{6,8},{8,10},{10,12},{12,14},{14,16},{16,18},{18... | collective-permute-start | bytes 9437192 | tf_op jit(solution)/shard_map/ppermute | solution.py:427
  130.7 7.0 %collective-permute-start.20 = (bf16[2,3,16,512]{3,2,1,0:T(8,128)(2,1)S(1)}, bf16[2,3,16,512]{3,2,1,0:T(8,128)(2,1)S(1)}, u32[]{:S(2)}, u32[]{:S(2)}) collective-permute-start(bf16[2,3,16,512]{3,2,1,0:T(8,128)(2,1)S(1)} %slice.163), channel_id=1, source_target_pairs={{0,24},{8,0},{16,8},{24,16},{1,25},{9,1},{17,9},{25,17},{2,26},{10... | collective-permute-start | bytes 294920 | tf_op jit(solution)/shard_map/ppermute | solution.py:24
  131.0 8.4 %collective-permute-start.26 = (bf16[2,3,16,512]{3,2,1,0:T(8,128)(2,1)S(1)}, bf16[2,3,16,512]{3,2,1,0:T(8,128)(2,1)S(1)}, u32[]{:S(2)}, u32[]{:S(2)}) collective-permute-start(bf16[2,3,16,512]{3,2,1,0:T(8,128)(2,1)S(1)} %slice.162), channel_id=1, source_target_pairs={{0,6},{2,0},{4,2},{6,4},{1,7},{3,1},{5,3},{7,5},{8,14},{10,8},{12,... | collective-permute-start | bytes 294920 | tf_op jit(solution)/shard_map/ppermute | solution.py:24
  137.7 4.8 %collective-permute-start.21 = (bf16[2,3,16,512]{3,2,1,0:T(8,128)(2,1)S(1)}, bf16[2,3,16,512]{3,2,1,0:T(8,128)(2,1)S(1)}, u32[]{:S(2)}, u32[]{:S(2)}) collective-permute-start(bf16[2,3,16,512]{3,2,1,0:T(8,128)(2,1)S(1)} %fusion.7), channel_id=1, source_target_pairs={{0,24},{8,0},{16,8},{24,16},{1,25},{9,1},{17,9},{25,17},{2,26},{10... | collective-permute-start | bytes 294920 | tf_op jit(solution)/shard_map/ppermute | solution.py:24
  139.4 168.1 %copy-start.39 = (f32[2048]{0:T(1024)S(1)}, f32[2048]{0:T(1024)}, u32[]{:S(2)}) copy-start(f32[2048]{0:T(1024)} %param.15) | copy-start | bytes 24580
  139.4 4.7 %collective-permute-start.27 = (bf16[2,3,16,512]{3,2,1,0:T(8,128)(2,1)S(1)}, bf16[2,3,16,512]{3,2,1,0:T(8,128)(2,1)S(1)}, u32[]{:S(2)}, u32[]{:S(2)}) collective-permute-start(bf16[2,3,16,512]{3,2,1,0:T(8,128)(2,1)S(1)} %fusion.4), channel_id=1, source_target_pairs={{0,6},{2,0},{4,2},{6,4},{1,7},{3,1},{5,3},{7,5},{8,14},{10,8},{12,... | collective-permute-start | bytes 294920 | tf_op jit(solution)/shard_map/ppermute | solution.py:24
  142.5 4.7 %collective-permute-start.22 = (bf16[2,3,16,512]{3,2,1,0:T(8,128)(2,1)S(1)}, bf16[2,3,16,512]{3,2,1,0:T(8,128)(2,1)S(1)}, u32[]{:S(2)}, u32[]{:S(2)}) collective-permute-start(bf16[2,3,16,512]{3,2,1,0:T(8,128)(2,1)S(1)} %fusion.6), channel_id=1, source_target_pairs={{0,24},{8,0},{16,8},{24,16},{1,25},{9,1},{17,9},{25,17},{2,26},{10... | collective-permute-start | bytes 294920 | tf_op jit(solution)/shard_map/ppermute | solution.py:24
  144.1 5.4 %collective-permute-start.28 = (bf16[2,3,16,512]{3,2,1,0:T(8,128)(2,1)S(1)}, bf16[2,3,16,512]{3,2,1,0:T(8,128)(2,1)S(1)}, u32[]{:S(2)}, u32[]{:S(2)}) collective-permute-start(bf16[2,3,16,512]{3,2,1,0:T(8,128)(2,1)S(1)} %fusion.3), channel_id=1, source_target_pairs={{0,6},{2,0},{4,2},{6,4},{1,7},{3,1},{5,3},{7,5},{8,14},{10,8},{12,... | collective-permute-start | bytes 294920 | tf_op jit(solution)/shard_map/ppermute | solution.py:24
  149.6 9.0 %collective-permute-start.30 = (bf16[2,2,3,16,512]{4,3,2,1,0:T(8,128)(2,1)S(1)}, bf16[2,2,3,16,512]{4,3,2,1,0:T(8,128)(2,1)}, u32[]{:S(2)}, u32[]{:S(2)}) collective-permute-start(bf16[2,2,3,16,512]{4,3,2,1,0:T(8,128)(2,1)S(1)} %pad_maximum_fusion.6), channel_id=1, source_target_pairs={{0,32},{32,0},{1,33},{33,1},{2,34},{34,2},{3,35},{35,3},{4,36},{36... | collective-permute-start | bytes 589832 | tf_op jit(solution)/shard_map/ppermute | solution.py:24
  151.1 8.7 %collective-permute-start.31 = (f32[2,8,384]{2,1,0:T(8,128)}, f32[2,8,384]{2,1,0:T(8,128)S(1)}, u32[]{:S(2)}, u32[]{:S(2)}) collective-permute-start(f32[2,8,384]{2,1,0:T(8,128)} %rev.10), channel_id=1, source_target_pairs={{0,1},{1,0},{64,65},{65,64},{2,3},{3,2},{66,67},{67,66},{4,5},{5,4... | collective-permute-start | bytes 73736 | tf_op jit(solution)/shard_map/ppermute | solution.py:371
  157.4 7.9 %collective-permute-start.33 = (f32[2,8,384]{2,1,0:T(8,128)}, f32[2,8,384]{2,1,0:T(8,128)S(1)}, u32[]{:S(2)}, u32[]{:S(2)}) collective-permute-start(f32[2,8,384]{2,1,0:T(8,128)} %rev.10), channel_id=1, source_target_pairs={{0,65},{65,0},{1,64},{64,1},{2,67},{67,2},{3,66},{66,3},{4,69},{69... | collective-permute-start | bytes 73736 | tf_op jit(solution)/shard_map/ppermute | solution.py:373
  158.6 6.7 %collective-permute-start.32 = (f32[2,8,384]{2,1,0:T(8,128)}, f32[2,8,384]{2,1,0:T(8,128)S(1)}, u32[]{:S(2)}, u32[]{:S(2)}) collective-permute-start(f32[2,8,384]{2,1,0:T(8,128)} %get-tuple-element.82.p0), channel_id=1, source_target_pairs={{0,64},{64,0},{1,65},{65,1},{2,66},{66,2},{3,67},{67,3},{4,68},{68... | collective-permute-start | bytes 73736 | tf_op jit(solution)/shard_map/ppermute | solution.py:372
  159.8 243.2 %collective-permute-start.47 = (bf16[4,384,1024]{2,1,0:T(8,128)(2,1)S(1)}, bf16[4,384,1024]{2,1,0:T(8,128)(2,1)}, u32[]{:S(2)}, u32[]{:S(2)}) collective-permute-start(bf16[4,384,1024]{2,1,0:T(8,128)(2,1)S(1)} %get-tuple-element.74.kb.k2.vb.v2), channel_id=1, source_target_pairs={{0,2},{2,4},{4,6},{6,8},{8,10},{10,12},{12,14},{14,16},{16,18},{18... | collective-permute-start | bytes 9437192 | tf_op jit(solution)/shard_map/ppermute | solution.py:427
  166.5 236.5 %collective-permute-start.46 = (bf16[4,384,1024]{2,1,0:T(8,128)(2,1)S(1)}, bf16[4,384,1024]{2,1,0:T(8,128)(2,1)}, u32[]{:S(2)}, u32[]{:S(2)}) collective-permute-start(bf16[4,384,1024]{2,1,0:T(8,128)(2,1)S(1)} %get-tuple-element.74.kb.k2.vb.v2), channel_id=1, source_target_pairs={{30,32},{31,33},{94,96},{95,97}} | collective-permute-start | bytes 9437192 | tf_op jit(solution)/shard_map/ppermute | solution.py:441
  170.7 3.9 collective-permute-start.40
  174.6 103.0 %collective-permute-start.34 = (bf16[2,3,16,512]{3,2,1,0:T(8,128)(2,1)S(1)}, bf16[2,3,16,512]{3,2,1,0:T(8,128)(2,1)S(1)}, u32[]{:S(2)}, u32[]{:S(2)}) collective-permute-start(bf16[2,3,16,512]{3,2,1,0:T(8,128)(2,1)S(1)} %get-tuple-element.106), channel_id=1, source_target_pairs={{0,24},{8,0},{16,8},{24,16},{1,25},{9,1},{17,9},{25,17},{2,26},{10... | collective-permute-start | bytes 294920 | tf_op jit(solution)/shard_map/ppermute | solution.py:24
  277.7 3.5 collective-permute-start.41
  281.1 5.5 %collective-permute-start.35 = (bf16[2,3,16,512]{3,2,1,0:T(8,128)(2,1)S(1)}, bf16[2,3,16,512]{3,2,1,0:T(8,128)(2,1)S(1)}, u32[]{:S(2)}, u32[]{:S(2)}) collective-permute-start(bf16[2,3,16,512]{3,2,1,0:T(8,128)(2,1)S(1)} %collective-permute-done.34), channel_id=1, source_target_pairs={{0,24},{8,0},{16,8},{24,16},{1,25},{9,1},{17,9},{25,17},{2,26},{10... | collective-permute-start | bytes 294920 | tf_op jit(solution)/shard_map/ppermute | solution.py:24
  286.6 3.8 collective-permute-start.42
  290.4 5.2 %collective-permute-start.36 = (bf16[2,3,16,512]{3,2,1,0:T(8,128)(2,1)S(1)}, bf16[2,3,16,512]{3,2,1,0:T(8,128)(2,1)S(1)}, u32[]{:S(2)}, u32[]{:S(2)}) collective-permute-start(bf16[2,3,16,512]{3,2,1,0:T(8,128)(2,1)S(1)} %collective-permute-done.35), channel_id=1, source_target_pairs={{0,24},{8,0},{16,8},{24,16},{1,25},{9,1},{17,9},{25,17},{2,26},{10... | collective-permute-start | bytes 294920 | tf_op jit(solution)/shard_map/ppermute | solution.py:24
  294.0 28.7 %copy-start.12 = (bf16[8,3,16,512]{3,2,1,0:T(8,128)(2,1)}, bf16[8,3,16,512]{3,2,1,0:T(8,128)(2,1)S(1)}, u32[]{:S(2)}) copy-start(bf16[8,3,16,512]{3,2,1,0:T(8,128)(2,1)S(1)} %pad_maximum_fusion.4.refs_4_) | copy-start | bytes 1179652
  295.6 9.2 %collective-permute-start.43 = (bf16[8,3,16,512]{3,2,1,0:T(8,128)(2,1)S(1)}, bf16[8,3,16,512]{3,2,1,0:T(8,128)(2,1)}, u32[]{:S(2)}, u32[]{:S(2)}) collective-permute-start(bf16[8,3,16,512]{3,2,1,0:T(8,128)(2,1)S(1)} %pad_maximum_fusion.4.refs_4_), channel_id=1, source_target_pairs={{0,24},{8,0},{16,8},{24,16},{1,25},{9,1},{17,9},{25,17},{2,26},{10... | collective-permute-start | bytes 1179656 | tf_op jit(solution)/shard_map/ppermute | solution.py:24
  304.8 7.7 %collective-permute-start.37 = (bf16[8,3,16,512]{3,2,1,0:T(8,128)(2,1)}, bf16[8,3,16,512]{3,2,1,0:T(8,128)(2,1)}, u32[]{:S(2)}, u32[]{:S(2)}) collective-permute-start(bf16[8,3,16,512]{3,2,1,0:T(8,128)(2,1)} %pad_maximum_fusion.3.refs_0_), channel_id=1, source_target_pairs={{0,6},{2,0},{4,2},{6,4},{1,7},{3,1},{5,3},{7,5},{8,14},{10,8},{12,... | collective-permute-start | bytes 1179656 | tf_op jit(solution)/shard_map/ppermute | solution.py:24
  312.5 41.5 %collective-permute-start.44 = (bf16[8,3,16,512]{3,2,1,0:T(8,128)(2,1)}, bf16[8,3,16,512]{3,2,1,0:T(8,128)(2,1)S(1)}, u32[]{:S(2)}, u32[]{:S(2)}) collective-permute-start(bf16[8,3,16,512]{3,2,1,0:T(8,128)(2,1)} %collective-permute-done.43.refs_5_), channel_id=1, source_target_pairs={{0,24},{8,0},{16,8},{24,16},{1,25},{9,1},{17,9},{25,17},{2,26},{10... | collective-permute-start | bytes 1179656 | tf_op jit(solution)/shard_map/ppermute | solution.py:24
  315.7 38.3 %collective-permute-start.38 = (bf16[8,3,16,512]{3,2,1,0:T(8,128)(2,1)}, bf16[8,3,16,512]{3,2,1,0:T(8,128)(2,1)S(1)}, u32[]{:S(2)}, u32[]{:S(2)}) collective-permute-start(bf16[8,3,16,512]{3,2,1,0:T(8,128)(2,1)} %collective-permute-done.37.refs_1_), channel_id=1, source_target_pairs={{0,6},{2,0},{4,2},{6,4},{1,7},{3,1},{5,3},{7,5},{8,14},{10,8},{12,... | collective-permute-start | bytes 1179656 | tf_op jit(solution)/shard_map/ppermute | solution.py:24
  340.3 36.6 %collective-permute-start.53 = (bf16[384,1024]{1,0:T(8,128)(2,1)}, bf16[384,1024]{1,0:T(8,128)(2,1)}, u32[]{:S(2)}, u32[]{:S(2)}) collective-permute-start(bf16[384,1024]{1,0:T(8,128)(2,1)} %get-tuple-element.86), channel_id=1, source_target_pairs={{0,1},{1,0},{2,3},{3,2},{4,5},{5,4},{6,7},{7,6},{8,9},{9,8},{10,11... | collective-permute-start | bytes 2359304 | tf_op jit(solution)/shard_map/ppermute | solution.py:24
  354.0 10.6 %collective-permute-start.45 = (bf16[8,3,16,512]{3,2,1,0:T(8,128)(2,1)S(1)}, bf16[8,3,16,512]{3,2,1,0:T(8,128)(2,1)S(1)}, u32[]{:S(2)}, u32[]{:S(2)}) collective-permute-start(bf16[8,3,16,512]{3,2,1,0:T(8,128)(2,1)S(1)} %collective-permute-done.44.refs_6_), channel_id=1, source_target_pairs={{0,24},{8,0},{16,8},{24,16},{1,25},{9,1},{17,9},{25,17},{2,26},{10... | collective-permute-start | bytes 1179656 | tf_op jit(solution)/shard_map/ppermute | solution.py:24
  354.0 10.6 %collective-permute-start.39 = (bf16[8,3,16,512]{3,2,1,0:T(8,128)(2,1)S(1)}, bf16[8,3,16,512]{3,2,1,0:T(8,128)(2,1)S(1)}, u32[]{:S(2)}, u32[]{:S(2)}) collective-permute-start(bf16[8,3,16,512]{3,2,1,0:T(8,128)(2,1)S(1)} %collective-permute-done.38.refs_2_), channel_id=1, source_target_pairs={{0,6},{2,0},{4,2},{6,4},{1,7},{3,1},{5,3},{7,5},{8,14},{10,8},{12,... | collective-permute-start | bytes 1179656 | tf_op jit(solution)/shard_map/ppermute | solution.py:24
  374.9 43.7 %collective-permute-start.50 = (f32[2,8,384]{2,1,0:T(8,128)S(1)}, f32[2,8,384]{2,1,0:T(8,128)S(1)}, u32[]{:S(2)}, u32[]{:S(2)}) collective-permute-start(f32[2,8,384]{2,1,0:T(8,128)S(1)} %rev.11), channel_id=1, source_target_pairs={{0,1},{1,0},{64,65},{65,64},{2,3},{3,2},{66,67},{67,66},{4,5},{5,4... | collective-permute-start | bytes 73736 | tf_op jit(solution)/shard_map/ppermute | solution.py:371
  375.9 42.8 %collective-permute-start.52 = (f32[2,8,384]{2,1,0:T(8,128)S(1)}, f32[2,8,384]{2,1,0:T(8,128)S(1)}, u32[]{:S(2)}, u32[]{:S(2)}) collective-permute-start(f32[2,8,384]{2,1,0:T(8,128)S(1)} %rev.11), channel_id=1, source_target_pairs={{0,65},{65,0},{1,64},{64,1},{2,67},{67,2},{3,66},{66,3},{4,69},{69... | collective-permute-start | bytes 73736 | tf_op jit(solution)/shard_map/ppermute | solution.py:373
  376.9 41.8 %collective-permute-start.51 = (f32[2,8,384]{2,1,0:T(8,128)}, f32[2,8,384]{2,1,0:T(8,128)S(1)}, u32[]{:S(2)}, u32[]{:S(2)}) collective-permute-start(f32[2,8,384]{2,1,0:T(8,128)} %get-tuple-element.77.p0), channel_id=1, source_target_pairs={{0,64},{64,0},{1,65},{65,1},{2,66},{66,2},{3,67},{67,3},{4,68},{68... | collective-permute-start | bytes 73736 | tf_op jit(solution)/shard_map/ppermute | solution.py:372
  377.3 25.8 %copy-start = (bf16[4,384,1024]{2,1,0:T(8,128)(2,1)S(1)}, bf16[4,384,1024]{2,1,0:T(8,128)(2,1)}, u32[]{:S(2)}) copy-start(bf16[4,384,1024]{2,1,0:T(8,128)(2,1)} %broadcast_select_fusion.k0.ka.v0.va) | copy-start | bytes 9437188
  425.5 3.9 collective-permute-start.54
  426.5 2.2 collective-permute-start.55
  (33 other events, 216.8 us)
where the time goes:
time: 458 us; the launch traced here: 456 us
  starting transfers between devices  219 us (48%)
  Pallas kernels  116 us (25%)
  waiting for transfers between devices  76.3 us (17%)
  local copies, waits for them, and re-layouts  23.4 us (5%)
  other arithmetic  20.5 us (4%)
    ppermute x46, starting transfers between devices, shift(): lax.ppermute(value, axis, [(i, (i + steps) % count) for i in range(count)])  195 us
    ppermute x46, waiting for transfers between devices, shift(): lax.ppermute(value, axis, [(i, (i + steps) % count) for i in range(count)])  76.3 us
    pallas_call x2, Pallas kernels, place(): pl.pallas_call(functools.partial(place_kernel, c), name='place', out_shap...  51.3 us
    pallas_call x2, Pallas kernels, attention(): pl.pallas_call(functools.partial(attention_kernel, c), name='window_atten...  23.6 us
    pallas_call x2, Pallas kernels, fast_apply(): pl.pallas_call(apply_kernel, name='fast_apply', out_shape=[jax.ShapeDtype...  16.3 us
    pallas_call x1, Pallas kernels, compute_grads(): pl.pallas_call(grads_kernel, name='fast_grads', out_shape=[jax.ShapeDtype...  13.1 us
    pallas_call x2, Pallas kernels, finish(): pl.pallas_call(finish_kernel, name='finish', out_shape=[jax.ShapeDtypeStr...  11.3 us
    ppermute x2, starting transfers between devices, on_device(): halo.append(lax.ppermute(pair[c], chips, row))  10.1 us
  transfers between devices with their start and end apart: 56, of which 25 were waited for; matrix products, arithmetic and copies ran while one was open for 7% of the time, Pallas kernels for 16%

commit v1 on v0

--- a/solution.py
+++ b/solution.py
@@ -159,7 +159,9 @@
     idx = (s_ref[1], s_ref[2], s_ref[3])
     load_weights(pieces, w_vmem, sem, idx, head)
     gate, up, down = w_vmem[head, 0], w_vmem[head, 1], w_vmem[head, 2]
+    core = s_ref[0]
     for j, q_ref in enumerate((q_own, q_rec)):
+        block = core if j == 0 else 1 - core
         q = q_ref[0]
         g = dot(q, gate, NN)
         u = dot(q, up, NN)
@@ -170,12 +172,12 @@
         power = jnp.transpose(jnp.broadcast_to(power, (TOK, 128)))[:8]
 
         @pl.when(head == 0)
-        def _(j=j, power=power):
-            pow_ref[j] = power
+        def _(block=block, power=power):
+            pow_ref[block] = power
 
         @pl.when(head == 1)
-        def _(j=j, power=power):
-            pow_ref[j] += power
+        def _(block=block, power=power):
+            pow_ref[block] += power
 
 
 def fast_apply(c, scal, pieces, q, q_rec):
@@ -255,66 +257,61 @@
     )(scal, q, q_rec, *(before, before, mine, mine) * 2)
 
 
-def finish_kernel(s_ref, fast_ref, p0, p1, p2, p3, gain_ref, att_ref, *refs):
-    own_ref, rec_ref = refs[-2:]
-    total = p0[...] + p1[...] + p2[...] + p3[...]
+def finish_kernel(count, s_ref, fast_ref, *refs):
+    powers, (gain_ref, att_ref), out_ref = refs[:count], refs[count : count + 2], refs[-1]
+    total = sum(p[0] for p in powers[1:]) + powers[0][0]
     rs = lax.rsqrt(total * (1.0 / 4096.0) + NORM_EPS)
-    for j in range(2):
-        col = jnp.transpose(rs[j])[:, :1]
-        out = (fast_ref[j] * gain_ref[...] * col + att_ref[j]).astype(bf16)
-        if j == 0:
-            own_ref[0] = out
-        else:
-            rec_ref[...] = out
+    col = jnp.transpose(rs)[:, :1]
+    out = (fast_ref[0] * gain_ref[...] * col + att_ref[0]).astype(bf16)
+    out_ref[...] = out.reshape(out_ref.shape)
 
 
 ROWS = 128
 
 
-def finish(c, scal, fast, powers, gain, att, layer):
-    both = pl.BlockSpec((2, ROWS, 2 * DH), lambda i, s: (0, i, 0))
-    power = pl.BlockSpec((2, 8, ROWS), lambda i, s: (0, 0, i))
+def finish(c, j, scal, fast, powers, gain, att, layer=None):
+    one = pl.BlockSpec((1, ROWS, 2 * DH), lambda i, s: (j, i, 0))
+    block = (lambda s: s[0]) if j == 0 else (lambda s: 1 - s[0])
+    power = pl.BlockSpec((1, 8, ROWS), lambda i, s: (block(s), 0, i))
     more = [] if layer is None else [layer]
+    if j == 0:
+        shape = (2, TOK, 4 * DH)
+        spec = pl.BlockSpec((1, ROWS, 2 * DH), lambda i, s: (c, i, s[0]))
+    else:
+        shape = (TOK, 2 * DH)
+        spec = pl.BlockSpec((ROWS, 2 * DH), lambda i, s: (i, 0))
+    count = len(powers)
     return pl.pallas_call(
-        finish_kernel,
+        functools.partial(finish_kernel, count),
         name="finish",
-        out_shape=[
-            jax.ShapeDtypeStruct((2, TOK, 4 * DH), bf16),
-            jax.ShapeDtypeStruct((TOK, 2 * DH), bf16),
-        ],
+        out_shape=jax.ShapeDtypeStruct(shape, bf16),
         grid_spec=pltpu.PrefetchScalarGridSpec(
             num_scalar_prefetch=1,
             grid=(TOK // ROWS,),
-            in_specs=[both] + [power] * 4 + [pl.BlockSpec((1, 2 * DH), lambda i, s: (0, 0)), both]
+            in_specs=[one] + [power] * count
+            + [pl.BlockSpec((1, 2 * DH), lambda i, s: (0, 0)), one]
             + [ANY] * len(more),
-            out_specs=[
-                pl.BlockSpec((1, ROWS, 2 * DH), lambda i, s: (c, i, s[0])),
-                pl.BlockSpec((ROWS, 2 * DH), lambda i, s: (i, 0)),
-            ],
+            out_specs=spec,
         ),
-        input_output_aliases={8: 0} if more else {},
+        input_output_aliases={count + 4: 0} if more else {},
         compiler_params=cparams(),
     )(scal, fast, *powers, gain, att, *more)
 
 
-def place_kernel(c, s_ref, arrived_ref, layer_ref, out_ref, sem):
-    column = pl.multiple_of((1 - s_ref[0]) * 2 * DH, 2 * DH)
-    copy = pltpu.make_async_copy(arrived_ref, out_ref.at[c, :, pl.ds(column, 2 * DH)], sem)
-    copy.start()
-    copy.wait()
+def place_kernel(s_ref, arrived_ref, layer_ref, out_ref):
+    out_ref[0] = arrived_ref[...]
 
 
 def place(c, scal, arrived, layer):
     return pl.pallas_call(
-        functools.partial(place_kernel, c),
+        place_kernel,
         name="place",
         out_shape=jax.ShapeDtypeStruct((2, TOK, 4 * DH), bf16),
         grid_spec=pltpu.PrefetchScalarGridSpec(
             num_scalar_prefetch=1,
-            grid=(1,),
-            in_specs=[ANY, ANY],
-            out_specs=ANY,
-            scratch_shapes=[pltpu.SemaphoreType.DMA(())],
+            grid=(3,),
+            in_specs=[pl.BlockSpec((TOK // 3, 2 * DH), lambda i, s: (i, 0)), ANY],
+            out_specs=pl.BlockSpec((1, TOK // 3, 2 * DH), lambda i, s: (c, i, 1 - s[0])),
         ),
         input_output_aliases={2: 0},
         compiler_params=cparams(),
@@ -364,14 +361,13 @@
     return jnp.stack(now)
 
 
-def power_parts(power):
-    flat = ("heads", "core")
-    swapped = power[::-1]
-    return [
-        lax.ppermute(swapped, flat, [(0, 1), (1, 0), (2, 3), (3, 2)]),
-        lax.ppermute(power, flat, [(0, 2), (2, 0), (1, 3), (3, 1)]),
-        lax.ppermute(swapped, flat, [(0, 3), (3, 0), (1, 2), (2, 1)]),
-    ]
+CORES = [(0, 1), (1, 0), (2, 3), (3, 2)]
+HALVES = [(0, 2), (2, 0), (1, 3), (3, 1)]
+ACROSS = [(0, 3), (3, 0), (1, 2), (2, 1)]
+
+
+def with_parts(power, pairs):
+    return [power] + [lax.ppermute(power, ("heads", "core"), p) for p in pairs]
 
 
 def on_device(queries, key_rows, value_rows, step_rates, w_gate, w_up, w_down, out_gain):
@@ -411,8 +407,7 @@
     rates = jnp.stack([r_own, r_rec], axis=1)[..., None]
 
     chips = ("yh", "z", "x")
-    row = [(i, (i + 1) % 32) for i in range(32) if i % 16 != 15]
-    turn = [(15, 16), (31, 0)]
+    row = [(i, (i + 1) % 32) for i in range(32)]
     pair = [
         jnp.where(
             core == 0,
@@ -422,23 +417,22 @@
         for c in range(2)
     ]
     pair[0], pair[1], *pieces = lax.optimization_barrier((pair[0], pair[1], *pieces))
-    halo = []
-    for c in range(2):
-        halo.append(lax.ppermute(pair[c], chips, row))
-    turned0 = lax.ppermute(pair[0], chips, turn)
+    halo0 = lax.ppermute(pair[0], chips, row)
+    halo1 = lax.ppermute(pair[1], chips, [p for p in row if p[0] % 16 != 15])
 
     slabs = compute_grads(scal, pieces, key_rows, value_rows, k_rec, v_rec, rates)
     fast0, pow0 = fast_apply(0, scal, pieces, queries, q_rec)
     half_sums = scatter_rings(slabs)
+    pow0 = sum(with_parts(pow0, (CORES,)))
     half_sums, pow0 = lax.optimization_barrier((half_sums, pow0))
     other_sums = shift(half_sums, "yh", 1)
-    powers0 = [pow0] + power_parts(pow0)
+    powers0 = with_parts(pow0, (HALVES,))
     grad_both = half_sums.astype(f32) + other_sums[:, ::-1].astype(f32)
     grad_both, pair1, *powers0 = lax.optimization_barrier((grad_both, pair[1], *powers0))
     new_both = both - grad_both
     new16 = new_both[:, 0]
     pieces2 = gather_rings(new_both.astype(bf16))
-    turned1 = lax.ppermute(pair1, chips, turn[:1])
+    turned1 = lax.ppermute(pair1, chips, [(15, 16)])
     own_rows = lax.dynamic_slice_in_dim(new16, core * 8, 8, 2)
     their_rows = shift(lax.dynamic_slice_in_dim(new16, (1 - core) * 8, 8, 2), "core", 1)
     new_all = jnp.where(
@@ -448,27 +442,21 @@
     )
 
     gain = lax.dynamic_slice_in_dim(out_gain, core * 1024, 1024, 0)[None]
-    at_turn = (z == 0) & (x == 0)
 
     def attend(c, before, mine):
         return attention(c, scal, queries, q_rec, before, mine)
 
-    before0 = jnp.where(at_turn, turned0, halo[0])
-    att0 = attend(0, before0, pair[0])
+    def complete(c, fast, powers, attended, layer):
+        out_rec = finish(c, 1, scal, fast, powers, gain, attended)
+        arrived = shift(out_rec, "core", 1)
+        layer = finish(c, 0, scal, fast, powers, gain, attended, layer)
+        return place(c, scal, arrived, layer)
+
+    layer_out = complete(0, fast0, powers0, attend(0, halo0, pair[0]), None)
+    before1 = jnp.where(chip == 0, halo0, jnp.where((z == 0) & (x == 0), turned1, halo1))
+    att1 = attend(1, before1, pair[1])
     fast1, pow1 = fast_apply(1, scal, pieces2, queries, q_rec)
-    powers1 = [pow1] + power_parts(pow1)
-    fast1, turned1, halo1, earlier0 = lax.optimization_barrier(
-        (fast1, turned1, halo[1], before0)
-    )
-    before1 = jnp.where(chip == 0, earlier0, jnp.where(at_turn, turned1, halo1))
-    att1 = attend(1, before1, pair[1])
-
-    def complete(c, fast, powers, attended, layer):
-        layer, out_rec = finish(c, scal, fast, powers, gain, attended, layer)
-        arrived = shift(out_rec, "core", 1)
-        return place(c, scal, arrived, layer)
-
-    layer_out = complete(0, fast0, powers0, att0, None)
+    powers1 = with_parts(pow1, (CORES, HALVES, ACROSS))
     layer_out = complete(1, fast1, powers1, att1, layer_out)
     return layer_out, new_all[:, 0], new_all[:, 1], new_all[:, 2]
 

time: 458 us -> 400 us (0.87)
  Pallas kernels: 116 us -> 77.9 us
  starting transfers between devices: 219 us -> 201 us
  waiting for transfers between devices: 76.3 us -> 84.6 us
  local copies, waits for them, and re-layouts: 23.4 us -> 18.1 us
  other arithmetic: 20.5 us -> 15.7 us
    pallas_call x4 -> x6, Pallas kernels: 62.7 us -> 24.9 us  [the longest x4 17.9 us: finish(): pl.pallas_call(functools.partial(finish_kernel, count), name='finish', ou...]
    ppermute x10 -> x8, waiting for transfers between devices: 0.03 us -> 28.8 us  [the longest x1 25 us: on_device(): halo0 = lax.ppermute(pair[0], chips, row)]
    ppermute x46, waiting for transfers between devices: 76.3 us -> 55.8 us  [shift(): lax.ppermute(value, axis, [(i, (i + steps) % count) for i in range(count)])]
    ppermute x10 -> x8, starting transfers between devices: 23.7 us -> 10.9 us  [the longest x5 4.96 us: with_parts(): return [power] + [lax.ppermute(power, ('heads', 'core'), p) for p in pairs]]
    ppermute x46, starting transfers between devices: 195 us -> 190 us  [shift(): lax.ppermute(value, axis, [(i, (i + steps) % count) for i in range(count)])]
  transfers between devices with their start and end apart: 56 -> 54, of which waited for: 25 -> 24; matrix products, arithmetic and copies ran while one was open for 7% -> 7% of each run, Pallas kernels for 16% -> 15%
where the time goes in v1:
time: 400 us; the launch traced here: 399 us
  starting transfers between devices  201 us (50%)
  waiting for transfers between devices  84.6 us (21%)
  Pallas kernels  77.9 us (19%)
  local copies, waits for them, and re-layouts  18.1 us (5%)
  other arithmetic  15.7 us (4%)
    ppermute x46, starting transfers between devices, shift(): lax.ppermute(value, axis, [(i, (i + steps) % count) for i in range(count)])  190 us
    ppermute x46, waiting for transfers between devices, shift(): lax.ppermute(value, axis, [(i, (i + steps) % count) for i in range(count)])  55.8 us
    ppermute x1, waiting for transfers between devices, on_device(): halo0 = lax.ppermute(pair[0], chips, row)  25 us
    pallas_call x2, Pallas kernels, attention(): pl.pallas_call(functools.partial(attention_kernel, c), name='window_atten...  23.4 us
    pallas_call x4, Pallas kernels, finish(): pl.pallas_call(functools.partial(finish_kernel, count), name='finish', ou...  17.9 us
    pallas_call x2, Pallas kernels, fast_apply(): pl.pallas_call(apply_kernel, name='fast_apply', out_shape=[jax.ShapeDtype...  16.3 us
    pallas_call x1, Pallas kernels, compute_grads(): pl.pallas_call(grads_kernel, name='fast_grads', out_shape=[jax.ShapeDtype...  13.2 us
  transfers between devices with their start and end apart: 54, of which 24 were waited for; matrix products, arithmetic and copies ran while one was open for 7% of the time, Pallas kernels for 15%

profile of v1, /device:TPU:1, one launch (start us, length us, event | category | flops | bytes accessed | tf_op | source)
XLA Modules:
  0.0 398.9 jit_solution(14384773020331613614)
XLA Ops:
  1.6 1.5 collective-permute-start
  4.7 3.0 collective-permute-start.1
  7.7 4.9 %collective-permute-done.1 = f32[2,3,16,512]{3,2,1,0:T(8,128)S(1)} collective-permute-done((f32[2,3,16,512]{3,2,1,0:T(8,128)}, f32[2,3,16,512]{3,2,1,0:T(8,128)S(1)}, u32[]{:S(2)}, u32[]{:S(2)}) %collective-permute-start.1) | collective-permute-done | bytes 196640 | tf_op jit(solution)/shard_map/ppermute | solution.py:24
  12.6 2.7 constant_dynamic-slice_fusion.7
  16.5 2.7 constant_dynamic-slice_fusion.5
  21.8 1.4 constant_dynamic-slice_fusion.8
  23.2 1.3 constant_dynamic-slice_fusion.6
  24.5 2.5 collective-permute-start.10
  29.5 1.8 collective-permute-done.10
  31.3 3.8 collective-permute-start.4
  35.0 1.3 collective-permute-start.5
  37.2 2.6 collective-permute-start.13
  40.0 1.3 collective-permute-start.14
  42.5 4.5 %collective-permute-start.7 = (bf16[8,3,16,512]{3,2,1,0:T(8,128)(2,1)S(1)}, bf16[8,3,16,512]{3,2,1,0:T(8,128)(2,1)S(1)}, u32[]{:S(2)}, u32[]{:S(2)}) collective-permute-start(bf16[8,3,16,512]{3,2,1,0:T(8,128)(2,1)S(1)} %pad_maximum_fusion.1.refs_0_), channel_id=1, source_target_pairs={{0,6},{2,0},{4,2},{6,4},{1,7},{3,1},{5,3},{7,5},{8,14},{10,8},{12,... | collective-permute-start | bytes 1179656 | tf_op jit(solution)/shard_map/ppermute | solution.py:24
  47.0 1.5 fusion.14
  48.6 1.5 fusion.15
  51.0 3.4 maximum_select_fusion
  54.4 6.6 %collective-permute-done.15.refs_7_ = bf16[8,3,16,512]{3,2,1,0:T(8,128)(2,1)S(1)} collective-permute-done((bf16[8,3,16,512]{3,2,1,0:T(8,128)(2,1)S(1)}, bf16[8,3,16,512]{3,2,1,0:T(8,128)(2,1)S(1)}, u32[]{:S(2)}, u32[]{:S(2)}) %collective-permute-start.15) | collective-permute-done | bytes 393248 | tf_op jit(solution)/shard_map/ppermute | solution.py:24
  62.3 7.4 %collective-permute-done.9.refs_3_ = bf16[8,3,16,512]{3,2,1,0:T(8,128)(2,1)S(1)} collective-permute-done((bf16[8,3,16,512]{3,2,1,0:T(8,128)(2,1)S(1)}, bf16[8,3,16,512]{3,2,1,0:T(8,128)(2,1)S(1)}, u32[]{:S(2)}, u32[]{:S(2)}) %collective-permute-start.9) | collective-permute-done | bytes 393248 | tf_op jit(solution)/shard_map/ppermute | solution.py:24
  70.4 13.2 %fast_grads.1 = (bf16[8,3,16,512]{3,2,1,0:T(8,128)(2,1)}, bf16[8,3,16,512]{3,2,1,0:T(8,128)(2,1)}, bf16[8,3,16,512]{3,2,1,0:T(8,128)(2,1)}, bf16[8,3,16,512]{3,2...) custom-call(s32[5]{0:T(128)} %stack.74.s_ref, ...), custom_call_target="tpu_custom_call" | custom-call | tf_op jit(solution)/shard_map/fast_grads/pallas_call | solution.py:132
  85.1 3.1 collective-permute-start.29
  88.2 3.6 collective-permute-start.23
  92.2 2.2 collective-permute-start.18
  94.4 5.5 %collective-permute-done.23 = bf16[8,3,16,512]{3,2,1,0:T(8,128)(2,1)S(1)} collective-permute-done((bf16[8,3,16,512]{3,2,1,0:T(8,128)(2,1)S(1)}, bf16[8,3,16,512]{3,2,1,0:T(8,128)(2,1)S(1)}, u32[]{:S(2)}, u32[]{:S(2)}) %collective-permute-start.23) | collective-permute-done | bytes 393248 | tf_op jit(solution)/shard_map/ppermute | solution.py:24
  100.1 3.5 collective-permute-start.24
  104.5 6.4 %collective-permute-done.24 = bf16[8,3,16,512]{3,2,1,0:T(8,128)(2,1)S(1)} collective-permute-done((bf16[8,3,16,512]{3,2,1,0:T(8,128)(2,1)S(1)}, bf16[8,3,16,512]{3,2,1,0:T(8,128)(2,1)S(1)}, u32[]{:S(2)}, u32[]{:S(2)}) %collective-permute-start.24) | collective-permute-done | bytes 393248 | tf_op jit(solution)/shard_map/ppermute | solution.py:24
  111.1 3.5 collective-permute-start.25
  115.7 8.2 %fast_apply.2 = (f32[2,384,1024]{2,1,0:T(8,128)}, f32[2,8,384]{2,1,0:T(8,128)}) custom-call(s32[5]{0:T(128)} %stack.74.s_ref, bf16[8,3,16,512]{3,2,1,0:T(8,128)(2,1)} %copy-done.6, bf16[8,3,16,512]{3,2,1,0:T(8,128)(2,1)} %copy-done.16, bf16[8,3,16,512]{3,2,1,0:T(8,128)(2,1)} %copy-done.17, bf16[8,3,16,512]{3,2,1,0:T(8,128)(2,1)} %copy-done.18, ...), custom_call_target="tpu_custom_call" | custom-call | tf_op jit(solution)/shard_map/fast_apply/pallas_call | solution.py:184
  123.9 2.3 collective-permute-start.30
  129.5 3.7 collective-permute-done.20
  133.3 1.6 collective-permute-start.21
  135.2 1.7 collective-permute-done.21
  136.9 2.8 collective-permute-start.22
  139.9 1.4 collective-permute-done.22
  141.3 2.2 collective-permute-done.28
  143.6 3.0 collective-permute-start.31
  146.6 3.6 collective-permute-start.50
  150.7 2.8 collective-permute-done.32.refs_1_
  153.4 2.3 collective-permute-start.49
  156.7 6.2 %collective-permute-start.33 = (bf16[2,3,16,512]{3,2,1,0:T(8,128)(2,1)S(1)}, bf16[2,3,16,512]{3,2,1,0:T(8,128)(2,1)S(1)}, u32[]{:S(2)}, u32[]{:S(2)}) collective-permute-start(bf16[2,3,16,512]{3,2,1,0:T(8,128)(2,1)S(1)} %get-tuple-element.86), channel_id=1, source_target_pairs={{0,24},{8,0},{16,8},{24,16},{1,25},{9,1},{17,9},{25,17},{2,26},{10... | collective-permute-start | bytes 294920 | tf_op jit(solution)/shard_map/ppermute | solution.py:24
  162.9 1.6 collective-permute-done.33
  164.5 3.4 collective-permute-start.34
  167.9 1.6 collective-permute-done.34
  169.6 3.4 collective-permute-start.35
  174.7 2.7 collective-permute-start.36
  177.4 2.7 collective-permute-done.42.refs_5_
  180.2 2.3 collective-permute-start.43
  182.5 2.8 collective-permute-start.37
  185.3 1.9 collective-permute-done.43.refs_6_
  187.2 3.5 collective-permute-start.44
  190.8 2.5 collective-permute-start.38
  193.8 25.0 %collective-permute-done.48.k0.ka.v0.va = bf16[4,384,1024]{2,1,0:T(8,128)(2,1)} collective-permute-done((bf16[4,384,1024]{2,1,0:T(8,128)(2,1)}, bf16[4,384,1024]{2,1,0:T(8,128)(2,1)}, u32[]{:S(2)}, u32[]{:S(2)}) %collective-permute-start.48) | collective-permute-done | bytes 3145760 | tf_op jit(solution)/shard_map/ppermute | solution.py:420
  218.8 11.8 %window_attention.3.refs_3_ = f32[2,384,1024]{2,1,0:T(8,128)} custom-call(s32[5]{0:T(128)} %stack.74.s_ref, bf16[2,384,2048]{2,1,0:T(8,128)(2,1)} %qo.1, bf16[2,384,1024]{2,1,0:T(8,128)(2,1)} %copy-done.2, bf16[4,384,1024]{2,1,0:T(8,128)(2,1)} %collective-permute-done.48.k0.ka.v0.va, bf16[4,384,1024]{2,1,0:T(8,128)(2,1)} %collective-permute-done.48.k0.ka.v0.va, ...), custom_call_target="tpu_custom_call" | custom-call | tf_op jit(solution)/shard_map/window_attention/pallas_call | solution.py:236
  230.6 4.4 %finish.5 = bf16[384,1024]{1,0:T(8,128)(2,1)} custom-call(s32[5]{0:T(128)} %stack.74.s_ref, f32[2,384,1024]{2,1,0:T(8,128)} %get-tuple-element.67.fast_ref, f32[2,8,384]{2,1,0:T(8,128)} %copy-done.31, f32[2,8,384]{2,1,0:T(8,128)} %copy-done.35, f32[1,1024]{1,0:T(1,128)} %bitcast.45, f32[2,384,1024]{2,1,0:T(8,128)} %window_attention.3.refs_3_), custom_call_target="tpu_custom_call" | custom-call | tf_op jit(solution)/shard_map/finish/pallas_call | solution.py:284
  235.0 111.5 %collective-permute-start.52 = (bf16[384,1024]{1,0:T(8,128)(2,1)}, bf16[384,1024]{1,0:T(8,128)(2,1)}, u32[]{:S(2)}, u32[]{:S(2)}) collective-permute-start(bf16[384,1024]{1,0:T(8,128)(2,1)} %finish.5), channel_id=1, source_target_pairs={{0,1},{1,0},{2,3},{3,2},{4,5},{5,4},{6,7},{7,6},{8,9},{9,8},{10,11... | collective-permute-start | bytes 2359304 | tf_op jit(solution)/shard_map/ppermute | solution.py:24
  346.6 8.1 %fast_apply.3 = (f32[2,384,1024]{2,1,0:T(8,128)}, f32[2,8,384]{2,1,0:T(8,128)}) custom-call(s32[5]{0:T(128)} %stack.74.s_ref, bf16[8,3,16,512]{3,2,1,0:T(8,128)(2,1)} %copy-done.12, bf16[8,3,16,512]{3,2,1,0:T(8,128)(2,1)} %copy-done.24, bf16[8,3,16,512]{3,2,1,0:T(8,128)(2,1)} %collective-permute-done.37.refs_2_, ...), custom_call_target="tpu_custom_call" | custom-call | tf_op jit(solution)/shard_map/fast_apply/pallas_call | solution.py:184
  356.9 4.9 %select_select_fusion.k0.ka.v0.va = bf16[4,384,1024]{2,1,0:T(8,128)(2,1)} fusion(bf16[4,384,1024]{2,1,0:T(8,128)(2,1)} %collective-permute-done.48.k0.ka.v0.va, bf16[4,384,1024]{2,1,0:T(8,128)(2,1)} %collective-permute-done.49, bf16[4,384,1024]{2,1,0:T(8,128)(2,1)} %collective-permute-done.50, pred[]{:T(512)S(6)} %and.7, pred[]{:T(512)S(6)} %eq.16), kind=kLoop, calls=%fused_computation.2 | loop fusion | flops 3145728 | bytes 12582914 | tf_op jit(solution)/shard_map/jit(_where)/select_n | solution.py:456
  361.9 11.7 %window_attention.2.refs_5_ = f32[2,384,1024]{2,1,0:T(8,128)} custom-call(s32[5]{0:T(128)} %stack.74.s_ref, bf16[2,384,2048]{2,1,0:T(8,128)(2,1)} %qo.1, bf16[2,384,1024]{2,1,0:T(8,128)(2,1)} %copy-done.2, bf16[4,384,1024]{2,1,0:T(8,128)(2,1)} %select_select_fusion.k0.ka.v0.va, bf16[4,384,1024]{2,1,0:T(8,128)(2,1)} %select_select_fusion.k0.ka.v0.va, ...), custom_call_target="tpu_custom_call" | custom-call | tf_op jit(solution)/shard_map/window_attention/pallas_call | solution.py:236
  374.2 4.6 %finish.4 = bf16[384,1024]{1,0:T(8,128)(2,1)} custom-call(s32[5]{0:T(128)} %stack.74.s_ref, f32[2,384,1024]{2,1,0:T(8,128)} %get-tuple-element.63.fast_ref, f32[2,8,384]{2,1,0:T(8,128)} %get-tuple-element.64.refs_0_, f32[2,8,384]{2,1,0:T(8,128)} %copy-done.32, f32[2,8,384]{2,1,0:T(8,128)} %copy-done.33, f32[2,8,384]{2,1,0:T(8,128)} %copy-done.34, ...), custom_call_target="tpu_custom_call" | custom-call | tf_op jit(solution)/shard_map/finish/pallas_call | solution.py:284
  379.4 2.0 collective-permute-done.53
  382.1 4.4 %finish.6.layer_ref = bf16[2,384,2048]{2,1,0:T(8,128)(2,1)} custom-call(s32[5]{0:T(128)} %stack.74.s_ref, f32[2,384,1024]{2,1,0:T(8,128)} %get-tuple-element.67.fast_ref, f32[2,8,384]{2,1,0:T(8,128)} %copy-done.31, f32[2,8,384]{2,1,0:T(8,128)} %copy-done.35, f32[1,1024]{1,0:T(1,128)} %bitcast.47, f32[2,384,1024]{2,1,0:T(8,128)} %window_attention.3.refs_3_), custom_call_target="tpu_custom_call" | custom-call | tf_op jit(solution)/shard_map/finish/pallas_call | solution.py:284
  386.5 3.5 place.2.refs_6_
  390.0 4.4 %finish.7.layer_ref = bf16[2,384,2048]{2,1,0:T(8,128)(2,1)} custom-call(s32[5]{0:T(128)} %stack.74.s_ref, f32[2,384,1024]{2,1,0:T(8,128)} %get-tuple-element.63.fast_ref, f32[2,8,384]{2,1,0:T(8,128)} %get-tuple-element.64.refs_0_, f32[2,8,384]{2,1,0:T(8,128)} %copy-done.32, f32[2,8,384]{2,1,0:T(8,128)} %copy-done.33, ...), custom_call_target="tpu_custom_call", output_to_operand_aliasing={{}: (8, {})} | custom-call | tf_op jit(solution)/shard_map/finish/pallas_call | solution.py:284
  395.4 3.5 place.3
  (182 shorter events, 30.8 us)
Async XLA Ops:
  1.6 2.4 collective-permute-start
  4.7 7.9 %collective-permute-start.1 = (f32[2,3,16,512]{3,2,1,0:T(8,128)}, f32[2,3,16,512]{3,2,1,0:T(8,128)S(1)}, u32[]{:S(2)}, u32[]{:S(2)}) collective-permute-start(f32[2,3,16,512]{3,2,1,0:T(8,128)} %maximum_select_fusion.3), channel_id=1, source_target_pairs={{0,32},{32,0},{1,33},{33,1},{2,34},{34,2},{3,35},{35,3},{4,36},{36... | collective-permute-start | bytes 589832 | tf_op jit(solution)/shard_map/ppermute | solution.py:24
  15.4 27.1 %collective-permute-start.2 = (bf16[2,384,1024]{2,1,0:T(8,128)(2,1)}, bf16[2,384,1024]{2,1,0:T(8,128)(2,1)}, u32[]{:S(2)}, u32[]{:S(2)}) collective-permute-start(bf16[2,384,1024]{2,1,0:T(8,128)(2,1)} %constant_dynamic-slice_fusion.7), channel_id=1, source_target_pairs={{0,1},{1,0},{2,3},{3,2},{4,5},{5,4},{6,7},{7,6},{8,9},{9,8},{10,11... | collective-permute-start | bytes 4718600 | tf_op jit(solution)/shard_map/ppermute | solution.py:24
  19.2 29.3 %collective-permute-start.3 = (bf16[2,384,1024]{2,1,0:T(8,128)(2,1)}, bf16[2,384,1024]{2,1,0:T(8,128)(2,1)}, u32[]{:S(2)}, u32[]{:S(2)}) collective-permute-start(bf16[2,384,1024]{2,1,0:T(8,128)(2,1)} %constant_dynamic-slice_fusion.5), channel_id=1, source_target_pairs={{0,1},{1,0},{2,3},{3,2},{4,5},{5,4},{6,7},{7,6},{8,9},{9,8},{10,11... | collective-permute-start | bytes 4718600 | tf_op jit(solution)/shard_map/ppermute | solution.py:24
  20.0 7.6 %collective-permute-start.16 = (f32[2,384]{1,0:T(2,128)S(1)}, f32[2,384]{1,0:T(2,128)S(1)}, u32[]{:S(2)}, u32[]{:S(2)}) collective-permute-start(f32[2,384]{1,0:T(2,128)S(1)} %get-tuple-element.92), channel_id=1, source_target_pairs={{0,1},{1,0},{2,3},{3,2},{4,5},{5,4},{6,7},{7,6},{8,9},{9,8},{10,11... | collective-permute-start | bytes 9224 | tf_op jit(solution)/shard_map/ppermute | solution.py:24
  24.5 6.8 %collective-permute-start.10 = (bf16[2,3,16,512]{3,2,1,0:T(8,128)(2,1)S(1)}, bf16[2,3,16,512]{3,2,1,0:T(8,128)(2,1)S(1)}, u32[]{:S(2)}, u32[]{:S(2)}) collective-permute-start(bf16[2,3,16,512]{3,2,1,0:T(8,128)(2,1)S(1)} %get-tuple-element.87), channel_id=1, source_target_pairs={{0,6},{2,0},{4,2},{6,4},{1,7},{3,1},{5,3},{7,5},{8,14},{10,8},{12,... | collective-permute-start | bytes 294920 | tf_op jit(solution)/shard_map/ppermute | solution.py:24
  27.1 8.0 %collective-permute-start.11 = (bf16[2,3,16,512]{3,2,1,0:T(8,128)(2,1)S(1)}, bf16[2,3,16,512]{3,2,1,0:T(8,128)(2,1)S(1)}, u32[]{:S(2)}, u32[]{:S(2)}) collective-permute-start(bf16[2,3,16,512]{3,2,1,0:T(8,128)(2,1)S(1)} %get-tuple-element.87), channel_id=1, source_target_pairs={{0,4},{2,6},{4,0},{6,2},{1,5},{3,7},{5,1},{7,3},{8,12},{10,14},{12... | collective-permute-start | bytes 294920 | tf_op jit(solution)/shard_map/ppermute | solution.py:24
  27.6 8.8 %collective-permute-start.12 = (bf16[2,3,16,512]{3,2,1,0:T(8,128)(2,1)S(1)}, bf16[2,3,16,512]{3,2,1,0:T(8,128)(2,1)S(1)}, u32[]{:S(2)}, u32[]{:S(2)}) collective-permute-start(bf16[2,3,16,512]{3,2,1,0:T(8,128)(2,1)S(1)} %get-tuple-element.87), channel_id=1, source_target_pairs={{0,2},{2,4},{4,6},{6,0},{1,3},{3,5},{5,7},{7,1},{8,10},{10,12},{12... | collective-permute-start | bytes 294920 | tf_op jit(solution)/shard_map/ppermute | solution.py:24
  31.3 5.9 %collective-permute-start.4 = (bf16[2,3,16,512]{3,2,1,0:T(8,128)(2,1)S(1)}, bf16[2,3,16,512]{3,2,1,0:T(8,128)(2,1)S(1)}, u32[]{:S(2)}, u32[]{:S(2)}) collective-permute-start(bf16[2,3,16,512]{3,2,1,0:T(8,128)(2,1)S(1)} %get-tuple-element.88), channel_id=1, source_target_pairs={{0,24},{8,0},{16,8},{24,16},{1,25},{9,1},{17,9},{25,17},{2,26},{10... | collective-permute-start | bytes 294920 | tf_op jit(solution)/shard_map/ppermute | solution.py:24
  35.0 5.0 %collective-permute-start.5 = (bf16[2,3,16,512]{3,2,1,0:T(8,128)(2,1)S(1)}, bf16[2,3,16,512]{3,2,1,0:T(8,128)(2,1)S(1)}, u32[]{:S(2)}, u32[]{:S(2)}) collective-permute-start(bf16[2,3,16,512]{3,2,1,0:T(8,128)(2,1)S(1)} %get-tuple-element.88), channel_id=1, source_target_pairs={{0,16},{8,24},{16,0},{24,8},{1,17},{9,25},{17,1},{25,9},{2,18},{10... | collective-permute-start | bytes 294920 | tf_op jit(solution)/shard_map/ppermute | solution.py:24
  36.3 6.0 %collective-permute-start.6 = (bf16[2,3,16,512]{3,2,1,0:T(8,128)(2,1)S(1)}, bf16[2,3,16,512]{3,2,1,0:T(8,128)(2,1)S(1)}, u32[]{:S(2)}, u32[]{:S(2)}) collective-permute-start(bf16[2,3,16,512]{3,2,1,0:T(8,128)(2,1)S(1)} %get-tuple-element.88), channel_id=1, source_target_pairs={{0,8},{8,16},{16,24},{24,0},{1,9},{9,17},{17,25},{25,1},{2,10},{10... | collective-permute-start | bytes 294920 | tf_op jit(solution)/shard_map/ppermute | solution.py:24
  37.2 12.9 %collective-permute-start.13 = (bf16[8,3,16,512]{3,2,1,0:T(8,128)(2,1)S(1)}, bf16[8,3,16,512]{3,2,1,0:T(8,128)(2,1)S(1)}, u32[]{:S(2)}, u32[]{:S(2)}) collective-permute-start(bf16[8,3,16,512]{3,2,1,0:T(8,128)(2,1)S(1)} %pad_maximum_fusion.2.refs_4_), channel_id=1, source_target_pairs={{0,24},{8,0},{16,8},{24,16},{1,25},{9,1},{17,9},{25,17},{2,26},{10... | collective-permute-start | bytes 1179656 | tf_op jit(solution)/shard_map/ppermute | solution.py:24
  40.0 14.4 %collective-permute-start.14 = (bf16[8,3,16,512]{3,2,1,0:T(8,128)(2,1)S(1)}, bf16[8,3,16,512]{3,2,1,0:T(8,128)(2,1)S(1)}, u32[]{:S(2)}, u32[]{:S(2)}) collective-permute-start(bf16[8,3,16,512]{3,2,1,0:T(8,128)(2,1)S(1)} %pad_maximum_fusion.2.refs_4_), channel_id=1, source_target_pairs={{0,16},{8,24},{16,0},{24,8},{1,17},{9,25},{17,1},{25,9},{2,18},{10... | collective-permute-start | bytes 1179656 | tf_op jit(solution)/shard_map/ppermute | solution.py:24
  42.4 18.6 %collective-permute-start.15 = (bf16[8,3,16,512]{3,2,1,0:T(8,128)(2,1)S(1)}, bf16[8,3,16,512]{3,2,1,0:T(8,128)(2,1)S(1)}, u32[]{:S(2)}, u32[]{:S(2)}) collective-permute-start(bf16[8,3,16,512]{3,2,1,0:T(8,128)(2,1)S(1)} %pad_maximum_fusion.2.refs_4_), channel_id=1, source_target_pairs={{0,8},{8,16},{16,24},{24,0},{1,9},{9,17},{17,25},{25,1},{2,10},{10... | collective-permute-start | bytes 1179656 | tf_op jit(solution)/shard_map/ppermute | solution.py:24
  42.5 19.8 %collective-permute-start.7 = (bf16[8,3,16,512]{3,2,1,0:T(8,128)(2,1)S(1)}, bf16[8,3,16,512]{3,2,1,0:T(8,128)(2,1)S(1)}, u32[]{:S(2)}, u32[]{:S(2)}) collective-permute-start(bf16[8,3,16,512]{3,2,1,0:T(8,128)(2,1)S(1)} %pad_maximum_fusion.1.refs_0_), channel_id=1, source_target_pairs={{0,6},{2,0},{4,2},{6,4},{1,7},{3,1},{5,3},{7,5},{8,14},{10,8},{12,... | collective-permute-start | bytes 1179656 | tf_op jit(solution)/shard_map/ppermute | solution.py:24
  48.5 13.8 %collective-permute-start.8 = (bf16[8,3,16,512]{3,2,1,0:T(8,128)(2,1)S(1)}, bf16[8,3,16,512]{3,2,1,0:T(8,128)(2,1)S(1)}, u32[]{:S(2)}, u32[]{:S(2)}) collective-permute-start(bf16[8,3,16,512]{3,2,1,0:T(8,128)(2,1)S(1)} %pad_maximum_fusion.1.refs_0_), channel_id=1, source_target_pairs={{0,4},{2,6},{4,0},{6,2},{1,5},{3,7},{5,1},{7,3},{8,12},{10,14},{12... | collective-permute-start | bytes 1179656 | tf_op jit(solution)/shard_map/ppermute | solution.py:24
  50.1 19.5 %collective-permute-start.9 = (bf16[8,3,16,512]{3,2,1,0:T(8,128)(2,1)S(1)}, bf16[8,3,16,512]{3,2,1,0:T(8,128)(2,1)S(1)}, u32[]{:S(2)}, u32[]{:S(2)}) collective-permute-start(bf16[8,3,16,512]{3,2,1,0:T(8,128)(2,1)S(1)} %pad_maximum_fusion.1.refs_0_), channel_id=1, source_target_pairs={{0,2},{2,4},{4,6},{6,0},{1,3},{3,5},{5,7},{7,1},{8,10},{10,12},{12... | collective-permute-start | bytes 1179656 | tf_op jit(solution)/shard_map/ppermute | solution.py:24
  54.4 99.0 %copy-start = (bf16[4,384,1024]{2,1,0:T(8,128)(2,1)}, bf16[4,384,1024]{2,1,0:T(8,128)(2,1)S(1)}, u32[]{:S(2)}) copy-start(bf16[4,384,1024]{2,1,0:T(8,128)(2,1)S(1)} %get-tuple-element.66.kb.k2.vb.v2) | copy-start | bytes 9437188
  83.6 20.0 %copy-start.28 = (bf16[8,3,16,512]{3,2,1,0:T(8,128)(2,1)S(1)}, bf16[8,3,16,512]{3,2,1,0:T(8,128)(2,1)}, u32[]{:S(2)}) copy-start(bf16[8,3,16,512]{3,2,1,0:T(8,128)(2,1)} %get-tuple-element.51) | copy-start | bytes 1179652
  83.6 27.3 %copy-start.27 = (bf16[8,3,16,512]{3,2,1,0:T(8,128)(2,1)S(1)}, bf16[8,3,16,512]{3,2,1,0:T(8,128)(2,1)}, u32[]{:S(2)}) copy-start(bf16[8,3,16,512]{3,2,1,0:T(8,128)(2,1)} %get-tuple-element.55) | copy-start | bytes 1179652
  83.6 8.5 %collective-permute-start.17 = (bf16[8,3,16,512]{3,2,1,0:T(8,128)(2,1)}, bf16[8,3,16,512]{3,2,1,0:T(8,128)(2,1)S(1)}, u32[]{:S(2)}, u32[]{:S(2)}) collective-permute-start(bf16[8,3,16,512]{3,2,1,0:T(8,128)(2,1)} %get-tuple-element.49), channel_id=1, source_target_pairs={{0,6},{2,0},{4,2},{6,4},{1,7},{3,1},{5,3},{7,5},{8,14},{10,8},{12,... | collective-permute-start | bytes 1179656 | tf_op jit(solution)/shard_map/ppermute | solution.py:24
  85.1 29.5 %collective-permute-start.29 = (bf16[2,384,1024]{2,1,0:T(8,128)(2,1)S(1)}, bf16[2,384,1024]{2,1,0:T(8,128)(2,1)S(1)}, u32[]{:S(2)}, u32[]{:S(2)}) collective-permute-start(bf16[2,384,1024]{2,1,0:T(8,128)(2,1)S(1)} %constant_dynamic-slice_fusion.2), channel_id=1, source_target_pairs={{0,1},{1,0},{2,3},{3,2},{4,5},{5,4},{6,7},{7,6},{8,9},{9,8},{10,11... | collective-permute-start | bytes 4718600 | tf_op jit(solution)/shard_map/ppermute | solution.py:24
  88.2 11.8 %collective-permute-start.23 = (bf16[8,3,16,512]{3,2,1,0:T(8,128)(2,1)S(1)}, bf16[8,3,16,512]{3,2,1,0:T(8,128)(2,1)S(1)}, u32[]{:S(2)}, u32[]{:S(2)}) collective-permute-start(bf16[8,3,16,512]{3,2,1,0:T(8,128)(2,1)S(1)} %copy-done.38), channel_id=1, source_target_pairs={{0,24},{8,0},{16,8},{24,16},{1,25},{9,1},{17,9},{25,17},{2,26},{10... | collective-permute-start | bytes 1179656 | tf_op jit(solution)/shard_map/ppermute | solution.py:24
  92.2 11.3 %collective-permute-start.18 = (bf16[8,3,16,512]{3,2,1,0:T(8,128)(2,1)S(1)}, bf16[8,3,16,512]{3,2,1,0:T(8,128)(2,1)S(1)}, u32[]{:S(2)}, u32[]{:S(2)}) collective-permute-start(bf16[8,3,16,512]{3,2,1,0:T(8,128)(2,1)S(1)} %add_convert_fusion.3), channel_id=1, source_target_pairs={{0,6},{2,0},{4,2},{6,4},{1,7},{3,1},{5,3},{7,5},{8,14},{10,8},{12,... | collective-permute-start | bytes 1179656 | tf_op jit(solution)/shard_map/ppermute | solution.py:24
  100.1 10.8 %collective-permute-start.24 = (bf16[8,3,16,512]{3,2,1,0:T(8,128)(2,1)S(1)}, bf16[8,3,16,512]{3,2,1,0:T(8,128)(2,1)S(1)}, u32[]{:S(2)}, u32[]{:S(2)}) collective-permute-start(bf16[8,3,16,512]{3,2,1,0:T(8,128)(2,1)S(1)} %add_convert_fusion.1), channel_id=1, source_target_pairs={{0,24},{8,0},{16,8},{24,16},{1,25},{9,1},{17,9},{25,17},{2,26},{10... | collective-permute-start | bytes 1179656 | tf_op jit(solution)/shard_map/ppermute | solution.py:24
  104.5 23.6 %collective-permute-start.19 = (bf16[8,3,16,512]{3,2,1,0:T(8,128)(2,1)}, bf16[8,3,16,512]{3,2,1,0:T(8,128)(2,1)}, u32[]{:S(2)}, u32[]{:S(2)}) collective-permute-start(bf16[8,3,16,512]{3,2,1,0:T(8,128)(2,1)} %add_convert_fusion.2), channel_id=1, source_target_pairs={{0,6},{2,0},{4,2},{6,4},{1,7},{3,1},{5,3},{7,5},{8,14},{10,8},{12,... | collective-permute-start | bytes 1179656 | tf_op jit(solution)/shard_map/ppermute | solution.py:24
  111.0 17.0 %copy-start.26 = (bf16[8,3,16,512]{3,2,1,0:T(8,128)(2,1)S(1)}, bf16[8,3,16,512]{3,2,1,0:T(8,128)(2,1)}, u32[]{:S(2)}) copy-start(bf16[8,3,16,512]{3,2,1,0:T(8,128)(2,1)} %get-tuple-element.52) | copy-start | bytes 1179652
  111.1 18.3 %copy-start.25 = (bf16[8,3,16,512]{3,2,1,0:T(8,128)(2,1)S(1)}, bf16[8,3,16,512]{3,2,1,0:T(8,128)(2,1)}, u32[]{:S(2)}) copy-start(bf16[8,3,16,512]{3,2,1,0:T(8,128)(2,1)} %get-tuple-element.56) | copy-start | bytes 1179652
  111.1 18.2 %collective-permute-start.25 = (bf16[8,3,16,512]{3,2,1,0:T(8,128)(2,1)S(1)}, bf16[8,3,16,512]{3,2,1,0:T(8,128)(2,1)S(1)}, u32[]{:S(2)}, u32[]{:S(2)}) collective-permute-start(bf16[8,3,16,512]{3,2,1,0:T(8,128)(2,1)S(1)} %add_convert_fusion), channel_id=1, source_target_pairs={{0,24},{8,0},{16,8},{24,16},{1,25},{9,1},{17,9},{25,17},{2,26},{10... | collective-permute-start | bytes 1179656 | tf_op jit(solution)/shard_map/ppermute | solution.py:24
  123.9 3.4 collective-permute-start.30
  128.0 22.2 %copy-start.31 = (f32[2,8,384]{2,1,0:T(8,128)}, f32[2,8,384]{2,1,0:T(8,128)S(1)}, u32[]{:S(2)}) copy-start(f32[2,8,384]{2,1,0:T(8,128)S(1)} %add.90.refs_0_) | copy-start | bytes 73732
  129.2 26.6 %copy-start.22 = (f32[2,3,16,512]{3,2,1,0:T(8,128)S(1)}, f32[2,3,16,512]{3,2,1,0:T(8,128)}, u32[]{:S(2)}) copy-start(f32[2,3,16,512]{3,2,1,0:T(8,128)} %copy-done.21) | copy-start | bytes 589828
  129.2 4.1 %collective-permute-start.20 = (bf16[2,3,16,512]{3,2,1,0:T(8,128)(2,1)S(1)}, bf16[2,3,16,512]{3,2,1,0:T(8,128)(2,1)S(1)}, u32[]{:S(2)}, u32[]{:S(2)}) collective-permute-start(bf16[2,3,16,512]{3,2,1,0:T(8,128)(2,1)S(1)} %slice.163), channel_id=1, source_target_pairs={{0,24},{8,0},{16,8},{24,16},{1,25},{9,1},{17,9},{25,17},{2,26},{10... | collective-permute-start | bytes 294920 | tf_op jit(solution)/shard_map/ppermute | solution.py:24
  129.5 5.4 %collective-permute-start.26 = (bf16[2,3,16,512]{3,2,1,0:T(8,128)(2,1)S(1)}, bf16[2,3,16,512]{3,2,1,0:T(8,128)(2,1)S(1)}, u32[]{:S(2)}, u32[]{:S(2)}) collective-permute-start(bf16[2,3,16,512]{3,2,1,0:T(8,128)(2,1)S(1)} %slice.162), channel_id=1, source_target_pairs={{0,6},{2,0},{4,2},{6,4},{1,7},{3,1},{5,3},{7,5},{8,14},{10,8},{12,... | collective-permute-start | bytes 294920 | tf_op jit(solution)/shard_map/ppermute | solution.py:24
  133.3 3.5 collective-permute-start.21
  134.9 58.3 %copy-start.37 = (f32[2048]{0:T(1024)S(1)}, f32[2048]{0:T(1024)}, u32[]{:S(2)}) copy-start(f32[2048]{0:T(1024)} %param.15) | copy-start | bytes 24580
  134.9 4.7 %collective-permute-start.27 = (bf16[2,3,16,512]{3,2,1,0:T(8,128)(2,1)S(1)}, bf16[2,3,16,512]{3,2,1,0:T(8,128)(2,1)S(1)}, u32[]{:S(2)}, u32[]{:S(2)}) collective-permute-start(bf16[2,3,16,512]{3,2,1,0:T(8,128)(2,1)S(1)} %fusion.4), channel_id=1, source_target_pairs={{0,6},{2,0},{4,2},{6,4},{1,7},{3,1},{5,3},{7,5},{8,14},{10,8},{12,... | collective-permute-start | bytes 294920 | tf_op jit(solution)/shard_map/ppermute | solution.py:24
  136.9 4.4 %collective-permute-start.22 = (bf16[2,3,16,512]{3,2,1,0:T(8,128)(2,1)S(1)}, bf16[2,3,16,512]{3,2,1,0:T(8,128)(2,1)S(1)}, u32[]{:S(2)}, u32[]{:S(2)}) collective-permute-start(bf16[2,3,16,512]{3,2,1,0:T(8,128)(2,1)S(1)} %fusion.6), channel_id=1, source_target_pairs={{0,24},{8,0},{16,8},{24,16},{1,25},{9,1},{17,9},{25,17},{2,26},{10... | collective-permute-start | bytes 294920 | tf_op jit(solution)/shard_map/ppermute | solution.py:24
  139.7 3.8 collective-permute-start.28
  143.6 7.0 %collective-permute-start.31 = (bf16[2,2,3,16,512]{4,3,2,1,0:T(8,128)(2,1)S(1)}, bf16[2,2,3,16,512]{4,3,2,1,0:T(8,128)(2,1)S(1)}, u32[]{:S(2)}, u32[]{:S(2)}) collective-permute-start(bf16[2,2,3,16,512]{4,3,2,1,0:T(8,128)(2,1)S(1)} %pad_maximum_fusion.6), channel_id=1, source_target_pairs={{0,32},{32,0},{1,33},{33,1},{2,34},{34,2},{3,35},{35,3},{4,36},{36... | collective-permute-start | bytes 589832 | tf_op jit(solution)/shard_map/ppermute | solution.py:24
  146.6 72.2 %collective-permute-start.48 = (bf16[4,384,1024]{2,1,0:T(8,128)(2,1)}, bf16[4,384,1024]{2,1,0:T(8,128)(2,1)}, u32[]{:S(2)}, u32[]{:S(2)}) collective-permute-start(bf16[4,384,1024]{2,1,0:T(8,128)(2,1)} %get-tuple-element.65.kb.k2.vb.v2), channel_id=1, source_target_pairs={{0,2},{2,4},{4,6},{6,8},{8,10},{10,12},{12,14},{14,16},{16,18},{18... | collective-permute-start | bytes 9437192 | tf_op jit(solution)/shard_map/ppermute | solution.py:420
  146.6 209.4 %collective-permute-start.50 = (bf16[4,384,1024]{2,1,0:T(8,128)(2,1)S(1)}, bf16[4,384,1024]{2,1,0:T(8,128)(2,1)}, u32[]{:S(2)}, u32[]{:S(2)}) collective-permute-start(bf16[4,384,1024]{2,1,0:T(8,128)(2,1)S(1)} %get-tuple-element.66.kb.k2.vb.v2), channel_id=1, source_target_pairs={{0,2},{2,4},{4,6},{6,8},{8,10},{10,12},{12,14},{14,16},{16,18},{18... | collective-permute-start | bytes 9437192 | tf_op jit(solution)/shard_map/ppermute | solution.py:421
  150.2 3.2 collective-permute-start.32
  153.4 19.6 %copy-start.35 = (f32[2,8,384]{2,1,0:T(8,128)}, f32[2,8,384]{2,1,0:T(8,128)S(1)}, u32[]{:S(2)}) copy-start(f32[2,8,384]{2,1,0:T(8,128)S(1)} %collective-permute-done.32.refs_1_) | copy-start | bytes 73732
  153.4 203.5 %collective-permute-start.49 = (bf16[4,384,1024]{2,1,0:T(8,128)(2,1)S(1)}, bf16[4,384,1024]{2,1,0:T(8,128)(2,1)}, u32[]{:S(2)}, u32[]{:S(2)}) collective-permute-start(bf16[4,384,1024]{2,1,0:T(8,128)(2,1)S(1)} %get-tuple-element.66.kb.k2.vb.v2), channel_id=1, source_target_pairs={{30,32},{31,33},{94,96},{95,97}} | collective-permute-start | bytes 9437192 | tf_op jit(solution)/shard_map/ppermute | solution.py:435
  156.6 6.3 %collective-permute-start.39 = (bf16[2,3,16,512]{3,2,1,0:T(8,128)(2,1)S(1)}, bf16[2,3,16,512]{3,2,1,0:T(8,128)(2,1)S(1)}, u32[]{:S(2)}, u32[]{:S(2)}) collective-permute-start(bf16[2,3,16,512]{3,2,1,0:T(8,128)(2,1)S(1)} %get-tuple-element.85), channel_id=1, source_target_pairs={{0,6},{2,0},{4,2},{6,4},{1,7},{3,1},{5,3},{7,5},{8,14},{10,8},{12,... | collective-permute-start | bytes 294920 | tf_op jit(solution)/shard_map/ppermute | solution.py:24
  156.7 7.8 %collective-permute-start.33 = (bf16[2,3,16,512]{3,2,1,0:T(8,128)(2,1)S(1)}, bf16[2,3,16,512]{3,2,1,0:T(8,128)(2,1)S(1)}, u32[]{:S(2)}, u32[]{:S(2)}) collective-permute-start(bf16[2,3,16,512]{3,2,1,0:T(8,128)(2,1)S(1)} %get-tuple-element.86), channel_id=1, source_target_pairs={{0,24},{8,0},{16,8},{24,16},{1,25},{9,1},{17,9},{25,17},{2,26},{10... | collective-permute-start | bytes 294920 | tf_op jit(solution)/shard_map/ppermute | solution.py:24
  162.8 5.1 %collective-permute-start.40 = (bf16[2,3,16,512]{3,2,1,0:T(8,128)(2,1)S(1)}, bf16[2,3,16,512]{3,2,1,0:T(8,128)(2,1)S(1)}, u32[]{:S(2)}, u32[]{:S(2)}) collective-permute-start(bf16[2,3,16,512]{3,2,1,0:T(8,128)(2,1)S(1)} %collective-permute-done.39), channel_id=1, source_target_pairs={{0,6},{2,0},{4,2},{6,4},{1,7},{3,1},{5,3},{7,5},{8,14},{10,8},{12,... | collective-permute-start | bytes 294920 | tf_op jit(solution)/shard_map/ppermute | solution.py:24
  164.5 5.1 %collective-permute-start.34 = (bf16[2,3,16,512]{3,2,1,0:T(8,128)(2,1)S(1)}, bf16[2,3,16,512]{3,2,1,0:T(8,128)(2,1)S(1)}, u32[]{:S(2)}, u32[]{:S(2)}) collective-permute-start(bf16[2,3,16,512]{3,2,1,0:T(8,128)(2,1)S(1)} %collective-permute-done.33), channel_id=1, source_target_pairs={{0,24},{8,0},{16,8},{24,16},{1,25},{9,1},{17,9},{25,17},{2,26},{10... | collective-permute-start | bytes 294920 | tf_op jit(solution)/shard_map/ppermute | solution.py:24
  167.9 5.1 %collective-permute-start.41 = (bf16[2,3,16,512]{3,2,1,0:T(8,128)(2,1)S(1)}, bf16[2,3,16,512]{3,2,1,0:T(8,128)(2,1)S(1)}, u32[]{:S(2)}, u32[]{:S(2)}) collective-permute-start(bf16[2,3,16,512]{3,2,1,0:T(8,128)(2,1)S(1)} %collective-permute-done.40), channel_id=1, source_target_pairs={{0,6},{2,0},{4,2},{6,4},{1,7},{3,1},{5,3},{7,5},{8,14},{10,8},{12,... | collective-permute-start | bytes 294920 | tf_op jit(solution)/shard_map/ppermute | solution.py:24
  169.6 5.1 %collective-permute-start.35 = (bf16[2,3,16,512]{3,2,1,0:T(8,128)(2,1)S(1)}, bf16[2,3,16,512]{3,2,1,0:T(8,128)(2,1)S(1)}, u32[]{:S(2)}, u32[]{:S(2)}) collective-permute-start(bf16[2,3,16,512]{3,2,1,0:T(8,128)(2,1)S(1)} %collective-permute-done.34), channel_id=1, source_target_pairs={{0,24},{8,0},{16,8},{24,16},{1,25},{9,1},{17,9},{25,17},{2,26},{10... | collective-permute-start | bytes 294920 | tf_op jit(solution)/shard_map/ppermute | solution.py:24
  173.1 57.5 %copy-start.11 = (bf16[8,3,16,512]{3,2,1,0:T(8,128)(2,1)}, bf16[8,3,16,512]{3,2,1,0:T(8,128)(2,1)S(1)}, u32[]{:S(2)}) copy-start(bf16[8,3,16,512]{3,2,1,0:T(8,128)(2,1)S(1)} %pad_maximum_fusion.4.refs_4_) | copy-start | bytes 1179652
  173.1 7.1 %collective-permute-start.42 = (bf16[8,3,16,512]{3,2,1,0:T(8,128)(2,1)S(1)}, bf16[8,3,16,512]{3,2,1,0:T(8,128)(2,1)S(1)}, u32[]{:S(2)}, u32[]{:S(2)}) collective-permute-start(bf16[8,3,16,512]{3,2,1,0:T(8,128)(2,1)S(1)} %pad_maximum_fusion.4.refs_4_), channel_id=1, source_target_pairs={{0,24},{8,0},{16,8},{24,16},{1,25},{9,1},{17,9},{25,17},{2,26},{10... | collective-permute-start | bytes 1179656 | tf_op jit(solution)/shard_map/ppermute | solution.py:24
  174.7 7.8 %collective-permute-start.36 = (bf16[8,3,16,512]{3,2,1,0:T(8,128)(2,1)S(1)}, bf16[8,3,16,512]{3,2,1,0:T(8,128)(2,1)S(1)}, u32[]{:S(2)}, u32[]{:S(2)}) collective-permute-start(bf16[8,3,16,512]{3,2,1,0:T(8,128)(2,1)S(1)} %pad_maximum_fusion.3.refs_0_), channel_id=1, source_target_pairs={{0,6},{2,0},{4,2},{6,4},{1,7},{3,1},{5,3},{7,5},{8,14},{10,8},{12,... | collective-permute-start | bytes 1179656 | tf_op jit(solution)/shard_map/ppermute | solution.py:24
  180.2 7.1 %collective-permute-start.43 = (bf16[8,3,16,512]{3,2,1,0:T(8,128)(2,1)S(1)}, bf16[8,3,16,512]{3,2,1,0:T(8,128)(2,1)}, u32[]{:S(2)}, u32[]{:S(2)}) collective-permute-start(bf16[8,3,16,512]{3,2,1,0:T(8,128)(2,1)S(1)} %collective-permute-done.42.refs_5_), channel_id=1, source_target_pairs={{0,24},{8,0},{16,8},{24,16},{1,25},{9,1},{17,9},{25,17},{2,26},{10... | collective-permute-start | bytes 1179656 | tf_op jit(solution)/shard_map/ppermute | solution.py:24
  182.5 8.2 %collective-permute-start.37 = (bf16[8,3,16,512]{3,2,1,0:T(8,128)(2,1)S(1)}, bf16[8,3,16,512]{3,2,1,0:T(8,128)(2,1)}, u32[]{:S(2)}, u32[]{:S(2)}) collective-permute-start(bf16[8,3,16,512]{3,2,1,0:T(8,128)(2,1)S(1)} %collective-permute-done.36.refs_1_), channel_id=1, source_target_pairs={{0,6},{2,0},{4,2},{6,4},{1,7},{3,1},{5,3},{7,5},{8,14},{10,8},{12,... | collective-permute-start | bytes 1179656 | tf_op jit(solution)/shard_map/ppermute | solution.py:24
  187.2 159.3 %collective-permute-start.44 = (bf16[8,3,16,512]{3,2,1,0:T(8,128)(2,1)}, bf16[8,3,16,512]{3,2,1,0:T(8,128)(2,1)}, u32[]{:S(2)}, u32[]{:S(2)}) collective-permute-start(bf16[8,3,16,512]{3,2,1,0:T(8,128)(2,1)} %collective-permute-done.43.refs_6_), channel_id=1, source_target_pairs={{0,24},{8,0},{16,8},{24,16},{1,25},{9,1},{17,9},{25,17},{2,26},{10... | collective-permute-start | bytes 1179656 | tf_op jit(solution)/shard_map/ppermute | solution.py:24
  190.8 155.8 %collective-permute-start.38 = (bf16[8,3,16,512]{3,2,1,0:T(8,128)(2,1)}, bf16[8,3,16,512]{3,2,1,0:T(8,128)(2,1)}, u32[]{:S(2)}, u32[]{:S(2)}) collective-permute-start(bf16[8,3,16,512]{3,2,1,0:T(8,128)(2,1)} %collective-permute-done.37.refs_2_), channel_id=1, source_target_pairs={{0,6},{2,0},{4,2},{6,4},{1,7},{3,1},{5,3},{7,5},{8,14},{10,8},{12,... | collective-permute-start | bytes 1179656 | tf_op jit(solution)/shard_map/ppermute | solution.py:24
  235.0 151.5 %collective-permute-start.52 = (bf16[384,1024]{1,0:T(8,128)(2,1)}, bf16[384,1024]{1,0:T(8,128)(2,1)}, u32[]{:S(2)}, u32[]{:S(2)}) collective-permute-start(bf16[384,1024]{1,0:T(8,128)(2,1)} %finish.5), channel_id=1, source_target_pairs={{0,1},{1,0},{2,3},{3,2},{4,5},{5,4},{6,7},{7,6},{8,9},{9,8},{10,11... | collective-permute-start | bytes 2359304 | tf_op jit(solution)/shard_map/ppermute | solution.py:24
  354.7 18.8 %collective-permute-start.45 = (f32[2,8,384]{2,1,0:T(8,128)}, f32[2,8,384]{2,1,0:T(8,128)S(1)}, u32[]{:S(2)}, u32[]{:S(2)}) collective-permute-start(f32[2,8,384]{2,1,0:T(8,128)} %get-tuple-element.64.refs_0_), channel_id=1, source_target_pairs={{0,1},{1,0},{64,65},{65,64},{2,3},{3,2},{66,67},{67,66},{4,5},{5,4... | collective-permute-start | bytes 73736 | tf_op jit(solution)/shard_map/ppermute | solution.py:370
  354.8 18.7 %collective-permute-start.46 = (f32[2,8,384]{2,1,0:T(8,128)}, f32[2,8,384]{2,1,0:T(8,128)S(1)}, u32[]{:S(2)}, u32[]{:S(2)}) collective-permute-start(f32[2,8,384]{2,1,0:T(8,128)} %get-tuple-element.64.refs_0_), channel_id=1, source_target_pairs={{0,64},{64,0},{1,65},{65,1},{2,66},{66,2},{3,67},{67,3},{4,68},{68... | collective-permute-start | bytes 73736 | tf_op jit(solution)/shard_map/ppermute | solution.py:370
  356.0 17.6 %collective-permute-start.47 = (f32[2,8,384]{2,1,0:T(8,128)}, f32[2,8,384]{2,1,0:T(8,128)S(1)}, u32[]{:S(2)}, u32[]{:S(2)}) collective-permute-start(f32[2,8,384]{2,1,0:T(8,128)} %get-tuple-element.64.refs_0_), channel_id=1, source_target_pairs={{0,65},{65,0},{1,64},{64,1},{2,67},{67,2},{3,66},{66,3},{4,69},{69... | collective-permute-start | bytes 73736 | tf_op jit(solution)/shard_map/ppermute | solution.py:370
  378.8 15.7 %collective-permute-start.51 = (bf16[384,1024]{1,0:T(8,128)(2,1)}, bf16[384,1024]{1,0:T(8,128)(2,1)S(1)}, u32[]{:S(2)}, u32[]{:S(2)}) collective-permute-start(bf16[384,1024]{1,0:T(8,128)(2,1)} %finish.4), channel_id=1, source_target_pairs={{0,1},{1,0},{2,3},{3,2},{4,5},{5,4},{6,7},{7,6},{8,9},{9,8},{10,11... | collective-permute-start | bytes 2359304 | tf_op jit(solution)/shard_map/ppermute | solution.py:24
  378.8 2.6 collective-permute-start.53
  (29 other events, 196.8 us)

commit v2 on v1

--- a/solution.py
+++ b/solution.py
@@ -82,6 +82,7 @@
     idx = (s_ref[1], s_ref[2], s_ref[3])
     load_weights(pieces, w_vmem, sem, idx, head)
     gate, up, down = w_vmem[head, 0], w_vmem[head, 1], w_vmem[head, 2]
+    halves = []
     for j, (k_ref, v_ref) in enumerate(((k_own, v_own), (k_rec, v_rec))):
         k = k_ref[0]
         rate = r_ref[0, j]
@@ -94,12 +95,11 @@
         active = (silu * u).astype(bf16)
         d_gate = (back * u * s * (1.0 + g * (1.0 - s))).astype(bf16)
         d_up = (back * silu).astype(bf16)
-        parts = (dot(k, d_gate, TN), dot(k, d_up, TN), dot(active, target, TN))
-        for m in range(3):
-            if j == 0:
-                sums[m] = parts[m]
-            else:
-                sums[m] += parts[m]
+        halves.append((k, target, active, d_gate, d_up))
+    k, target, active, d_gate, d_up = (jnp.concatenate(pair, axis=0) for pair in zip(*halves))
+    sums[0] = dot(k, d_gate, TN)
+    sums[1] = dot(k, d_up, TN)
+    sums[2] = dot(active, target, TN)
     yh, z, x = idx
     for kind in range(2):
 
@@ -205,117 +205,103 @@
     )(scal, *pieces, q, q_rec)
 
 
-def attention_kernel(c, s_ref, qo, qr, k0, ka, kb, k2, v0, va, vb, v2, out_ref):
-    block = pl.program_id(1)
+LOG2E = 1.4426950408889634
+
+
+def finish_kernel(c, j, sources, count, s_ref, *refs):
+    core, chip = s_ref[0], s_ref[5]
+    block = core if j == 0 else 1 - core
+    q_ref, refs = refs[0], refs[1:]
+    before, refs = refs[: 4 * sources], refs[4 * sources :]
+    kb, k2, vb, v2, fast_ref, gain_ref = refs[:6]
+    powers, out_ref = refs[6 : 6 + count], refs[-1]
+    k0, ka, v0, va = (before[i][0] for i in range(4))
+    for more in range(1, sources):
+        here = chosen(s_ref) == more
+        k0, ka, v0, va = (
+            jnp.where(here, before[4 * more + i][0], old) for i, old in enumerate((k0, ka, v0, va))
+        )
+    first = block == 0
+    keys = (k0, jnp.where(first, ka, kb[0]), k2[0])
+    values = (v0, jnp.where(first, va, vb[0]), v2[0])
     row = lax.broadcasted_iota(jnp.int32, (TOK, TOK), 0)
     col = lax.broadcasted_iota(jnp.int32, (TOK, TOK), 1)
-    q = jnp.where(s_ref[0] == block, qo[0], qr[0])
-    keys = (k0[0], jnp.where(block == 0, ka[0], kb[0]), k2[0])
-    values = (v0[0], jnp.where(block == 0, va[0], vb[0]), v2[0])
-    scores = [dot(q, k, NT) * SCALE for k in keys]
+    scores = [dot(q_ref[0], k, NT) for k in keys]
+    low = row
     if c == 0:
-        low = jnp.where(s_ref[4] == 1, TOK, row)
-        scores[1] = jnp.where(col >= jnp.where((s_ref[4] == 1) & (block == 0), TOK, 0), scores[1], MASKED)
-    else:
-        low = row
+        low = jnp.where(chip == 0, TOK, row)
+        scores[1] = jnp.where(col >= jnp.where((chip == 0) & first, TOK, 0), scores[1], MASKED)
     scores[0] = jnp.where(col > low, scores[0], MASKED)
     scores[2] = jnp.where(col <= row, scores[2], MASKED)
     peak = jnp.max(jnp.maximum(jnp.maximum(scores[0], scores[1]), scores[2]), axis=-1, keepdims=True)
-    weights = [jnp.exp(s - peak) for s in scores]
-    total = jnp.sum(weights[0] + weights[1] + weights[2], axis=-1, keepdims=True)
-    inv = 1.0 / total
-    out_ref[0] = sum(
-        dot((w * inv).astype(bf16), v, NN) for w, v in zip(weights, values)
-    )
-
-
-def attention(c, scal, q, q_rec, before, mine):
-    def block(at):
-        return pl.BlockSpec((1, TOK, DH), lambda h, b, s: (at(b), 0, h))
-
-    return pl.pallas_call(
-        functools.partial(attention_kernel, c),
-        name="window_attention",
-        out_shape=jax.ShapeDtypeStruct((2, TOK, 2 * DH), f32),
-        grid_spec=pltpu.PrefetchScalarGridSpec(
-            num_scalar_prefetch=1,
-            grid=(2, 2),
-            in_specs=[
-                pl.BlockSpec((1, TOK, DH), lambda h, b, s: (c, 0, s[0] * 2 + h)),
-                pl.BlockSpec((1, TOK, DH), lambda h, b, s: (c, 0, h)),
-            ]
-            + [
-                block(at)
-                for o in (0, 2)
-                for at in (lambda b, o=o: o + b, lambda b, o=o: o + 1, lambda b, o=o: o, lambda b, o=o: o + b)
-            ],
-            out_specs=pl.BlockSpec(
-                (1, TOK, DH), lambda h, b, s: (jnp.where(s[0] == b, 0, 1), 0, h)
-            ),
-        ),
-        compiler_params=cparams(),
-    )(scal, q, q_rec, *(before, before, mine, mine) * 2)
-
-
-def finish_kernel(count, s_ref, fast_ref, *refs):
-    powers, (gain_ref, att_ref), out_ref = refs[:count], refs[count : count + 2], refs[-1]
+    weights = [jnp.exp2((s - peak) * (SCALE * LOG2E)) for s in scores]
+    inv = 1.0 / jnp.sum(weights[0] + weights[1] + weights[2], axis=-1, keepdims=True)
+    attended = sum(dot((w * inv).astype(bf16), v, NN) for w, v in zip(weights, values))
+
     total = sum(p[0] for p in powers[1:]) + powers[0][0]
     rs = lax.rsqrt(total * (1.0 / 4096.0) + NORM_EPS)
     col = jnp.transpose(rs)[:, :1]
-    out = (fast_ref[0] * gain_ref[...] * col + att_ref[0]).astype(bf16)
+    out = (fast_ref[0] * gain_ref[...] * col + attended).astype(bf16)
     out_ref[...] = out.reshape(out_ref.shape)
 
 
-ROWS = 128
-
-
-def finish(c, j, scal, fast, powers, gain, att, layer=None):
-    one = pl.BlockSpec((1, ROWS, 2 * DH), lambda i, s: (j, i, 0))
-    block = (lambda s: s[0]) if j == 0 else (lambda s: 1 - s[0])
-    power = pl.BlockSpec((1, 8, ROWS), lambda i, s: (block(s), 0, i))
-    more = [] if layer is None else [layer]
+def chosen(s):
+    return jnp.where(s[5] == 0, 2, jnp.where(s[4] == 1, 1, 0))
+
+
+def finish(c, j, scal, q, q_rec, mine, before, fast, powers, gain, layer=None):
+    def block(s):
+        return s[0] if j == 0 else 1 - s[0]
+
+    def spec(at, holds=lambda s: True):
+        return pl.BlockSpec(
+            (1, TOK, DH),
+            lambda h, s: (jnp.where(holds(s), at(s), 0), 0, jnp.where(holds(s), h, 0)),
+        )
+
+    def always(at):
+        return pl.BlockSpec((1, TOK, DH), lambda h, s: (at(s), 0, h))
+
+    sources = len(before)
+    q_spec = own_spec(c) if j == 0 else rec_spec(c)
+    specs = [q_spec]
+    operands = [q if j == 0 else q_rec]
+    for i, array in enumerate(before):
+        holds = (lambda s, i=i: chosen(s) == i) if sources > 1 else (lambda s: True)
+        specs += [
+            spec(block, holds), spec(lambda s: 1, holds),
+            spec(lambda s: 2 + block(s), holds), spec(lambda s: 3, holds),
+        ]
+        operands += [array] * 4
+    specs += [
+        always(lambda s: 0), always(block), always(lambda s: 2), always(lambda s: 2 + block(s)),
+        pl.BlockSpec((1, TOK, DH), lambda h, s: (j, 0, h)),
+        pl.BlockSpec((1, DH), lambda h, s: (0, h)),
+    ]
+    operands += [mine] * 4 + [fast, gain]
+    specs += [pl.BlockSpec((1, 8, TOK), lambda h, s: (block(s), 0, 0))] * len(powers)
+    operands += powers
+    aliases = {}
+    if layer is not None:
+        aliases = {len(operands) + 1: 0}
+        specs.append(ANY)
+        operands.append(layer)
     if j == 0:
         shape = (2, TOK, 4 * DH)
-        spec = pl.BlockSpec((1, ROWS, 2 * DH), lambda i, s: (c, i, s[0]))
+        out_spec = pl.BlockSpec((1, TOK, DH), lambda h, s: (c, 0, s[0] * 2 + h))
     else:
         shape = (TOK, 2 * DH)
-        spec = pl.BlockSpec((ROWS, 2 * DH), lambda i, s: (i, 0))
-    count = len(powers)
+        out_spec = pl.BlockSpec((TOK, DH), lambda h, s: (0, h))
     return pl.pallas_call(
-        functools.partial(finish_kernel, count),
-        name="finish",
+        functools.partial(finish_kernel, c, j, sources, len(powers)),
+        name="attend_finish",
         out_shape=jax.ShapeDtypeStruct(shape, bf16),
         grid_spec=pltpu.PrefetchScalarGridSpec(
-            num_scalar_prefetch=1,
-            grid=(TOK // ROWS,),
-            in_specs=[one] + [power] * count
-            + [pl.BlockSpec((1, 2 * DH), lambda i, s: (0, 0)), one]
-            + [ANY] * len(more),
-            out_specs=spec,
+            num_scalar_prefetch=1, grid=(2,), in_specs=specs, out_specs=out_spec
         ),
-        input_output_aliases={count + 4: 0} if more else {},
+        input_output_aliases=aliases,
         compiler_params=cparams(),
-    )(scal, fast, *powers, gain, att, *more)
-
-
-def place_kernel(s_ref, arrived_ref, layer_ref, out_ref):
-    out_ref[0] = arrived_ref[...]
-
-
-def place(c, scal, arrived, layer):
-    return pl.pallas_call(
-        place_kernel,
-        name="place",
-        out_shape=jax.ShapeDtypeStruct((2, TOK, 4 * DH), bf16),
-        grid_spec=pltpu.PrefetchScalarGridSpec(
-            num_scalar_prefetch=1,
-            grid=(3,),
-            in_specs=[pl.BlockSpec((TOK // 3, 2 * DH), lambda i, s: (i, 0)), ANY],
-            out_specs=pl.BlockSpec((1, TOK // 3, 2 * DH), lambda i, s: (c, i, 1 - s[0])),
-        ),
-        input_output_aliases={2: 0},
-        compiler_params=cparams(),
-    )(scal, arrived, layer)
+    )(scal, *operands)
 
 
 def gather_direct(both):
@@ -374,8 +360,8 @@
     core = lax.axis_index("core")
     yh, z, x = lax.axis_index("yh"), lax.axis_index("z"), lax.axis_index("x")
     chip = (yh * 4 + z) * 4 + x
-    first = (chip == 0).astype(jnp.int32)
-    scal = jnp.stack([core, yh, z, x, first]).astype(jnp.int32)
+    turn = ((z == 0) & (x == 0)).astype(jnp.int32)
+    scal = jnp.stack([core, yh, z, x, turn, chip]).astype(jnp.int32)
 
     masters = jnp.stack([w_gate, w_up, w_down], axis=1)
     mine = lax.dynamic_slice_in_dim(masters, core * 2, 2, 0)
@@ -443,21 +429,17 @@
 
     gain = lax.dynamic_slice_in_dim(out_gain, core * 1024, 1024, 0)[None]
 
-    def attend(c, before, mine):
-        return attention(c, scal, queries, q_rec, before, mine)
-
-    def complete(c, fast, powers, attended, layer):
-        out_rec = finish(c, 1, scal, fast, powers, gain, attended)
+    def complete(c, before, fast, powers, layer):
+        args = (scal, queries, q_rec, pair[c], before, fast, powers, gain)
+        out_rec = finish(c, 1, *args)
         arrived = shift(out_rec, "core", 1)
-        layer = finish(c, 0, scal, fast, powers, gain, attended, layer)
-        return place(c, scal, arrived, layer)
-
-    layer_out = complete(0, fast0, powers0, attend(0, halo0, pair[0]), None)
-    before1 = jnp.where(chip == 0, halo0, jnp.where((z == 0) & (x == 0), turned1, halo1))
-    att1 = attend(1, before1, pair[1])
+        layer = finish(c, 0, *args, layer)
+        return lax.dynamic_update_slice(layer, arrived[None], (c, 0, (1 - core) * 1024))
+
+    layer_out = complete(0, [halo0], fast0, powers0, None)
     fast1, pow1 = fast_apply(1, scal, pieces2, queries, q_rec)
     powers1 = with_parts(pow1, (CORES, HALVES, ACROSS))
-    layer_out = complete(1, fast1, powers1, att1, layer_out)
+    layer_out = complete(1, [halo1, turned1, halo0], fast1, powers1, layer_out)
     return layer_out, new_all[:, 0], new_all[:, 1], new_all[:, 2]
 
 

time: 400 us -> 385 us (0.963)
  starting transfers between devices: 201 us -> 227 us
  waiting for transfers between devices: 84.6 us -> 60.8 us
  Pallas kernels: 77.9 us -> 62.1 us
  other arithmetic: 15.7 us -> 11 us
    ppermute x1, waiting for transfers between devices: 25 us -> 0.01 us  [on_device(): halo0 = lax.ppermute(pair[0], chips, row)]
    ppermute x46, starting transfers between devices: 190 us -> 212 us  [shift(): lax.ppermute(value, axis, [(i, (i + steps) % count) for i in range(count)])]
    pallas_call x8 -> x4, Pallas kernels: 48.4 us -> 33.8 us  [finish(): pl.pallas_call(functools.partial(finish_kernel, c, j, sources, len(powers...]
    select_n x1 -> x0, other arithmetic: 4.92 us -> none  [on_device(): jnp.where(chip == 0, halo0, jnp.where((z == 0) & (x == 0), turned1, halo1))]
  transfers between devices with their start and end apart: 54 -> 54, of which waited for: 24 -> 26; matrix products, arithmetic and copies ran while one was open for 7% -> 6% of each run, Pallas kernels for 15% -> 13%
where the time goes in v2:
time: 385 us; the launch traced here: 383 us
  starting transfers between devices  227 us (59%)
  Pallas kernels  62.1 us (16%)
  waiting for transfers between devices  60.8 us (16%)
  local copies, waits for them, and re-layouts  20.7 us (5%)
  other arithmetic  11 us (3%)
    ppermute x46, starting transfers between devices, shift(): lax.ppermute(value, axis, [(i, (i + steps) % count) for i in range(count)])  212 us
    ppermute x46, waiting for transfers between devices, shift(): lax.ppermute(value, axis, [(i, (i + steps) % count) for i in range(count)])  55.2 us
    pallas_call x4, Pallas kernels, finish(): pl.pallas_call(functools.partial(finish_kernel, c, j, sources, len(powers...  33.8 us
    pallas_call x2, Pallas kernels, fast_apply(): pl.pallas_call(apply_kernel, name='fast_apply', out_shape=[jax.ShapeDtype...  16.3 us
    pallas_call x1, Pallas kernels, compute_grads(): pl.pallas_call(grads_kernel, name='fast_grads', out_shape=[jax.ShapeDtype...  12 us
  transfers between devices with their start and end apart: 54, of which 26 were waited for; matrix products, arithmetic and copies ran while one was open for 6% of the time, Pallas kernels for 13%

profile of v2, /device:TPU:1, one launch (start us, length us, event | category | flops | bytes accessed | tf_op | source)
XLA Modules:
  0.0 383.2 jit_solution(6247289223787035873)
XLA Ops:
  1.6 1.5 collective-permute-start
  4.0 3.1 collective-permute-start.1
  7.1 4.8 %collective-permute-done.1 = f32[2,3,16,512]{3,2,1,0:T(8,128)} collective-permute-done((f32[2,3,16,512]{3,2,1,0:T(8,128)S(1)}, f32[2,3,16,512]{3,2,1,0:T(8,128)}, u32[]{:S(2)}, u32[]{:S(2)}) %collective-permute-start.1) | collective-permute-done | bytes 196640 | tf_op jit(solution)/shard_map/ppermute | solution.py:24
  11.9 2.7 constant_dynamic-slice_fusion.5
  15.8 1.3 constant_dynamic-slice_fusion.7
  18.7 1.8 collective-permute-start.6
  20.5 3.3 collective-permute-start.5
  24.9 2.7 constant_dynamic-slice_fusion.8
  27.6 1.3 constant_dynamic-slice_fusion.6
  32.1 2.5 collective-permute-start.11
  37.1 2.1 collective-permute-done.11
  42.0 1.7 fusion.15
  43.7 1.6 collective-permute-start.14
  45.3 1.5 fusion.14
  46.8 2.1 collective-permute-done.9.refs_3_
  48.9 1.5 collective-permute-start.13
  50.5 3.5 maximum_select_fusion
  54.7 2.4 collective-permute-done.7.refs_1_
  57.1 2.0 collective-permute-done.14.refs_6_
  60.7 12.0 %fast_grads.1 = (bf16[8,3,16,512]{3,2,1,0:T(8,128)(2,1)}, bf16[8,3,16,512]{3,2,1,0:T(8,128)(2,1)}, bf16[8,3,16,512]{3,2,1,0:T(8,128)(2,1)}, bf16[8,3,16,512]{3,2...) custom-call(s32[6]{0:T(128)} %stack.78.s_ref, ...), custom_call_target="tpu_custom_call" | custom-call | tf_op jit(solution)/shard_map/fast_grads/pallas_call | solution.py:132
  72.8 2.5 collective-permute-start.18
  75.5 4.0 %collective-permute-start.30 = (bf16[2,384,1024]{2,1,0:T(8,128)(2,1)S(1)}, bf16[2,384,1024]{2,1,0:T(8,128)(2,1)S(1)}, u32[]{:S(2)}, u32[]{:S(2)}) collective-permute-start(bf16[2,384,1024]{2,1,0:T(8,128)(2,1)S(1)} %constant_dynamic-slice_fusion.2), channel_id=1, source_target_pairs={{0,1},{1,0},{2,3},{3,2},{4,5},{5,4},{6,7},{7,6},{8,9},{9,8},{10,11... | collective-permute-start | bytes 4718600 | tf_op jit(solution)/shard_map/ppermute | solution.py:24
  79.5 2.7 collective-permute-start.24
  82.3 3.1 collective-permute-start.19
  85.4 4.6 %collective-permute-done.24 = bf16[8,3,16,512]{3,2,1,0:T(8,128)(2,1)S(1)} collective-permute-done((bf16[8,3,16,512]{3,2,1,0:T(8,128)(2,1)S(1)}, bf16[8,3,16,512]{3,2,1,0:T(8,128)(2,1)S(1)}, u32[]{:S(2)}, u32[]{:S(2)}) %collective-permute-start.24) | collective-permute-done | bytes 393248 | tf_op jit(solution)/shard_map/ppermute | solution.py:24
  90.2 3.5 collective-permute-start.25
  95.1 5.6 %collective-permute-done.25 = bf16[8,3,16,512]{3,2,1,0:T(8,128)(2,1)S(1)} collective-permute-done((bf16[8,3,16,512]{3,2,1,0:T(8,128)(2,1)S(1)}, bf16[8,3,16,512]{3,2,1,0:T(8,128)(2,1)S(1)}, u32[]{:S(2)}, u32[]{:S(2)}) %collective-permute-start.25) | collective-permute-done | bytes 393248 | tf_op jit(solution)/shard_map/ppermute | solution.py:24
  100.8 3.5 collective-permute-start.26
  105.5 8.1 %fast_apply.2 = (f32[2,384,1024]{2,1,0:T(8,128)}, f32[2,8,384]{2,1,0:T(8,128)}) custom-call(s32[6]{0:T(128)} %stack.78.s_ref, bf16[8,3,16,512]{3,2,1,0:T(8,128)(2,1)} %copy-done.6, bf16[8,3,16,512]{3,2,1,0:T(8,128)(2,1)} %copy-done.16, bf16[8,3,16,512]{3,2,1,0:T(8,128)(2,1)} %copy-done.15, bf16[8,3,16,512]{3,2,1,0:T(8,128)(2,1)} %copy-done.14, ...), custom_call_target="tpu_custom_call" | custom-call | tf_op jit(solution)/shard_map/fast_apply/pallas_call | solution.py:184
  113.6 2.7 collective-permute-start.31
  120.1 3.2 collective-permute-done.21
  123.3 1.5 collective-permute-start.22
  125.5 1.3 collective-permute-done.22
  126.9 2.8 collective-permute-start.23
  131.3 2.5 collective-permute-done.29
  133.8 3.0 collective-permute-start.32
  136.8 1.8 collective-permute-start.35
  138.6 3.6 collective-permute-start.16
  142.7 2.2 collective-permute-done.33.refs_12_
  144.9 2.3 collective-permute-start.34
  148.2 134.2 %collective-permute-start.36 = (bf16[2,3,16,512]{3,2,1,0:T(8,128)(2,1)S(1)}, bf16[2,3,16,512]{3,2,1,0:T(8,128)(2,1)S(1)}, u32[]{:S(2)}, u32[]{:S(2)}) collective-permute-start(bf16[2,3,16,512]{3,2,1,0:T(8,128)(2,1)S(1)} %get-tuple-element.86), channel_id=1, source_target_pairs={{0,24},{8,0},{16,8},{24,16},{1,25},{9,1},{17,9},{25,17},{2,26},{10... | collective-permute-start | bytes 294920 | tf_op jit(solution)/shard_map/ppermute | solution.py:24
  282.5 1.6 collective-permute-done.36
  284.1 3.0 collective-permute-start.37
  287.1 1.6 collective-permute-done.37
  288.8 3.0 collective-permute-start.38
  291.8 1.6 collective-permute-done.38
  293.6 2.0 collective-permute-done.44
  296.8 4.5 %collective-permute-done.39.refs_1_ = bf16[8,3,16,512]{3,2,1,0:T(8,128)(2,1)S(1)} collective-permute-done((bf16[8,3,16,512]{3,2,1,0:T(8,128)(2,1)S(1)}, bf16[8,3,16,512]{3,2,1,0:T(8,128)(2,1)S(1)}, u32[]{:S(2)}, u32[]{:S(2)}) %collective-permute-start.39) | collective-permute-done | bytes 393248 | tf_op jit(solution)/shard_map/ppermute | solution.py:24
  301.3 1.7 collective-permute-start.40
  302.9 2.1 collective-permute-start.46
  305.0 5.1 %collective-permute-done.40.refs_2_ = bf16[8,3,16,512]{3,2,1,0:T(8,128)(2,1)} collective-permute-done((bf16[8,3,16,512]{3,2,1,0:T(8,128)(2,1)S(1)}, bf16[8,3,16,512]{3,2,1,0:T(8,128)(2,1)}, u32[]{:S(2)}, u32[]{:S(2)}) %collective-permute-start.40) | collective-permute-done | bytes 393248 | tf_op jit(solution)/shard_map/ppermute | solution.py:24
  311.0 2.4 collective-permute-done.46.refs_6_
  313.4 1.3 collective-permute-start.47
  315.3 1.6 copy-done
  317.0 7.6 %attend_finish.5 = bf16[384,1024]{1,0:T(8,128)(2,1)} custom-call(s32[6]{0:T(128)} %stack.78.s_ref, bf16[2,384,1024]{2,1,0:T(8,128)(2,1)} %copy-done.3, bf16[4,384,1024]{2,1,0:T(8,128)(2,1)} %copy-done, bf16[4,384,1024]{2,1,0:T(8,128)(2,1)} %copy-done, bf16[4,384,1024]{2,1,0:T(8,128)(2,1)} %copy-done, bf16[4,384,1024]{2,1,0:T(8,128)(2,1)} %copy-done, ...), custom_call_target="tpu_custom_call" | custom-call | tf_op jit(solution)/shard_map/attend_finish/pallas_call | solution.py:295
  324.6 10.2 %collective-permute-start.51 = (bf16[384,1024]{1,0:T(8,128)(2,1)}, bf16[384,1024]{1,0:T(8,128)(2,1)S(1)}, u32[]{:S(2)}, u32[]{:S(2)}) collective-permute-start(bf16[384,1024]{1,0:T(8,128)(2,1)} %attend_finish.5), channel_id=1, source_target_pairs={{0,1},{1,0},{2,3},{3,2},{4,5},{5,4},{6,7},{7,6},{8,9},{9,8},{10,11... | collective-permute-start | bytes 2359304 | tf_op jit(solution)/shard_map/ppermute | solution.py:24
  334.8 8.2 %fast_apply.3 = (f32[2,384,1024]{2,1,0:T(8,128)}, f32[2,8,384]{2,1,0:T(8,128)}) custom-call(s32[6]{0:T(128)} %stack.78.s_ref, bf16[8,3,16,512]{3,2,1,0:T(8,128)(2,1)} %copy-done.12, bf16[8,3,16,512]{3,2,1,0:T(8,128)(2,1)} %copy-done.20, bf16[8,3,16,512]{3,2,1,0:T(8,128)(2,1)} %collective-permute-done.40.refs_2_, ...), custom_call_target="tpu_custom_call" | custom-call | tf_op jit(solution)/shard_map/fast_apply/pallas_call | solution.py:184
  343.0 3.8 %collective-permute-start.50 = (f32[2,8,384]{2,1,0:T(8,128)}, f32[2,8,384]{2,1,0:T(8,128)S(1)}, u32[]{:S(2)}, u32[]{:S(2)}) collective-permute-start(f32[2,8,384]{2,1,0:T(8,128)} %get-tuple-element.66.refs_19_), channel_id=1, source_target_pairs={{0,65},{65,0},{1,64},{64,1},{2,67},{67,2},{3,66},{66,3},{4,69},{69... | collective-permute-start | bytes 73736 | tf_op jit(solution)/shard_map/ppermute | solution.py:356
  347.3 1.3 collective-permute-done.50.refs_22_
  350.3 9.3 %attend_finish.7 = bf16[384,1024]{1,0:T(8,128)(2,1)} custom-call(s32[6]{0:T(128)} %stack.78.s_ref, bf16[2,384,1024]{2,1,0:T(8,128)(2,1)} %copy-done.3, bf16[4,384,1024]{2,1,0:T(8,128)(2,1)} %collective-permute-done.16.refs_1_.refs_2_.refs_3_.refs_4_, bf16[4,384,1024]{2,1,0:T(8,128)(2,1)} %collective-permute-done.16.refs_1_.refs_2_.refs_3_.refs_4_, ...), custom_call_target="tpu_custom_call" | custom-call | tf_op jit(solution)/shard_map/attend_finish/pallas_call | solution.py:295
  359.6 1.7 collective-permute-start.52
  361.5 2.1 collective-permute-done.53
  364.3 7.6 %attend_finish.4 = bf16[2,384,2048]{2,1,0:T(8,128)(2,1)} custom-call(s32[6]{0:T(128)} %stack.78.s_ref, bf16[2,384,2048]{2,1,0:T(8,128)(2,1)} %refs_0_.1, bf16[4,384,1024]{2,1,0:T(8,128)(2,1)} %copy-done, bf16[4,384,1024]{2,1,0:T(8,128)(2,1)} %copy-done, bf16[4,384,1024]{2,1,0:T(8,128)(2,1)} %copy-done, bf16[4,384,1024]{2,1,0:T(8,128)(2,1)} %copy-done, ...), custom_call_target="tpu_custom_call" | custom-call | tf_op jit(solution)/shard_map/attend_finish/pallas_call | solution.py:295
  372.8 9.4 %attend_finish.6 = bf16[2,384,2048]{2,1,0:T(8,128)(2,1)} custom-call(s32[6]{0:T(128)} %stack.78.s_ref, bf16[2,384,2048]{2,1,0:T(8,128)(2,1)} %refs_0_.1, bf16[4,384,1024]{2,1,0:T(8,128)(2,1)} %collective-permute-done.16.refs_1_.refs_2_.refs_3_.refs_4_, ...), custom_call_target="tpu_custom_call", output_to_operand_aliasing={{}: (24, {})} | custom-call | tf_op jit(solution)/shard_map/attend_finish/pallas_call | solution.py:295
  (173 shorter events, 35.1 us)
Async XLA Ops:
  1.6 2.4 collective-permute-start
  4.0 7.9 %collective-permute-start.1 = (f32[2,3,16,512]{3,2,1,0:T(8,128)S(1)}, f32[2,3,16,512]{3,2,1,0:T(8,128)}, u32[]{:S(2)}, u32[]{:S(2)}) collective-permute-start(f32[2,3,16,512]{3,2,1,0:T(8,128)S(1)} %maximum_select_fusion.2), channel_id=1, source_target_pairs={{0,32},{32,0},{1,33},{33,1},{2,34},{34,2},{3,35},{35,3},{4,36},{36... | collective-permute-start | bytes 589832 | tf_op jit(solution)/shard_map/ppermute | solution.py:24
  14.6 26.6 %collective-permute-start.3 = (bf16[2,384,1024]{2,1,0:T(8,128)(2,1)}, bf16[2,384,1024]{2,1,0:T(8,128)(2,1)}, u32[]{:S(2)}, u32[]{:S(2)}) collective-permute-start(bf16[2,384,1024]{2,1,0:T(8,128)(2,1)} %constant_dynamic-slice_fusion.5), channel_id=1, source_target_pairs={{0,1},{1,0},{2,3},{3,2},{4,5},{5,4},{6,7},{7,6},{8,9},{9,8},{10,11... | collective-permute-start | bytes 4718600 | tf_op jit(solution)/shard_map/ppermute | solution.py:24
  17.1 26.6 %collective-permute-start.2 = (bf16[2,384,1024]{2,1,0:T(8,128)(2,1)}, bf16[2,384,1024]{2,1,0:T(8,128)(2,1)}, u32[]{:S(2)}, u32[]{:S(2)}) collective-permute-start(bf16[2,384,1024]{2,1,0:T(8,128)(2,1)} %constant_dynamic-slice_fusion.7), channel_id=1, source_target_pairs={{0,1},{1,0},{2,3},{3,2},{4,5},{5,4},{6,7},{7,6},{8,9},{9,8},{10,11... | collective-permute-start | bytes 4718600 | tf_op jit(solution)/shard_map/ppermute | solution.py:24
  18.7 12.2 %collective-permute-start.6 = (bf16[2,3,16,512]{3,2,1,0:T(8,128)(2,1)S(1)}, bf16[2,3,16,512]{3,2,1,0:T(8,128)(2,1)}, u32[]{:S(2)}, u32[]{:S(2)}) collective-permute-start(bf16[2,3,16,512]{3,2,1,0:T(8,128)(2,1)S(1)} %get-tuple-element.88), channel_id=1, source_target_pairs={{0,8},{8,16},{16,24},{24,0},{1,9},{9,17},{17,25},{25,1},{2,10},{10... | collective-permute-start | bytes 294920 | tf_op jit(solution)/shard_map/ppermute | solution.py:24
  20.5 11.6 %collective-permute-start.5 = (bf16[2,3,16,512]{3,2,1,0:T(8,128)(2,1)S(1)}, bf16[2,3,16,512]{3,2,1,0:T(8,128)(2,1)}, u32[]{:S(2)}, u32[]{:S(2)}) collective-permute-start(bf16[2,3,16,512]{3,2,1,0:T(8,128)(2,1)S(1)} %get-tuple-element.88), channel_id=1, source_target_pairs={{0,16},{8,24},{16,0},{24,8},{1,17},{9,25},{17,1},{25,9},{2,18},{10... | collective-permute-start | bytes 294920 | tf_op jit(solution)/shard_map/ppermute | solution.py:24
  23.8 5.1 %collective-permute-start.17 = (f32[2,384]{1,0:T(2,128)S(1)}, f32[2,384]{1,0:T(2,128)S(1)}, u32[]{:S(2)}, u32[]{:S(2)}) collective-permute-start(f32[2,384]{1,0:T(2,128)S(1)} %get-tuple-element.92), channel_id=1, source_target_pairs={{0,1},{1,0},{2,3},{3,2},{4,5},{5,4},{6,7},{7,6},{8,9},{9,8},{10,11... | collective-permute-start | bytes 9224 | tf_op jit(solution)/shard_map/ppermute | solution.py:24
  28.9 5.6 %collective-permute-start.4 = (bf16[2,3,16,512]{3,2,1,0:T(8,128)(2,1)S(1)}, bf16[2,3,16,512]{3,2,1,0:T(8,128)(2,1)S(1)}, u32[]{:S(2)}, u32[]{:S(2)}) collective-permute-start(bf16[2,3,16,512]{3,2,1,0:T(8,128)(2,1)S(1)} %get-tuple-element.88), channel_id=1, source_target_pairs={{0,24},{8,0},{16,8},{24,16},{1,25},{9,1},{17,9},{25,17},{2,26},{10... | collective-permute-start | bytes 294920 | tf_op jit(solution)/shard_map/ppermute | solution.py:24
  30.9 5.9 %collective-permute-start.12 = (bf16[2,3,16,512]{3,2,1,0:T(8,128)(2,1)S(1)}, bf16[2,3,16,512]{3,2,1,0:T(8,128)(2,1)S(1)}, u32[]{:S(2)}, u32[]{:S(2)}) collective-permute-start(bf16[2,3,16,512]{3,2,1,0:T(8,128)(2,1)S(1)} %get-tuple-element.87), channel_id=1, source_target_pairs={{0,2},{2,4},{4,6},{6,0},{1,3},{3,5},{5,7},{7,1},{8,10},{10,12},{12... | collective-permute-start | bytes 294920 | tf_op jit(solution)/shard_map/ppermute | solution.py:24
  32.1 7.1 %collective-permute-start.11 = (bf16[2,3,16,512]{3,2,1,0:T(8,128)(2,1)S(1)}, bf16[2,3,16,512]{3,2,1,0:T(8,128)(2,1)S(1)}, u32[]{:S(2)}, u32[]{:S(2)}) collective-permute-start(bf16[2,3,16,512]{3,2,1,0:T(8,128)(2,1)S(1)} %get-tuple-element.87), channel_id=1, source_target_pairs={{0,4},{2,6},{4,0},{6,2},{1,5},{3,7},{5,1},{7,3},{8,12},{10,14},{12... | collective-permute-start | bytes 294920 | tf_op jit(solution)/shard_map/ppermute | solution.py:24
  34.5 5.3 %collective-permute-start.10 = (bf16[2,3,16,512]{3,2,1,0:T(8,128)(2,1)S(1)}, bf16[2,3,16,512]{3,2,1,0:T(8,128)(2,1)S(1)}, u32[]{:S(2)}, u32[]{:S(2)}) collective-permute-start(bf16[2,3,16,512]{3,2,1,0:T(8,128)(2,1)S(1)} %get-tuple-element.87), channel_id=1, source_target_pairs={{0,6},{2,0},{4,2},{6,4},{1,7},{3,1},{5,3},{7,5},{8,14},{10,8},{12,... | collective-permute-start | bytes 294920 | tf_op jit(solution)/shard_map/ppermute | solution.py:24
  36.8 12.2 %collective-permute-start.9 = (bf16[8,3,16,512]{3,2,1,0:T(8,128)(2,1)S(1)}, bf16[8,3,16,512]{3,2,1,0:T(8,128)(2,1)S(1)}, u32[]{:S(2)}, u32[]{:S(2)}) collective-permute-start(bf16[8,3,16,512]{3,2,1,0:T(8,128)(2,1)S(1)} %pad_maximum_fusion.1.refs_0_), channel_id=1, source_target_pairs={{0,2},{2,4},{4,6},{6,0},{1,3},{3,5},{5,7},{7,1},{8,10},{10,12},{12... | collective-permute-start | bytes 1179656 | tf_op jit(solution)/shard_map/ppermute | solution.py:24
  39.2 15.4 %collective-permute-start.8 = (bf16[8,3,16,512]{3,2,1,0:T(8,128)(2,1)S(1)}, bf16[8,3,16,512]{3,2,1,0:T(8,128)(2,1)S(1)}, u32[]{:S(2)}, u32[]{:S(2)}) collective-permute-start(bf16[8,3,16,512]{3,2,1,0:T(8,128)(2,1)S(1)} %pad_maximum_fusion.1.refs_0_), channel_id=1, source_target_pairs={{0,4},{2,6},{4,0},{6,2},{1,5},{3,7},{5,1},{7,3},{8,12},{10,14},{12... | collective-permute-start | bytes 1179656 | tf_op jit(solution)/shard_map/ppermute | solution.py:24
  39.8 17.3 %collective-permute-start.7 = (bf16[8,3,16,512]{3,2,1,0:T(8,128)(2,1)S(1)}, bf16[8,3,16,512]{3,2,1,0:T(8,128)(2,1)S(1)}, u32[]{:S(2)}, u32[]{:S(2)}) collective-permute-start(bf16[8,3,16,512]{3,2,1,0:T(8,128)(2,1)S(1)} %pad_maximum_fusion.1.refs_0_), channel_id=1, source_target_pairs={{0,6},{2,0},{4,2},{6,4},{1,7},{3,1},{5,3},{7,5},{8,14},{10,8},{12,... | collective-permute-start | bytes 1179656 | tf_op jit(solution)/shard_map/ppermute | solution.py:24
  41.2 15.9 %collective-permute-start.15 = (bf16[8,3,16,512]{3,2,1,0:T(8,128)(2,1)S(1)}, bf16[8,3,16,512]{3,2,1,0:T(8,128)(2,1)S(1)}, u32[]{:S(2)}, u32[]{:S(2)}) collective-permute-start(bf16[8,3,16,512]{3,2,1,0:T(8,128)(2,1)S(1)} %pad_maximum_fusion.2.refs_4_), channel_id=1, source_target_pairs={{0,8},{8,16},{16,24},{24,0},{1,9},{9,17},{17,25},{25,1},{2,10},{10... | collective-permute-start | bytes 1179656 | tf_op jit(solution)/shard_map/ppermute | solution.py:24
  43.7 15.4 %collective-permute-start.14 = (bf16[8,3,16,512]{3,2,1,0:T(8,128)(2,1)S(1)}, bf16[8,3,16,512]{3,2,1,0:T(8,128)(2,1)S(1)}, u32[]{:S(2)}, u32[]{:S(2)}) collective-permute-start(bf16[8,3,16,512]{3,2,1,0:T(8,128)(2,1)S(1)} %pad_maximum_fusion.2.refs_4_), channel_id=1, source_target_pairs={{0,16},{8,24},{16,0},{24,8},{1,17},{9,25},{17,1},{25,9},{2,18},{10... | collective-permute-start | bytes 1179656 | tf_op jit(solution)/shard_map/ppermute | solution.py:24
  48.9 11.0 %collective-permute-start.13 = (bf16[8,3,16,512]{3,2,1,0:T(8,128)(2,1)S(1)}, bf16[8,3,16,512]{3,2,1,0:T(8,128)(2,1)S(1)}, u32[]{:S(2)}, u32[]{:S(2)}) collective-permute-start(bf16[8,3,16,512]{3,2,1,0:T(8,128)(2,1)S(1)} %pad_maximum_fusion.2.refs_4_), channel_id=1, source_target_pairs={{0,24},{8,0},{16,8},{24,16},{1,25},{9,1},{17,9},{25,17},{2,26},{10... | collective-permute-start | bytes 1179656 | tf_op jit(solution)/shard_map/ppermute | solution.py:24
  53.9 82.9 %copy-start.1 = (bf16[4,384,1024]{2,1,0:T(8,128)(2,1)}, bf16[4,384,1024]{2,1,0:T(8,128)(2,1)S(1)}, u32[]{:S(2)}) copy-start(bf16[4,384,1024]{2,1,0:T(8,128)(2,1)S(1)} %get-tuple-element.63.refs_5_.refs_6_.refs_7_.refs_8_) | copy-start | bytes 9437188
  72.8 20.9 %copy-start.25 = (bf16[8,3,16,512]{3,2,1,0:T(8,128)(2,1)S(1)}, bf16[8,3,16,512]{3,2,1,0:T(8,128)(2,1)}, u32[]{:S(2)}) copy-start(bf16[8,3,16,512]{3,2,1,0:T(8,128)(2,1)} %get-tuple-element.53) | copy-start | bytes 1179652
  72.8 27.9 %copy-start.24 = (bf16[8,3,16,512]{3,2,1,0:T(8,128)(2,1)S(1)}, bf16[8,3,16,512]{3,2,1,0:T(8,128)(2,1)}, u32[]{:S(2)}) copy-start(bf16[8,3,16,512]{3,2,1,0:T(8,128)(2,1)} %get-tuple-element.57) | copy-start | bytes 1179652
  72.8 9.3 %collective-permute-start.18 = (bf16[8,3,16,512]{3,2,1,0:T(8,128)(2,1)}, bf16[8,3,16,512]{3,2,1,0:T(8,128)(2,1)S(1)}, u32[]{:S(2)}, u32[]{:S(2)}) collective-permute-start(bf16[8,3,16,512]{3,2,1,0:T(8,128)(2,1)} %get-tuple-element.51), channel_id=1, source_target_pairs={{0,6},{2,0},{4,2},{6,4},{1,7},{3,1},{5,3},{7,5},{8,14},{10,8},{12,... | collective-permute-start | bytes 1179656 | tf_op jit(solution)/shard_map/ppermute | solution.py:24
  75.5 28.8 %collective-permute-start.30 = (bf16[2,384,1024]{2,1,0:T(8,128)(2,1)S(1)}, bf16[2,384,1024]{2,1,0:T(8,128)(2,1)S(1)}, u32[]{:S(2)}, u32[]{:S(2)}) collective-permute-start(bf16[2,384,1024]{2,1,0:T(8,128)(2,1)S(1)} %constant_dynamic-slice_fusion.2), channel_id=1, source_target_pairs={{0,1},{1,0},{2,3},{3,2},{4,5},{5,4},{6,7},{7,6},{8,9},{9,8},{10,11... | collective-permute-start | bytes 4718600 | tf_op jit(solution)/shard_map/ppermute | solution.py:24
  79.5 10.5 %collective-permute-start.24 = (bf16[8,3,16,512]{3,2,1,0:T(8,128)(2,1)S(1)}, bf16[8,3,16,512]{3,2,1,0:T(8,128)(2,1)S(1)}, u32[]{:S(2)}, u32[]{:S(2)}) collective-permute-start(bf16[8,3,16,512]{3,2,1,0:T(8,128)(2,1)S(1)} %copy-done.35), channel_id=1, source_target_pairs={{0,24},{8,0},{16,8},{24,16},{1,25},{9,1},{17,9},{25,17},{2,26},{10... | collective-permute-start | bytes 1179656 | tf_op jit(solution)/shard_map/ppermute | solution.py:24
  82.3 11.4 %collective-permute-start.19 = (bf16[8,3,16,512]{3,2,1,0:T(8,128)(2,1)S(1)}, bf16[8,3,16,512]{3,2,1,0:T(8,128)(2,1)S(1)}, u32[]{:S(2)}, u32[]{:S(2)}) collective-permute-start(bf16[8,3,16,512]{3,2,1,0:T(8,128)(2,1)S(1)} %add_convert_fusion.3), channel_id=1, source_target_pairs={{0,6},{2,0},{4,2},{6,4},{1,7},{3,1},{5,3},{7,5},{8,14},{10,8},{12,... | collective-permute-start | bytes 1179656 | tf_op jit(solution)/shard_map/ppermute | solution.py:24
  90.2 10.5 %collective-permute-start.25 = (bf16[8,3,16,512]{3,2,1,0:T(8,128)(2,1)S(1)}, bf16[8,3,16,512]{3,2,1,0:T(8,128)(2,1)S(1)}, u32[]{:S(2)}, u32[]{:S(2)}) collective-permute-start(bf16[8,3,16,512]{3,2,1,0:T(8,128)(2,1)S(1)} %add_convert_fusion.1), channel_id=1, source_target_pairs={{0,24},{8,0},{16,8},{24,16},{1,25},{9,1},{17,9},{25,17},{2,26},{10... | collective-permute-start | bytes 1179656 | tf_op jit(solution)/shard_map/ppermute | solution.py:24
  94.5 23.5 %collective-permute-start.20 = (bf16[8,3,16,512]{3,2,1,0:T(8,128)(2,1)}, bf16[8,3,16,512]{3,2,1,0:T(8,128)(2,1)}, u32[]{:S(2)}, u32[]{:S(2)}) collective-permute-start(bf16[8,3,16,512]{3,2,1,0:T(8,128)(2,1)} %add_convert_fusion.2), channel_id=1, source_target_pairs={{0,6},{2,0},{4,2},{6,4},{1,7},{3,1},{5,3},{7,5},{8,14},{10,8},{12,... | collective-permute-start | bytes 1179656 | tf_op jit(solution)/shard_map/ppermute | solution.py:24
  100.8 18.5 %collective-permute-start.26 = (bf16[8,3,16,512]{3,2,1,0:T(8,128)(2,1)S(1)}, bf16[8,3,16,512]{3,2,1,0:T(8,128)(2,1)S(1)}, u32[]{:S(2)}, u32[]{:S(2)}) collective-permute-start(bf16[8,3,16,512]{3,2,1,0:T(8,128)(2,1)S(1)} %add_convert_fusion), channel_id=1, source_target_pairs={{0,24},{8,0},{16,8},{24,16},{1,25},{9,1},{17,9},{25,17},{2,26},{10... | collective-permute-start | bytes 1179656 | tf_op jit(solution)/shard_map/ppermute | solution.py:24
  113.6 3.7 collective-permute-start.31
  118.1 24.2 %copy-start.28 = (f32[2,8,384]{2,1,0:T(8,128)}, f32[2,8,384]{2,1,0:T(8,128)S(1)}, u32[]{:S(2)}) copy-start(f32[2,8,384]{2,1,0:T(8,128)S(1)} %add.92.refs_11_) | copy-start | bytes 73732
  119.2 4.1 %collective-permute-start.21 = (bf16[2,3,16,512]{3,2,1,0:T(8,128)(2,1)S(1)}, bf16[2,3,16,512]{3,2,1,0:T(8,128)(2,1)S(1)}, u32[]{:S(2)}, u32[]{:S(2)}) collective-permute-start(bf16[2,3,16,512]{3,2,1,0:T(8,128)(2,1)S(1)} %slice.163), channel_id=1, source_target_pairs={{0,24},{8,0},{16,8},{24,16},{1,25},{9,1},{17,9},{25,17},{2,26},{10... | collective-permute-start | bytes 294920 | tf_op jit(solution)/shard_map/ppermute | solution.py:24
  119.5 5.4 %collective-permute-start.27 = (bf16[2,3,16,512]{3,2,1,0:T(8,128)(2,1)S(1)}, bf16[2,3,16,512]{3,2,1,0:T(8,128)(2,1)S(1)}, u32[]{:S(2)}, u32[]{:S(2)}) collective-permute-start(bf16[2,3,16,512]{3,2,1,0:T(8,128)(2,1)S(1)} %slice.162), channel_id=1, source_target_pairs={{0,6},{2,0},{4,2},{6,4},{1,7},{3,1},{5,3},{7,5},{8,14},{10,8},{12,... | collective-permute-start | bytes 294920 | tf_op jit(solution)/shard_map/ppermute | solution.py:24
  123.3 3.5 collective-permute-start.22
  124.9 189.8 %copy-start.34 = (f32[2048]{0:T(1024)S(1)}, f32[2048]{0:T(1024)}, u32[]{:S(2)}) copy-start(f32[2048]{0:T(1024)} %param.15) | copy-start | bytes 24580
  124.9 4.7 %collective-permute-start.28 = (bf16[2,3,16,512]{3,2,1,0:T(8,128)(2,1)S(1)}, bf16[2,3,16,512]{3,2,1,0:T(8,128)(2,1)S(1)}, u32[]{:S(2)}, u32[]{:S(2)}) collective-permute-start(bf16[2,3,16,512]{3,2,1,0:T(8,128)(2,1)S(1)} %fusion.4), channel_id=1, source_target_pairs={{0,6},{2,0},{4,2},{6,4},{1,7},{3,1},{5,3},{7,5},{8,14},{10,8},{12,... | collective-permute-start | bytes 294920 | tf_op jit(solution)/shard_map/ppermute | solution.py:24
  126.9 4.4 %collective-permute-start.23 = (bf16[2,3,16,512]{3,2,1,0:T(8,128)(2,1)S(1)}, bf16[2,3,16,512]{3,2,1,0:T(8,128)(2,1)S(1)}, u32[]{:S(2)}, u32[]{:S(2)}) collective-permute-start(bf16[2,3,16,512]{3,2,1,0:T(8,128)(2,1)S(1)} %fusion.6), channel_id=1, source_target_pairs={{0,24},{8,0},{16,8},{24,16},{1,25},{9,1},{17,9},{25,17},{2,26},{10... | collective-permute-start | bytes 294920 | tf_op jit(solution)/shard_map/ppermute | solution.py:24
  129.7 4.1 %collective-permute-start.29 = (bf16[2,3,16,512]{3,2,1,0:T(8,128)(2,1)S(1)}, bf16[2,3,16,512]{3,2,1,0:T(8,128)(2,1)S(1)}, u32[]{:S(2)}, u32[]{:S(2)}) collective-permute-start(bf16[2,3,16,512]{3,2,1,0:T(8,128)(2,1)S(1)} %fusion.3), channel_id=1, source_target_pairs={{0,6},{2,0},{4,2},{6,4},{1,7},{3,1},{5,3},{7,5},{8,14},{10,8},{12,... | collective-permute-start | bytes 294920 | tf_op jit(solution)/shard_map/ppermute | solution.py:24
  133.8 8.8 %collective-permute-start.32 = (bf16[2,2,3,16,512]{4,3,2,1,0:T(8,128)(2,1)S(1)}, bf16[2,2,3,16,512]{4,3,2,1,0:T(8,128)(2,1)S(1)}, u32[]{:S(2)}, u32[]{:S(2)}) collective-permute-start(bf16[2,2,3,16,512]{4,3,2,1,0:T(8,128)(2,1)S(1)} %pad_maximum_fusion.6), channel_id=1, source_target_pairs={{0,32},{32,0},{1,33},{33,1},{2,34},{34,2},{3,35},{35,3},{4,36},{36... | collective-permute-start | bytes 589832 | tf_op jit(solution)/shard_map/ppermute | solution.py:24
  136.8 178.5 %collective-permute-start.35 = (bf16[4,384,1024]{2,1,0:T(8,128)(2,1)S(1)}, bf16[4,384,1024]{2,1,0:T(8,128)(2,1)S(1)}, u32[]{:S(2)}, u32[]{:S(2)}) collective-permute-start(bf16[4,384,1024]{2,1,0:T(8,128)(2,1)S(1)} %get-tuple-element.63.refs_5_.refs_6_.refs_7_.refs_8_), channel_id=1, source_target_pairs={{0,2},{2,4},{4,6},{6,8},{8,10},{10,12},{12,14},{14,16},{16,18},{18... | collective-permute-start | bytes 9437192 | tf_op jit(solution)/shard_map/ppermute | solution.py:406
  138.6 208.4 %collective-permute-start.16 = (bf16[4,384,1024]{2,1,0:T(8,128)(2,1)}, bf16[4,384,1024]{2,1,0:T(8,128)(2,1)}, u32[]{:S(2)}, u32[]{:S(2)}) collective-permute-start(bf16[4,384,1024]{2,1,0:T(8,128)(2,1)} %get-tuple-element.62.refs_13_.refs_14_.refs_15_.refs_16_), channel_id=1, source_target_pairs={{0,2},{2,4},{4,6},{6,8},{8,10},{10,12},{12,14},{14,16},{16,18},{18... | collective-permute-start | bytes 9437192 | tf_op jit(solution)/shard_map/ppermute | solution.py:407
  142.2 2.7 collective-permute-start.33
  144.9 170.4 %copy-start.29 = (f32[2,8,384]{2,1,0:T(8,128)}, f32[2,8,384]{2,1,0:T(8,128)S(1)}, u32[]{:S(2)}) copy-start(f32[2,8,384]{2,1,0:T(8,128)S(1)} %collective-permute-done.33.refs_12_) | copy-start | bytes 73732
  144.9 204.8 %collective-permute-start.34 = (bf16[4,384,1024]{2,1,0:T(8,128)(2,1)}, bf16[4,384,1024]{2,1,0:T(8,128)(2,1)}, u32[]{:S(2)}, u32[]{:S(2)}) collective-permute-start(bf16[4,384,1024]{2,1,0:T(8,128)(2,1)} %get-tuple-element.62.refs_13_.refs_14_.refs_15_.refs_16_), channel_id=1, source_target_pairs={{30,32},{31,33},{94,96},{95,97}} | collective-permute-start | bytes 9437192 | tf_op jit(solution)/shard_map/ppermute | solution.py:421
  148.2 135.9 %collective-permute-start.36 = (bf16[2,3,16,512]{3,2,1,0:T(8,128)(2,1)S(1)}, bf16[2,3,16,512]{3,2,1,0:T(8,128)(2,1)S(1)}, u32[]{:S(2)}, u32[]{:S(2)}) collective-permute-start(bf16[2,3,16,512]{3,2,1,0:T(8,128)(2,1)S(1)} %get-tuple-element.86), channel_id=1, source_target_pairs={{0,24},{8,0},{16,8},{24,16},{1,25},{9,1},{17,9},{25,17},{2,26},{10... | collective-permute-start | bytes 294920 | tf_op jit(solution)/shard_map/ppermute | solution.py:24
  282.5 4.7 %collective-permute-start.42 = (bf16[2,3,16,512]{3,2,1,0:T(8,128)(2,1)S(1)}, bf16[2,3,16,512]{3,2,1,0:T(8,128)(2,1)S(1)}, u32[]{:S(2)}, u32[]{:S(2)}) collective-permute-start(bf16[2,3,16,512]{3,2,1,0:T(8,128)(2,1)S(1)} %get-tuple-element.85), channel_id=1, source_target_pairs={{0,6},{2,0},{4,2},{6,4},{1,7},{3,1},{5,3},{7,5},{8,14},{10,8},{12,... | collective-permute-start | bytes 294920 | tf_op jit(solution)/shard_map/ppermute | solution.py:24
  284.1 4.7 %collective-permute-start.37 = (bf16[2,3,16,512]{3,2,1,0:T(8,128)(2,1)S(1)}, bf16[2,3,16,512]{3,2,1,0:T(8,128)(2,1)S(1)}, u32[]{:S(2)}, u32[]{:S(2)}) collective-permute-start(bf16[2,3,16,512]{3,2,1,0:T(8,128)(2,1)S(1)} %collective-permute-done.36), channel_id=1, source_target_pairs={{0,24},{8,0},{16,8},{24,16},{1,25},{9,1},{17,9},{25,17},{2,26},{10... | collective-permute-start | bytes 294920 | tf_op jit(solution)/shard_map/ppermute | solution.py:24
  287.1 4.7 %collective-permute-start.43 = (bf16[2,3,16,512]{3,2,1,0:T(8,128)(2,1)S(1)}, bf16[2,3,16,512]{3,2,1,0:T(8,128)(2,1)S(1)}, u32[]{:S(2)}, u32[]{:S(2)}) collective-permute-start(bf16[2,3,16,512]{3,2,1,0:T(8,128)(2,1)S(1)} %collective-permute-done.42), channel_id=1, source_target_pairs={{0,6},{2,0},{4,2},{6,4},{1,7},{3,1},{5,3},{7,5},{8,14},{10,8},{12,... | collective-permute-start | bytes 294920 | tf_op jit(solution)/shard_map/ppermute | solution.py:24
  288.8 4.7 %collective-permute-start.38 = (bf16[2,3,16,512]{3,2,1,0:T(8,128)(2,1)S(1)}, bf16[2,3,16,512]{3,2,1,0:T(8,128)(2,1)S(1)}, u32[]{:S(2)}, u32[]{:S(2)}) collective-permute-start(bf16[2,3,16,512]{3,2,1,0:T(8,128)(2,1)S(1)} %collective-permute-done.37), channel_id=1, source_target_pairs={{0,24},{8,0},{16,8},{24,16},{1,25},{9,1},{17,9},{25,17},{2,26},{10... | collective-permute-start | bytes 294920 | tf_op jit(solution)/shard_map/ppermute | solution.py:24
  291.8 3.8 collective-permute-start.44
  293.5 31.0 %copy-start.12 = (bf16[8,3,16,512]{3,2,1,0:T(8,128)(2,1)}, bf16[8,3,16,512]{3,2,1,0:T(8,128)(2,1)S(1)}, u32[]{:S(2)}) copy-start(bf16[8,3,16,512]{3,2,1,0:T(8,128)(2,1)S(1)} %pad_maximum_fusion.3.refs_0_) | copy-start | bytes 1179652
  293.5 7.7 %collective-permute-start.39 = (bf16[8,3,16,512]{3,2,1,0:T(8,128)(2,1)S(1)}, bf16[8,3,16,512]{3,2,1,0:T(8,128)(2,1)S(1)}, u32[]{:S(2)}, u32[]{:S(2)}) collective-permute-start(bf16[8,3,16,512]{3,2,1,0:T(8,128)(2,1)S(1)} %pad_maximum_fusion.3.refs_0_), channel_id=1, source_target_pairs={{0,6},{2,0},{4,2},{6,4},{1,7},{3,1},{5,3},{7,5},{8,14},{10,8},{12,... | collective-permute-start | bytes 1179656 | tf_op jit(solution)/shard_map/ppermute | solution.py:24
  295.6 28.9 %copy-start.13 = (bf16[8,3,16,512]{3,2,1,0:T(8,128)(2,1)}, bf16[8,3,16,512]{3,2,1,0:T(8,128)(2,1)S(1)}, u32[]{:S(2)}) copy-start(bf16[8,3,16,512]{3,2,1,0:T(8,128)(2,1)S(1)} %pad_maximum_fusion.4.refs_4_) | copy-start | bytes 1179652
  295.6 7.3 %collective-permute-start.45 = (bf16[8,3,16,512]{3,2,1,0:T(8,128)(2,1)S(1)}, bf16[8,3,16,512]{3,2,1,0:T(8,128)(2,1)S(1)}, u32[]{:S(2)}, u32[]{:S(2)}) collective-permute-start(bf16[8,3,16,512]{3,2,1,0:T(8,128)(2,1)S(1)} %pad_maximum_fusion.4.refs_4_), channel_id=1, source_target_pairs={{0,24},{8,0},{16,8},{24,16},{1,25},{9,1},{17,9},{25,17},{2,26},{10... | collective-permute-start | bytes 1179656 | tf_op jit(solution)/shard_map/ppermute | solution.py:24
  301.3 23.3 %copy-start.20 = (bf16[8,3,16,512]{3,2,1,0:T(8,128)(2,1)}, bf16[8,3,16,512]{3,2,1,0:T(8,128)(2,1)S(1)}, u32[]{:S(2)}) copy-start(bf16[8,3,16,512]{3,2,1,0:T(8,128)(2,1)S(1)} %collective-permute-done.39.refs_1_) | copy-start | bytes 1179652
  301.3 8.9 %collective-permute-start.40 = (bf16[8,3,16,512]{3,2,1,0:T(8,128)(2,1)S(1)}, bf16[8,3,16,512]{3,2,1,0:T(8,128)(2,1)}, u32[]{:S(2)}, u32[]{:S(2)}) collective-permute-start(bf16[8,3,16,512]{3,2,1,0:T(8,128)(2,1)S(1)} %collective-permute-done.39.refs_1_), channel_id=1, source_target_pairs={{0,6},{2,0},{4,2},{6,4},{1,7},{3,1},{5,3},{7,5},{8,14},{10,8},{12,... | collective-permute-start | bytes 1179656 | tf_op jit(solution)/shard_map/ppermute | solution.py:24
  302.9 21.6 %copy-start.21 = (bf16[8,3,16,512]{3,2,1,0:T(8,128)(2,1)}, bf16[8,3,16,512]{3,2,1,0:T(8,128)(2,1)S(1)}, u32[]{:S(2)}) copy-start(bf16[8,3,16,512]{3,2,1,0:T(8,128)(2,1)S(1)} %collective-permute-done.45.refs_5_) | copy-start | bytes 1179652
  302.9 10.5 %collective-permute-start.46 = (bf16[8,3,16,512]{3,2,1,0:T(8,128)(2,1)S(1)}, bf16[8,3,16,512]{3,2,1,0:T(8,128)(2,1)}, u32[]{:S(2)}, u32[]{:S(2)}) collective-permute-start(bf16[8,3,16,512]{3,2,1,0:T(8,128)(2,1)S(1)} %collective-permute-done.45.refs_5_), channel_id=1, source_target_pairs={{0,24},{8,0},{16,8},{24,16},{1,25},{9,1},{17,9},{25,17},{2,26},{10... | collective-permute-start | bytes 1179656 | tf_op jit(solution)/shard_map/ppermute | solution.py:24
  310.1 24.7 %collective-permute-start.41 = (bf16[8,3,16,512]{3,2,1,0:T(8,128)(2,1)}, bf16[8,3,16,512]{3,2,1,0:T(8,128)(2,1)}, u32[]{:S(2)}, u32[]{:S(2)}) collective-permute-start(bf16[8,3,16,512]{3,2,1,0:T(8,128)(2,1)} %collective-permute-done.40.refs_2_), channel_id=1, source_target_pairs={{0,6},{2,0},{4,2},{6,4},{1,7},{3,1},{5,3},{7,5},{8,14},{10,8},{12,... | collective-permute-start | bytes 1179656 | tf_op jit(solution)/shard_map/ppermute | solution.py:24
  313.4 21.4 %collective-permute-start.47 = (bf16[8,3,16,512]{3,2,1,0:T(8,128)(2,1)}, bf16[8,3,16,512]{3,2,1,0:T(8,128)(2,1)}, u32[]{:S(2)}, u32[]{:S(2)}) collective-permute-start(bf16[8,3,16,512]{3,2,1,0:T(8,128)(2,1)} %collective-permute-done.46.refs_6_), channel_id=1, source_target_pairs={{0,24},{8,0},{16,8},{24,16},{1,25},{9,1},{17,9},{25,17},{2,26},{10... | collective-permute-start | bytes 1179656 | tf_op jit(solution)/shard_map/ppermute | solution.py:24
  324.6 47.3 %collective-permute-start.51 = (bf16[384,1024]{1,0:T(8,128)(2,1)}, bf16[384,1024]{1,0:T(8,128)(2,1)S(1)}, u32[]{:S(2)}, u32[]{:S(2)}) collective-permute-start(bf16[384,1024]{1,0:T(8,128)(2,1)} %attend_finish.5), channel_id=1, source_target_pairs={{0,1},{1,0},{2,3},{3,2},{4,5},{5,4},{6,7},{7,6},{8,9},{9,8},{10,11... | collective-permute-start | bytes 2359304 | tf_op jit(solution)/shard_map/ppermute | solution.py:24
  343.0 5.7 %collective-permute-start.50 = (f32[2,8,384]{2,1,0:T(8,128)}, f32[2,8,384]{2,1,0:T(8,128)S(1)}, u32[]{:S(2)}, u32[]{:S(2)}) collective-permute-start(f32[2,8,384]{2,1,0:T(8,128)} %get-tuple-element.66.refs_19_), channel_id=1, source_target_pairs={{0,65},{65,0},{1,64},{64,1},{2,67},{67,2},{3,66},{66,3},{4,69},{69... | collective-permute-start | bytes 73736 | tf_op jit(solution)/shard_map/ppermute | solution.py:356
  346.8 2.9 collective-permute-start.49
  347.0 2.7 collective-permute-start.48
  359.6 22.6 %collective-permute-start.52 = (bf16[384,1024]{1,0:T(8,128)(2,1)}, bf16[384,1024]{1,0:T(8,128)(2,1)S(1)}, u32[]{:S(2)}, u32[]{:S(2)}) collective-permute-start(bf16[384,1024]{1,0:T(8,128)(2,1)} %attend_finish.7), channel_id=1, source_target_pairs={{0,1},{1,0},{2,3},{3,2},{4,5},{5,4},{6,7},{7,6},{8,9},{9,8},{10,11... | collective-permute-start | bytes 2359304 | tf_op jit(solution)/shard_map/ppermute | solution.py:24
  361.4 2.2 collective-permute-start.53
  (26 other events, 200.6 us)

commit v3 on v2

--- a/solution.py
+++ b/solution.py
@@ -37,38 +37,35 @@
     return pltpu.CompilerParams(vmem_limit_bytes=56 * 1024 * 1024, **kw)
 
 
-def piece_rows(kind, part, idx, item):
+def piece_rows(kind, part, idx, item, sign):
     yh, z, x = idx
-    a, k = item % 2, item // 2
+    a, k = lax.rem(item, 2), lax.div(item, 2)
     y = lax.rem(yh + a, 2)
-    if kind == 0:
-        zz, xx = lax.rem(z + k, 4), lax.rem(x + part, 4)
-    else:
-        zz, xx = lax.rem(z + part, 4), lax.rem(x + k, 4)
+    zz = lax.rem(z + 4 + sign * (k if kind == 0 else part), 4)
+    xx = lax.rem(x + 4 + sign * (part if kind == 0 else k), 4)
     return pl.multiple_of(y * 256 + zz * 64 + xx * 16, 16)
 
 
-def weight_copies(head, pieces, w_vmem, sem, idx):
-    for part in range(4):
-        for item in range(8):
-            row = piece_rows(head, part, idx, item)
-            yield pltpu.make_async_copy(
-                pieces[head * 4 + part].at[item],
-                w_vmem.at[head, :, pl.ds(row, 16), :],
-                sem.at[head],
-            )
-
-
-def load_weights(pieces, w_vmem, sem, idx, head_now):
-    @pl.when(head_now == 0)
+def load_weights(pieces, w_vmem, sem, idx, head_now, half):
+    @pl.when((head_now == 0) & (half == 0))
     def _():
         for head in range(2):
-            for copy in weight_copies(head, pieces, w_vmem, sem, idx):
-                copy.start()
+
+            def start(item, carry, head=head):
+                for part in range(4):
+                    row = piece_rows(head, part, idx, item, 1)
+                    pltpu.make_async_copy(
+                        pieces[head * 4 + part].at[item],
+                        w_vmem.at[head, :, pl.ds(row, 16), :],
+                        sem.at[head],
+                    ).start()
+                return carry
+
+            lax.fori_loop(0, 8, start, 0)
 
     for head in range(2):
 
-        @pl.when(head_now == head)
+        @pl.when((head_now == head) & (half == 0))
         def _(head=head):
             pltpu.make_async_copy(w_vmem.at[head], w_vmem.at[head], sem.at[head]).wait()
 
@@ -77,71 +74,73 @@
     pieces = refs[:8]
     k_own, v_own, k_rec, v_rec, r_ref = refs[8:13]
     outs = refs[13:21]
-    w_vmem, sums, sem = refs[21:]
-    head = pl.program_id(0)
+    w_vmem, held, sums, sem = refs[21:]
+    head, half = pl.program_id(0), pl.program_id(1)
     idx = (s_ref[1], s_ref[2], s_ref[3])
-    load_weights(pieces, w_vmem, sem, idx, head)
+    load_weights(pieces, w_vmem, sem, idx, head, half)
     gate, up, down = w_vmem[head, 0], w_vmem[head, 1], w_vmem[head, 2]
-    halves = []
-    for j, (k_ref, v_ref) in enumerate(((k_own, v_own), (k_rec, v_rec))):
-        k = k_ref[0]
-        rate = r_ref[0, j]
-        target = (-(rate * v_ref[0].astype(f32))).astype(bf16)
-        g = dot(k, gate, NN)
-        u = dot(k, up, NN)
-        back = dot(target, down, NT)
-        s = jax.nn.sigmoid(g)
-        silu = g * s
-        active = (silu * u).astype(bf16)
-        d_gate = (back * u * s * (1.0 + g * (1.0 - s))).astype(bf16)
-        d_up = (back * silu).astype(bf16)
-        halves.append((k, target, active, d_gate, d_up))
-    k, target, active, d_gate, d_up = (jnp.concatenate(pair, axis=0) for pair in zip(*halves))
-    sums[0] = dot(k, d_gate, TN)
-    sums[1] = dot(k, d_up, TN)
-    sums[2] = dot(active, target, TN)
-    yh, z, x = idx
+    k = jnp.where(half == 0, k_own[0], k_rec[0])
+    v = jnp.where(half == 0, v_own[0], v_rec[0])
+    target = (-(r_ref[0, half] * v.astype(f32))).astype(bf16)
+    g = dot(k, gate, NN)
+    u = dot(k, up, NN)
+    back = dot(target, down, NT)
+    s = jax.nn.sigmoid(g)
+    silu = g * s
+    rows = pl.ds(pl.multiple_of(half * TOK, TOK), TOK)
+    held[0, rows] = k
+    held[1, rows] = target
+    held[2, rows] = (silu * u).astype(bf16)
+    held[3, rows] = (back * u * s * (1.0 + g * (1.0 - s))).astype(bf16)
+    held[4, rows] = (back * silu).astype(bf16)
+
+    @pl.when(half == 1)
+    def _():
+        sums[0] = dot(held[0], held[3], TN)
+        sums[1] = dot(held[0], held[4], TN)
+        sums[2] = dot(held[2], held[1], TN)
+
     for kind in range(2):
 
-        @pl.when(head == kind)
+        @pl.when((head == kind) & (half == 1))
         def _(kind=kind):
-            for part in range(4):
-                for item in range(8):
-                    a, k = item % 2, item // 2
-                    y = lax.rem(yh + a, 2)
-                    zz = lax.rem(z + 4 - (k if kind == 0 else part), 4)
-                    xx = lax.rem(x + 4 - (part if kind == 0 else k), 4)
-                    row = pl.multiple_of(y * 256 + zz * 64 + xx * 16, 16)
+            def store(item, carry):
+                for part in range(4):
+                    row = piece_rows(kind, part, idx, item, -1)
                     for m in range(3):
                         outs[kind * 4 + part][item, m] = sums[m, pl.ds(row, 16), :].astype(bf16)
+                return carry
+
+            lax.fori_loop(0, 8, store, 0)
 
 
 def own_spec(c):
-    return pl.BlockSpec((1, TOK, DH), lambda h, s: (c, 0, s[0] * 2 + h))
+    return pl.BlockSpec((1, TOK, DH), lambda *at: (c, 0, at[-1][0] * 2 + at[0]))
 
 
 def rec_spec(c):
-    return pl.BlockSpec((1, TOK, DH), lambda h, s: (c, 0, h))
+    return pl.BlockSpec((1, TOK, DH), lambda *at: (c, 0, at[0]))
 
 
 ANY = pl.BlockSpec(memory_space=pl.ANY)
 
 
 def compute_grads(scal, pieces, k, v, k_rec, v_rec, rates):
-    whole = pl.BlockSpec((8, 3, 16, DH), lambda h, s: (0, 0, 0, 0))
+    whole = pl.BlockSpec((8, 3, 16, DH), lambda h, j, s: (0, 0, 0, 0))
     return pl.pallas_call(
         grads_kernel,
         name="fast_grads",
         out_shape=[jax.ShapeDtypeStruct((8, 3, 16, DH), bf16)] * 8,
         grid_spec=pltpu.PrefetchScalarGridSpec(
             num_scalar_prefetch=1,
-            grid=(2,),
+            grid=(2, 2),
             in_specs=[ANY] * 8
             + [own_spec(0), own_spec(0), rec_spec(0), rec_spec(0)]
-            + [pl.BlockSpec((1, 2, TOK, 1), lambda h, s: (h, 0, 0, 0))],
+            + [pl.BlockSpec((1, 2, TOK, 1), lambda h, j, s: (h, 0, 0, 0))],
             out_specs=[whole] * 8,
             scratch_shapes=[
                 pltpu.VMEM((2, 3, DH, DH), bf16),
+                pltpu.VMEM((5, 2 * TOK, DH), bf16),
                 pltpu.VMEM((3, DH, DH), f32),
                 pltpu.SemaphoreType.DMA((2,)),
             ],
@@ -155,29 +154,27 @@
     q_own, q_rec = refs[8:10]
     out_ref, pow_ref = refs[10:12]
     w_vmem, sem = refs[12:]
-    head = pl.program_id(0)
+    head, half = pl.program_id(0), pl.program_id(1)
     idx = (s_ref[1], s_ref[2], s_ref[3])
-    load_weights(pieces, w_vmem, sem, idx, head)
+    load_weights(pieces, w_vmem, sem, idx, head, half)
     gate, up, down = w_vmem[head, 0], w_vmem[head, 1], w_vmem[head, 2]
-    core = s_ref[0]
-    for j, q_ref in enumerate((q_own, q_rec)):
-        block = core if j == 0 else 1 - core
-        q = q_ref[0]
-        g = dot(q, gate, NN)
-        u = dot(q, up, NN)
-        active = (g * jax.nn.sigmoid(g) * u).astype(bf16)
-        out = dot(active, down, NN)
-        out_ref[j] = out
-        power = jnp.sum(out * out, axis=-1, keepdims=True)
-        power = jnp.transpose(jnp.broadcast_to(power, (TOK, 128)))[:8]
-
-        @pl.when(head == 0)
-        def _(block=block, power=power):
-            pow_ref[block] = power
-
-        @pl.when(head == 1)
-        def _(block=block, power=power):
-            pow_ref[block] += power
+    block = jnp.where(half == 0, s_ref[0], 1 - s_ref[0])
+    q = jnp.where(half == 0, q_own[0], q_rec[0])
+    g = dot(q, gate, NN)
+    u = dot(q, up, NN)
+    active = (g * jax.nn.sigmoid(g) * u).astype(bf16)
+    out = dot(active, down, NN)
+    out_ref[0] = out
+    power = jnp.sum(out * out, axis=-1, keepdims=True)
+    power = jnp.transpose(jnp.broadcast_to(power, (TOK, 128)))[:8]
+
+    @pl.when(head == 0)
+    def _():
+        pow_ref[block] = power
+
+    @pl.when(head == 1)
+    def _():
+        pow_ref[block] += power
 
 
 def fast_apply(c, scal, pieces, q, q_rec):
@@ -190,11 +187,11 @@
         ],
         grid_spec=pltpu.PrefetchScalarGridSpec(
             num_scalar_prefetch=1,
-            grid=(2,),
+            grid=(2, 2),
             in_specs=[ANY] * 8 + [own_spec(c), rec_spec(c)],
             out_specs=[
-                pl.BlockSpec((2, TOK, DH), lambda h, s: (0, 0, h)),
-                pl.BlockSpec((2, 8, TOK), lambda h, s: (0, 0, 0)),
+                pl.BlockSpec((1, TOK, DH), lambda h, j, s: (j, 0, h)),
+                pl.BlockSpec((2, 8, TOK), lambda h, j, s: (0, 0, 0)),
             ],
             scratch_shapes=[
                 pltpu.VMEM((2, 3, DH, DH), bf16),
@@ -208,48 +205,129 @@
 LOG2E = 1.4426950408889634
 
 
+def partial_attention(q, blocks):
+    scores = []
+    for k, _, mask in blocks:
+        s = dot(q, k, NT)
+        scores.append(s if mask is None else jnp.where(mask, s, MASKED))
+    peak = jnp.max(functools.reduce(jnp.maximum, scores), axis=-1, keepdims=True)
+    weights = [jnp.exp2((s - peak) * (SCALE * LOG2E)) for s in scores]
+    total = jnp.sum(sum(weights[1:], weights[0]), axis=-1, keepdims=True)
+    acc = sum(dot(w.astype(bf16), v, NN) for w, (_, v, _) in zip(weights, blocks))
+    return acc, peak, total
+
+
+def local_kernel(s_ref, qo, qr, kb, k2, vb, v2, acc_ref, stat_ref):
+    block = pl.program_id(1)
+    q = jnp.where(s_ref[0] == block, qo[0], qr[0])
+    row = lax.broadcasted_iota(jnp.int32, (TOK, TOK), 0)
+    col = lax.broadcasted_iota(jnp.int32, (TOK, TOK), 1)
+    lane = lax.broadcasted_iota(jnp.int32, (TOK, 128), 1)
+    for b in range(2):
+
+        @pl.when(block == b)
+        def _(b=b):
+            blocks = [(k2[0], v2[0], col <= row)]
+            if b == 1:
+                blocks.append((kb[0], vb[0], None))
+            acc, peak, total = partial_attention(q, blocks)
+            acc_ref[0] = acc
+            stat_ref[0, 0] = jnp.where(lane < 64, peak, total)
+
+
+def attend_local(c, scal, q, q_rec, mine):
+    def block(at):
+        return pl.BlockSpec((1, TOK, DH), lambda h, b, s: (at(b), 0, h))
+
+    return pl.pallas_call(
+        local_kernel,
+        name="attend_local",
+        out_shape=[
+            jax.ShapeDtypeStruct((2, TOK, 2 * DH), f32),
+            jax.ShapeDtypeStruct((2, 2, TOK, 128), f32),
+        ],
+        grid_spec=pltpu.PrefetchScalarGridSpec(
+            num_scalar_prefetch=1,
+            grid=(2, 2),
+            in_specs=[
+                pl.BlockSpec((1, TOK, DH), lambda h, b, s: (c, 0, s[0] * 2 + h)),
+                pl.BlockSpec((1, TOK, DH), lambda h, b, s: (c, 0, h)),
+                block(lambda b: 0), block(lambda b: b), block(lambda b: 2), block(lambda b: 2 + b),
+            ],
+            out_specs=[
+                pl.BlockSpec((1, TOK, DH), lambda h, b, s: (b, 0, h)),
+                pl.BlockSpec((1, 1, TOK, 128), lambda h, b, s: (b, h, 0, 0)),
+            ],
+        ),
+        compiler_params=cparams(),
+    )(scal, q, q_rec, mine, mine, mine, mine)
+
+
 def finish_kernel(c, j, sources, count, s_ref, *refs):
     core, chip = s_ref[0], s_ref[5]
     block = core if j == 0 else 1 - core
     q_ref, refs = refs[0], refs[1:]
     before, refs = refs[: 4 * sources], refs[4 * sources :]
-    kb, k2, vb, v2, fast_ref, gain_ref = refs[:6]
-    powers, out_ref = refs[6 : 6 + count], refs[-1]
-    k0, ka, v0, va = (before[i][0] for i in range(4))
-    for more in range(1, sources):
-        here = chosen(s_ref) == more
-        k0, ka, v0, va = (
-            jnp.where(here, before[4 * more + i][0], old) for i, old in enumerate((k0, ka, v0, va))
-        )
-    first = block == 0
-    keys = (k0, jnp.where(first, ka, kb[0]), k2[0])
-    values = (v0, jnp.where(first, va, vb[0]), v2[0])
+    own, refs = (refs[:4], refs[4:]) if c == 0 else (refs[:2], refs[2:])
+    fast_ref, gain_ref = refs[:2]
+    powers = refs[2 : 2 + count]
+    out_ref = refs[-1]
     row = lax.broadcasted_iota(jnp.int32, (TOK, TOK), 0)
     col = lax.broadcasted_iota(jnp.int32, (TOK, TOK), 1)
+    total = sum(p[0] for p in powers[1:]) + powers[0][0]
+    rs = lax.rsqrt(total * (1.0 / 4096.0) + NORM_EPS)
+    fast = fast_ref[0] * gain_ref[...] * jnp.transpose(rs)[:, :1]
+
+    def put(attended):
+        out_ref[...] = (fast + attended).astype(bf16).reshape(out_ref.shape)
+
+    if c == 1:
+        acc_ref, stat_ref = own
+
+        def here(i):
+            found = before[i][0]
+            for more in range(1, sources):
+                found = jnp.where(chosen(s_ref) == more, before[4 * more + i][0], found)
+            return found
+
+        for b in range(2):
+
+            @pl.when(block == b)
+            def _(b=b):
+                blocks = [(here(0), here(2), col > row)]
+                if b == 0:
+                    blocks.append((here(1), here(3), None))
+                acc, peak, total = partial_attention(q_ref[0], blocks)
+                peak_own, total_own = stat_ref[0, 0, :, :1], stat_ref[0, 0, :, 64:65]
+                top = jnp.maximum(peak, peak_own)
+                scale = jnp.exp2((peak - top) * (SCALE * LOG2E))
+                scale_own = jnp.exp2((peak_own - top) * (SCALE * LOG2E))
+                inv = 1.0 / (total * scale + total_own * scale_own)
+                put(acc * (scale * inv) + acc_ref[0] * (scale_own * inv))
+
+        return
+
+    kb, k2, vb, v2 = own
+    k0, ka, v0, va = before
+    first = block == 0
+    keys = (k0[0], jnp.where(first, ka[0], kb[0]), k2[0])
+    values = (v0[0], jnp.where(first, va[0], vb[0]), v2[0])
     scores = [dot(q_ref[0], k, NT) for k in keys]
-    low = row
-    if c == 0:
-        low = jnp.where(chip == 0, TOK, row)
-        scores[1] = jnp.where(col >= jnp.where((chip == 0) & first, TOK, 0), scores[1], MASKED)
+    low = jnp.where(chip == 0, TOK, row)
+    scores[1] = jnp.where(col >= jnp.where((chip == 0) & first, TOK, 0), scores[1], MASKED)
     scores[0] = jnp.where(col > low, scores[0], MASKED)
     scores[2] = jnp.where(col <= row, scores[2], MASKED)
     peak = jnp.max(jnp.maximum(jnp.maximum(scores[0], scores[1]), scores[2]), axis=-1, keepdims=True)
     weights = [jnp.exp2((s - peak) * (SCALE * LOG2E)) for s in scores]
     inv = 1.0 / jnp.sum(weights[0] + weights[1] + weights[2], axis=-1, keepdims=True)
-    attended = sum(dot((w * inv).astype(bf16), v, NN) for w, v in zip(weights, values))
-
-    total = sum(p[0] for p in powers[1:]) + powers[0][0]
-    rs = lax.rsqrt(total * (1.0 / 4096.0) + NORM_EPS)
-    col = jnp.transpose(rs)[:, :1]
-    out = (fast_ref[0] * gain_ref[...] * col + attended).astype(bf16)
-    out_ref[...] = out.reshape(out_ref.shape)
+    put(sum(dot((w * inv).astype(bf16), v, NN) for w, v in zip(weights, values)))
 
 
 def chosen(s):
     return jnp.where(s[5] == 0, 2, jnp.where(s[4] == 1, 1, 0))
 
 
-def finish(c, j, scal, q, q_rec, mine, before, fast, powers, gain, layer=None):
+def finish(c, j, scal, q, q_rec, own, before, fast, powers, gain, layer=None):
     def block(s):
         return s[0] if j == 0 else 1 - s[0]
 
@@ -273,12 +351,21 @@
             spec(lambda s: 2 + block(s), holds), spec(lambda s: 3, holds),
         ]
         operands += [array] * 4
+    if c == 0:
+        specs += [
+            always(lambda s: 0), always(block), always(lambda s: 2), always(lambda s: 2 + block(s))
+        ]
+        operands += [own] * 4
+    else:
+        specs += [
+            always(block), pl.BlockSpec((1, 1, TOK, 128), lambda h, s: (block(s), h, 0, 0))
+        ]
+        operands += list(own)
     specs += [
-        always(lambda s: 0), always(block), always(lambda s: 2), always(lambda s: 2 + block(s)),
         pl.BlockSpec((1, TOK, DH), lambda h, s: (j, 0, h)),
         pl.BlockSpec((1, DH), lambda h, s: (0, h)),
     ]
-    operands += [mine] * 4 + [fast, gain]
+    operands += [fast, gain]
     specs += [pl.BlockSpec((1, 8, TOK), lambda h, s: (block(s), 0, 0))] * len(powers)
     operands += powers
     aliases = {}
@@ -429,17 +516,18 @@
 
     gain = lax.dynamic_slice_in_dim(out_gain, core * 1024, 1024, 0)[None]
 
-    def complete(c, before, fast, powers, layer):
-        args = (scal, queries, q_rec, pair[c], before, fast, powers, gain)
+    def complete(c, own, before, fast, powers, layer):
+        args = (scal, queries, q_rec, own, before, fast, powers, gain)
         out_rec = finish(c, 1, *args)
         arrived = shift(out_rec, "core", 1)
         layer = finish(c, 0, *args, layer)
         return lax.dynamic_update_slice(layer, arrived[None], (c, 0, (1 - core) * 1024))
 
-    layer_out = complete(0, [halo0], fast0, powers0, None)
+    local1 = attend_local(1, scal, queries, q_rec, pair[1])
+    layer_out = complete(0, pair[0], [halo0], fast0, powers0, None)
     fast1, pow1 = fast_apply(1, scal, pieces2, queries, q_rec)
     powers1 = with_parts(pow1, (CORES, HALVES, ACROSS))
-    layer_out = complete(1, [halo1, turned1, halo0], fast1, powers1, layer_out)
+    layer_out = complete(1, local1, [halo1, turned1, halo0], fast1, powers1, layer_out)
     return layer_out, new_all[:, 0], new_all[:, 1], new_all[:, 2]
 
 

time: 385 us -> 339 us (0.88)
  starting transfers between devices: 227 us -> 105 us
  waiting for transfers between devices: 60.8 us -> 129 us
  Pallas kernels: 62.1 us -> 71.2 us
    ppermute x46, starting transfers between devices: 212 us -> 91.5 us  [shift(): lax.ppermute(value, axis, [(i, (i + steps) % count) for i in range(count)])]
    ppermute x1, waiting for transfers between devices: 0.01 us -> 79.1 us  [on_device(): halo0 = lax.ppermute(pair[0], chips, row)]
    ppermute x46, waiting for transfers between devices: 55.2 us -> 46.3 us  [shift(): lax.ppermute(value, axis, [(i, (i + steps) % count) for i in range(count)])]
    pallas_call x0 -> x1, Pallas kernels: none -> 8.33 us  [attend_local(): pl.pallas_call(local_kernel, name='attend_local', out_shape=[jax.ShapeDty...]
  transfers between devices with their start and end apart: 54 -> 54, of which waited for: 26 -> 23; matrix products, arithmetic and copies ran while one was open for 6% -> 7% of each run, Pallas kernels for 13% -> 17%
where the time goes in v3:
time: 339 us; the launch traced here: 338 us
  waiting for transfers between devices  129 us (38%)
  starting transfers between devices  105 us (31%)
  Pallas kernels  71.2 us (21%)
  local copies, waits for them, and re-layouts  20.8 us (6%)
  other arithmetic  11 us (3%)
    ppermute x46, starting transfers between devices, shift(): lax.ppermute(value, axis, [(i, (i + steps) % count) for i in range(count)])  91.5 us
    ppermute x1, waiting for transfers between devices, on_device(): halo0 = lax.ppermute(pair[0], chips, row)  79.1 us
    ppermute x46, waiting for transfers between devices, shift(): lax.ppermute(value, axis, [(i, (i + steps) % count) for i in range(count)])  46.3 us
    pallas_call x4, Pallas kernels, finish(): pl.pallas_call(functools.partial(finish_kernel, c, j, sources, len(powers...  32.8 us
    pallas_call x2, Pallas kernels, fast_apply(): pl.pallas_call(apply_kernel, name='fast_apply', out_shape=[jax.ShapeDtype...  16.8 us
    pallas_call x1, Pallas kernels, compute_grads(): pl.pallas_call(grads_kernel, name='fast_grads', out_shape=[jax.ShapeDtype...  13.3 us
    pallas_call x1, Pallas kernels, attend_local(): pl.pallas_call(local_kernel, name='attend_local', out_shape=[jax.ShapeDty...  8.33 us
  transfers between devices with their start and end apart: 54, of which 23 were waited for; matrix products, arithmetic and copies ran while one was open for 7% of the time, Pallas kernels for 17%

profile of v3, /device:TPU:1, one launch (start us, length us, event | category | flops | bytes accessed | tf_op | source)
XLA Modules:
  0.0 337.6 jit_solution(15479790437565987344)
XLA Ops:
  1.6 1.5 collective-permute-start
  4.0 3.1 collective-permute-start.1
  7.1 4.8 %collective-permute-done.1 = f32[2,3,16,512]{3,2,1,0:T(8,128)} collective-permute-done((f32[2,3,16,512]{3,2,1,0:T(8,128)S(1)}, f32[2,3,16,512]{3,2,1,0:T(8,128)}, u32[]{:S(2)}, u32[]{:S(2)}) %collective-permute-start.1) | collective-permute-done | bytes 196640 | tf_op jit(solution)/shard_map/ppermute | solution.py:24
  11.9 2.7 constant_dynamic-slice_fusion.5
  15.8 1.3 constant_dynamic-slice_fusion.7
  18.7 1.8 collective-permute-start.6
  20.4 3.3 collective-permute-start.5
  24.9 2.7 constant_dynamic-slice_fusion.8
  27.6 1.3 constant_dynamic-slice_fusion.6
  29.7 1.3 copy.19.refs_12_
  31.0 1.2 collective-permute-start.12
  32.2 2.5 collective-permute-start.11
  37.2 2.1 collective-permute-done.11
  39.9 1.2 collective-permute-start.7
  42.1 1.7 fusion.15
  43.8 1.5 collective-permute-start.14
  45.3 1.5 fusion.14
  46.8 2.1 collective-permute-done.9.refs_3_
  48.9 1.5 collective-permute-start.13
  50.4 3.4 %maximum_select_fusion = (bf16[4,384,1024]{2,1,0:T(8,128)(2,1)S(1)}, bf16[4,384,1024]{2,1,0:T(8,128)(2,1)}) fusion(bf16[1,384,1024]{2,1,0:T(8,128)(2,1)S(1)} %get-tuple-element.83, bf16[1,384,1024]{2,1,0:T(8,128)(2,1)S(1)} %copy-done.11, bf16[1,384,1024]{2,1,0:T(8,128)(2,1)S(1)} %get-tuple-element.81, bf16[1,384,1024]{2,1,0:T(8,128)(2,1)S(1)} %copy-done.9, ...), kind=kLoop, calls=%fused_computation | loop fusion | flops 22020096 | bytes 12582913 | tf_op jit(solution)/shard_map/jit(_where)/select_n | solution.py:485
  54.7 2.3 collective-permute-done.7.refs_1_
  57.1 2.0 collective-permute-done.14.refs_6_
  60.8 13.3 %fast_grads.1 = (bf16[8,3,16,512]{3,2,1,0:T(8,128)(2,1)}, bf16[8,3,16,512]{3,2,1,0:T(8,128)(2,1)}, bf16[8,3,16,512]{3,2,1,0:T(8,128)(2,1)}, bf16[8,3,16,512]{3,2...) custom-call(s32[6]{0:T(128)} %stack.78.s_ref, ...), custom_call_target="tpu_custom_call" | custom-call | tf_op jit(solution)/shard_map/fast_grads/pallas_call | solution.py:130
  74.1 2.5 collective-permute-start.18
  76.9 4.0 %collective-permute-start.30 = (bf16[2,384,1024]{2,1,0:T(8,128)(2,1)S(1)}, bf16[2,384,1024]{2,1,0:T(8,128)(2,1)S(1)}, u32[]{:S(2)}, u32[]{:S(2)}) collective-permute-start(bf16[2,384,1024]{2,1,0:T(8,128)(2,1)S(1)} %constant_dynamic-slice_fusion.2), channel_id=1, source_target_pairs={{0,1},{1,0},{2,3},{3,2},{4,5},{5,4},{6,7},{7,6},{8,9},{9,8},{10,11... | collective-permute-start | bytes 4718600 | tf_op jit(solution)/shard_map/ppermute | solution.py:24
  80.8 2.6 collective-permute-start.24
  83.5 3.1 collective-permute-start.19
  86.6 4.8 %collective-permute-done.24 = bf16[8,3,16,512]{3,2,1,0:T(8,128)(2,1)S(1)} collective-permute-done((bf16[8,3,16,512]{3,2,1,0:T(8,128)(2,1)S(1)}, bf16[8,3,16,512]{3,2,1,0:T(8,128)(2,1)S(1)}, u32[]{:S(2)}, u32[]{:S(2)}) %collective-permute-start.24) | collective-permute-done | bytes 393248 | tf_op jit(solution)/shard_map/ppermute | solution.py:24
  91.5 3.4 collective-permute-start.25
  96.5 5.4 %collective-permute-done.25 = bf16[8,3,16,512]{3,2,1,0:T(8,128)(2,1)S(1)} collective-permute-done((bf16[8,3,16,512]{3,2,1,0:T(8,128)(2,1)S(1)}, bf16[8,3,16,512]{3,2,1,0:T(8,128)(2,1)S(1)}, u32[]{:S(2)}, u32[]{:S(2)}) %collective-permute-start.25) | collective-permute-done | bytes 393248 | tf_op jit(solution)/shard_map/ppermute | solution.py:24
  102.1 3.5 %collective-permute-start.26 = (bf16[8,3,16,512]{3,2,1,0:T(8,128)(2,1)S(1)}, bf16[8,3,16,512]{3,2,1,0:T(8,128)(2,1)S(1)}, u32[]{:S(2)}, u32[]{:S(2)}) collective-permute-start(bf16[8,3,16,512]{3,2,1,0:T(8,128)(2,1)S(1)} %add_convert_fusion), channel_id=1, source_target_pairs={{0,24},{8,0},{16,8},{24,16},{1,25},{9,1},{17,9},{25,17},{2,26},{10... | collective-permute-start | bytes 1179656 | tf_op jit(solution)/shard_map/ppermute | solution.py:24
  106.7 8.4 %fast_apply.2 = (f32[2,384,1024]{2,1,0:T(8,128)}, f32[2,8,384]{2,1,0:T(8,128)}) custom-call(s32[6]{0:T(128)} %stack.78.s_ref, bf16[8,3,16,512]{3,2,1,0:T(8,128)(2,1)} %copy-done.6, bf16[8,3,16,512]{3,2,1,0:T(8,128)(2,1)} %copy-done.16, bf16[8,3,16,512]{3,2,1,0:T(8,128)(2,1)} %copy-done.15, bf16[8,3,16,512]{3,2,1,0:T(8,128)(2,1)} %copy-done.14, ...), custom_call_target="tpu_custom_call" | custom-call | tf_op jit(solution)/shard_map/fast_apply/pallas_call | solution.py:181
  115.1 2.7 collective-permute-start.31
  121.8 3.1 collective-permute-done.21
  124.9 1.6 collective-permute-start.22
  128.4 2.8 collective-permute-start.23
  132.9 2.6 collective-permute-done.29
  135.6 3.0 collective-permute-start.32
  138.6 5.4 %collective-permute-start.16 = (bf16[4,384,1024]{2,1,0:T(8,128)(2,1)}, bf16[4,384,1024]{2,1,0:T(8,128)(2,1)}, u32[]{:S(2)}, u32[]{:S(2)}) collective-permute-start(bf16[4,384,1024]{2,1,0:T(8,128)(2,1)} %get-tuple-element.64.kb.k2.vb.v2), channel_id=1, source_target_pairs={{0,2},{2,4},{4,6},{6,8},{8,10},{10,12},{12,14},{14,16},{16,18},{18... | collective-permute-start | bytes 9437192 | tf_op jit(solution)/shard_map/ppermute | solution.py:494
  144.5 2.2 collective-permute-done.33.refs_12_
  146.8 2.4 collective-permute-start.34
  150.3 7.1 %collective-permute-start.42 = (bf16[2,3,16,512]{3,2,1,0:T(8,128)(2,1)S(1)}, bf16[2,3,16,512]{3,2,1,0:T(8,128)(2,1)S(1)}, u32[]{:S(2)}, u32[]{:S(2)}) collective-permute-start(bf16[2,3,16,512]{3,2,1,0:T(8,128)(2,1)S(1)} %get-tuple-element.89), channel_id=1, source_target_pairs={{0,6},{2,0},{4,2},{6,4},{1,7},{3,1},{5,3},{7,5},{8,14},{10,8},{12,... | collective-permute-start | bytes 294920 | tf_op jit(solution)/shard_map/ppermute | solution.py:24
  157.4 1.6 collective-permute-done.42
  159.0 3.0 collective-permute-start.43
  162.5 1.7 collective-permute-done.43
  164.2 3.7 %collective-permute-start.44 = (bf16[2,3,16,512]{3,2,1,0:T(8,128)(2,1)S(1)}, bf16[2,3,16,512]{3,2,1,0:T(8,128)(2,1)S(1)}, u32[]{:S(2)}, u32[]{:S(2)}) collective-permute-start(bf16[2,3,16,512]{3,2,1,0:T(8,128)(2,1)S(1)} %collective-permute-done.43), channel_id=1, source_target_pairs={{0,6},{2,0},{4,2},{6,4},{1,7},{3,1},{5,3},{7,5},{8,14},{10,8},{12,... | collective-permute-start | bytes 294920 | tf_op jit(solution)/shard_map/ppermute | solution.py:24
  168.0 1.7 collective-permute-start.39
  169.7 3.4 %collective-permute-start.45 = (bf16[8,3,16,512]{3,2,1,0:T(8,128)(2,1)S(1)}, bf16[8,3,16,512]{3,2,1,0:T(8,128)(2,1)S(1)}, u32[]{:S(2)}, u32[]{:S(2)}) collective-permute-start(bf16[8,3,16,512]{3,2,1,0:T(8,128)(2,1)S(1)} %pad_maximum_fusion.4.refs_4_), channel_id=1, source_target_pairs={{0,24},{8,0},{16,8},{24,16},{1,25},{9,1},{17,9},{25,17},{2,26},{10... | collective-permute-start | bytes 1179656 | tf_op jit(solution)/shard_map/ppermute | solution.py:24
  173.2 1.9 collective-permute-done.39.refs_1_
  175.0 3.0 collective-permute-start.40
  178.1 3.9 %collective-permute-start.46 = (bf16[8,3,16,512]{3,2,1,0:T(8,128)(2,1)S(1)}, bf16[8,3,16,512]{3,2,1,0:T(8,128)(2,1)}, u32[]{:S(2)}, u32[]{:S(2)}) collective-permute-start(bf16[8,3,16,512]{3,2,1,0:T(8,128)(2,1)S(1)} %collective-permute-done.45.refs_5_), channel_id=1, source_target_pairs={{0,24},{8,0},{16,8},{24,16},{1,25},{9,1},{17,9},{25,17},{2,26},{10... | collective-permute-start | bytes 1179656 | tf_op jit(solution)/shard_map/ppermute | solution.py:24
  181.9 4.8 %collective-permute-done.40.refs_2_ = bf16[8,3,16,512]{3,2,1,0:T(8,128)(2,1)} collective-permute-done((bf16[8,3,16,512]{3,2,1,0:T(8,128)(2,1)S(1)}, bf16[8,3,16,512]{3,2,1,0:T(8,128)(2,1)}, u32[]{:S(2)}, u32[]{:S(2)}) %collective-permute-start.40) | collective-permute-done | bytes 393248 | tf_op jit(solution)/shard_map/ppermute | solution.py:24
  186.7 3.4 %collective-permute-start.41 = (bf16[8,3,16,512]{3,2,1,0:T(8,128)(2,1)}, bf16[8,3,16,512]{3,2,1,0:T(8,128)(2,1)}, u32[]{:S(2)}, u32[]{:S(2)}) collective-permute-start(bf16[8,3,16,512]{3,2,1,0:T(8,128)(2,1)} %collective-permute-done.40.refs_2_), channel_id=1, source_target_pairs={{0,6},{2,0},{4,2},{6,4},{1,7},{3,1},{5,3},{7,5},{8,14},{10,8},{12,... | collective-permute-start | bytes 1179656 | tf_op jit(solution)/shard_map/ppermute | solution.py:24
  190.6 3.5 %collective-permute-start.47 = (bf16[8,3,16,512]{3,2,1,0:T(8,128)(2,1)}, bf16[8,3,16,512]{3,2,1,0:T(8,128)(2,1)}, u32[]{:S(2)}, u32[]{:S(2)}) collective-permute-start(bf16[8,3,16,512]{3,2,1,0:T(8,128)(2,1)} %collective-permute-done.46.refs_6_), channel_id=1, source_target_pairs={{0,24},{8,0},{16,8},{24,16},{1,25},{9,1},{17,9},{25,17},{2,26},{10... | collective-permute-start | bytes 1179656 | tf_op jit(solution)/shard_map/ppermute | solution.py:24
  194.7 79.1 %collective-permute-done.35.refs_1_.refs_2_.refs_3_.refs_4_.refs_9_.refs_10_.refs_11_.refs_12_ = bf16[4,384,1024]{2,1,0:T(8,128)(2,1)S(1)} collective-permute-done((bf16[4,384,1024]{2,1,0:T(8,128)(2,1)S(1)}, bf16[4,384,1024]{2,1,0:T(8,128)(2,1)S(1)}, u32[]{:S(2)}, u32[]{:S(2)}) %collective-permute-start.35) | collective-permute-done | bytes 3145760 | tf_op jit(solution)/shard_map/ppermute | solution.py:493
  273.8 1.6 copy-done
  275.4 7.6 %attend_finish.5 = bf16[384,1024]{1,0:T(8,128)(2,1)} custom-call(s32[6]{0:T(128)} %stack.78.s_ref, bf16[2,384,1024]{2,1,0:T(8,128)(2,1)} %copy-done.3, bf16[4,384,1024]{2,1,0:T(8,128)(2,1)} %copy-done, bf16[4,384,1024]{2,1,0:T(8,128)(2,1)} %copy-done, bf16[4,384,1024]{2,1,0:T(8,128)(2,1)} %copy-done, bf16[4,384,1024]{2,1,0:T(8,128)(2,1)} %copy-done, ...), custom_call_target="tpu_custom_call" | custom-call | tf_op jit(solution)/shard_map/attend_finish/pallas_call | solution.py:382
  283.0 4.4 %collective-permute-start.51 = (bf16[384,1024]{1,0:T(8,128)(2,1)}, bf16[384,1024]{1,0:T(8,128)(2,1)S(1)}, u32[]{:S(2)}, u32[]{:S(2)}) collective-permute-start(bf16[384,1024]{1,0:T(8,128)(2,1)} %attend_finish.5), channel_id=1, source_target_pairs={{0,1},{1,0},{2,3},{3,2},{4,5},{5,4},{6,7},{7,6},{8,9},{9,8},{10,11... | collective-permute-start | bytes 2359304 | tf_op jit(solution)/shard_map/ppermute | solution.py:24
  287.5 8.4 %fast_apply.3 = (f32[2,384,1024]{2,1,0:T(8,128)}, f32[2,8,384]{2,1,0:T(8,128)}) custom-call(s32[6]{0:T(128)} %stack.78.s_ref, bf16[8,3,16,512]{3,2,1,0:T(8,128)(2,1)} %copy-done.12, bf16[8,3,16,512]{3,2,1,0:T(8,128)(2,1)} %copy-done.20, bf16[8,3,16,512]{3,2,1,0:T(8,128)(2,1)} %collective-permute-done.40.refs_2_, ...), custom_call_target="tpu_custom_call" | custom-call | tf_op jit(solution)/shard_map/fast_apply/pallas_call | solution.py:181
  298.1 8.3 %attend_local.1 = (f32[2,384,1024]{2,1,0:T(8,128)}, f32[2,2,384,128]{3,2,1,0:T(8,128)}) custom-call(s32[6]{0:T(128)} %stack.78.s_ref, bf16[2,384,2048]{2,1,0:T(8,128)(2,1)} %refs_0_.1, bf16[2,384,1024]{2,1,0:T(8,128)(2,1)} %copy-done.3, bf16[4,384,1024]{2,1,0:T(8,128)(2,1)} %get-tuple-element.64.kb.k2.vb.v2, ...), custom_call_target="tpu_custom_call" | custom-call | tf_op jit(solution)/shard_map/attend_local/pallas_call | solution.py:242
  307.1 8.9 %attend_finish.7 = bf16[384,1024]{1,0:T(8,128)(2,1)} custom-call(s32[6]{0:T(128)} %stack.78.s_ref, bf16[2,384,1024]{2,1,0:T(8,128)(2,1)} %copy-done.3, bf16[4,384,1024]{2,1,0:T(8,128)(2,1)} %collective-permute-done.16.refs_1_.refs_2_.refs_3_.refs_4_, bf16[4,384,1024]{2,1,0:T(8,128)(2,1)} %collective-permute-done.16.refs_1_.refs_2_.refs_3_.refs_4_, ...), custom_call_target="tpu_custom_call" | custom-call | tf_op jit(solution)/shard_map/attend_finish/pallas_call | solution.py:382
  317.0 1.8 collective-permute-done.53
  319.5 7.6 %attend_finish.4 = bf16[2,384,2048]{2,1,0:T(8,128)(2,1)} custom-call(s32[6]{0:T(128)} %stack.78.s_ref, bf16[2,384,2048]{2,1,0:T(8,128)(2,1)} %refs_0_.1, bf16[4,384,1024]{2,1,0:T(8,128)(2,1)} %copy-done, bf16[4,384,1024]{2,1,0:T(8,128)(2,1)} %copy-done, bf16[4,384,1024]{2,1,0:T(8,128)(2,1)} %copy-done, bf16[4,384,1024]{2,1,0:T(8,128)(2,1)} %copy-done, ...), custom_call_target="tpu_custom_call" | custom-call | tf_op jit(solution)/shard_map/attend_finish/pallas_call | solution.py:382
  328.0 8.7 %attend_finish.6 = bf16[2,384,2048]{2,1,0:T(8,128)(2,1)} custom-call(s32[6]{0:T(128)} %stack.78.s_ref, bf16[2,384,2048]{2,1,0:T(8,128)(2,1)} %refs_0_.1, bf16[4,384,1024]{2,1,0:T(8,128)(2,1)} %collective-permute-done.16.refs_1_.refs_2_.refs_3_.refs_4_, ...), custom_call_target="tpu_custom_call", output_to_operand_aliasing={{}: (22, {})} | custom-call | tf_op jit(solution)/shard_map/attend_finish/pallas_call | solution.py:382
  (174 shorter events, 33.9 us)
Async XLA Ops:
  1.6 2.4 collective-permute-start
  4.0 7.9 %collective-permute-start.1 = (f32[2,3,16,512]{3,2,1,0:T(8,128)S(1)}, f32[2,3,16,512]{3,2,1,0:T(8,128)}, u32[]{:S(2)}, u32[]{:S(2)}) collective-permute-start(f32[2,3,16,512]{3,2,1,0:T(8,128)S(1)} %maximum_select_fusion.2), channel_id=1, source_target_pairs={{0,32},{32,0},{1,33},{33,1},{2,34},{34,2},{3,35},{35,3},{4,36},{36... | collective-permute-start | bytes 589832 | tf_op jit(solution)/shard_map/ppermute | solution.py:24
  14.6 26.6 %collective-permute-start.3 = (bf16[2,384,1024]{2,1,0:T(8,128)(2,1)}, bf16[2,384,1024]{2,1,0:T(8,128)(2,1)}, u32[]{:S(2)}, u32[]{:S(2)}) collective-permute-start(bf16[2,384,1024]{2,1,0:T(8,128)(2,1)} %constant_dynamic-slice_fusion.5), channel_id=1, source_target_pairs={{0,1},{1,0},{2,3},{3,2},{4,5},{5,4},{6,7},{7,6},{8,9},{9,8},{10,11... | collective-permute-start | bytes 4718600 | tf_op jit(solution)/shard_map/ppermute | solution.py:24
  17.1 26.7 %collective-permute-start.2 = (bf16[2,384,1024]{2,1,0:T(8,128)(2,1)}, bf16[2,384,1024]{2,1,0:T(8,128)(2,1)}, u32[]{:S(2)}, u32[]{:S(2)}) collective-permute-start(bf16[2,384,1024]{2,1,0:T(8,128)(2,1)} %constant_dynamic-slice_fusion.7), channel_id=1, source_target_pairs={{0,1},{1,0},{2,3},{3,2},{4,5},{5,4},{6,7},{7,6},{8,9},{9,8},{10,11... | collective-permute-start | bytes 4718600 | tf_op jit(solution)/shard_map/ppermute | solution.py:24
  18.7 12.3 %collective-permute-start.6 = (bf16[2,3,16,512]{3,2,1,0:T(8,128)(2,1)S(1)}, bf16[2,3,16,512]{3,2,1,0:T(8,128)(2,1)}, u32[]{:S(2)}, u32[]{:S(2)}) collective-permute-start(bf16[2,3,16,512]{3,2,1,0:T(8,128)(2,1)S(1)} %get-tuple-element.92), channel_id=1, source_target_pairs={{0,8},{8,16},{16,24},{24,0},{1,9},{9,17},{17,25},{25,1},{2,10},{10... | collective-permute-start | bytes 294920 | tf_op jit(solution)/shard_map/ppermute | solution.py:24
  20.4 11.7 %collective-permute-start.5 = (bf16[2,3,16,512]{3,2,1,0:T(8,128)(2,1)S(1)}, bf16[2,3,16,512]{3,2,1,0:T(8,128)(2,1)}, u32[]{:S(2)}, u32[]{:S(2)}) collective-permute-start(bf16[2,3,16,512]{3,2,1,0:T(8,128)(2,1)S(1)} %get-tuple-element.92), channel_id=1, source_target_pairs={{0,16},{8,24},{16,0},{24,8},{1,17},{9,25},{17,1},{25,9},{2,18},{10... | collective-permute-start | bytes 294920 | tf_op jit(solution)/shard_map/ppermute | solution.py:24
  23.8 5.2 %collective-permute-start.17 = (f32[2,384]{1,0:T(2,128)S(1)}, f32[2,384]{1,0:T(2,128)S(1)}, u32[]{:S(2)}, u32[]{:S(2)}) collective-permute-start(f32[2,384]{1,0:T(2,128)S(1)} %get-tuple-element.96), channel_id=1, source_target_pairs={{0,1},{1,0},{2,3},{3,2},{4,5},{5,4},{6,7},{7,6},{8,9},{9,8},{10,11... | collective-permute-start | bytes 9224 | tf_op jit(solution)/shard_map/ppermute | solution.py:24
  28.9 5.7 %collective-permute-start.4 = (bf16[2,3,16,512]{3,2,1,0:T(8,128)(2,1)S(1)}, bf16[2,3,16,512]{3,2,1,0:T(8,128)(2,1)S(1)}, u32[]{:S(2)}, u32[]{:S(2)}) collective-permute-start(bf16[2,3,16,512]{3,2,1,0:T(8,128)(2,1)S(1)} %get-tuple-element.92), channel_id=1, source_target_pairs={{0,24},{8,0},{16,8},{24,16},{1,25},{9,1},{17,9},{25,17},{2,26},{10... | collective-permute-start | bytes 294920 | tf_op jit(solution)/shard_map/ppermute | solution.py:24
  31.0 5.8 %collective-permute-start.12 = (bf16[2,3,16,512]{3,2,1,0:T(8,128)(2,1)S(1)}, bf16[2,3,16,512]{3,2,1,0:T(8,128)(2,1)S(1)}, u32[]{:S(2)}, u32[]{:S(2)}) collective-permute-start(bf16[2,3,16,512]{3,2,1,0:T(8,128)(2,1)S(1)} %get-tuple-element.91), channel_id=1, source_target_pairs={{0,2},{2,4},{4,6},{6,0},{1,3},{3,5},{5,7},{7,1},{8,10},{10,12},{12... | collective-permute-start | bytes 294920 | tf_op jit(solution)/shard_map/ppermute | solution.py:24
  32.2 7.1 %collective-permute-start.11 = (bf16[2,3,16,512]{3,2,1,0:T(8,128)(2,1)S(1)}, bf16[2,3,16,512]{3,2,1,0:T(8,128)(2,1)S(1)}, u32[]{:S(2)}, u32[]{:S(2)}) collective-permute-start(bf16[2,3,16,512]{3,2,1,0:T(8,128)(2,1)S(1)} %get-tuple-element.91), channel_id=1, source_target_pairs={{0,4},{2,6},{4,0},{6,2},{1,5},{3,7},{5,1},{7,3},{8,12},{10,14},{12... | collective-permute-start | bytes 294920 | tf_op jit(solution)/shard_map/ppermute | solution.py:24
  34.6 5.3 %collective-permute-start.10 = (bf16[2,3,16,512]{3,2,1,0:T(8,128)(2,1)S(1)}, bf16[2,3,16,512]{3,2,1,0:T(8,128)(2,1)S(1)}, u32[]{:S(2)}, u32[]{:S(2)}) collective-permute-start(bf16[2,3,16,512]{3,2,1,0:T(8,128)(2,1)S(1)} %get-tuple-element.91), channel_id=1, source_target_pairs={{0,6},{2,0},{4,2},{6,4},{1,7},{3,1},{5,3},{7,5},{8,14},{10,8},{12,... | collective-permute-start | bytes 294920 | tf_op jit(solution)/shard_map/ppermute | solution.py:24
  36.8 12.1 %collective-permute-start.9 = (bf16[8,3,16,512]{3,2,1,0:T(8,128)(2,1)S(1)}, bf16[8,3,16,512]{3,2,1,0:T(8,128)(2,1)S(1)}, u32[]{:S(2)}, u32[]{:S(2)}) collective-permute-start(bf16[8,3,16,512]{3,2,1,0:T(8,128)(2,1)S(1)} %pad_maximum_fusion.1.refs_0_), channel_id=1, source_target_pairs={{0,2},{2,4},{4,6},{6,0},{1,3},{3,5},{5,7},{7,1},{8,10},{10,12},{12... | collective-permute-start | bytes 1179656 | tf_op jit(solution)/shard_map/ppermute | solution.py:24
  39.3 15.4 %collective-permute-start.8 = (bf16[8,3,16,512]{3,2,1,0:T(8,128)(2,1)S(1)}, bf16[8,3,16,512]{3,2,1,0:T(8,128)(2,1)S(1)}, u32[]{:S(2)}, u32[]{:S(2)}) collective-permute-start(bf16[8,3,16,512]{3,2,1,0:T(8,128)(2,1)S(1)} %pad_maximum_fusion.1.refs_0_), channel_id=1, source_target_pairs={{0,4},{2,6},{4,0},{6,2},{1,5},{3,7},{5,1},{7,3},{8,12},{10,14},{12... | collective-permute-start | bytes 1179656 | tf_op jit(solution)/shard_map/ppermute | solution.py:24
  39.9 17.2 %collective-permute-start.7 = (bf16[8,3,16,512]{3,2,1,0:T(8,128)(2,1)S(1)}, bf16[8,3,16,512]{3,2,1,0:T(8,128)(2,1)S(1)}, u32[]{:S(2)}, u32[]{:S(2)}) collective-permute-start(bf16[8,3,16,512]{3,2,1,0:T(8,128)(2,1)S(1)} %pad_maximum_fusion.1.refs_0_), channel_id=1, source_target_pairs={{0,6},{2,0},{4,2},{6,4},{1,7},{3,1},{5,3},{7,5},{8,14},{10,8},{12,... | collective-permute-start | bytes 1179656 | tf_op jit(solution)/shard_map/ppermute | solution.py:24
  41.3 15.9 %collective-permute-start.15 = (bf16[8,3,16,512]{3,2,1,0:T(8,128)(2,1)S(1)}, bf16[8,3,16,512]{3,2,1,0:T(8,128)(2,1)S(1)}, u32[]{:S(2)}, u32[]{:S(2)}) collective-permute-start(bf16[8,3,16,512]{3,2,1,0:T(8,128)(2,1)S(1)} %pad_maximum_fusion.2.refs_4_), channel_id=1, source_target_pairs={{0,8},{8,16},{16,24},{24,0},{1,9},{9,17},{17,25},{25,1},{2,10},{10... | collective-permute-start | bytes 1179656 | tf_op jit(solution)/shard_map/ppermute | solution.py:24
  43.8 15.3 %collective-permute-start.14 = (bf16[8,3,16,512]{3,2,1,0:T(8,128)(2,1)S(1)}, bf16[8,3,16,512]{3,2,1,0:T(8,128)(2,1)S(1)}, u32[]{:S(2)}, u32[]{:S(2)}) collective-permute-start(bf16[8,3,16,512]{3,2,1,0:T(8,128)(2,1)S(1)} %pad_maximum_fusion.2.refs_4_), channel_id=1, source_target_pairs={{0,16},{8,24},{16,0},{24,8},{1,17},{9,25},{17,1},{25,9},{2,18},{10... | collective-permute-start | bytes 1179656 | tf_op jit(solution)/shard_map/ppermute | solution.py:24
  48.9 11.1 %collective-permute-start.13 = (bf16[8,3,16,512]{3,2,1,0:T(8,128)(2,1)S(1)}, bf16[8,3,16,512]{3,2,1,0:T(8,128)(2,1)S(1)}, u32[]{:S(2)}, u32[]{:S(2)}) collective-permute-start(bf16[8,3,16,512]{3,2,1,0:T(8,128)(2,1)S(1)} %pad_maximum_fusion.2.refs_4_), channel_id=1, source_target_pairs={{0,24},{8,0},{16,8},{24,16},{1,25},{9,1},{17,9},{25,17},{2,26},{10... | collective-permute-start | bytes 1179656 | tf_op jit(solution)/shard_map/ppermute | solution.py:24
  53.9 90.1 %copy-start.1 = (bf16[4,384,1024]{2,1,0:T(8,128)(2,1)}, bf16[4,384,1024]{2,1,0:T(8,128)(2,1)S(1)}, u32[]{:S(2)}) copy-start(bf16[4,384,1024]{2,1,0:T(8,128)(2,1)S(1)} %get-tuple-element.65.refs_5_.refs_6_.refs_7_.refs_8_) | copy-start | bytes 9437188
  74.1 20.8 %copy-start.25 = (bf16[8,3,16,512]{3,2,1,0:T(8,128)(2,1)S(1)}, bf16[8,3,16,512]{3,2,1,0:T(8,128)(2,1)}, u32[]{:S(2)}) copy-start(bf16[8,3,16,512]{3,2,1,0:T(8,128)(2,1)} %get-tuple-element.55) | copy-start | bytes 1179652
  74.1 27.8 %copy-start.24 = (bf16[8,3,16,512]{3,2,1,0:T(8,128)(2,1)S(1)}, bf16[8,3,16,512]{3,2,1,0:T(8,128)(2,1)}, u32[]{:S(2)}) copy-start(bf16[8,3,16,512]{3,2,1,0:T(8,128)(2,1)} %get-tuple-element.59) | copy-start | bytes 1179652
  74.1 9.3 %collective-permute-start.18 = (bf16[8,3,16,512]{3,2,1,0:T(8,128)(2,1)}, bf16[8,3,16,512]{3,2,1,0:T(8,128)(2,1)S(1)}, u32[]{:S(2)}, u32[]{:S(2)}) collective-permute-start(bf16[8,3,16,512]{3,2,1,0:T(8,128)(2,1)} %get-tuple-element.53), channel_id=1, source_target_pairs={{0,6},{2,0},{4,2},{6,4},{1,7},{3,1},{5,3},{7,5},{8,14},{10,8},{12,... | collective-permute-start | bytes 1179656 | tf_op jit(solution)/shard_map/ppermute | solution.py:24
  76.9 28.7 %collective-permute-start.30 = (bf16[2,384,1024]{2,1,0:T(8,128)(2,1)S(1)}, bf16[2,384,1024]{2,1,0:T(8,128)(2,1)S(1)}, u32[]{:S(2)}, u32[]{:S(2)}) collective-permute-start(bf16[2,384,1024]{2,1,0:T(8,128)(2,1)S(1)} %constant_dynamic-slice_fusion.2), channel_id=1, source_target_pairs={{0,1},{1,0},{2,3},{3,2},{4,5},{5,4},{6,7},{7,6},{8,9},{9,8},{10,11... | collective-permute-start | bytes 4718600 | tf_op jit(solution)/shard_map/ppermute | solution.py:24
  80.8 10.6 %collective-permute-start.24 = (bf16[8,3,16,512]{3,2,1,0:T(8,128)(2,1)S(1)}, bf16[8,3,16,512]{3,2,1,0:T(8,128)(2,1)S(1)}, u32[]{:S(2)}, u32[]{:S(2)}) collective-permute-start(bf16[8,3,16,512]{3,2,1,0:T(8,128)(2,1)S(1)} %copy-done.35), channel_id=1, source_target_pairs={{0,24},{8,0},{16,8},{24,16},{1,25},{9,1},{17,9},{25,17},{2,26},{10... | collective-permute-start | bytes 1179656 | tf_op jit(solution)/shard_map/ppermute | solution.py:24
  83.5 11.4 %collective-permute-start.19 = (bf16[8,3,16,512]{3,2,1,0:T(8,128)(2,1)S(1)}, bf16[8,3,16,512]{3,2,1,0:T(8,128)(2,1)S(1)}, u32[]{:S(2)}, u32[]{:S(2)}) collective-permute-start(bf16[8,3,16,512]{3,2,1,0:T(8,128)(2,1)S(1)} %add_convert_fusion.3), channel_id=1, source_target_pairs={{0,6},{2,0},{4,2},{6,4},{1,7},{3,1},{5,3},{7,5},{8,14},{10,8},{12,... | collective-permute-start | bytes 1179656 | tf_op jit(solution)/shard_map/ppermute | solution.py:24
  91.5 10.4 %collective-permute-start.25 = (bf16[8,3,16,512]{3,2,1,0:T(8,128)(2,1)S(1)}, bf16[8,3,16,512]{3,2,1,0:T(8,128)(2,1)S(1)}, u32[]{:S(2)}, u32[]{:S(2)}) collective-permute-start(bf16[8,3,16,512]{3,2,1,0:T(8,128)(2,1)S(1)} %add_convert_fusion.1), channel_id=1, source_target_pairs={{0,24},{8,0},{16,8},{24,16},{1,25},{9,1},{17,9},{25,17},{2,26},{10... | collective-permute-start | bytes 1179656 | tf_op jit(solution)/shard_map/ppermute | solution.py:24
  95.8 23.8 %collective-permute-start.20 = (bf16[8,3,16,512]{3,2,1,0:T(8,128)(2,1)}, bf16[8,3,16,512]{3,2,1,0:T(8,128)(2,1)}, u32[]{:S(2)}, u32[]{:S(2)}) collective-permute-start(bf16[8,3,16,512]{3,2,1,0:T(8,128)(2,1)} %add_convert_fusion.2), channel_id=1, source_target_pairs={{0,6},{2,0},{4,2},{6,4},{1,7},{3,1},{5,3},{7,5},{8,14},{10,8},{12,... | collective-permute-start | bytes 1179656 | tf_op jit(solution)/shard_map/ppermute | solution.py:24
  102.1 18.8 %collective-permute-start.26 = (bf16[8,3,16,512]{3,2,1,0:T(8,128)(2,1)S(1)}, bf16[8,3,16,512]{3,2,1,0:T(8,128)(2,1)S(1)}, u32[]{:S(2)}, u32[]{:S(2)}) collective-permute-start(bf16[8,3,16,512]{3,2,1,0:T(8,128)(2,1)S(1)} %add_convert_fusion), channel_id=1, source_target_pairs={{0,24},{8,0},{16,8},{24,16},{1,25},{9,1},{17,9},{25,17},{2,26},{10... | collective-permute-start | bytes 1179656 | tf_op jit(solution)/shard_map/ppermute | solution.py:24
  115.1 3.7 %collective-permute-start.31 = (f32[2,8,384]{2,1,0:T(8,128)}, f32[2,8,384]{2,1,0:T(8,128)S(1)}, u32[]{:S(2)}, u32[]{:S(2)}) collective-permute-start(f32[2,8,384]{2,1,0:T(8,128)} %get-tuple-element.61), channel_id=1, source_target_pairs={{0,1},{1,0},{64,65},{65,64},{2,3},{3,2},{66,67},{67,66},{4,5},{5,4... | collective-permute-start | bytes 73736 | tf_op jit(solution)/shard_map/ppermute | solution.py:443
  119.6 24.4 %copy-start.28 = (f32[2,8,384]{2,1,0:T(8,128)}, f32[2,8,384]{2,1,0:T(8,128)S(1)}, u32[]{:S(2)}) copy-start(f32[2,8,384]{2,1,0:T(8,128)S(1)} %add.92.refs_11_) | copy-start | bytes 73732
  120.8 4.1 %collective-permute-start.21 = (bf16[2,3,16,512]{3,2,1,0:T(8,128)(2,1)S(1)}, bf16[2,3,16,512]{3,2,1,0:T(8,128)(2,1)S(1)}, u32[]{:S(2)}, u32[]{:S(2)}) collective-permute-start(bf16[2,3,16,512]{3,2,1,0:T(8,128)(2,1)S(1)} %slice.163), channel_id=1, source_target_pairs={{0,24},{8,0},{16,8},{24,16},{1,25},{9,1},{17,9},{25,17},{2,26},{10... | collective-permute-start | bytes 294920 | tf_op jit(solution)/shard_map/ppermute | solution.py:24
  121.0 5.4 %collective-permute-start.27 = (bf16[2,3,16,512]{3,2,1,0:T(8,128)(2,1)S(1)}, bf16[2,3,16,512]{3,2,1,0:T(8,128)(2,1)S(1)}, u32[]{:S(2)}, u32[]{:S(2)}) collective-permute-start(bf16[2,3,16,512]{3,2,1,0:T(8,128)(2,1)S(1)} %slice.162), channel_id=1, source_target_pairs={{0,6},{2,0},{4,2},{6,4},{1,7},{3,1},{5,3},{7,5},{8,14},{10,8},{12,... | collective-permute-start | bytes 294920 | tf_op jit(solution)/shard_map/ppermute | solution.py:24
  124.9 3.5 %collective-permute-start.22 = (bf16[2,3,16,512]{3,2,1,0:T(8,128)(2,1)S(1)}, bf16[2,3,16,512]{3,2,1,0:T(8,128)(2,1)S(1)}, u32[]{:S(2)}, u32[]{:S(2)}) collective-permute-start(bf16[2,3,16,512]{3,2,1,0:T(8,128)(2,1)S(1)} %fusion.7), channel_id=1, source_target_pairs={{0,24},{8,0},{16,8},{24,16},{1,25},{9,1},{17,9},{25,17},{2,26},{10... | collective-permute-start | bytes 294920 | tf_op jit(solution)/shard_map/ppermute | solution.py:24
  126.5 67.7 %copy-start.34 = (f32[2048]{0:T(1024)S(1)}, f32[2048]{0:T(1024)}, u32[]{:S(2)}) copy-start(f32[2048]{0:T(1024)} %param.15) | copy-start | bytes 24580
  126.5 4.7 %collective-permute-start.28 = (bf16[2,3,16,512]{3,2,1,0:T(8,128)(2,1)S(1)}, bf16[2,3,16,512]{3,2,1,0:T(8,128)(2,1)S(1)}, u32[]{:S(2)}, u32[]{:S(2)}) collective-permute-start(bf16[2,3,16,512]{3,2,1,0:T(8,128)(2,1)S(1)} %fusion.4), channel_id=1, source_target_pairs={{0,6},{2,0},{4,2},{6,4},{1,7},{3,1},{5,3},{7,5},{8,14},{10,8},{12,... | collective-permute-start | bytes 294920 | tf_op jit(solution)/shard_map/ppermute | solution.py:24
  128.4 4.4 %collective-permute-start.23 = (bf16[2,3,16,512]{3,2,1,0:T(8,128)(2,1)S(1)}, bf16[2,3,16,512]{3,2,1,0:T(8,128)(2,1)S(1)}, u32[]{:S(2)}, u32[]{:S(2)}) collective-permute-start(bf16[2,3,16,512]{3,2,1,0:T(8,128)(2,1)S(1)} %fusion.6), channel_id=1, source_target_pairs={{0,24},{8,0},{16,8},{24,16},{1,25},{9,1},{17,9},{25,17},{2,26},{10... | collective-permute-start | bytes 294920 | tf_op jit(solution)/shard_map/ppermute | solution.py:24
  131.2 4.3 %collective-permute-start.29 = (bf16[2,3,16,512]{3,2,1,0:T(8,128)(2,1)S(1)}, bf16[2,3,16,512]{3,2,1,0:T(8,128)(2,1)S(1)}, u32[]{:S(2)}, u32[]{:S(2)}) collective-permute-start(bf16[2,3,16,512]{3,2,1,0:T(8,128)(2,1)S(1)} %fusion.3), channel_id=1, source_target_pairs={{0,6},{2,0},{4,2},{6,4},{1,7},{3,1},{5,3},{7,5},{8,14},{10,8},{12,... | collective-permute-start | bytes 294920 | tf_op jit(solution)/shard_map/ppermute | solution.py:24
  135.6 8.9 %collective-permute-start.32 = (bf16[2,2,3,16,512]{4,3,2,1,0:T(8,128)(2,1)S(1)}, bf16[2,2,3,16,512]{4,3,2,1,0:T(8,128)(2,1)S(1)}, u32[]{:S(2)}, u32[]{:S(2)}) collective-permute-start(bf16[2,2,3,16,512]{4,3,2,1,0:T(8,128)(2,1)S(1)} %pad_maximum_fusion.6), channel_id=1, source_target_pairs={{0,32},{32,0},{1,33},{33,1},{2,34},{34,2},{3,35},{35,3},{4,36},{36... | collective-permute-start | bytes 589832 | tf_op jit(solution)/shard_map/ppermute | solution.py:24
  138.6 158.8 %collective-permute-start.16 = (bf16[4,384,1024]{2,1,0:T(8,128)(2,1)}, bf16[4,384,1024]{2,1,0:T(8,128)(2,1)}, u32[]{:S(2)}, u32[]{:S(2)}) collective-permute-start(bf16[4,384,1024]{2,1,0:T(8,128)(2,1)} %get-tuple-element.64.kb.k2.vb.v2), channel_id=1, source_target_pairs={{0,2},{2,4},{4,6},{6,8},{8,10},{10,12},{12,14},{14,16},{16,18},{18... | collective-permute-start | bytes 9437192 | tf_op jit(solution)/shard_map/ppermute | solution.py:494
  144.0 129.8 %collective-permute-start.35 = (bf16[4,384,1024]{2,1,0:T(8,128)(2,1)S(1)}, bf16[4,384,1024]{2,1,0:T(8,128)(2,1)S(1)}, u32[]{:S(2)}, u32[]{:S(2)}) collective-permute-start(bf16[4,384,1024]{2,1,0:T(8,128)(2,1)S(1)} %get-tuple-element.65.refs_5_.refs_6_.refs_7_.refs_8_), channel_id=1, source_target_pairs={{0,2},{2,4},{4,6},{6,8},{8,10},{10,12},{12,14},{14,16},{16,18},{18... | collective-permute-start | bytes 9437192 | tf_op jit(solution)/shard_map/ppermute | solution.py:493
  144.0 2.8 collective-permute-start.33
  146.8 127.0 %copy-start.32 = (f32[2,8,384]{2,1,0:T(8,128)}, f32[2,8,384]{2,1,0:T(8,128)S(1)}, u32[]{:S(2)}) copy-start(f32[2,8,384]{2,1,0:T(8,128)S(1)} %collective-permute-done.33.refs_12_) | copy-start | bytes 73732
  146.8 159.8 %collective-permute-start.34 = (bf16[4,384,1024]{2,1,0:T(8,128)(2,1)}, bf16[4,384,1024]{2,1,0:T(8,128)(2,1)}, u32[]{:S(2)}, u32[]{:S(2)}) collective-permute-start(bf16[4,384,1024]{2,1,0:T(8,128)(2,1)} %get-tuple-element.64.kb.k2.vb.v2), channel_id=1, source_target_pairs={{30,32},{31,33},{94,96},{95,97}} | collective-permute-start | bytes 9437192 | tf_op jit(solution)/shard_map/ppermute | solution.py:508
  150.2 7.2 %collective-permute-start.36 = (bf16[2,3,16,512]{3,2,1,0:T(8,128)(2,1)S(1)}, bf16[2,3,16,512]{3,2,1,0:T(8,128)(2,1)S(1)}, u32[]{:S(2)}, u32[]{:S(2)}) collective-permute-start(bf16[2,3,16,512]{3,2,1,0:T(8,128)(2,1)S(1)} %get-tuple-element.90), channel_id=1, source_target_pairs={{0,24},{8,0},{16,8},{24,16},{1,25},{9,1},{17,9},{25,17},{2,26},{10... | collective-permute-start | bytes 294920 | tf_op jit(solution)/shard_map/ppermute | solution.py:24
  150.3 8.7 %collective-permute-start.42 = (bf16[2,3,16,512]{3,2,1,0:T(8,128)(2,1)S(1)}, bf16[2,3,16,512]{3,2,1,0:T(8,128)(2,1)S(1)}, u32[]{:S(2)}, u32[]{:S(2)}) collective-permute-start(bf16[2,3,16,512]{3,2,1,0:T(8,128)(2,1)S(1)} %get-tuple-element.89), channel_id=1, source_target_pairs={{0,6},{2,0},{4,2},{6,4},{1,7},{3,1},{5,3},{7,5},{8,14},{10,8},{12,... | collective-permute-start | bytes 294920 | tf_op jit(solution)/shard_map/ppermute | solution.py:24
  157.3 4.7 %collective-permute-start.37 = (bf16[2,3,16,512]{3,2,1,0:T(8,128)(2,1)S(1)}, bf16[2,3,16,512]{3,2,1,0:T(8,128)(2,1)S(1)}, u32[]{:S(2)}, u32[]{:S(2)}) collective-permute-start(bf16[2,3,16,512]{3,2,1,0:T(8,128)(2,1)S(1)} %collective-permute-done.36), channel_id=1, source_target_pairs={{0,24},{8,0},{16,8},{24,16},{1,25},{9,1},{17,9},{25,17},{2,26},{10... | collective-permute-start | bytes 294920 | tf_op jit(solution)/shard_map/ppermute | solution.py:24
  159.0 5.2 %collective-permute-start.43 = (bf16[2,3,16,512]{3,2,1,0:T(8,128)(2,1)S(1)}, bf16[2,3,16,512]{3,2,1,0:T(8,128)(2,1)S(1)}, u32[]{:S(2)}, u32[]{:S(2)}) collective-permute-start(bf16[2,3,16,512]{3,2,1,0:T(8,128)(2,1)S(1)} %collective-permute-done.42), channel_id=1, source_target_pairs={{0,6},{2,0},{4,2},{6,4},{1,7},{3,1},{5,3},{7,5},{8,14},{10,8},{12,... | collective-permute-start | bytes 294920 | tf_op jit(solution)/shard_map/ppermute | solution.py:24
  162.0 5.9 %collective-permute-start.38 = (bf16[2,3,16,512]{3,2,1,0:T(8,128)(2,1)S(1)}, bf16[2,3,16,512]{3,2,1,0:T(8,128)(2,1)S(1)}, u32[]{:S(2)}, u32[]{:S(2)}) collective-permute-start(bf16[2,3,16,512]{3,2,1,0:T(8,128)(2,1)S(1)} %collective-permute-done.37), channel_id=1, source_target_pairs={{0,24},{8,0},{16,8},{24,16},{1,25},{9,1},{17,9},{25,17},{2,26},{10... | collective-permute-start | bytes 294920 | tf_op jit(solution)/shard_map/ppermute | solution.py:24
  164.2 5.5 %collective-permute-start.44 = (bf16[2,3,16,512]{3,2,1,0:T(8,128)(2,1)S(1)}, bf16[2,3,16,512]{3,2,1,0:T(8,128)(2,1)S(1)}, u32[]{:S(2)}, u32[]{:S(2)}) collective-permute-start(bf16[2,3,16,512]{3,2,1,0:T(8,128)(2,1)S(1)} %collective-permute-done.43), channel_id=1, source_target_pairs={{0,6},{2,0},{4,2},{6,4},{1,7},{3,1},{5,3},{7,5},{8,14},{10,8},{12,... | collective-permute-start | bytes 294920 | tf_op jit(solution)/shard_map/ppermute | solution.py:24
  167.9 115.1 %copy-start.12 = (bf16[8,3,16,512]{3,2,1,0:T(8,128)(2,1)}, bf16[8,3,16,512]{3,2,1,0:T(8,128)(2,1)S(1)}, u32[]{:S(2)}) copy-start(bf16[8,3,16,512]{3,2,1,0:T(8,128)(2,1)S(1)} %pad_maximum_fusion.3.refs_0_) | copy-start | bytes 1179652
  168.0 7.1 %collective-permute-start.39 = (bf16[8,3,16,512]{3,2,1,0:T(8,128)(2,1)S(1)}, bf16[8,3,16,512]{3,2,1,0:T(8,128)(2,1)S(1)}, u32[]{:S(2)}, u32[]{:S(2)}) collective-permute-start(bf16[8,3,16,512]{3,2,1,0:T(8,128)(2,1)S(1)} %pad_maximum_fusion.3.refs_0_), channel_id=1, source_target_pairs={{0,6},{2,0},{4,2},{6,4},{1,7},{3,1},{5,3},{7,5},{8,14},{10,8},{12,... | collective-permute-start | bytes 1179656 | tf_op jit(solution)/shard_map/ppermute | solution.py:24
  169.7 113.3 %copy-start.13 = (bf16[8,3,16,512]{3,2,1,0:T(8,128)(2,1)}, bf16[8,3,16,512]{3,2,1,0:T(8,128)(2,1)S(1)}, u32[]{:S(2)}) copy-start(bf16[8,3,16,512]{3,2,1,0:T(8,128)(2,1)S(1)} %pad_maximum_fusion.4.refs_4_) | copy-start | bytes 1179652
  169.7 8.3 %collective-permute-start.45 = (bf16[8,3,16,512]{3,2,1,0:T(8,128)(2,1)S(1)}, bf16[8,3,16,512]{3,2,1,0:T(8,128)(2,1)S(1)}, u32[]{:S(2)}, u32[]{:S(2)}) collective-permute-start(bf16[8,3,16,512]{3,2,1,0:T(8,128)(2,1)S(1)} %pad_maximum_fusion.4.refs_4_), channel_id=1, source_target_pairs={{0,24},{8,0},{16,8},{24,16},{1,25},{9,1},{17,9},{25,17},{2,26},{10... | collective-permute-start | bytes 1179656 | tf_op jit(solution)/shard_map/ppermute | solution.py:24
  175.0 108.0 %copy-start.20 = (bf16[8,3,16,512]{3,2,1,0:T(8,128)(2,1)}, bf16[8,3,16,512]{3,2,1,0:T(8,128)(2,1)S(1)}, u32[]{:S(2)}) copy-start(bf16[8,3,16,512]{3,2,1,0:T(8,128)(2,1)S(1)} %collective-permute-done.39.refs_1_) | copy-start | bytes 1179652
  175.0 11.7 %collective-permute-start.40 = (bf16[8,3,16,512]{3,2,1,0:T(8,128)(2,1)S(1)}, bf16[8,3,16,512]{3,2,1,0:T(8,128)(2,1)}, u32[]{:S(2)}, u32[]{:S(2)}) collective-permute-start(bf16[8,3,16,512]{3,2,1,0:T(8,128)(2,1)S(1)} %collective-permute-done.39.refs_1_), channel_id=1, source_target_pairs={{0,6},{2,0},{4,2},{6,4},{1,7},{3,1},{5,3},{7,5},{8,14},{10,8},{12,... | collective-permute-start | bytes 1179656 | tf_op jit(solution)/shard_map/ppermute | solution.py:24
  178.1 105.0 %copy-start.21 = (bf16[8,3,16,512]{3,2,1,0:T(8,128)(2,1)}, bf16[8,3,16,512]{3,2,1,0:T(8,128)(2,1)S(1)}, u32[]{:S(2)}) copy-start(bf16[8,3,16,512]{3,2,1,0:T(8,128)(2,1)S(1)} %collective-permute-done.45.refs_5_) | copy-start | bytes 1179652
  178.1 12.5 %collective-permute-start.46 = (bf16[8,3,16,512]{3,2,1,0:T(8,128)(2,1)S(1)}, bf16[8,3,16,512]{3,2,1,0:T(8,128)(2,1)}, u32[]{:S(2)}, u32[]{:S(2)}) collective-permute-start(bf16[8,3,16,512]{3,2,1,0:T(8,128)(2,1)S(1)} %collective-permute-done.45.refs_5_), channel_id=1, source_target_pairs={{0,24},{8,0},{16,8},{24,16},{1,25},{9,1},{17,9},{25,17},{2,26},{10... | collective-permute-start | bytes 1179656 | tf_op jit(solution)/shard_map/ppermute | solution.py:24
  186.7 100.8 %collective-permute-start.41 = (bf16[8,3,16,512]{3,2,1,0:T(8,128)(2,1)}, bf16[8,3,16,512]{3,2,1,0:T(8,128)(2,1)}, u32[]{:S(2)}, u32[]{:S(2)}) collective-permute-start(bf16[8,3,16,512]{3,2,1,0:T(8,128)(2,1)} %collective-permute-done.40.refs_2_), channel_id=1, source_target_pairs={{0,6},{2,0},{4,2},{6,4},{1,7},{3,1},{5,3},{7,5},{8,14},{10,8},{12,... | collective-permute-start | bytes 1179656 | tf_op jit(solution)/shard_map/ppermute | solution.py:24
  190.6 96.9 %collective-permute-start.47 = (bf16[8,3,16,512]{3,2,1,0:T(8,128)(2,1)}, bf16[8,3,16,512]{3,2,1,0:T(8,128)(2,1)}, u32[]{:S(2)}, u32[]{:S(2)}) collective-permute-start(bf16[8,3,16,512]{3,2,1,0:T(8,128)(2,1)} %collective-permute-done.46.refs_6_), channel_id=1, source_target_pairs={{0,24},{8,0},{16,8},{24,16},{1,25},{9,1},{17,9},{25,17},{2,26},{10... | collective-permute-start | bytes 1179656 | tf_op jit(solution)/shard_map/ppermute | solution.py:24
  283.0 44.0 %collective-permute-start.51 = (bf16[384,1024]{1,0:T(8,128)(2,1)}, bf16[384,1024]{1,0:T(8,128)(2,1)S(1)}, u32[]{:S(2)}, u32[]{:S(2)}) collective-permute-start(bf16[384,1024]{1,0:T(8,128)(2,1)} %attend_finish.5), channel_id=1, source_target_pairs={{0,1},{1,0},{2,3},{3,2},{4,5},{5,4},{6,7},{7,6},{8,9},{9,8},{10,11... | collective-permute-start | bytes 2359304 | tf_op jit(solution)/shard_map/ppermute | solution.py:24
  295.9 10.6 %collective-permute-start.50 = (f32[2,8,384]{2,1,0:T(8,128)}, f32[2,8,384]{2,1,0:T(8,128)S(1)}, u32[]{:S(2)}, u32[]{:S(2)}) collective-permute-start(f32[2,8,384]{2,1,0:T(8,128)} %get-tuple-element.70.refs_17_), channel_id=1, source_target_pairs={{0,65},{65,0},{1,64},{64,1},{2,67},{67,2},{3,66},{66,3},{4,69},{69... | collective-permute-start | bytes 73736 | tf_op jit(solution)/shard_map/ppermute | solution.py:443
  296.3 10.2 %collective-permute-start.49 = (f32[2,8,384]{2,1,0:T(8,128)}, f32[2,8,384]{2,1,0:T(8,128)S(1)}, u32[]{:S(2)}, u32[]{:S(2)}) collective-permute-start(f32[2,8,384]{2,1,0:T(8,128)} %get-tuple-element.70.refs_17_), channel_id=1, source_target_pairs={{0,64},{64,0},{1,65},{65,1},{2,66},{66,2},{3,67},{67,3},{4,68},{68... | collective-permute-start | bytes 73736 | tf_op jit(solution)/shard_map/ppermute | solution.py:443
  297.4 9.1 %collective-permute-start.48 = (f32[2,8,384]{2,1,0:T(8,128)}, f32[2,8,384]{2,1,0:T(8,128)S(1)}, u32[]{:S(2)}, u32[]{:S(2)}) collective-permute-start(f32[2,8,384]{2,1,0:T(8,128)} %get-tuple-element.70.refs_17_), channel_id=1, source_target_pairs={{0,1},{1,0},{64,65},{65,64},{2,3},{3,2},{66,67},{67,66},{4,5},{5,4... | collective-permute-start | bytes 73736 | tf_op jit(solution)/shard_map/ppermute | solution.py:443
  316.1 20.6 %collective-permute-start.52 = (bf16[384,1024]{1,0:T(8,128)(2,1)}, bf16[384,1024]{1,0:T(8,128)(2,1)S(1)}, u32[]{:S(2)}, u32[]{:S(2)}) collective-permute-start(bf16[384,1024]{1,0:T(8,128)(2,1)} %attend_finish.7), channel_id=1, source_target_pairs={{0,1},{1,0},{2,3},{3,2},{4,5},{5,4},{6,7},{7,6},{8,9},{9,8},{10,11... | collective-permute-start | bytes 2359304 | tf_op jit(solution)/shard_map/ppermute | solution.py:24
  316.2 2.6 collective-permute-start.53
  (26 other events, 201.7 us)

commit v4 on v3

--- a/solution.py
+++ b/solution.py
@@ -263,11 +263,48 @@
     )(scal, q, q_rec, mine, mine, mine, mine)
 
 
+def load_before(s_ref, before, block, kv, sem):
+    head_now = pl.program_id(0)
+
+    @pl.when(head_now == 0)
+    def _():
+        for i, array in enumerate(before):
+            @pl.when(chosen(s_ref) == i)
+            def _(array=array):
+                for head in range(2):
+
+                    def start(at, slot, head=head):
+                        pltpu.make_async_copy(
+                            array.at[at, :, pl.ds(head * DH, DH)], kv.at[head, slot], sem.at[head]
+                        ).start()
+
+                    start(block, 0)
+                    start(2 + block, 1)
+
+                    @pl.when(block == 0)
+                    def _(start=start):
+                        start(1, 2)
+                        start(3, 3)
+
+    for head in range(2):
+        for b in range(2):
+
+            @pl.when((head_now == head) & (block == b))
+            def _(head=head, b=b):
+                slots = kv.at[head, pl.ds(0, 4 - 2 * b)]
+                pltpu.make_async_copy(slots, slots, sem.at[head]).wait()
+
+
 def finish_kernel(c, j, sources, count, s_ref, *refs):
     core, chip = s_ref[0], s_ref[5]
     block = core if j == 0 else 1 - core
     q_ref, refs = refs[0], refs[1:]
-    before, refs = refs[: 4 * sources], refs[4 * sources :]
+    if c == 1:
+        before, refs = refs[:sources], refs[sources:]
+        kv, sem, refs = refs[-2], refs[-1], refs[:-2]
+        load_before(s_ref, before, block, kv, sem)
+    else:
+        before, refs = refs[:4], refs[4:]
     own, refs = (refs[:4], refs[4:]) if c == 0 else (refs[:2], refs[2:])
     fast_ref, gain_ref = refs[:2]
     powers = refs[2 : 2 + count]
@@ -284,19 +321,15 @@
     if c == 1:
         acc_ref, stat_ref = own
 
-        def here(i):
-            found = before[i][0]
-            for more in range(1, sources):
-                found = jnp.where(chosen(s_ref) == more, before[4 * more + i][0], found)
-            return found
+        head = pl.program_id(0)
 
         for b in range(2):
 
             @pl.when(block == b)
             def _(b=b):
-                blocks = [(here(0), here(2), col > row)]
+                blocks = [(kv[head, 0], kv[head, 1], col > row)]
                 if b == 0:
-                    blocks.append((here(1), here(3), None))
+                    blocks.append((kv[head, 2], kv[head, 3], None))
                 acc, peak, total = partial_attention(q_ref[0], blocks)
                 peak_own, total_own = stat_ref[0, 0, :, :1], stat_ref[0, 0, :, 64:65]
                 top = jnp.maximum(peak, peak_own)
@@ -331,12 +364,6 @@
     def block(s):
         return s[0] if j == 0 else 1 - s[0]
 
-    def spec(at, holds=lambda s: True):
-        return pl.BlockSpec(
-            (1, TOK, DH),
-            lambda h, s: (jnp.where(holds(s), at(s), 0), 0, jnp.where(holds(s), h, 0)),
-        )
-
     def always(at):
         return pl.BlockSpec((1, TOK, DH), lambda h, s: (at(s), 0, h))
 
@@ -344,13 +371,14 @@
     q_spec = own_spec(c) if j == 0 else rec_spec(c)
     specs = [q_spec]
     operands = [q if j == 0 else q_rec]
-    for i, array in enumerate(before):
-        holds = (lambda s, i=i: chosen(s) == i) if sources > 1 else (lambda s: True)
-        specs += [
-            spec(block, holds), spec(lambda s: 1, holds),
-            spec(lambda s: 2 + block(s), holds), spec(lambda s: 3, holds),
-        ]
-        operands += [array] * 4
+    scratch = []
+    if c == 0:
+        specs += [always(block), always(lambda s: 1), always(lambda s: 2 + block(s)), always(lambda s: 3)]
+        operands += before * 4
+    else:
+        specs += [ANY] * sources
+        operands += before
+        scratch = [pltpu.VMEM((2, 4, TOK, DH), bf16), pltpu.SemaphoreType.DMA((2,))]
     if c == 0:
         specs += [
             always(lambda s: 0), always(block), always(lambda s: 2), always(lambda s: 2 + block(s))
@@ -384,7 +412,11 @@
         name="attend_finish",
         out_shape=jax.ShapeDtypeStruct(shape, bf16),
         grid_spec=pltpu.PrefetchScalarGridSpec(
-            num_scalar_prefetch=1, grid=(2,), in_specs=specs, out_specs=out_spec
+            num_scalar_prefetch=1,
+            grid=(2,),
+            in_specs=specs,
+            out_specs=out_spec,
+            scratch_shapes=scratch,
         ),
         input_output_aliases=aliases,
         compiler_params=cparams(),

time: 339 us -> 338 us (level)
  no operation moved by 1% of the time
where the time goes in v4:
time: 338 us; the launch traced here: 337 us
  waiting for transfers between devices  129 us (38%)
  starting transfers between devices  105 us (31%)
  Pallas kernels  70.3 us (21%)
  local copies, waits for them, and re-layouts  20.8 us (6%)
  other arithmetic  11 us (3%)
    ppermute x46, starting transfers between devices, shift(): lax.ppermute(value, axis, [(i, (i + steps) % count) for i in range(count)])  91.5 us
    ppermute x1, waiting for transfers between devices, on_device(): halo0 = lax.ppermute(pair[0], chips, row)  79.1 us
    ppermute x46, waiting for transfers between devices, shift(): lax.ppermute(value, axis, [(i, (i + steps) % count) for i in range(count)])  46.3 us
    pallas_call x4, Pallas kernels, finish(): pl.pallas_call(functools.partial(finish_kernel, c, j, sources, len(powers...  31.9 us
    pallas_call x2, Pallas kernels, fast_apply(): pl.pallas_call(apply_kernel, name='fast_apply', out_shape=[jax.ShapeDtype...  16.8 us
    pallas_call x1, Pallas kernels, compute_grads(): pl.pallas_call(grads_kernel, name='fast_grads', out_shape=[jax.ShapeDtype...  13.3 us
    pallas_call x1, Pallas kernels, attend_local(): pl.pallas_call(local_kernel, name='attend_local', out_shape=[jax.ShapeDty...  8.33 us
  transfers between devices with their start and end apart: 54, of which 23 were waited for; matrix products, arithmetic and copies ran while one was open for 7% of the time, Pallas kernels for 17%

profile of v4, /device:TPU:1, one launch (start us, length us, event | category | flops | bytes accessed | tf_op | source)
XLA Modules:
  0.0 336.8 jit_solution(16473802025510063462)
XLA Ops:
  1.6 1.5 collective-permute-start
  4.0 3.1 collective-permute-start.1
  7.1 4.8 %collective-permute-done.1 = f32[2,3,16,512]{3,2,1,0:T(8,128)} collective-permute-done((f32[2,3,16,512]{3,2,1,0:T(8,128)S(1)}, f32[2,3,16,512]{3,2,1,0:T(8,128)}, u32[]{:S(2)}, u32[]{:S(2)}) %collective-permute-start.1) | collective-permute-done | bytes 196640 | tf_op jit(solution)/shard_map/ppermute | solution.py:24
  11.9 2.7 constant_dynamic-slice_fusion.5
  15.8 1.3 constant_dynamic-slice_fusion.7
  18.7 1.8 collective-permute-start.6
  20.4 3.3 collective-permute-start.5
  24.9 2.7 constant_dynamic-slice_fusion.8
  27.6 1.3 constant_dynamic-slice_fusion.6
  29.7 1.3 copy.19.refs_12_
  31.0 1.2 collective-permute-start.12
  32.2 2.5 collective-permute-start.11
  37.2 2.1 collective-permute-done.11
  39.9 1.2 collective-permute-start.7
  42.1 1.7 fusion.15
  43.8 1.5 collective-permute-start.14
  45.3 1.5 fusion.14
  46.8 2.1 collective-permute-done.9.refs_3_
  48.9 1.5 collective-permute-start.13
  50.4 3.4 %maximum_select_fusion = (bf16[4,384,1024]{2,1,0:T(8,128)(2,1)S(1)}, bf16[4,384,1024]{2,1,0:T(8,128)(2,1)}) fusion(bf16[1,384,1024]{2,1,0:T(8,128)(2,1)S(1)} %get-tuple-element.83, bf16[1,384,1024]{2,1,0:T(8,128)(2,1)S(1)} %copy-done.11, bf16[1,384,1024]{2,1,0:T(8,128)(2,1)S(1)} %get-tuple-element.81, bf16[1,384,1024]{2,1,0:T(8,128)(2,1)S(1)} %copy-done.9, ...), kind=kLoop, calls=%fused_computation | loop fusion | flops 22020096 | bytes 12582913 | tf_op jit(solution)/shard_map/jit(_where)/select_n | solution.py:517
  54.7 2.3 collective-permute-done.7.refs_1_
  57.1 2.0 collective-permute-done.14.refs_6_
  60.8 13.3 %fast_grads.1 = (bf16[8,3,16,512]{3,2,1,0:T(8,128)(2,1)}, bf16[8,3,16,512]{3,2,1,0:T(8,128)(2,1)}, bf16[8,3,16,512]{3,2,1,0:T(8,128)(2,1)}, bf16[8,3,16,512]{3,2...) custom-call(s32[6]{0:T(128)} %stack.78.s_ref, ...), custom_call_target="tpu_custom_call" | custom-call | tf_op jit(solution)/shard_map/fast_grads/pallas_call | solution.py:130
  74.1 2.5 collective-permute-start.18
  76.9 4.0 %collective-permute-start.30 = (bf16[2,384,1024]{2,1,0:T(8,128)(2,1)S(1)}, bf16[2,384,1024]{2,1,0:T(8,128)(2,1)S(1)}, u32[]{:S(2)}, u32[]{:S(2)}) collective-permute-start(bf16[2,384,1024]{2,1,0:T(8,128)(2,1)S(1)} %constant_dynamic-slice_fusion.2), channel_id=1, source_target_pairs={{0,1},{1,0},{2,3},{3,2},{4,5},{5,4},{6,7},{7,6},{8,9},{9,8},{10,11... | collective-permute-start | bytes 4718600 | tf_op jit(solution)/shard_map/ppermute | solution.py:24
  80.8 2.6 collective-permute-start.24
  83.5 3.1 collective-permute-start.19
  86.6 4.8 %collective-permute-done.24 = bf16[8,3,16,512]{3,2,1,0:T(8,128)(2,1)S(1)} collective-permute-done((bf16[8,3,16,512]{3,2,1,0:T(8,128)(2,1)S(1)}, bf16[8,3,16,512]{3,2,1,0:T(8,128)(2,1)S(1)}, u32[]{:S(2)}, u32[]{:S(2)}) %collective-permute-start.24) | collective-permute-done | bytes 393248 | tf_op jit(solution)/shard_map/ppermute | solution.py:24
  91.5 3.4 collective-permute-start.25
  96.5 5.4 %collective-permute-done.25 = bf16[8,3,16,512]{3,2,1,0:T(8,128)(2,1)S(1)} collective-permute-done((bf16[8,3,16,512]{3,2,1,0:T(8,128)(2,1)S(1)}, bf16[8,3,16,512]{3,2,1,0:T(8,128)(2,1)S(1)}, u32[]{:S(2)}, u32[]{:S(2)}) %collective-permute-start.25) | collective-permute-done | bytes 393248 | tf_op jit(solution)/shard_map/ppermute | solution.py:24
  102.1 3.5 %collective-permute-start.26 = (bf16[8,3,16,512]{3,2,1,0:T(8,128)(2,1)S(1)}, bf16[8,3,16,512]{3,2,1,0:T(8,128)(2,1)S(1)}, u32[]{:S(2)}, u32[]{:S(2)}) collective-permute-start(bf16[8,3,16,512]{3,2,1,0:T(8,128)(2,1)S(1)} %add_convert_fusion), channel_id=1, source_target_pairs={{0,24},{8,0},{16,8},{24,16},{1,25},{9,1},{17,9},{25,17},{2,26},{10... | collective-permute-start | bytes 1179656 | tf_op jit(solution)/shard_map/ppermute | solution.py:24
  106.7 8.4 %fast_apply.2 = (f32[2,384,1024]{2,1,0:T(8,128)}, f32[2,8,384]{2,1,0:T(8,128)}) custom-call(s32[6]{0:T(128)} %stack.78.s_ref, bf16[8,3,16,512]{3,2,1,0:T(8,128)(2,1)} %copy-done.6, bf16[8,3,16,512]{3,2,1,0:T(8,128)(2,1)} %copy-done.16, bf16[8,3,16,512]{3,2,1,0:T(8,128)(2,1)} %copy-done.15, bf16[8,3,16,512]{3,2,1,0:T(8,128)(2,1)} %copy-done.14, ...), custom_call_target="tpu_custom_call" | custom-call | tf_op jit(solution)/shard_map/fast_apply/pallas_call | solution.py:181
  115.1 2.7 collective-permute-start.31
  121.8 3.1 collective-permute-done.21
  124.9 1.6 collective-permute-start.22
  128.4 2.8 collective-permute-start.23
  132.9 2.6 collective-permute-done.29
  135.6 3.0 collective-permute-start.32
  138.6 5.4 %collective-permute-start.16 = (bf16[4,384,1024]{2,1,0:T(8,128)(2,1)}, bf16[4,384,1024]{2,1,0:T(8,128)(2,1)}, u32[]{:S(2)}, u32[]{:S(2)}) collective-permute-start(bf16[4,384,1024]{2,1,0:T(8,128)(2,1)} %get-tuple-element.64.kb.k2.vb.v2), channel_id=1, source_target_pairs={{0,2},{2,4},{4,6},{6,8},{8,10},{10,12},{12,14},{14,16},{16,18},{18... | collective-permute-start | bytes 9437192 | tf_op jit(solution)/shard_map/ppermute | solution.py:526
  144.5 2.2 collective-permute-done.33.refs_12_
  146.8 2.4 collective-permute-start.34
  150.3 7.1 %collective-permute-start.42 = (bf16[2,3,16,512]{3,2,1,0:T(8,128)(2,1)S(1)}, bf16[2,3,16,512]{3,2,1,0:T(8,128)(2,1)S(1)}, u32[]{:S(2)}, u32[]{:S(2)}) collective-permute-start(bf16[2,3,16,512]{3,2,1,0:T(8,128)(2,1)S(1)} %get-tuple-element.89), channel_id=1, source_target_pairs={{0,6},{2,0},{4,2},{6,4},{1,7},{3,1},{5,3},{7,5},{8,14},{10,8},{12,... | collective-permute-start | bytes 294920 | tf_op jit(solution)/shard_map/ppermute | solution.py:24
  157.4 1.6 collective-permute-done.42
  159.0 3.0 collective-permute-start.43
  162.5 1.7 collective-permute-done.43
  164.2 3.7 %collective-permute-start.44 = (bf16[2,3,16,512]{3,2,1,0:T(8,128)(2,1)S(1)}, bf16[2,3,16,512]{3,2,1,0:T(8,128)(2,1)S(1)}, u32[]{:S(2)}, u32[]{:S(2)}) collective-permute-start(bf16[2,3,16,512]{3,2,1,0:T(8,128)(2,1)S(1)} %collective-permute-done.43), channel_id=1, source_target_pairs={{0,6},{2,0},{4,2},{6,4},{1,7},{3,1},{5,3},{7,5},{8,14},{10,8},{12,... | collective-permute-start | bytes 294920 | tf_op jit(solution)/shard_map/ppermute | solution.py:24
  168.0 1.7 collective-permute-start.39
  169.7 3.4 %collective-permute-start.45 = (bf16[8,3,16,512]{3,2,1,0:T(8,128)(2,1)S(1)}, bf16[8,3,16,512]{3,2,1,0:T(8,128)(2,1)S(1)}, u32[]{:S(2)}, u32[]{:S(2)}) collective-permute-start(bf16[8,3,16,512]{3,2,1,0:T(8,128)(2,1)S(1)} %pad_maximum_fusion.4.refs_4_), channel_id=1, source_target_pairs={{0,24},{8,0},{16,8},{24,16},{1,25},{9,1},{17,9},{25,17},{2,26},{10... | collective-permute-start | bytes 1179656 | tf_op jit(solution)/shard_map/ppermute | solution.py:24
  173.2 1.9 collective-permute-done.39.refs_1_
  175.0 3.0 collective-permute-start.40
  178.1 3.9 %collective-permute-start.46 = (bf16[8,3,16,512]{3,2,1,0:T(8,128)(2,1)S(1)}, bf16[8,3,16,512]{3,2,1,0:T(8,128)(2,1)}, u32[]{:S(2)}, u32[]{:S(2)}) collective-permute-start(bf16[8,3,16,512]{3,2,1,0:T(8,128)(2,1)S(1)} %collective-permute-done.45.refs_5_), channel_id=1, source_target_pairs={{0,24},{8,0},{16,8},{24,16},{1,25},{9,1},{17,9},{25,17},{2,26},{10... | collective-permute-start | bytes 1179656 | tf_op jit(solution)/shard_map/ppermute | solution.py:24
  181.9 4.8 %collective-permute-done.40.refs_2_ = bf16[8,3,16,512]{3,2,1,0:T(8,128)(2,1)} collective-permute-done((bf16[8,3,16,512]{3,2,1,0:T(8,128)(2,1)S(1)}, bf16[8,3,16,512]{3,2,1,0:T(8,128)(2,1)}, u32[]{:S(2)}, u32[]{:S(2)}) %collective-permute-start.40) | collective-permute-done | bytes 393248 | tf_op jit(solution)/shard_map/ppermute | solution.py:24
  186.7 3.4 %collective-permute-start.41 = (bf16[8,3,16,512]{3,2,1,0:T(8,128)(2,1)}, bf16[8,3,16,512]{3,2,1,0:T(8,128)(2,1)}, u32[]{:S(2)}, u32[]{:S(2)}) collective-permute-start(bf16[8,3,16,512]{3,2,1,0:T(8,128)(2,1)} %collective-permute-done.40.refs_2_), channel_id=1, source_target_pairs={{0,6},{2,0},{4,2},{6,4},{1,7},{3,1},{5,3},{7,5},{8,14},{10,8},{12,... | collective-permute-start | bytes 1179656 | tf_op jit(solution)/shard_map/ppermute | solution.py:24
  190.6 3.5 %collective-permute-start.47 = (bf16[8,3,16,512]{3,2,1,0:T(8,128)(2,1)}, bf16[8,3,16,512]{3,2,1,0:T(8,128)(2,1)}, u32[]{:S(2)}, u32[]{:S(2)}) collective-permute-start(bf16[8,3,16,512]{3,2,1,0:T(8,128)(2,1)} %collective-permute-done.46.refs_6_), channel_id=1, source_target_pairs={{0,24},{8,0},{16,8},{24,16},{1,25},{9,1},{17,9},{25,17},{2,26},{10... | collective-permute-start | bytes 1179656 | tf_op jit(solution)/shard_map/ppermute | solution.py:24
  194.7 79.1 %collective-permute-done.35.refs_1_.refs_2_.refs_3_.refs_4_ = bf16[4,384,1024]{2,1,0:T(8,128)(2,1)S(1)} collective-permute-done((bf16[4,384,1024]{2,1,0:T(8,128)(2,1)S(1)}, bf16[4,384,1024]{2,1,0:T(8,128)(2,1)S(1)}, u32[]{:S(2)}, u32[]{:S(2)}) %collective-permute-start.35) | collective-permute-done | bytes 3145760 | tf_op jit(solution)/shard_map/ppermute | solution.py:525
  273.8 1.6 copy-done
  275.4 7.6 %attend_finish.5 = bf16[384,1024]{1,0:T(8,128)(2,1)} custom-call(s32[6]{0:T(128)} %stack.78.s_ref, bf16[2,384,1024]{2,1,0:T(8,128)(2,1)} %copy-done.3, bf16[4,384,1024]{2,1,0:T(8,128)(2,1)} %copy-done, bf16[4,384,1024]{2,1,0:T(8,128)(2,1)} %copy-done, bf16[4,384,1024]{2,1,0:T(8,128)(2,1)} %copy-done, bf16[4,384,1024]{2,1,0:T(8,128)(2,1)} %copy-done, ...), custom_call_target="tpu_custom_call" | custom-call | tf_op jit(solution)/shard_map/attend_finish/pallas_call | solution.py:410
  283.0 4.4 %collective-permute-start.51 = (bf16[384,1024]{1,0:T(8,128)(2,1)}, bf16[384,1024]{1,0:T(8,128)(2,1)S(1)}, u32[]{:S(2)}, u32[]{:S(2)}) collective-permute-start(bf16[384,1024]{1,0:T(8,128)(2,1)} %attend_finish.5), channel_id=1, source_target_pairs={{0,1},{1,0},{2,3},{3,2},{4,5},{5,4},{6,7},{7,6},{8,9},{9,8},{10,11... | collective-permute-start | bytes 2359304 | tf_op jit(solution)/shard_map/ppermute | solution.py:24
  287.5 8.4 %fast_apply.3 = (f32[2,384,1024]{2,1,0:T(8,128)}, f32[2,8,384]{2,1,0:T(8,128)}) custom-call(s32[6]{0:T(128)} %stack.78.s_ref, bf16[8,3,16,512]{3,2,1,0:T(8,128)(2,1)} %copy-done.12, bf16[8,3,16,512]{3,2,1,0:T(8,128)(2,1)} %copy-done.20, bf16[8,3,16,512]{3,2,1,0:T(8,128)(2,1)} %collective-permute-done.40.refs_2_, ...), custom_call_target="tpu_custom_call" | custom-call | tf_op jit(solution)/shard_map/fast_apply/pallas_call | solution.py:181
  298.1 8.3 %attend_local.1 = (f32[2,384,1024]{2,1,0:T(8,128)}, f32[2,2,384,128]{3,2,1,0:T(8,128)}) custom-call(s32[6]{0:T(128)} %stack.78.s_ref, bf16[2,384,2048]{2,1,0:T(8,128)(2,1)} %refs_0_.1, bf16[2,384,1024]{2,1,0:T(8,128)(2,1)} %copy-done.3, bf16[4,384,1024]{2,1,0:T(8,128)(2,1)} %get-tuple-element.64.kb.k2.vb.v2, ...), custom_call_target="tpu_custom_call" | custom-call | tf_op jit(solution)/shard_map/attend_local/pallas_call | solution.py:242
  307.1 8.7 %attend_finish.7 = bf16[384,1024]{1,0:T(8,128)(2,1)} custom-call(s32[6]{0:T(128)} %stack.78.s_ref, bf16[2,384,1024]{2,1,0:T(8,128)(2,1)} %copy-done.3, bf16[4,384,1024]{2,1,0:T(8,128)(2,1)} %collective-permute-done.16.refs_1_, bf16[4,384,1024]{2,1,0:T(8,128)(2,1)} %collective-permute-done.34.refs_2_, bf16[4,384,1024]{2,1,0:T(8,128)(2,1)} %copy-done, ...), custom_call_target="tpu_custom_call" | custom-call | tf_op jit(solution)/shard_map/attend_finish/pallas_call | solution.py:410
  316.8 1.8 collective-permute-done.53
  319.2 7.6 %attend_finish.4 = bf16[2,384,2048]{2,1,0:T(8,128)(2,1)} custom-call(s32[6]{0:T(128)} %stack.78.s_ref, bf16[2,384,2048]{2,1,0:T(8,128)(2,1)} %refs_0_.1, bf16[4,384,1024]{2,1,0:T(8,128)(2,1)} %copy-done, bf16[4,384,1024]{2,1,0:T(8,128)(2,1)} %copy-done, bf16[4,384,1024]{2,1,0:T(8,128)(2,1)} %copy-done, bf16[4,384,1024]{2,1,0:T(8,128)(2,1)} %copy-done, ...), custom_call_target="tpu_custom_call" | custom-call | tf_op jit(solution)/shard_map/attend_finish/pallas_call | solution.py:410
  327.8 8.0 %attend_finish.6 = bf16[2,384,2048]{2,1,0:T(8,128)(2,1)} custom-call(s32[6]{0:T(128)} %stack.78.s_ref, bf16[2,384,2048]{2,1,0:T(8,128)(2,1)} %refs_0_.1, bf16[4,384,1024]{2,1,0:T(8,128)(2,1)} %collective-permute-done.16.refs_1_, bf16[4,384,1024]{2,1,0:T(8,128)(2,1)} %collective-permute-done.34.refs_2_, ...), custom_call_target="tpu_custom_call", output_to_operand_aliasing={{}: (13, {})} | custom-call | tf_op jit(solution)/shard_map/attend_finish/pallas_call | solution.py:410
  (174 shorter events, 33.9 us)
Async XLA Ops:
  1.6 2.4 collective-permute-start
  4.0 7.9 %collective-permute-start.1 = (f32[2,3,16,512]{3,2,1,0:T(8,128)S(1)}, f32[2,3,16,512]{3,2,1,0:T(8,128)}, u32[]{:S(2)}, u32[]{:S(2)}) collective-permute-start(f32[2,3,16,512]{3,2,1,0:T(8,128)S(1)} %maximum_select_fusion.2), channel_id=1, source_target_pairs={{0,32},{32,0},{1,33},{33,1},{2,34},{34,2},{3,35},{35,3},{4,36},{36... | collective-permute-start | bytes 589832 | tf_op jit(solution)/shard_map/ppermute | solution.py:24
  14.6 26.6 %collective-permute-start.3 = (bf16[2,384,1024]{2,1,0:T(8,128)(2,1)}, bf16[2,384,1024]{2,1,0:T(8,128)(2,1)}, u32[]{:S(2)}, u32[]{:S(2)}) collective-permute-start(bf16[2,384,1024]{2,1,0:T(8,128)(2,1)} %constant_dynamic-slice_fusion.5), channel_id=1, source_target_pairs={{0,1},{1,0},{2,3},{3,2},{4,5},{5,4},{6,7},{7,6},{8,9},{9,8},{10,11... | collective-permute-start | bytes 4718600 | tf_op jit(solution)/shard_map/ppermute | solution.py:24
  17.1 26.7 %collective-permute-start.2 = (bf16[2,384,1024]{2,1,0:T(8,128)(2,1)}, bf16[2,384,1024]{2,1,0:T(8,128)(2,1)}, u32[]{:S(2)}, u32[]{:S(2)}) collective-permute-start(bf16[2,384,1024]{2,1,0:T(8,128)(2,1)} %constant_dynamic-slice_fusion.7), channel_id=1, source_target_pairs={{0,1},{1,0},{2,3},{3,2},{4,5},{5,4},{6,7},{7,6},{8,9},{9,8},{10,11... | collective-permute-start | bytes 4718600 | tf_op jit(solution)/shard_map/ppermute | solution.py:24
  18.7 12.3 %collective-permute-start.6 = (bf16[2,3,16,512]{3,2,1,0:T(8,128)(2,1)S(1)}, bf16[2,3,16,512]{3,2,1,0:T(8,128)(2,1)}, u32[]{:S(2)}, u32[]{:S(2)}) collective-permute-start(bf16[2,3,16,512]{3,2,1,0:T(8,128)(2,1)S(1)} %get-tuple-element.92), channel_id=1, source_target_pairs={{0,8},{8,16},{16,24},{24,0},{1,9},{9,17},{17,25},{25,1},{2,10},{10... | collective-permute-start | bytes 294920 | tf_op jit(solution)/shard_map/ppermute | solution.py:24
  20.4 11.7 %collective-permute-start.5 = (bf16[2,3,16,512]{3,2,1,0:T(8,128)(2,1)S(1)}, bf16[2,3,16,512]{3,2,1,0:T(8,128)(2,1)}, u32[]{:S(2)}, u32[]{:S(2)}) collective-permute-start(bf16[2,3,16,512]{3,2,1,0:T(8,128)(2,1)S(1)} %get-tuple-element.92), channel_id=1, source_target_pairs={{0,16},{8,24},{16,0},{24,8},{1,17},{9,25},{17,1},{25,9},{2,18},{10... | collective-permute-start | bytes 294920 | tf_op jit(solution)/shard_map/ppermute | solution.py:24
  23.8 5.2 %collective-permute-start.17 = (f32[2,384]{1,0:T(2,128)S(1)}, f32[2,384]{1,0:T(2,128)S(1)}, u32[]{:S(2)}, u32[]{:S(2)}) collective-permute-start(f32[2,384]{1,0:T(2,128)S(1)} %get-tuple-element.96), channel_id=1, source_target_pairs={{0,1},{1,0},{2,3},{3,2},{4,5},{5,4},{6,7},{7,6},{8,9},{9,8},{10,11... | collective-permute-start | bytes 9224 | tf_op jit(solution)/shard_map/ppermute | solution.py:24
  28.9 5.7 %collective-permute-start.4 = (bf16[2,3,16,512]{3,2,1,0:T(8,128)(2,1)S(1)}, bf16[2,3,16,512]{3,2,1,0:T(8,128)(2,1)S(1)}, u32[]{:S(2)}, u32[]{:S(2)}) collective-permute-start(bf16[2,3,16,512]{3,2,1,0:T(8,128)(2,1)S(1)} %get-tuple-element.92), channel_id=1, source_target_pairs={{0,24},{8,0},{16,8},{24,16},{1,25},{9,1},{17,9},{25,17},{2,26},{10... | collective-permute-start | bytes 294920 | tf_op jit(solution)/shard_map/ppermute | solution.py:24
  31.0 5.8 %collective-permute-start.12 = (bf16[2,3,16,512]{3,2,1,0:T(8,128)(2,1)S(1)}, bf16[2,3,16,512]{3,2,1,0:T(8,128)(2,1)S(1)}, u32[]{:S(2)}, u32[]{:S(2)}) collective-permute-start(bf16[2,3,16,512]{3,2,1,0:T(8,128)(2,1)S(1)} %get-tuple-element.91), channel_id=1, source_target_pairs={{0,2},{2,4},{4,6},{6,0},{1,3},{3,5},{5,7},{7,1},{8,10},{10,12},{12... | collective-permute-start | bytes 294920 | tf_op jit(solution)/shard_map/ppermute | solution.py:24
  32.2 7.1 %collective-permute-start.11 = (bf16[2,3,16,512]{3,2,1,0:T(8,128)(2,1)S(1)}, bf16[2,3,16,512]{3,2,1,0:T(8,128)(2,1)S(1)}, u32[]{:S(2)}, u32[]{:S(2)}) collective-permute-start(bf16[2,3,16,512]{3,2,1,0:T(8,128)(2,1)S(1)} %get-tuple-element.91), channel_id=1, source_target_pairs={{0,4},{2,6},{4,0},{6,2},{1,5},{3,7},{5,1},{7,3},{8,12},{10,14},{12... | collective-permute-start | bytes 294920 | tf_op jit(solution)/shard_map/ppermute | solution.py:24
  34.6 5.3 %collective-permute-start.10 = (bf16[2,3,16,512]{3,2,1,0:T(8,128)(2,1)S(1)}, bf16[2,3,16,512]{3,2,1,0:T(8,128)(2,1)S(1)}, u32[]{:S(2)}, u32[]{:S(2)}) collective-permute-start(bf16[2,3,16,512]{3,2,1,0:T(8,128)(2,1)S(1)} %get-tuple-element.91), channel_id=1, source_target_pairs={{0,6},{2,0},{4,2},{6,4},{1,7},{3,1},{5,3},{7,5},{8,14},{10,8},{12,... | collective-permute-start | bytes 294920 | tf_op jit(solution)/shard_map/ppermute | solution.py:24
  36.8 12.1 %collective-permute-start.9 = (bf16[8,3,16,512]{3,2,1,0:T(8,128)(2,1)S(1)}, bf16[8,3,16,512]{3,2,1,0:T(8,128)(2,1)S(1)}, u32[]{:S(2)}, u32[]{:S(2)}) collective-permute-start(bf16[8,3,16,512]{3,2,1,0:T(8,128)(2,1)S(1)} %pad_maximum_fusion.1.refs_0_), channel_id=1, source_target_pairs={{0,2},{2,4},{4,6},{6,0},{1,3},{3,5},{5,7},{7,1},{8,10},{10,12},{12... | collective-permute-start | bytes 1179656 | tf_op jit(solution)/shard_map/ppermute | solution.py:24
  39.3 15.4 %collective-permute-start.8 = (bf16[8,3,16,512]{3,2,1,0:T(8,128)(2,1)S(1)}, bf16[8,3,16,512]{3,2,1,0:T(8,128)(2,1)S(1)}, u32[]{:S(2)}, u32[]{:S(2)}) collective-permute-start(bf16[8,3,16,512]{3,2,1,0:T(8,128)(2,1)S(1)} %pad_maximum_fusion.1.refs_0_), channel_id=1, source_target_pairs={{0,4},{2,6},{4,0},{6,2},{1,5},{3,7},{5,1},{7,3},{8,12},{10,14},{12... | collective-permute-start | bytes 1179656 | tf_op jit(solution)/shard_map/ppermute | solution.py:24
  39.9 17.2 %collective-permute-start.7 = (bf16[8,3,16,512]{3,2,1,0:T(8,128)(2,1)S(1)}, bf16[8,3,16,512]{3,2,1,0:T(8,128)(2,1)S(1)}, u32[]{:S(2)}, u32[]{:S(2)}) collective-permute-start(bf16[8,3,16,512]{3,2,1,0:T(8,128)(2,1)S(1)} %pad_maximum_fusion.1.refs_0_), channel_id=1, source_target_pairs={{0,6},{2,0},{4,2},{6,4},{1,7},{3,1},{5,3},{7,5},{8,14},{10,8},{12,... | collective-permute-start | bytes 1179656 | tf_op jit(solution)/shard_map/ppermute | solution.py:24
  41.3 15.9 %collective-permute-start.15 = (bf16[8,3,16,512]{3,2,1,0:T(8,128)(2,1)S(1)}, bf16[8,3,16,512]{3,2,1,0:T(8,128)(2,1)S(1)}, u32[]{:S(2)}, u32[]{:S(2)}) collective-permute-start(bf16[8,3,16,512]{3,2,1,0:T(8,128)(2,1)S(1)} %pad_maximum_fusion.2.refs_4_), channel_id=1, source_target_pairs={{0,8},{8,16},{16,24},{24,0},{1,9},{9,17},{17,25},{25,1},{2,10},{10... | collective-permute-start | bytes 1179656 | tf_op jit(solution)/shard_map/ppermute | solution.py:24
  43.8 15.3 %collective-permute-start.14 = (bf16[8,3,16,512]{3,2,1,0:T(8,128)(2,1)S(1)}, bf16[8,3,16,512]{3,2,1,0:T(8,128)(2,1)S(1)}, u32[]{:S(2)}, u32[]{:S(2)}) collective-permute-start(bf16[8,3,16,512]{3,2,1,0:T(8,128)(2,1)S(1)} %pad_maximum_fusion.2.refs_4_), channel_id=1, source_target_pairs={{0,16},{8,24},{16,0},{24,8},{1,17},{9,25},{17,1},{25,9},{2,18},{10... | collective-permute-start | bytes 1179656 | tf_op jit(solution)/shard_map/ppermute | solution.py:24
  48.9 11.1 %collective-permute-start.13 = (bf16[8,3,16,512]{3,2,1,0:T(8,128)(2,1)S(1)}, bf16[8,3,16,512]{3,2,1,0:T(8,128)(2,1)S(1)}, u32[]{:S(2)}, u32[]{:S(2)}) collective-permute-start(bf16[8,3,16,512]{3,2,1,0:T(8,128)(2,1)S(1)} %pad_maximum_fusion.2.refs_4_), channel_id=1, source_target_pairs={{0,24},{8,0},{16,8},{24,16},{1,25},{9,1},{17,9},{25,17},{2,26},{10... | collective-permute-start | bytes 1179656 | tf_op jit(solution)/shard_map/ppermute | solution.py:24
  53.9 90.1 %copy-start.1 = (bf16[4,384,1024]{2,1,0:T(8,128)(2,1)}, bf16[4,384,1024]{2,1,0:T(8,128)(2,1)S(1)}, u32[]{:S(2)}) copy-start(bf16[4,384,1024]{2,1,0:T(8,128)(2,1)S(1)} %get-tuple-element.65.refs_5_.refs_6_.refs_7_.refs_8_) | copy-start | bytes 9437188
  74.1 20.8 %copy-start.25 = (bf16[8,3,16,512]{3,2,1,0:T(8,128)(2,1)S(1)}, bf16[8,3,16,512]{3,2,1,0:T(8,128)(2,1)}, u32[]{:S(2)}) copy-start(bf16[8,3,16,512]{3,2,1,0:T(8,128)(2,1)} %get-tuple-element.55) | copy-start | bytes 1179652
  74.1 27.8 %copy-start.24 = (bf16[8,3,16,512]{3,2,1,0:T(8,128)(2,1)S(1)}, bf16[8,3,16,512]{3,2,1,0:T(8,128)(2,1)}, u32[]{:S(2)}) copy-start(bf16[8,3,16,512]{3,2,1,0:T(8,128)(2,1)} %get-tuple-element.59) | copy-start | bytes 1179652
  74.1 9.3 %collective-permute-start.18 = (bf16[8,3,16,512]{3,2,1,0:T(8,128)(2,1)}, bf16[8,3,16,512]{3,2,1,0:T(8,128)(2,1)S(1)}, u32[]{:S(2)}, u32[]{:S(2)}) collective-permute-start(bf16[8,3,16,512]{3,2,1,0:T(8,128)(2,1)} %get-tuple-element.53), channel_id=1, source_target_pairs={{0,6},{2,0},{4,2},{6,4},{1,7},{3,1},{5,3},{7,5},{8,14},{10,8},{12,... | collective-permute-start | bytes 1179656 | tf_op jit(solution)/shard_map/ppermute | solution.py:24
  76.9 28.7 %collective-permute-start.30 = (bf16[2,384,1024]{2,1,0:T(8,128)(2,1)S(1)}, bf16[2,384,1024]{2,1,0:T(8,128)(2,1)S(1)}, u32[]{:S(2)}, u32[]{:S(2)}) collective-permute-start(bf16[2,384,1024]{2,1,0:T(8,128)(2,1)S(1)} %constant_dynamic-slice_fusion.2), channel_id=1, source_target_pairs={{0,1},{1,0},{2,3},{3,2},{4,5},{5,4},{6,7},{7,6},{8,9},{9,8},{10,11... | collective-permute-start | bytes 4718600 | tf_op jit(solution)/shard_map/ppermute | solution.py:24
  80.8 10.6 %collective-permute-start.24 = (bf16[8,3,16,512]{3,2,1,0:T(8,128)(2,1)S(1)}, bf16[8,3,16,512]{3,2,1,0:T(8,128)(2,1)S(1)}, u32[]{:S(2)}, u32[]{:S(2)}) collective-permute-start(bf16[8,3,16,512]{3,2,1,0:T(8,128)(2,1)S(1)} %copy-done.35), channel_id=1, source_target_pairs={{0,24},{8,0},{16,8},{24,16},{1,25},{9,1},{17,9},{25,17},{2,26},{10... | collective-permute-start | bytes 1179656 | tf_op jit(solution)/shard_map/ppermute | solution.py:24
  83.5 11.4 %collective-permute-start.19 = (bf16[8,3,16,512]{3,2,1,0:T(8,128)(2,1)S(1)}, bf16[8,3,16,512]{3,2,1,0:T(8,128)(2,1)S(1)}, u32[]{:S(2)}, u32[]{:S(2)}) collective-permute-start(bf16[8,3,16,512]{3,2,1,0:T(8,128)(2,1)S(1)} %add_convert_fusion.3), channel_id=1, source_target_pairs={{0,6},{2,0},{4,2},{6,4},{1,7},{3,1},{5,3},{7,5},{8,14},{10,8},{12,... | collective-permute-start | bytes 1179656 | tf_op jit(solution)/shard_map/ppermute | solution.py:24
  91.5 10.4 %collective-permute-start.25 = (bf16[8,3,16,512]{3,2,1,0:T(8,128)(2,1)S(1)}, bf16[8,3,16,512]{3,2,1,0:T(8,128)(2,1)S(1)}, u32[]{:S(2)}, u32[]{:S(2)}) collective-permute-start(bf16[8,3,16,512]{3,2,1,0:T(8,128)(2,1)S(1)} %add_convert_fusion.1), channel_id=1, source_target_pairs={{0,24},{8,0},{16,8},{24,16},{1,25},{9,1},{17,9},{25,17},{2,26},{10... | collective-permute-start | bytes 1179656 | tf_op jit(solution)/shard_map/ppermute | solution.py:24
  95.8 23.8 %collective-permute-start.20 = (bf16[8,3,16,512]{3,2,1,0:T(8,128)(2,1)}, bf16[8,3,16,512]{3,2,1,0:T(8,128)(2,1)}, u32[]{:S(2)}, u32[]{:S(2)}) collective-permute-start(bf16[8,3,16,512]{3,2,1,0:T(8,128)(2,1)} %add_convert_fusion.2), channel_id=1, source_target_pairs={{0,6},{2,0},{4,2},{6,4},{1,7},{3,1},{5,3},{7,5},{8,14},{10,8},{12,... | collective-permute-start | bytes 1179656 | tf_op jit(solution)/shard_map/ppermute | solution.py:24
  102.1 18.8 %collective-permute-start.26 = (bf16[8,3,16,512]{3,2,1,0:T(8,128)(2,1)S(1)}, bf16[8,3,16,512]{3,2,1,0:T(8,128)(2,1)S(1)}, u32[]{:S(2)}, u32[]{:S(2)}) collective-permute-start(bf16[8,3,16,512]{3,2,1,0:T(8,128)(2,1)S(1)} %add_convert_fusion), channel_id=1, source_target_pairs={{0,24},{8,0},{16,8},{24,16},{1,25},{9,1},{17,9},{25,17},{2,26},{10... | collective-permute-start | bytes 1179656 | tf_op jit(solution)/shard_map/ppermute | solution.py:24
  115.1 3.7 %collective-permute-start.31 = (f32[2,8,384]{2,1,0:T(8,128)}, f32[2,8,384]{2,1,0:T(8,128)S(1)}, u32[]{:S(2)}, u32[]{:S(2)}) collective-permute-start(f32[2,8,384]{2,1,0:T(8,128)} %get-tuple-element.61), channel_id=1, source_target_pairs={{0,1},{1,0},{64,65},{65,64},{2,3},{3,2},{66,67},{67,66},{4,5},{5,4... | collective-permute-start | bytes 73736 | tf_op jit(solution)/shard_map/ppermute | solution.py:475
  119.6 24.4 %copy-start.28 = (f32[2,8,384]{2,1,0:T(8,128)}, f32[2,8,384]{2,1,0:T(8,128)S(1)}, u32[]{:S(2)}) copy-start(f32[2,8,384]{2,1,0:T(8,128)S(1)} %add.92.refs_11_) | copy-start | bytes 73732
  120.8 4.1 %collective-permute-start.21 = (bf16[2,3,16,512]{3,2,1,0:T(8,128)(2,1)S(1)}, bf16[2,3,16,512]{3,2,1,0:T(8,128)(2,1)S(1)}, u32[]{:S(2)}, u32[]{:S(2)}) collective-permute-start(bf16[2,3,16,512]{3,2,1,0:T(8,128)(2,1)S(1)} %slice.163), channel_id=1, source_target_pairs={{0,24},{8,0},{16,8},{24,16},{1,25},{9,1},{17,9},{25,17},{2,26},{10... | collective-permute-start | bytes 294920 | tf_op jit(solution)/shard_map/ppermute | solution.py:24
  121.0 5.4 %collective-permute-start.27 = (bf16[2,3,16,512]{3,2,1,0:T(8,128)(2,1)S(1)}, bf16[2,3,16,512]{3,2,1,0:T(8,128)(2,1)S(1)}, u32[]{:S(2)}, u32[]{:S(2)}) collective-permute-start(bf16[2,3,16,512]{3,2,1,0:T(8,128)(2,1)S(1)} %slice.162), channel_id=1, source_target_pairs={{0,6},{2,0},{4,2},{6,4},{1,7},{3,1},{5,3},{7,5},{8,14},{10,8},{12,... | collective-permute-start | bytes 294920 | tf_op jit(solution)/shard_map/ppermute | solution.py:24
  124.9 3.5 %collective-permute-start.22 = (bf16[2,3,16,512]{3,2,1,0:T(8,128)(2,1)S(1)}, bf16[2,3,16,512]{3,2,1,0:T(8,128)(2,1)S(1)}, u32[]{:S(2)}, u32[]{:S(2)}) collective-permute-start(bf16[2,3,16,512]{3,2,1,0:T(8,128)(2,1)S(1)} %fusion.7), channel_id=1, source_target_pairs={{0,24},{8,0},{16,8},{24,16},{1,25},{9,1},{17,9},{25,17},{2,26},{10... | collective-permute-start | bytes 294920 | tf_op jit(solution)/shard_map/ppermute | solution.py:24
  126.5 67.7 %copy-start.34 = (f32[2048]{0:T(1024)S(1)}, f32[2048]{0:T(1024)}, u32[]{:S(2)}) copy-start(f32[2048]{0:T(1024)} %param.15) | copy-start | bytes 24580
  126.5 4.7 %collective-permute-start.28 = (bf16[2,3,16,512]{3,2,1,0:T(8,128)(2,1)S(1)}, bf16[2,3,16,512]{3,2,1,0:T(8,128)(2,1)S(1)}, u32[]{:S(2)}, u32[]{:S(2)}) collective-permute-start(bf16[2,3,16,512]{3,2,1,0:T(8,128)(2,1)S(1)} %fusion.4), channel_id=1, source_target_pairs={{0,6},{2,0},{4,2},{6,4},{1,7},{3,1},{5,3},{7,5},{8,14},{10,8},{12,... | collective-permute-start | bytes 294920 | tf_op jit(solution)/shard_map/ppermute | solution.py:24
  128.4 4.4 %collective-permute-start.23 = (bf16[2,3,16,512]{3,2,1,0:T(8,128)(2,1)S(1)}, bf16[2,3,16,512]{3,2,1,0:T(8,128)(2,1)S(1)}, u32[]{:S(2)}, u32[]{:S(2)}) collective-permute-start(bf16[2,3,16,512]{3,2,1,0:T(8,128)(2,1)S(1)} %fusion.6), channel_id=1, source_target_pairs={{0,24},{8,0},{16,8},{24,16},{1,25},{9,1},{17,9},{25,17},{2,26},{10... | collective-permute-start | bytes 294920 | tf_op jit(solution)/shard_map/ppermute | solution.py:24
  131.2 4.3 %collective-permute-start.29 = (bf16[2,3,16,512]{3,2,1,0:T(8,128)(2,1)S(1)}, bf16[2,3,16,512]{3,2,1,0:T(8,128)(2,1)S(1)}, u32[]{:S(2)}, u32[]{:S(2)}) collective-permute-start(bf16[2,3,16,512]{3,2,1,0:T(8,128)(2,1)S(1)} %fusion.3), channel_id=1, source_target_pairs={{0,6},{2,0},{4,2},{6,4},{1,7},{3,1},{5,3},{7,5},{8,14},{10,8},{12,... | collective-permute-start | bytes 294920 | tf_op jit(solution)/shard_map/ppermute | solution.py:24
  135.6 8.9 %collective-permute-start.32 = (bf16[2,2,3,16,512]{4,3,2,1,0:T(8,128)(2,1)S(1)}, bf16[2,2,3,16,512]{4,3,2,1,0:T(8,128)(2,1)S(1)}, u32[]{:S(2)}, u32[]{:S(2)}) collective-permute-start(bf16[2,2,3,16,512]{4,3,2,1,0:T(8,128)(2,1)S(1)} %pad_maximum_fusion.6), channel_id=1, source_target_pairs={{0,32},{32,0},{1,33},{33,1},{2,34},{34,2},{3,35},{35,3},{4,36},{36... | collective-permute-start | bytes 589832 | tf_op jit(solution)/shard_map/ppermute | solution.py:24
  138.6 158.8 %collective-permute-start.16 = (bf16[4,384,1024]{2,1,0:T(8,128)(2,1)}, bf16[4,384,1024]{2,1,0:T(8,128)(2,1)}, u32[]{:S(2)}, u32[]{:S(2)}) collective-permute-start(bf16[4,384,1024]{2,1,0:T(8,128)(2,1)} %get-tuple-element.64.kb.k2.vb.v2), channel_id=1, source_target_pairs={{0,2},{2,4},{4,6},{6,8},{8,10},{10,12},{12,14},{14,16},{16,18},{18... | collective-permute-start | bytes 9437192 | tf_op jit(solution)/shard_map/ppermute | solution.py:526
  144.0 129.8 %collective-permute-start.35 = (bf16[4,384,1024]{2,1,0:T(8,128)(2,1)S(1)}, bf16[4,384,1024]{2,1,0:T(8,128)(2,1)S(1)}, u32[]{:S(2)}, u32[]{:S(2)}) collective-permute-start(bf16[4,384,1024]{2,1,0:T(8,128)(2,1)S(1)} %get-tuple-element.65.refs_5_.refs_6_.refs_7_.refs_8_), channel_id=1, source_target_pairs={{0,2},{2,4},{4,6},{6,8},{8,10},{10,12},{12,14},{14,16},{16,18},{18... | collective-permute-start | bytes 9437192 | tf_op jit(solution)/shard_map/ppermute | solution.py:525
  144.0 2.8 collective-permute-start.33
  146.8 127.0 %copy-start.32 = (f32[2,8,384]{2,1,0:T(8,128)}, f32[2,8,384]{2,1,0:T(8,128)S(1)}, u32[]{:S(2)}) copy-start(f32[2,8,384]{2,1,0:T(8,128)S(1)} %collective-permute-done.33.refs_12_) | copy-start | bytes 73732
  146.8 159.8 %collective-permute-start.34 = (bf16[4,384,1024]{2,1,0:T(8,128)(2,1)}, bf16[4,384,1024]{2,1,0:T(8,128)(2,1)}, u32[]{:S(2)}, u32[]{:S(2)}) collective-permute-start(bf16[4,384,1024]{2,1,0:T(8,128)(2,1)} %get-tuple-element.64.kb.k2.vb.v2), channel_id=1, source_target_pairs={{30,32},{31,33},{94,96},{95,97}} | collective-permute-start | bytes 9437192 | tf_op jit(solution)/shard_map/ppermute | solution.py:540
  150.2 7.2 %collective-permute-start.36 = (bf16[2,3,16,512]{3,2,1,0:T(8,128)(2,1)S(1)}, bf16[2,3,16,512]{3,2,1,0:T(8,128)(2,1)S(1)}, u32[]{:S(2)}, u32[]{:S(2)}) collective-permute-start(bf16[2,3,16,512]{3,2,1,0:T(8,128)(2,1)S(1)} %get-tuple-element.90), channel_id=1, source_target_pairs={{0,24},{8,0},{16,8},{24,16},{1,25},{9,1},{17,9},{25,17},{2,26},{10... | collective-permute-start | bytes 294920 | tf_op jit(solution)/shard_map/ppermute | solution.py:24
  150.3 8.7 %collective-permute-start.42 = (bf16[2,3,16,512]{3,2,1,0:T(8,128)(2,1)S(1)}, bf16[2,3,16,512]{3,2,1,0:T(8,128)(2,1)S(1)}, u32[]{:S(2)}, u32[]{:S(2)}) collective-permute-start(bf16[2,3,16,512]{3,2,1,0:T(8,128)(2,1)S(1)} %get-tuple-element.89), channel_id=1, source_target_pairs={{0,6},{2,0},{4,2},{6,4},{1,7},{3,1},{5,3},{7,5},{8,14},{10,8},{12,... | collective-permute-start | bytes 294920 | tf_op jit(solution)/shard_map/ppermute | solution.py:24
  157.3 4.7 %collective-permute-start.37 = (bf16[2,3,16,512]{3,2,1,0:T(8,128)(2,1)S(1)}, bf16[2,3,16,512]{3,2,1,0:T(8,128)(2,1)S(1)}, u32[]{:S(2)}, u32[]{:S(2)}) collective-permute-start(bf16[2,3,16,512]{3,2,1,0:T(8,128)(2,1)S(1)} %collective-permute-done.36), channel_id=1, source_target_pairs={{0,24},{8,0},{16,8},{24,16},{1,25},{9,1},{17,9},{25,17},{2,26},{10... | collective-permute-start | bytes 294920 | tf_op jit(solution)/shard_map/ppermute | solution.py:24
  159.0 5.2 %collective-permute-start.43 = (bf16[2,3,16,512]{3,2,1,0:T(8,128)(2,1)S(1)}, bf16[2,3,16,512]{3,2,1,0:T(8,128)(2,1)S(1)}, u32[]{:S(2)}, u32[]{:S(2)}) collective-permute-start(bf16[2,3,16,512]{3,2,1,0:T(8,128)(2,1)S(1)} %collective-permute-done.42), channel_id=1, source_target_pairs={{0,6},{2,0},{4,2},{6,4},{1,7},{3,1},{5,3},{7,5},{8,14},{10,8},{12,... | collective-permute-start | bytes 294920 | tf_op jit(solution)/shard_map/ppermute | solution.py:24
  162.0 5.9 %collective-permute-start.38 = (bf16[2,3,16,512]{3,2,1,0:T(8,128)(2,1)S(1)}, bf16[2,3,16,512]{3,2,1,0:T(8,128)(2,1)S(1)}, u32[]{:S(2)}, u32[]{:S(2)}) collective-permute-start(bf16[2,3,16,512]{3,2,1,0:T(8,128)(2,1)S(1)} %collective-permute-done.37), channel_id=1, source_target_pairs={{0,24},{8,0},{16,8},{24,16},{1,25},{9,1},{17,9},{25,17},{2,26},{10... | collective-permute-start | bytes 294920 | tf_op jit(solution)/shard_map/ppermute | solution.py:24
  164.2 5.5 %collective-permute-start.44 = (bf16[2,3,16,512]{3,2,1,0:T(8,128)(2,1)S(1)}, bf16[2,3,16,512]{3,2,1,0:T(8,128)(2,1)S(1)}, u32[]{:S(2)}, u32[]{:S(2)}) collective-permute-start(bf16[2,3,16,512]{3,2,1,0:T(8,128)(2,1)S(1)} %collective-permute-done.43), channel_id=1, source_target_pairs={{0,6},{2,0},{4,2},{6,4},{1,7},{3,1},{5,3},{7,5},{8,14},{10,8},{12,... | collective-permute-start | bytes 294920 | tf_op jit(solution)/shard_map/ppermute | solution.py:24
  167.9 115.1 %copy-start.12 = (bf16[8,3,16,512]{3,2,1,0:T(8,128)(2,1)}, bf16[8,3,16,512]{3,2,1,0:T(8,128)(2,1)S(1)}, u32[]{:S(2)}) copy-start(bf16[8,3,16,512]{3,2,1,0:T(8,128)(2,1)S(1)} %pad_maximum_fusion.3.refs_0_) | copy-start | bytes 1179652
  168.0 7.1 %collective-permute-start.39 = (bf16[8,3,16,512]{3,2,1,0:T(8,128)(2,1)S(1)}, bf16[8,3,16,512]{3,2,1,0:T(8,128)(2,1)S(1)}, u32[]{:S(2)}, u32[]{:S(2)}) collective-permute-start(bf16[8,3,16,512]{3,2,1,0:T(8,128)(2,1)S(1)} %pad_maximum_fusion.3.refs_0_), channel_id=1, source_target_pairs={{0,6},{2,0},{4,2},{6,4},{1,7},{3,1},{5,3},{7,5},{8,14},{10,8},{12,... | collective-permute-start | bytes 1179656 | tf_op jit(solution)/shard_map/ppermute | solution.py:24
  169.7 113.3 %copy-start.13 = (bf16[8,3,16,512]{3,2,1,0:T(8,128)(2,1)}, bf16[8,3,16,512]{3,2,1,0:T(8,128)(2,1)S(1)}, u32[]{:S(2)}) copy-start(bf16[8,3,16,512]{3,2,1,0:T(8,128)(2,1)S(1)} %pad_maximum_fusion.4.refs_4_) | copy-start | bytes 1179652
  169.7 8.3 %collective-permute-start.45 = (bf16[8,3,16,512]{3,2,1,0:T(8,128)(2,1)S(1)}, bf16[8,3,16,512]{3,2,1,0:T(8,128)(2,1)S(1)}, u32[]{:S(2)}, u32[]{:S(2)}) collective-permute-start(bf16[8,3,16,512]{3,2,1,0:T(8,128)(2,1)S(1)} %pad_maximum_fusion.4.refs_4_), channel_id=1, source_target_pairs={{0,24},{8,0},{16,8},{24,16},{1,25},{9,1},{17,9},{25,17},{2,26},{10... | collective-permute-start | bytes 1179656 | tf_op jit(solution)/shard_map/ppermute | solution.py:24
  175.0 108.0 %copy-start.20 = (bf16[8,3,16,512]{3,2,1,0:T(8,128)(2,1)}, bf16[8,3,16,512]{3,2,1,0:T(8,128)(2,1)S(1)}, u32[]{:S(2)}) copy-start(bf16[8,3,16,512]{3,2,1,0:T(8,128)(2,1)S(1)} %collective-permute-done.39.refs_1_) | copy-start | bytes 1179652
  175.0 11.7 %collective-permute-start.40 = (bf16[8,3,16,512]{3,2,1,0:T(8,128)(2,1)S(1)}, bf16[8,3,16,512]{3,2,1,0:T(8,128)(2,1)}, u32[]{:S(2)}, u32[]{:S(2)}) collective-permute-start(bf16[8,3,16,512]{3,2,1,0:T(8,128)(2,1)S(1)} %collective-permute-done.39.refs_1_), channel_id=1, source_target_pairs={{0,6},{2,0},{4,2},{6,4},{1,7},{3,1},{5,3},{7,5},{8,14},{10,8},{12,... | collective-permute-start | bytes 1179656 | tf_op jit(solution)/shard_map/ppermute | solution.py:24
  178.1 105.0 %copy-start.21 = (bf16[8,3,16,512]{3,2,1,0:T(8,128)(2,1)}, bf16[8,3,16,512]{3,2,1,0:T(8,128)(2,1)S(1)}, u32[]{:S(2)}) copy-start(bf16[8,3,16,512]{3,2,1,0:T(8,128)(2,1)S(1)} %collective-permute-done.45.refs_5_) | copy-start | bytes 1179652
  178.1 12.5 %collective-permute-start.46 = (bf16[8,3,16,512]{3,2,1,0:T(8,128)(2,1)S(1)}, bf16[8,3,16,512]{3,2,1,0:T(8,128)(2,1)}, u32[]{:S(2)}, u32[]{:S(2)}) collective-permute-start(bf16[8,3,16,512]{3,2,1,0:T(8,128)(2,1)S(1)} %collective-permute-done.45.refs_5_), channel_id=1, source_target_pairs={{0,24},{8,0},{16,8},{24,16},{1,25},{9,1},{17,9},{25,17},{2,26},{10... | collective-permute-start | bytes 1179656 | tf_op jit(solution)/shard_map/ppermute | solution.py:24
  186.7 100.8 %collective-permute-start.41 = (bf16[8,3,16,512]{3,2,1,0:T(8,128)(2,1)}, bf16[8,3,16,512]{3,2,1,0:T(8,128)(2,1)}, u32[]{:S(2)}, u32[]{:S(2)}) collective-permute-start(bf16[8,3,16,512]{3,2,1,0:T(8,128)(2,1)} %collective-permute-done.40.refs_2_), channel_id=1, source_target_pairs={{0,6},{2,0},{4,2},{6,4},{1,7},{3,1},{5,3},{7,5},{8,14},{10,8},{12,... | collective-permute-start | bytes 1179656 | tf_op jit(solution)/shard_map/ppermute | solution.py:24
  190.6 96.9 %collective-permute-start.47 = (bf16[8,3,16,512]{3,2,1,0:T(8,128)(2,1)}, bf16[8,3,16,512]{3,2,1,0:T(8,128)(2,1)}, u32[]{:S(2)}, u32[]{:S(2)}) collective-permute-start(bf16[8,3,16,512]{3,2,1,0:T(8,128)(2,1)} %collective-permute-done.46.refs_6_), channel_id=1, source_target_pairs={{0,24},{8,0},{16,8},{24,16},{1,25},{9,1},{17,9},{25,17},{2,26},{10... | collective-permute-start | bytes 1179656 | tf_op jit(solution)/shard_map/ppermute | solution.py:24
  283.0 43.8 %collective-permute-start.51 = (bf16[384,1024]{1,0:T(8,128)(2,1)}, bf16[384,1024]{1,0:T(8,128)(2,1)S(1)}, u32[]{:S(2)}, u32[]{:S(2)}) collective-permute-start(bf16[384,1024]{1,0:T(8,128)(2,1)} %attend_finish.5), channel_id=1, source_target_pairs={{0,1},{1,0},{2,3},{3,2},{4,5},{5,4},{6,7},{7,6},{8,9},{9,8},{10,11... | collective-permute-start | bytes 2359304 | tf_op jit(solution)/shard_map/ppermute | solution.py:24
  295.9 10.6 %collective-permute-start.50 = (f32[2,8,384]{2,1,0:T(8,128)}, f32[2,8,384]{2,1,0:T(8,128)S(1)}, u32[]{:S(2)}, u32[]{:S(2)}) collective-permute-start(f32[2,8,384]{2,1,0:T(8,128)} %get-tuple-element.70.refs_8_), channel_id=1, source_target_pairs={{0,65},{65,0},{1,64},{64,1},{2,67},{67,2},{3,66},{66,3},{4,69},{69... | collective-permute-start | bytes 73736 | tf_op jit(solution)/shard_map/ppermute | solution.py:475
  296.3 10.2 %collective-permute-start.49 = (f32[2,8,384]{2,1,0:T(8,128)}, f32[2,8,384]{2,1,0:T(8,128)S(1)}, u32[]{:S(2)}, u32[]{:S(2)}) collective-permute-start(f32[2,8,384]{2,1,0:T(8,128)} %get-tuple-element.70.refs_8_), channel_id=1, source_target_pairs={{0,64},{64,0},{1,65},{65,1},{2,66},{66,2},{3,67},{67,3},{4,68},{68... | collective-permute-start | bytes 73736 | tf_op jit(solution)/shard_map/ppermute | solution.py:475
  297.4 9.1 %collective-permute-start.48 = (f32[2,8,384]{2,1,0:T(8,128)}, f32[2,8,384]{2,1,0:T(8,128)S(1)}, u32[]{:S(2)}, u32[]{:S(2)}) collective-permute-start(f32[2,8,384]{2,1,0:T(8,128)} %get-tuple-element.70.refs_8_), channel_id=1, source_target_pairs={{0,1},{1,0},{64,65},{65,64},{2,3},{3,2},{66,67},{67,66},{4,5},{5,4... | collective-permute-start | bytes 73736 | tf_op jit(solution)/shard_map/ppermute | solution.py:475
  315.8 20.0 %collective-permute-start.52 = (bf16[384,1024]{1,0:T(8,128)(2,1)}, bf16[384,1024]{1,0:T(8,128)(2,1)S(1)}, u32[]{:S(2)}, u32[]{:S(2)}) collective-permute-start(bf16[384,1024]{1,0:T(8,128)(2,1)} %attend_finish.7), channel_id=1, source_target_pairs={{0,1},{1,0},{2,3},{3,2},{4,5},{5,4},{6,7},{7,6},{8,9},{9,8},{10,11... | collective-permute-start | bytes 2359304 | tf_op jit(solution)/shard_map/ppermute | solution.py:24
  315.9 2.6 collective-permute-start.53
  (26 other events, 201.7 us)

commit v5 on v3

--- a/solution.py
+++ b/solution.py
@@ -33,8 +33,8 @@
 TN = ((0,), (0,))
 
 
-def cparams(**kw):
-    return pltpu.CompilerParams(vmem_limit_bytes=56 * 1024 * 1024, **kw)
+def cparams(mib):
+    return pltpu.CompilerParams(vmem_limit_bytes=mib * 1024 * 1024)
 
 
 def piece_rows(kind, part, idx, item, sign):
@@ -145,7 +145,7 @@
                 pltpu.SemaphoreType.DMA((2,)),
             ],
         ),
-        compiler_params=cparams(),
+        compiler_params=cparams(36),
     )(scal, *pieces, k, v, k_rec, v_rec, rates)
 
 
@@ -198,7 +198,7 @@
                 pltpu.SemaphoreType.DMA((2,)),
             ],
         ),
-        compiler_params=cparams(),
+        compiler_params=cparams(20),
     )(scal, *pieces, q, q_rec)
 
 
@@ -259,16 +259,96 @@
                 pl.BlockSpec((1, 1, TOK, 128), lambda h, b, s: (b, h, 0, 0)),
             ],
         ),
-        compiler_params=cparams(),
+        compiler_params=cparams(24),
     )(scal, q, q_rec, mine, mine, mine, mine)
 
 
-def finish_kernel(c, j, sources, count, s_ref, *refs):
+def tail_kernel(s_ref, *refs):
+    before, (qo, qr, acc_ref, stat_ref, out_ref, kv, sem) = refs[:3], refs[3:]
+    head, block = pl.program_id(0), pl.program_id(1)
+
+    @pl.when((head == 0) & (block == 0))
+    def _():
+        for i, array in enumerate(before):
+            @pl.when(chosen(s_ref) == i)
+            def _(array=array):
+                for h in range(2):
+                    pltpu.make_async_copy(
+                        array.at[:, :, pl.ds(h * DH, DH)], kv.at[h], sem.at[h]
+                    ).start()
+
+    for h in range(2):
+
+        @pl.when((head == h) & (block == 0))
+        def _(h=h):
+            pltpu.make_async_copy(kv.at[h], kv.at[h], sem.at[h]).wait()
+
+    q = jnp.where(s_ref[0] == block, qo[0], qr[0])
+    row = lax.broadcasted_iota(jnp.int32, (TOK, TOK), 0)
+    col = lax.broadcasted_iota(jnp.int32, (TOK, TOK), 1)
+    for b in range(2):
+
+        @pl.when(block == b)
+        def _(b=b):
+            blocks = [(kv[head, b], kv[head, 2 + b], col > row)]
+            if b == 0:
+                blocks.append((kv[head, 1], kv[head, 3], None))
+            acc, peak, total = partial_attention(q, blocks)
+            peak_own, total_own = stat_ref[0, 0, :, :1], stat_ref[0, 0, :, 64:65]
+            top = jnp.maximum(peak, peak_own)
+            scale = jnp.exp2((peak - top) * (SCALE * LOG2E))
+            scale_own = jnp.exp2((peak_own - top) * (SCALE * LOG2E))
+            inv = 1.0 / (total * scale + total_own * scale_own)
+            out_ref[0] = acc * (scale * inv) + acc_ref[0] * (scale_own * inv)
+
+
+def attend_tail(c, scal, q, q_rec, local, before):
+    return pl.pallas_call(
+        tail_kernel,
+        name="attend_tail",
+        out_shape=jax.ShapeDtypeStruct((2, TOK, 2 * DH), f32),
+        grid_spec=pltpu.PrefetchScalarGridSpec(
+            num_scalar_prefetch=1,
+            grid=(2, 2),
+            in_specs=[ANY] * 3
+            + [
+                pl.BlockSpec((1, TOK, DH), lambda h, b, s: (c, 0, s[0] * 2 + h)),
+                pl.BlockSpec((1, TOK, DH), lambda h, b, s: (c, 0, h)),
+                pl.BlockSpec((1, TOK, DH), lambda h, b, s: (b, 0, h)),
+                pl.BlockSpec((1, 1, TOK, 128), lambda h, b, s: (b, h, 0, 0)),
+            ],
+            out_specs=pl.BlockSpec((1, TOK, DH), lambda h, b, s: (b, 0, h)),
+            scratch_shapes=[pltpu.VMEM((2, 4, TOK, DH), bf16), pltpu.SemaphoreType.DMA((2,))],
+        ),
+        compiler_params=cparams(24),
+    )(scal, *before, q, q_rec, *local)
+
+
+def norm_kernel(j, count, s_ref, fast_ref, att_ref, gain_ref, *refs):
+    powers, out_ref = refs[:count], refs[-1]
+    block = s_ref[0] if j == 0 else 1 - s_ref[0]
+    total = sum((p[block] for p in powers[1:]), powers[0][block])
+    rs = lax.rsqrt(total * (1.0 / 4096.0) + NORM_EPS)
+    col = jnp.transpose(rs)[:, :1]
+    out_ref[...] = (fast_ref[j] * gain_ref[...] * col + att_ref[block]).astype(bf16)
+
+
+def norm_add(j, scal, fast, att, gain, powers):
+    whole = pl.BlockSpec(memory_space=pltpu.VMEM)
+    return pl.pallas_call(
+        functools.partial(norm_kernel, j, len(powers)),
+        name="norm_add",
+        out_shape=jax.ShapeDtypeStruct((TOK, 2 * DH), bf16),
+        in_specs=[pl.BlockSpec(memory_space=pltpu.SMEM)] + [whole] * (3 + len(powers)),
+        out_specs=whole,
+        compiler_params=cparams(20),
+    )(scal, fast, att, gain, *powers)
+
+
+def finish_kernel(j, count, s_ref, *refs):
     core, chip = s_ref[0], s_ref[5]
     block = core if j == 0 else 1 - core
-    q_ref, refs = refs[0], refs[1:]
-    before, refs = refs[: 4 * sources], refs[4 * sources :]
-    own, refs = (refs[:4], refs[4:]) if c == 0 else (refs[:2], refs[2:])
+    q_ref, before, own, refs = refs[0], refs[1:5], refs[5:9], refs[9:]
     fast_ref, gain_ref = refs[:2]
     powers = refs[2 : 2 + count]
     out_ref = refs[-1]
@@ -280,32 +360,6 @@
 
     def put(attended):
         out_ref[...] = (fast + attended).astype(bf16).reshape(out_ref.shape)
-
-    if c == 1:
-        acc_ref, stat_ref = own
-
-        def here(i):
-            found = before[i][0]
-            for more in range(1, sources):
-                found = jnp.where(chosen(s_ref) == more, before[4 * more + i][0], found)
-            return found
-
-        for b in range(2):
-
-            @pl.when(block == b)
-            def _(b=b):
-                blocks = [(here(0), here(2), col > row)]
-                if b == 0:
-                    blocks.append((here(1), here(3), None))
-                acc, peak, total = partial_attention(q_ref[0], blocks)
-                peak_own, total_own = stat_ref[0, 0, :, :1], stat_ref[0, 0, :, 64:65]
-                top = jnp.maximum(peak, peak_own)
-                scale = jnp.exp2((peak - top) * (SCALE * LOG2E))
-                scale_own = jnp.exp2((peak_own - top) * (SCALE * LOG2E))
-                inv = 1.0 / (total * scale + total_own * scale_own)
-                put(acc * (scale * inv) + acc_ref[0] * (scale_own * inv))
-
-        return
 
     kb, k2, vb, v2 = own
     k0, ka, v0, va = before
@@ -380,14 +434,14 @@
         shape = (TOK, 2 * DH)
         out_spec = pl.BlockSpec((TOK, DH), lambda h, s: (0, h))
     return pl.pallas_call(
-        functools.partial(finish_kernel, c, j, sources, len(powers)),
+        functools.partial(finish_kernel, j, len(powers)),
         name="attend_finish",
         out_shape=jax.ShapeDtypeStruct(shape, bf16),
         grid_spec=pltpu.PrefetchScalarGridSpec(
             num_scalar_prefetch=1, grid=(2,), in_specs=specs, out_specs=out_spec
         ),
         input_output_aliases=aliases,
-        compiler_params=cparams(),
+        compiler_params=cparams(24),
     )(scal, *operands)
 
 
@@ -527,7 +581,12 @@
     layer_out = complete(0, pair[0], [halo0], fast0, powers0, None)
     fast1, pow1 = fast_apply(1, scal, pieces2, queries, q_rec)
     powers1 = with_parts(pow1, (CORES, HALVES, ACROSS))
-    layer_out = complete(1, local1, [halo1, turned1, halo0], fast1, powers1, layer_out)
+    att1 = attend_tail(1, scal, queries, q_rec, local1, [halo1, turned1, halo0])
+    out_rec = norm_add(1, scal, fast1, att1, gain, powers1)
+    arrived = shift(out_rec, "core", 1)
+    out_own = norm_add(0, scal, fast1, att1, gain, powers1)
+    layer_out = lax.dynamic_update_slice(layer_out, out_own[None], (1, 0, core * 1024))
+    layer_out = lax.dynamic_update_slice(layer_out, arrived[None], (1, 0, (1 - core) * 1024))
     return layer_out, new_all[:, 0], new_all[:, 1], new_all[:, 2]
 
 

time: 339 us -> 380 us (1.12)
  starting transfers between devices: 105 us -> 228 us
  waiting for transfers between devices: 129 us -> 62.7 us
  Pallas kernels: 71.2 us -> 53.8 us
  local copies, waits for them, and re-layouts: 20.8 us -> 26.1 us
    ppermute x46, starting transfers between devices: 91.5 us -> 213 us  [shift(): lax.ppermute(value, axis, [(i, (i + steps) % count) for i in range(count)])]
    ppermute x1, waiting for transfers between devices: 79.1 us -> 0.01 us  [on_device(): halo0 = lax.ppermute(pair[0], chips, row)]
    ppermute x46, waiting for transfers between devices: 46.3 us -> 59.6 us  [shift(): lax.ppermute(value, axis, [(i, (i + steps) % count) for i in range(count)])]
    pallas_call x4 -> x5, Pallas kernels: 32.8 us -> 21.5 us  [the longest x2 11.8 us: finish(): pl.pallas_call(functools.partial(finish_kernel, j, len(powers)), name='at...]
    unnamed x72 -> x66, local copies, waits for them, and re-layouts: 4.23 us -> 7.9 us
  transfers between devices with their start and end apart: 54 -> 54, of which waited for: 23 -> 23; matrix products, arithmetic and copies ran while one was open for 7% -> 6% of each run, Pallas kernels for 17% -> 11%
where the time goes in v5:
time: 380 us
  starting transfers between devices  228 us (60%)
  waiting for transfers between devices  62.7 us (16%)
  Pallas kernels  53.8 us (14%)
  local copies, waits for them, and re-layouts  26.1 us (7%)
  other arithmetic  7.34 us (2%)
    ppermute x46, starting transfers between devices, shift(): lax.ppermute(value, axis, [(i, (i + steps) % count) for i in range(count)])  213 us
    ppermute x46, waiting for transfers between devices, shift(): lax.ppermute(value, axis, [(i, (i + steps) % count) for i in range(count)])  59.6 us
    pallas_call x2, Pallas kernels, fast_apply(): pl.pallas_call(apply_kernel, name='fast_apply', out_shape=[jax.ShapeDtype...  13.6 us
    pallas_call x2, Pallas kernels, finish(): pl.pallas_call(functools.partial(finish_kernel, j, len(powers)), name='at...  11.8 us
    pallas_call x1, Pallas kernels, compute_grads(): pl.pallas_call(grads_kernel, name='fast_grads', out_shape=[jax.ShapeDtype...  11.7 us
    ppermute x5, starting transfers between devices, with_parts(): return [power] + [lax.ppermute(power, ('heads', 'core'), p) for p in pairs]  8.14 us
    unnamed x66, local copies, waits for them, and re-layouts  7.9 us
    pallas_call x1, Pallas kernels, attend_tail(): pl.pallas_call(tail_kernel, name='attend_tail', out_shape=jax.ShapeDtypeS...  7.87 us
  transfers between devices with their start and end apart: 54, of which 23 were waited for; matrix products, arithmetic and copies ran while one was open for 6% of the time, Pallas kernels for 11%

profile of v5, /device:TPU:1, one launch (start us, length us, event | category | flops | bytes accessed | tf_op | source)
XLA Modules:
  0.0 379.6 jit_solution(12509054362175899157)
XLA Ops:
  1.6 1.5 collective-permute-start
  4.0 3.1 collective-permute-start.1
  7.1 4.7 %collective-permute-done.1 = f32[2,3,16,512]{3,2,1,0:T(8,128)S(1)} collective-permute-done((f32[2,3,16,512]{3,2,1,0:T(8,128)S(1)}, f32[2,3,16,512]{3,2,1,0:T(8,128)S(1)}, u32[]{:S(2)}, u32[]{:S(2)}) %collective-permute-start.1) | collective-permute-done | bytes 196640 | tf_op jit(solution)/shard_map/ppermute | solution.py:24
  11.8 2.7 constant_dynamic-slice_fusion.5
  15.7 1.3 constant_dynamic-slice_fusion.7
  17.2 1.8 collective-permute-start.6
  18.9 3.3 collective-permute-start.5
  23.4 2.7 constant_dynamic-slice_fusion.8
  26.1 1.3 constant_dynamic-slice_fusion.6
  30.6 2.5 collective-permute-start.11
  35.6 2.1 collective-permute-done.11
  40.5 1.6 fusion.15
  42.1 1.7 collective-permute-start.14
  43.8 1.5 fusion.14
  45.3 2.1 collective-permute-done.9.refs_3_
  47.4 1.5 collective-permute-start.13
  49.0 3.4 maximum_select_fusion
  53.2 2.4 collective-permute-done.7.refs_1_
  55.5 2.0 collective-permute-done.14.refs_6_
  58.5 11.7 %fast_grads.1 = (bf16[8,3,16,512]{3,2,1,0:T(8,128)(2,1)S(1)}, bf16[8,3,16,512]{3,2,1,0:T(8,128)(2,1)S(1)}, bf16[8,3,16,512]{3,2,1,0:T(8,128)(2,1)S(1)}, bf16[8,3...) custom-call(s32[6]{0:T(128)S(1)} %stack.78.s_ref, ...), custom_call_target="tpu_custom_call" | custom-call | tf_op jit(solution)/shard_map/fast_grads/pallas_call | solution.py:130
  70.1 2.5 collective-permute-start.19
  72.8 4.0 %collective-permute-start.17 = (bf16[2,384,1024]{2,1,0:T(8,128)(2,1)S(1)}, bf16[2,384,1024]{2,1,0:T(8,128)(2,1)S(1)}, u32[]{:S(2)}, u32[]{:S(2)}) collective-permute-start(bf16[2,384,1024]{2,1,0:T(8,128)(2,1)S(1)} %constant_dynamic-slice_fusion.4), channel_id=1, source_target_pairs={{0,1},{1,0},{2,3},{3,2},{4,5},{5,4},{6,7},{7,6},{8,9},{9,8},{10,11... | collective-permute-start | bytes 4718600 | tf_op jit(solution)/shard_map/ppermute | solution.py:24
  76.8 2.7 collective-permute-start.25
  79.6 2.8 collective-permute-start.20
  82.4 5.4 %collective-permute-done.25 = bf16[8,3,16,512]{3,2,1,0:T(8,128)(2,1)S(1)} collective-permute-done((bf16[8,3,16,512]{3,2,1,0:T(8,128)(2,1)S(1)}, bf16[8,3,16,512]{3,2,1,0:T(8,128)(2,1)S(1)}, u32[]{:S(2)}, u32[]{:S(2)}) %collective-permute-start.25) | collective-permute-done | bytes 393248 | tf_op jit(solution)/shard_map/ppermute | solution.py:24
  88.0 3.5 collective-permute-start.26
  92.1 6.9 %collective-permute-done.26 = bf16[8,3,16,512]{3,2,1,0:T(8,128)(2,1)S(1)} collective-permute-done((bf16[8,3,16,512]{3,2,1,0:T(8,128)(2,1)S(1)}, bf16[8,3,16,512]{3,2,1,0:T(8,128)(2,1)S(1)}, u32[]{:S(2)}, u32[]{:S(2)}) %collective-permute-start.26) | collective-permute-done | bytes 393248 | tf_op jit(solution)/shard_map/ppermute | solution.py:24
  99.1 3.5 collective-permute-start.27
  102.6 6.8 %fast_apply.2 = (f32[2,384,1024]{2,1,0:T(8,128)S(1)}, f32[2,8,384]{2,1,0:T(8,128)S(1)}) custom-call(s32[6]{0:T(128)S(1)} %stack.78.s_ref, bf16[8,3,16,512]{3,2,1,0:T(8,128)(2,1)S(1)} %pad_maximum_fusion.1.refs_0_, bf16[8,3,16,512]{3,2,1,0:T(8,128)(2,1)S(1)} %collective-permute-done.7.refs_1_, bf16[8,3,16,512]{3,2,1,0:T(8,128)(2,1)S(1)} %collective-permute-done.8.refs_2_, ...), custom_call_target="tpu_custom_call" | custom-call | tf_op jit(solution)/shard_map/fast_apply/pallas_call | solution.py:181
  109.4 2.2 collective-permute-start.31
  113.2 3.5 collective-permute-done.22
  116.7 1.5 collective-permute-start.23
  118.6 1.6 collective-permute-done.23
  120.3 2.7 collective-permute-start.24
  123.4 1.3 collective-permute-done.24
  124.7 2.2 collective-permute-done.30
  127.0 3.0 collective-permute-start.32
  130.0 1.7 collective-permute-start.16
  131.6 3.6 collective-permute-start.47
  135.6 2.2 collective-permute-done.33.refs_12_
  137.9 2.4 collective-permute-start.48
  141.1 134.4 %collective-permute-start.35 = (bf16[2,3,16,512]{3,2,1,0:T(8,128)(2,1)S(1)}, bf16[2,3,16,512]{3,2,1,0:T(8,128)(2,1)S(1)}, u32[]{:S(2)}, u32[]{:S(2)}) collective-permute-start(bf16[2,3,16,512]{3,2,1,0:T(8,128)(2,1)S(1)} %get-tuple-element.90), channel_id=1, source_target_pairs={{0,24},{8,0},{16,8},{24,16},{1,25},{9,1},{17,9},{25,17},{2,26},{10... | collective-permute-start | bytes 294920 | tf_op jit(solution)/shard_map/ppermute | solution.py:24
  275.5 1.6 collective-permute-done.35
  277.2 3.0 collective-permute-start.36
  280.2 1.6 collective-permute-done.36
  281.9 3.0 collective-permute-start.37
  284.9 1.6 collective-permute-done.37
  286.7 1.7 collective-permute-done.43
  288.5 1.4 collective-permute-start.44
  290.6 3.9 %collective-permute-done.38.refs_1_ = bf16[8,3,16,512]{3,2,1,0:T(8,128)(2,1)S(1)} collective-permute-done((bf16[8,3,16,512]{3,2,1,0:T(8,128)(2,1)S(1)}, bf16[8,3,16,512]{3,2,1,0:T(8,128)(2,1)S(1)}, u32[]{:S(2)}, u32[]{:S(2)}) %collective-permute-start.38) | collective-permute-done | bytes 393248 | tf_op jit(solution)/shard_map/ppermute | solution.py:24
  296.3 2.6 collective-permute-start.45
  298.9 4.8 %collective-permute-done.39.refs_2_ = bf16[8,3,16,512]{3,2,1,0:T(8,128)(2,1)} collective-permute-done((bf16[8,3,16,512]{3,2,1,0:T(8,128)(2,1)S(1)}, bf16[8,3,16,512]{3,2,1,0:T(8,128)(2,1)}, u32[]{:S(2)}, u32[]{:S(2)}) %collective-permute-start.39) | collective-permute-done | bytes 393248 | tf_op jit(solution)/shard_map/ppermute | solution.py:24
  304.5 5.9 %attend_finish.3 = bf16[384,1024]{1,0:T(8,128)(2,1)} custom-call(s32[6]{0:T(128)S(1)} %stack.78.s_ref, bf16[2,384,1024]{2,1,0:T(8,128)(2,1)S(1)} %collective-permute-done.17.refs_9_.refs_0_.qr.refs_4_, bf16[4,384,1024]{2,1,0:T(8,128)(2,1)S(1)} %collective-permute-done.16.refs_1_.refs_2_.refs_3_.refs_4_, ...), custom_call_target="tpu_custom_call" | custom-call | tf_op jit(solution)/shard_map/attend_finish/pallas_call | solution.py:436
  310.4 8.8 %collective-permute-start.34 = (bf16[384,1024]{1,0:T(8,128)(2,1)}, bf16[384,1024]{1,0:T(8,128)(2,1)}, u32[]{:S(2)}, u32[]{:S(2)}) collective-permute-start(bf16[384,1024]{1,0:T(8,128)(2,1)} %attend_finish.3), channel_id=1, source_target_pairs={{0,1},{1,0},{2,3},{3,2},{4,5},{5,4},{6,7},{7,6},{8,9},{9,8},{10,11... | collective-permute-start | bytes 2359304 | tf_op jit(solution)/shard_map/ppermute | solution.py:24
  319.2 5.1 %collective-permute-start.46 = (bf16[8,3,16,512]{3,2,1,0:T(8,128)(2,1)}, bf16[8,3,16,512]{3,2,1,0:T(8,128)(2,1)}, u32[]{:S(2)}, u32[]{:S(2)}) collective-permute-start(bf16[8,3,16,512]{3,2,1,0:T(8,128)(2,1)} %collective-permute-done.45.refs_6_), channel_id=1, source_target_pairs={{0,24},{8,0},{16,8},{24,16},{1,25},{9,1},{17,9},{25,17},{2,26},{10... | collective-permute-start | bytes 1179656 | tf_op jit(solution)/shard_map/ppermute | solution.py:24
  325.7 7.3 %collective-permute-done.46.refs_7_ = bf16[8,3,16,512]{3,2,1,0:T(8,128)(2,1)} collective-permute-done((bf16[8,3,16,512]{3,2,1,0:T(8,128)(2,1)}, bf16[8,3,16,512]{3,2,1,0:T(8,128)(2,1)}, u32[]{:S(2)}, u32[]{:S(2)}) %collective-permute-start.46) | collective-permute-done | bytes 393248 | tf_op jit(solution)/shard_map/ppermute | solution.py:24
  333.0 1.9 copy-done.3
  334.9 1.4 copy-done.6
  339.3 6.8 %fast_apply.3 = (f32[2,384,1024]{2,1,0:T(8,128)S(1)}, f32[2,8,384]{2,1,0:T(8,128)S(1)}) custom-call(s32[6]{0:T(128)S(1)} %stack.78.s_ref, bf16[8,3,16,512]{3,2,1,0:T(8,128)(2,1)S(1)} %pad_maximum_fusion.3.refs_0_, bf16[8,3,16,512]{3,2,1,0:T(8,128)(2,1)S(1)} %copy-done.18, bf16[8,3,16,512]{3,2,1,0:T(8,128)(2,1)} %collective-permute-done.39.refs_2_, ...), custom_call_target="tpu_custom_call" | custom-call | tf_op jit(solution)/shard_map/fast_apply/pallas_call | solution.py:181
  346.1 5.1 %collective-permute-start.51 = (f32[2,8,384]{2,1,0:T(8,128)S(1)}, f32[2,8,384]{2,1,0:T(8,128)S(1)}, u32[]{:S(2)}, u32[]{:S(2)}) collective-permute-start(f32[2,8,384]{2,1,0:T(8,128)S(1)} %get-tuple-element.73.refs_0_), channel_id=1, source_target_pairs={{0,65},{65,0},{1,64},{64,1},{2,67},{67,2},{3,66},{66,3},{4,69},{69... | collective-permute-start | bytes 73736 | tf_op jit(solution)/shard_map/ppermute | solution.py:497
  351.7 7.1 %attend_local.1 = (f32[2,384,1024]{2,1,0:T(8,128)S(1)}, f32[2,2,384,128]{3,2,1,0:T(8,128)S(1)}) custom-call(s32[6]{0:T(128)S(1)} %stack.78.s_ref, bf16[2,384,2048]{2,1,0:T(8,128)(2,1)S(1)} %copy-done.4, bf16[2,384,1024]{2,1,0:T(8,128)(2,1)S(1)} %copy-done.7, bf16[4,384,1024]{2,1,0:T(8,128)(2,1)} %get-tuple-element.70.kb.k2.vb.v2, ...), custom_call_target="tpu_custom_call" | custom-call | tf_op jit(solution)/shard_map/attend_local/pallas_call | solution.py:242
  358.7 7.9 %attend_tail.1.att_ref = f32[2,384,1024]{2,1,0:T(8,128)S(1)} custom-call(s32[6]{0:T(128)S(1)} %stack.78.s_ref, bf16[4,384,1024]{2,1,0:T(8,128)(2,1)} %collective-permute-done.47.refs_0_, bf16[4,384,1024]{2,1,0:T(8,128)(2,1)} %collective-permute-done.48.refs_1_, bf16[4,384,1024]{2,1,0:T(8,128)(2,1)S(1)} %copy-done.1, bf16[2,384,2048]{2,1,0:T(8,128)(2,1)S(1)} %copy-done.4, ...), custom_call_target="tpu_custom_call" | custom-call | tf_op jit(solution)/shard_map/attend_tail/pallas_call | solution.py:306
  368.8 5.9 %attend_finish.2 = bf16[2,384,2048]{2,1,0:T(8,128)(2,1)} custom-call(s32[6]{0:T(128)S(1)} %stack.78.s_ref, bf16[2,384,2048]{2,1,0:T(8,128)(2,1)S(1)} %copy-done.4, bf16[4,384,1024]{2,1,0:T(8,128)(2,1)S(1)} %copy-done.1, bf16[4,384,1024]{2,1,0:T(8,128)(2,1)S(1)} %copy-done.1, bf16[4,384,1024]{2,1,0:T(8,128)(2,1)S(1)} %copy-done.1, ...), custom_call_target="tpu_custom_call" | custom-call | tf_op jit(solution)/shard_map/attend_finish/pallas_call | solution.py:436
  374.7 2.1 bitcast_dynamic-update-slice_fusion.2
  (170 shorter events, 32.6 us)
Async XLA Ops:
  1.6 2.4 collective-permute-start
  4.0 7.8 %collective-permute-start.1 = (f32[2,3,16,512]{3,2,1,0:T(8,128)S(1)}, f32[2,3,16,512]{3,2,1,0:T(8,128)S(1)}, u32[]{:S(2)}, u32[]{:S(2)}) collective-permute-start(f32[2,3,16,512]{3,2,1,0:T(8,128)S(1)} %maximum_select_fusion.2), channel_id=1, source_target_pairs={{0,32},{32,0},{1,33},{33,1},{2,34},{34,2},{3,35},{35,3},{4,36},{36... | collective-permute-start | bytes 589832 | tf_op jit(solution)/shard_map/ppermute | solution.py:24
  7.1 15.1 %copy-start.31 = (f32[4,2,384]{2,1,0:T(2,128)S(1)}, f32[4,2,384]{2,1,0:T(2,128)}, u32[]{:S(2)}) copy-start(f32[4,2,384]{2,1,0:T(2,128)} %param.11) | copy-start | bytes 36868
  14.5 25.1 %collective-permute-start.3 = (bf16[2,384,1024]{2,1,0:T(8,128)(2,1)}, bf16[2,384,1024]{2,1,0:T(8,128)(2,1)}, u32[]{:S(2)}, u32[]{:S(2)}) collective-permute-start(bf16[2,384,1024]{2,1,0:T(8,128)(2,1)} %constant_dynamic-slice_fusion.5), channel_id=1, source_target_pairs={{0,1},{1,0},{2,3},{3,2},{4,5},{5,4},{6,7},{7,6},{8,9},{9,8},{10,11... | collective-permute-start | bytes 4718600 | tf_op jit(solution)/shard_map/ppermute | solution.py:24
  17.0 25.1 %collective-permute-start.2 = (bf16[2,384,1024]{2,1,0:T(8,128)(2,1)}, bf16[2,384,1024]{2,1,0:T(8,128)(2,1)}, u32[]{:S(2)}, u32[]{:S(2)}) collective-permute-start(bf16[2,384,1024]{2,1,0:T(8,128)(2,1)} %constant_dynamic-slice_fusion.7), channel_id=1, source_target_pairs={{0,1},{1,0},{2,3},{3,2},{4,5},{5,4},{6,7},{7,6},{8,9},{9,8},{10,11... | collective-permute-start | bytes 4718600 | tf_op jit(solution)/shard_map/ppermute | solution.py:24
  17.2 12.2 %collective-permute-start.6 = (bf16[2,3,16,512]{3,2,1,0:T(8,128)(2,1)S(1)}, bf16[2,3,16,512]{3,2,1,0:T(8,128)(2,1)}, u32[]{:S(2)}, u32[]{:S(2)}) collective-permute-start(bf16[2,3,16,512]{3,2,1,0:T(8,128)(2,1)S(1)} %get-tuple-element.92), channel_id=1, source_target_pairs={{0,8},{8,16},{16,24},{24,0},{1,9},{9,17},{17,25},{25,1},{2,10},{10... | collective-permute-start | bytes 294920 | tf_op jit(solution)/shard_map/ppermute | solution.py:24
  18.9 11.6 %collective-permute-start.5 = (bf16[2,3,16,512]{3,2,1,0:T(8,128)(2,1)S(1)}, bf16[2,3,16,512]{3,2,1,0:T(8,128)(2,1)}, u32[]{:S(2)}, u32[]{:S(2)}) collective-permute-start(bf16[2,3,16,512]{3,2,1,0:T(8,128)(2,1)S(1)} %get-tuple-element.92), channel_id=1, source_target_pairs={{0,16},{8,24},{16,0},{24,8},{1,17},{9,25},{17,1},{25,9},{2,18},{10... | collective-permute-start | bytes 294920 | tf_op jit(solution)/shard_map/ppermute | solution.py:24
  22.3 5.2 %collective-permute-start.18 = (f32[2,384]{1,0:T(2,128)S(1)}, f32[2,384]{1,0:T(2,128)S(1)}, u32[]{:S(2)}, u32[]{:S(2)}) collective-permute-start(f32[2,384]{1,0:T(2,128)S(1)} %get-tuple-element.96), channel_id=1, source_target_pairs={{0,1},{1,0},{2,3},{3,2},{4,5},{5,4},{6,7},{7,6},{8,9},{9,8},{10,11... | collective-permute-start | bytes 9224 | tf_op jit(solution)/shard_map/ppermute | solution.py:24
  27.4 5.6 %collective-permute-start.4 = (bf16[2,3,16,512]{3,2,1,0:T(8,128)(2,1)S(1)}, bf16[2,3,16,512]{3,2,1,0:T(8,128)(2,1)S(1)}, u32[]{:S(2)}, u32[]{:S(2)}) collective-permute-start(bf16[2,3,16,512]{3,2,1,0:T(8,128)(2,1)S(1)} %get-tuple-element.92), channel_id=1, source_target_pairs={{0,24},{8,0},{16,8},{24,16},{1,25},{9,1},{17,9},{25,17},{2,26},{10... | collective-permute-start | bytes 294920 | tf_op jit(solution)/shard_map/ppermute | solution.py:24
  29.4 5.9 %collective-permute-start.12 = (bf16[2,3,16,512]{3,2,1,0:T(8,128)(2,1)S(1)}, bf16[2,3,16,512]{3,2,1,0:T(8,128)(2,1)S(1)}, u32[]{:S(2)}, u32[]{:S(2)}) collective-permute-start(bf16[2,3,16,512]{3,2,1,0:T(8,128)(2,1)S(1)} %get-tuple-element.91), channel_id=1, source_target_pairs={{0,2},{2,4},{4,6},{6,0},{1,3},{3,5},{5,7},{7,1},{8,10},{10,12},{12... | collective-permute-start | bytes 294920 | tf_op jit(solution)/shard_map/ppermute | solution.py:24
  30.6 7.1 %collective-permute-start.11 = (bf16[2,3,16,512]{3,2,1,0:T(8,128)(2,1)S(1)}, bf16[2,3,16,512]{3,2,1,0:T(8,128)(2,1)S(1)}, u32[]{:S(2)}, u32[]{:S(2)}) collective-permute-start(bf16[2,3,16,512]{3,2,1,0:T(8,128)(2,1)S(1)} %get-tuple-element.91), channel_id=1, source_target_pairs={{0,4},{2,6},{4,0},{6,2},{1,5},{3,7},{5,1},{7,3},{8,12},{10,14},{12... | collective-permute-start | bytes 294920 | tf_op jit(solution)/shard_map/ppermute | solution.py:24
  33.0 5.3 %collective-permute-start.10 = (bf16[2,3,16,512]{3,2,1,0:T(8,128)(2,1)S(1)}, bf16[2,3,16,512]{3,2,1,0:T(8,128)(2,1)S(1)}, u32[]{:S(2)}, u32[]{:S(2)}) collective-permute-start(bf16[2,3,16,512]{3,2,1,0:T(8,128)(2,1)S(1)} %get-tuple-element.91), channel_id=1, source_target_pairs={{0,6},{2,0},{4,2},{6,4},{1,7},{3,1},{5,3},{7,5},{8,14},{10,8},{12,... | collective-permute-start | bytes 294920 | tf_op jit(solution)/shard_map/ppermute | solution.py:24
  35.2 12.1 %collective-permute-start.9 = (bf16[8,3,16,512]{3,2,1,0:T(8,128)(2,1)S(1)}, bf16[8,3,16,512]{3,2,1,0:T(8,128)(2,1)S(1)}, u32[]{:S(2)}, u32[]{:S(2)}) collective-permute-start(bf16[8,3,16,512]{3,2,1,0:T(8,128)(2,1)S(1)} %pad_maximum_fusion.1.refs_0_), channel_id=1, source_target_pairs={{0,2},{2,4},{4,6},{6,0},{1,3},{3,5},{5,7},{7,1},{8,10},{10,12},{12... | collective-permute-start | bytes 1179656 | tf_op jit(solution)/shard_map/ppermute | solution.py:24
  37.7 15.4 %collective-permute-start.8 = (bf16[8,3,16,512]{3,2,1,0:T(8,128)(2,1)S(1)}, bf16[8,3,16,512]{3,2,1,0:T(8,128)(2,1)S(1)}, u32[]{:S(2)}, u32[]{:S(2)}) collective-permute-start(bf16[8,3,16,512]{3,2,1,0:T(8,128)(2,1)S(1)} %pad_maximum_fusion.1.refs_0_), channel_id=1, source_target_pairs={{0,4},{2,6},{4,0},{6,2},{1,5},{3,7},{5,1},{7,3},{8,12},{10,14},{12... | collective-permute-start | bytes 1179656 | tf_op jit(solution)/shard_map/ppermute | solution.py:24
  38.3 17.2 %collective-permute-start.7 = (bf16[8,3,16,512]{3,2,1,0:T(8,128)(2,1)S(1)}, bf16[8,3,16,512]{3,2,1,0:T(8,128)(2,1)S(1)}, u32[]{:S(2)}, u32[]{:S(2)}) collective-permute-start(bf16[8,3,16,512]{3,2,1,0:T(8,128)(2,1)S(1)} %pad_maximum_fusion.1.refs_0_), channel_id=1, source_target_pairs={{0,6},{2,0},{4,2},{6,4},{1,7},{3,1},{5,3},{7,5},{8,14},{10,8},{12,... | collective-permute-start | bytes 1179656 | tf_op jit(solution)/shard_map/ppermute | solution.py:24
  39.6 15.9 %collective-permute-start.15 = (bf16[8,3,16,512]{3,2,1,0:T(8,128)(2,1)S(1)}, bf16[8,3,16,512]{3,2,1,0:T(8,128)(2,1)S(1)}, u32[]{:S(2)}, u32[]{:S(2)}) collective-permute-start(bf16[8,3,16,512]{3,2,1,0:T(8,128)(2,1)S(1)} %pad_maximum_fusion.2.refs_4_), channel_id=1, source_target_pairs={{0,8},{8,16},{16,24},{24,0},{1,9},{9,17},{17,25},{25,1},{2,10},{10... | collective-permute-start | bytes 1179656 | tf_op jit(solution)/shard_map/ppermute | solution.py:24
  42.1 15.5 %collective-permute-start.14 = (bf16[8,3,16,512]{3,2,1,0:T(8,128)(2,1)S(1)}, bf16[8,3,16,512]{3,2,1,0:T(8,128)(2,1)S(1)}, u32[]{:S(2)}, u32[]{:S(2)}) collective-permute-start(bf16[8,3,16,512]{3,2,1,0:T(8,128)(2,1)S(1)} %pad_maximum_fusion.2.refs_4_), channel_id=1, source_target_pairs={{0,16},{8,24},{16,0},{24,8},{1,17},{9,25},{17,1},{25,9},{2,18},{10... | collective-permute-start | bytes 1179656 | tf_op jit(solution)/shard_map/ppermute | solution.py:24
  47.4 11.1 %collective-permute-start.13 = (bf16[8,3,16,512]{3,2,1,0:T(8,128)(2,1)S(1)}, bf16[8,3,16,512]{3,2,1,0:T(8,128)(2,1)S(1)}, u32[]{:S(2)}, u32[]{:S(2)}) collective-permute-start(bf16[8,3,16,512]{3,2,1,0:T(8,128)(2,1)S(1)} %pad_maximum_fusion.2.refs_4_), channel_id=1, source_target_pairs={{0,24},{8,0},{16,8},{24,16},{1,25},{9,1},{17,9},{25,17},{2,26},{10... | collective-permute-start | bytes 1179656 | tf_op jit(solution)/shard_map/ppermute | solution.py:24
  58.5 14.2 %copy-start.2 = (bf16[2,384,2048]{2,1,0:T(8,128)(2,1)S(1)}, bf16[2,384,2048]{2,1,0:T(8,128)(2,1)}, u32[]{:S(2)}) copy-start(bf16[2,384,2048]{2,1,0:T(8,128)(2,1)} %refs_3_) | copy-start | bytes 9437188
  70.1 9.3 %collective-permute-start.19 = (bf16[8,3,16,512]{3,2,1,0:T(8,128)(2,1)S(1)}, bf16[8,3,16,512]{3,2,1,0:T(8,128)(2,1)S(1)}, u32[]{:S(2)}, u32[]{:S(2)}) collective-permute-start(bf16[8,3,16,512]{3,2,1,0:T(8,128)(2,1)S(1)} %get-tuple-element.54), channel_id=1, source_target_pairs={{0,6},{2,0},{4,2},{6,4},{1,7},{3,1},{5,3},{7,5},{8,14},{10,8},{12,... | collective-permute-start | bytes 1179656 | tf_op jit(solution)/shard_map/ppermute | solution.py:24
  72.8 29.8 %collective-permute-start.17 = (bf16[2,384,1024]{2,1,0:T(8,128)(2,1)S(1)}, bf16[2,384,1024]{2,1,0:T(8,128)(2,1)S(1)}, u32[]{:S(2)}, u32[]{:S(2)}) collective-permute-start(bf16[2,384,1024]{2,1,0:T(8,128)(2,1)S(1)} %constant_dynamic-slice_fusion.4), channel_id=1, source_target_pairs={{0,1},{1,0},{2,3},{3,2},{4,5},{5,4},{6,7},{7,6},{8,9},{9,8},{10,11... | collective-permute-start | bytes 4718600 | tf_op jit(solution)/shard_map/ppermute | solution.py:24
  76.8 11.0 %collective-permute-start.25 = (bf16[8,3,16,512]{3,2,1,0:T(8,128)(2,1)S(1)}, bf16[8,3,16,512]{3,2,1,0:T(8,128)(2,1)S(1)}, u32[]{:S(2)}, u32[]{:S(2)}) collective-permute-start(bf16[8,3,16,512]{3,2,1,0:T(8,128)(2,1)S(1)} %get-tuple-element.58), channel_id=1, source_target_pairs={{0,24},{8,0},{16,8},{24,16},{1,25},{9,1},{17,9},{25,17},{2,26},{10... | collective-permute-start | bytes 1179656 | tf_op jit(solution)/shard_map/ppermute | solution.py:24
  79.6 11.9 %collective-permute-start.20 = (bf16[8,3,16,512]{3,2,1,0:T(8,128)(2,1)S(1)}, bf16[8,3,16,512]{3,2,1,0:T(8,128)(2,1)S(1)}, u32[]{:S(2)}, u32[]{:S(2)}) collective-permute-start(bf16[8,3,16,512]{3,2,1,0:T(8,128)(2,1)S(1)} %add_convert_fusion.3), channel_id=1, source_target_pairs={{0,6},{2,0},{4,2},{6,4},{1,7},{3,1},{5,3},{7,5},{8,14},{10,8},{12,... | collective-permute-start | bytes 1179656 | tf_op jit(solution)/shard_map/ppermute | solution.py:24
  88.0 11.0 %collective-permute-start.26 = (bf16[8,3,16,512]{3,2,1,0:T(8,128)(2,1)S(1)}, bf16[8,3,16,512]{3,2,1,0:T(8,128)(2,1)S(1)}, u32[]{:S(2)}, u32[]{:S(2)}) collective-permute-start(bf16[8,3,16,512]{3,2,1,0:T(8,128)(2,1)S(1)} %add_convert_fusion.1), channel_id=1, source_target_pairs={{0,24},{8,0},{16,8},{24,16},{1,25},{9,1},{17,9},{25,17},{2,26},{10... | collective-permute-start | bytes 1179656 | tf_op jit(solution)/shard_map/ppermute | solution.py:24
  91.6 20.9 %collective-permute-start.21 = (bf16[8,3,16,512]{3,2,1,0:T(8,128)(2,1)S(1)}, bf16[8,3,16,512]{3,2,1,0:T(8,128)(2,1)S(1)}, u32[]{:S(2)}, u32[]{:S(2)}) collective-permute-start(bf16[8,3,16,512]{3,2,1,0:T(8,128)(2,1)S(1)} %add_convert_fusion.2), channel_id=1, source_target_pairs={{0,6},{2,0},{4,2},{6,4},{1,7},{3,1},{5,3},{7,5},{8,14},{10,8},{12,... | collective-permute-start | bytes 1179656 | tf_op jit(solution)/shard_map/ppermute | solution.py:24
  99.1 13.6 %collective-permute-start.27 = (bf16[8,3,16,512]{3,2,1,0:T(8,128)(2,1)S(1)}, bf16[8,3,16,512]{3,2,1,0:T(8,128)(2,1)S(1)}, u32[]{:S(2)}, u32[]{:S(2)}) collective-permute-start(bf16[8,3,16,512]{3,2,1,0:T(8,128)(2,1)S(1)} %add_convert_fusion), channel_id=1, source_target_pairs={{0,24},{8,0},{16,8},{24,16},{1,25},{9,1},{17,9},{25,17},{2,26},{10... | collective-permute-start | bytes 1179656 | tf_op jit(solution)/shard_map/ppermute | solution.py:24
  102.6 201.9 %copy-start.5 = (bf16[2,384,1024]{2,1,0:T(8,128)(2,1)}, bf16[2,384,1024]{2,1,0:T(8,128)(2,1)S(1)}, u32[]{:S(2)}) copy-start(bf16[2,384,1024]{2,1,0:T(8,128)(2,1)S(1)} %collective-permute-done.17.refs_9_.refs_0_.qr.refs_4_) | copy-start | bytes 4718596
  109.4 195.1 %copy-start.12 = (f32[2,384,1024]{2,1,0:T(8,128)}, f32[2,384,1024]{2,1,0:T(8,128)S(1)}, u32[]{:S(2)}) copy-start(f32[2,384,1024]{2,1,0:T(8,128)S(1)} %get-tuple-element.52.refs_9_) | copy-start | bytes 9437188
  109.4 3.0 collective-permute-start.31
  112.4 192.1 %copy-start.21 = (f32[2,8,384]{2,1,0:T(8,128)}, f32[2,8,384]{2,1,0:T(8,128)S(1)}, u32[]{:S(2)}) copy-start(f32[2,8,384]{2,1,0:T(8,128)S(1)} %add.93.refs_11_) | copy-start | bytes 73732
  112.6 27.7 %copy-start.30 = (f32[2,1,3,16,512]{4,3,2,1,0:T(8,128)S(1)}, f32[2,1,3,16,512]{4,3,2,1,0:T(8,128)}, u32[]{:S(2)}) copy-start(f32[2,1,3,16,512]{4,3,2,1,0:T(8,128)} %copy-done.29) | copy-start | bytes 589828
  112.6 4.1 %collective-permute-start.22 = (bf16[2,3,16,512]{3,2,1,0:T(8,128)(2,1)S(1)}, bf16[2,3,16,512]{3,2,1,0:T(8,128)(2,1)S(1)}, u32[]{:S(2)}, u32[]{:S(2)}) collective-permute-start(bf16[2,3,16,512]{3,2,1,0:T(8,128)(2,1)S(1)} %slice.163), channel_id=1, source_target_pairs={{0,24},{8,0},{16,8},{24,16},{1,25},{9,1},{17,9},{25,17},{2,26},{10... | collective-permute-start | bytes 294920 | tf_op jit(solution)/shard_map/ppermute | solution.py:24
  112.8 5.4 %collective-permute-start.28 = (bf16[2,3,16,512]{3,2,1,0:T(8,128)(2,1)S(1)}, bf16[2,3,16,512]{3,2,1,0:T(8,128)(2,1)S(1)}, u32[]{:S(2)}, u32[]{:S(2)}) collective-permute-start(bf16[2,3,16,512]{3,2,1,0:T(8,128)(2,1)S(1)} %slice.162), channel_id=1, source_target_pairs={{0,6},{2,0},{4,2},{6,4},{1,7},{3,1},{5,3},{7,5},{8,14},{10,8},{12,... | collective-permute-start | bytes 294920 | tf_op jit(solution)/shard_map/ppermute | solution.py:24
  116.7 3.5 collective-permute-start.23
  118.3 186.2 %copy-start.32 = (f32[2048]{0:T(1024)S(1)}, f32[2048]{0:T(1024)}, u32[]{:S(2)}) copy-start(f32[2048]{0:T(1024)} %param.15) | copy-start | bytes 24580
  118.3 4.7 %collective-permute-start.29 = (bf16[2,3,16,512]{3,2,1,0:T(8,128)(2,1)S(1)}, bf16[2,3,16,512]{3,2,1,0:T(8,128)(2,1)S(1)}, u32[]{:S(2)}, u32[]{:S(2)}) collective-permute-start(bf16[2,3,16,512]{3,2,1,0:T(8,128)(2,1)S(1)} %fusion.4), channel_id=1, source_target_pairs={{0,6},{2,0},{4,2},{6,4},{1,7},{3,1},{5,3},{7,5},{8,14},{10,8},{12,... | collective-permute-start | bytes 294920 | tf_op jit(solution)/shard_map/ppermute | solution.py:24
  120.3 4.4 %collective-permute-start.24 = (bf16[2,3,16,512]{3,2,1,0:T(8,128)(2,1)S(1)}, bf16[2,3,16,512]{3,2,1,0:T(8,128)(2,1)S(1)}, u32[]{:S(2)}, u32[]{:S(2)}) collective-permute-start(bf16[2,3,16,512]{3,2,1,0:T(8,128)(2,1)S(1)} %fusion.6), channel_id=1, source_target_pairs={{0,24},{8,0},{16,8},{24,16},{1,25},{9,1},{17,9},{25,17},{2,26},{10... | collective-permute-start | bytes 294920 | tf_op jit(solution)/shard_map/ppermute | solution.py:24
  123.0 3.9 %collective-permute-start.30 = (bf16[2,3,16,512]{3,2,1,0:T(8,128)(2,1)S(1)}, bf16[2,3,16,512]{3,2,1,0:T(8,128)(2,1)S(1)}, u32[]{:S(2)}, u32[]{:S(2)}) collective-permute-start(bf16[2,3,16,512]{3,2,1,0:T(8,128)(2,1)S(1)} %fusion.3), channel_id=1, source_target_pairs={{0,6},{2,0},{4,2},{6,4},{1,7},{3,1},{5,3},{7,5},{8,14},{10,8},{12,... | collective-permute-start | bytes 294920 | tf_op jit(solution)/shard_map/ppermute | solution.py:24
  127.0 8.6 %collective-permute-start.32 = (bf16[2,2,3,16,512]{4,3,2,1,0:T(8,128)(2,1)S(1)}, bf16[2,2,3,16,512]{4,3,2,1,0:T(8,128)(2,1)S(1)}, u32[]{:S(2)}, u32[]{:S(2)}) collective-permute-start(bf16[2,2,3,16,512]{4,3,2,1,0:T(8,128)(2,1)S(1)} %pad_maximum_fusion.6), channel_id=1, source_target_pairs={{0,32},{32,0},{1,33},{33,1},{2,34},{34,2},{3,35},{35,3},{4,36},{36... | collective-permute-start | bytes 589832 | tf_op jit(solution)/shard_map/ppermute | solution.py:24
  130.0 174.5 %collective-permute-start.16 = (bf16[4,384,1024]{2,1,0:T(8,128)(2,1)S(1)}, bf16[4,384,1024]{2,1,0:T(8,128)(2,1)S(1)}, u32[]{:S(2)}, u32[]{:S(2)}) collective-permute-start(bf16[4,384,1024]{2,1,0:T(8,128)(2,1)S(1)} %get-tuple-element.43.refs_5_.refs_6_.refs_7_.refs_8_), channel_id=1, source_target_pairs={{0,2},{2,4},{4,6},{6,8},{8,10},{10,12},{12,14},{14,16},{16,18},{18... | collective-permute-start | bytes 9437192 | tf_op jit(solution)/shard_map/ppermute | solution.py:547
  131.6 219.5 %collective-permute-start.47 = (bf16[4,384,1024]{2,1,0:T(8,128)(2,1)}, bf16[4,384,1024]{2,1,0:T(8,128)(2,1)}, u32[]{:S(2)}, u32[]{:S(2)}) collective-permute-start(bf16[4,384,1024]{2,1,0:T(8,128)(2,1)} %get-tuple-element.70.kb.k2.vb.v2), channel_id=1, source_target_pairs={{0,2},{2,4},{4,6},{6,8},{8,10},{10,12},{12,14},{14,16},{16,18},{18... | collective-permute-start | bytes 9437192 | tf_op jit(solution)/shard_map/ppermute | solution.py:548
  135.2 2.7 collective-permute-start.33
  137.9 172.5 %copy-start.23 = (f32[2,8,384]{2,1,0:T(8,128)}, f32[2,8,384]{2,1,0:T(8,128)S(1)}, u32[]{:S(2)}) copy-start(f32[2,8,384]{2,1,0:T(8,128)S(1)} %collective-permute-done.33.refs_12_) | copy-start | bytes 73732
  137.9 213.3 %collective-permute-start.48 = (bf16[4,384,1024]{2,1,0:T(8,128)(2,1)}, bf16[4,384,1024]{2,1,0:T(8,128)(2,1)}, u32[]{:S(2)}, u32[]{:S(2)}) collective-permute-start(bf16[4,384,1024]{2,1,0:T(8,128)(2,1)} %get-tuple-element.70.kb.k2.vb.v2), channel_id=1, source_target_pairs={{30,32},{31,33},{94,96},{95,97}} | collective-permute-start | bytes 9437192 | tf_op jit(solution)/shard_map/ppermute | solution.py:562
  141.1 136.1 %collective-permute-start.35 = (bf16[2,3,16,512]{3,2,1,0:T(8,128)(2,1)S(1)}, bf16[2,3,16,512]{3,2,1,0:T(8,128)(2,1)S(1)}, u32[]{:S(2)}, u32[]{:S(2)}) collective-permute-start(bf16[2,3,16,512]{3,2,1,0:T(8,128)(2,1)S(1)} %get-tuple-element.90), channel_id=1, source_target_pairs={{0,24},{8,0},{16,8},{24,16},{1,25},{9,1},{17,9},{25,17},{2,26},{10... | collective-permute-start | bytes 294920 | tf_op jit(solution)/shard_map/ppermute | solution.py:24
  275.5 4.7 %collective-permute-start.41 = (bf16[2,3,16,512]{3,2,1,0:T(8,128)(2,1)S(1)}, bf16[2,3,16,512]{3,2,1,0:T(8,128)(2,1)S(1)}, u32[]{:S(2)}, u32[]{:S(2)}) collective-permute-start(bf16[2,3,16,512]{3,2,1,0:T(8,128)(2,1)S(1)} %get-tuple-element.89), channel_id=1, source_target_pairs={{0,6},{2,0},{4,2},{6,4},{1,7},{3,1},{5,3},{7,5},{8,14},{10,8},{12,... | collective-permute-start | bytes 294920 | tf_op jit(solution)/shard_map/ppermute | solution.py:24
  277.2 4.7 %collective-permute-start.36 = (bf16[2,3,16,512]{3,2,1,0:T(8,128)(2,1)S(1)}, bf16[2,3,16,512]{3,2,1,0:T(8,128)(2,1)S(1)}, u32[]{:S(2)}, u32[]{:S(2)}) collective-permute-start(bf16[2,3,16,512]{3,2,1,0:T(8,128)(2,1)S(1)} %collective-permute-done.35), channel_id=1, source_target_pairs={{0,24},{8,0},{16,8},{24,16},{1,25},{9,1},{17,9},{25,17},{2,26},{10... | collective-permute-start | bytes 294920 | tf_op jit(solution)/shard_map/ppermute | solution.py:24
  280.2 4.7 %collective-permute-start.42 = (bf16[2,3,16,512]{3,2,1,0:T(8,128)(2,1)S(1)}, bf16[2,3,16,512]{3,2,1,0:T(8,128)(2,1)S(1)}, u32[]{:S(2)}, u32[]{:S(2)}) collective-permute-start(bf16[2,3,16,512]{3,2,1,0:T(8,128)(2,1)S(1)} %collective-permute-done.41), channel_id=1, source_target_pairs={{0,6},{2,0},{4,2},{6,4},{1,7},{3,1},{5,3},{7,5},{8,14},{10,8},{12,... | collective-permute-start | bytes 294920 | tf_op jit(solution)/shard_map/ppermute | solution.py:24
  281.9 4.7 %collective-permute-start.37 = (bf16[2,3,16,512]{3,2,1,0:T(8,128)(2,1)S(1)}, bf16[2,3,16,512]{3,2,1,0:T(8,128)(2,1)S(1)}, u32[]{:S(2)}, u32[]{:S(2)}) collective-permute-start(bf16[2,3,16,512]{3,2,1,0:T(8,128)(2,1)S(1)} %collective-permute-done.36), channel_id=1, source_target_pairs={{0,24},{8,0},{16,8},{24,16},{1,25},{9,1},{17,9},{25,17},{2,26},{10... | collective-permute-start | bytes 294920 | tf_op jit(solution)/shard_map/ppermute | solution.py:24
  284.9 3.5 collective-permute-start.43
  286.6 7.9 %collective-permute-start.38 = (bf16[8,3,16,512]{3,2,1,0:T(8,128)(2,1)S(1)}, bf16[8,3,16,512]{3,2,1,0:T(8,128)(2,1)S(1)}, u32[]{:S(2)}, u32[]{:S(2)}) collective-permute-start(bf16[8,3,16,512]{3,2,1,0:T(8,128)(2,1)S(1)} %pad_maximum_fusion.3.refs_0_), channel_id=1, source_target_pairs={{0,6},{2,0},{4,2},{6,4},{1,7},{3,1},{5,3},{7,5},{8,14},{10,8},{12,... | collective-permute-start | bytes 1179656 | tf_op jit(solution)/shard_map/ppermute | solution.py:24
  288.5 7.9 %collective-permute-start.44 = (bf16[8,3,16,512]{3,2,1,0:T(8,128)(2,1)S(1)}, bf16[8,3,16,512]{3,2,1,0:T(8,128)(2,1)S(1)}, u32[]{:S(2)}, u32[]{:S(2)}) collective-permute-start(bf16[8,3,16,512]{3,2,1,0:T(8,128)(2,1)S(1)} %pad_maximum_fusion.4.refs_4_), channel_id=1, source_target_pairs={{0,24},{8,0},{16,8},{24,16},{1,25},{9,1},{17,9},{25,17},{2,26},{10... | collective-permute-start | bytes 1179656 | tf_op jit(solution)/shard_map/ppermute | solution.py:24
  294.5 9.2 %collective-permute-start.39 = (bf16[8,3,16,512]{3,2,1,0:T(8,128)(2,1)S(1)}, bf16[8,3,16,512]{3,2,1,0:T(8,128)(2,1)}, u32[]{:S(2)}, u32[]{:S(2)}) collective-permute-start(bf16[8,3,16,512]{3,2,1,0:T(8,128)(2,1)S(1)} %collective-permute-done.38.refs_1_), channel_id=1, source_target_pairs={{0,6},{2,0},{4,2},{6,4},{1,7},{3,1},{5,3},{7,5},{8,14},{10,8},{12,... | collective-permute-start | bytes 1179656 | tf_op jit(solution)/shard_map/ppermute | solution.py:24
  296.3 14.1 %copy-start.19 = (bf16[8,3,16,512]{3,2,1,0:T(8,128)(2,1)}, bf16[8,3,16,512]{3,2,1,0:T(8,128)(2,1)S(1)}, u32[]{:S(2)}) copy-start(bf16[8,3,16,512]{3,2,1,0:T(8,128)(2,1)S(1)} %collective-permute-done.44.refs_5_) | copy-start | bytes 1179652
  296.3 22.9 %collective-permute-start.45 = (bf16[8,3,16,512]{3,2,1,0:T(8,128)(2,1)S(1)}, bf16[8,3,16,512]{3,2,1,0:T(8,128)(2,1)}, u32[]{:S(2)}, u32[]{:S(2)}) collective-permute-start(bf16[8,3,16,512]{3,2,1,0:T(8,128)(2,1)S(1)} %collective-permute-done.44.refs_5_), channel_id=1, source_target_pairs={{0,24},{8,0},{16,8},{24,16},{1,25},{9,1},{17,9},{25,17},{2,26},{10... | collective-permute-start | bytes 1179656 | tf_op jit(solution)/shard_map/ppermute | solution.py:24
  303.7 21.5 %collective-permute-start.40 = (bf16[8,3,16,512]{3,2,1,0:T(8,128)(2,1)}, bf16[8,3,16,512]{3,2,1,0:T(8,128)(2,1)}, u32[]{:S(2)}, u32[]{:S(2)}) collective-permute-start(bf16[8,3,16,512]{3,2,1,0:T(8,128)(2,1)} %collective-permute-done.39.refs_2_), channel_id=1, source_target_pairs={{0,6},{2,0},{4,2},{6,4},{1,7},{3,1},{5,3},{7,5},{8,14},{10,8},{12,... | collective-permute-start | bytes 1179656 | tf_op jit(solution)/shard_map/ppermute | solution.py:24
  310.4 64.3 %collective-permute-start.34 = (bf16[384,1024]{1,0:T(8,128)(2,1)}, bf16[384,1024]{1,0:T(8,128)(2,1)}, u32[]{:S(2)}, u32[]{:S(2)}) collective-permute-start(bf16[384,1024]{1,0:T(8,128)(2,1)} %attend_finish.3), channel_id=1, source_target_pairs={{0,1},{1,0},{2,3},{3,2},{4,5},{5,4},{6,7},{7,6},{8,9},{9,8},{10,11... | collective-permute-start | bytes 2359304 | tf_op jit(solution)/shard_map/ppermute | solution.py:24
  319.2 13.8 %collective-permute-start.46 = (bf16[8,3,16,512]{3,2,1,0:T(8,128)(2,1)}, bf16[8,3,16,512]{3,2,1,0:T(8,128)(2,1)}, u32[]{:S(2)}, u32[]{:S(2)}) collective-permute-start(bf16[8,3,16,512]{3,2,1,0:T(8,128)(2,1)} %collective-permute-done.45.refs_6_), channel_id=1, source_target_pairs={{0,24},{8,0},{16,8},{24,16},{1,25},{9,1},{17,9},{25,17},{2,26},{10... | collective-permute-start | bytes 1179656 | tf_op jit(solution)/shard_map/ppermute | solution.py:24
  325.3 42.8 %collective-permute-start.53 = (f32[2,3,8,512]{3,2,1,0:T(8,128)S(1)}, f32[2,3,8,512]{3,2,1,0:T(8,128)S(1)}, u32[]{:S(2)}, u32[]{:S(2)}) collective-permute-start(f32[2,3,8,512]{3,2,1,0:T(8,128)S(1)} %get-tuple-element.88), channel_id=1, source_target_pairs={{0,1},{1,0},{2,3},{3,2},{4,5},{5,4},{6,7},{7,6},{8,9},{9,8},{10,11... | collective-permute-start | bytes 294920 | tf_op jit(solution)/shard_map/ppermute | solution.py:24
  346.1 12.7 %copy-start.1 = (bf16[4,384,1024]{2,1,0:T(8,128)(2,1)S(1)}, bf16[4,384,1024]{2,1,0:T(8,128)(2,1)}, u32[]{:S(2)}) copy-start(bf16[4,384,1024]{2,1,0:T(8,128)(2,1)} %copy-done) | copy-start | bytes 9437188
  346.1 20.5 %collective-permute-start.51 = (f32[2,8,384]{2,1,0:T(8,128)S(1)}, f32[2,8,384]{2,1,0:T(8,128)S(1)}, u32[]{:S(2)}, u32[]{:S(2)}) collective-permute-start(f32[2,8,384]{2,1,0:T(8,128)S(1)} %get-tuple-element.73.refs_0_), channel_id=1, source_target_pairs={{0,65},{65,0},{1,64},{64,1},{2,67},{67,2},{3,66},{66,3},{4,69},{69... | collective-permute-start | bytes 73736 | tf_op jit(solution)/shard_map/ppermute | solution.py:497
  351.2 15.5 %collective-permute-start.50 = (f32[2,8,384]{2,1,0:T(8,128)S(1)}, f32[2,8,384]{2,1,0:T(8,128)S(1)}, u32[]{:S(2)}, u32[]{:S(2)}) collective-permute-start(f32[2,8,384]{2,1,0:T(8,128)S(1)} %get-tuple-element.73.refs_0_), channel_id=1, source_target_pairs={{0,64},{64,0},{1,65},{65,1},{2,66},{66,2},{3,67},{67,3},{4,68},{68... | collective-permute-start | bytes 73736 | tf_op jit(solution)/shard_map/ppermute | solution.py:497
  351.2 15.5 %collective-permute-start.49 = (f32[2,8,384]{2,1,0:T(8,128)S(1)}, f32[2,8,384]{2,1,0:T(8,128)S(1)}, u32[]{:S(2)}, u32[]{:S(2)}) collective-permute-start(f32[2,8,384]{2,1,0:T(8,128)S(1)} %get-tuple-element.73.refs_0_), channel_id=1, source_target_pairs={{0,1},{1,0},{64,65},{65,64},{2,3},{3,2},{66,67},{67,66},{4,5},{5,4... | collective-permute-start | bytes 73736 | tf_op jit(solution)/shard_map/ppermute | solution.py:497
  367.6 11.0 %collective-permute-start.52 = (bf16[384,1024]{1,0:T(8,128)(2,1)S(1)}, bf16[384,1024]{1,0:T(8,128)(2,1)S(1)}, u32[]{:S(2)}, u32[]{:S(2)}) collective-permute-start(bf16[384,1024]{1,0:T(8,128)(2,1)S(1)} %norm_add.3), channel_id=1, source_target_pairs={{0,1},{1,0},{2,3},{3,2},{4,5},{5,4},{6,7},{7,6},{8,9},{9,8},{10,11... | collective-permute-start | bytes 2359304 | tf_op jit(solution)/shard_map/ppermute | solution.py:24
  (23 other events, 141.0 us)

commit v6 on v5

--- a/solution.py
+++ b/solution.py
@@ -557,11 +557,11 @@
     grad_both = half_sums.astype(f32) + other_sums[:, ::-1].astype(f32)
     grad_both, pair1, *powers0 = lax.optimization_barrier((grad_both, pair[1], *powers0))
     new_both = both - grad_both
-    new16 = new_both[:, 0]
     pieces2 = gather_rings(new_both.astype(bf16))
     turned1 = lax.ppermute(pair1, chips, [(15, 16)])
-    own_rows = lax.dynamic_slice_in_dim(new16, core * 8, 8, 2)
-    their_rows = shift(lax.dynamic_slice_in_dim(new16, (1 - core) * 8, 8, 2), "core", 1)
+    own_rows = lax.dynamic_slice(new_both, (0, 0, 0, core * 8, 0), (2, 1, 3, 8, 512))[:, 0]
+    their_rows = lax.dynamic_slice(new_both, (0, 0, 0, (1 - core) * 8, 0), (2, 1, 3, 8, 512))
+    their_rows = shift(their_rows[:, 0], "core", 1)
     new_all = jnp.where(
         core == 0,
         jnp.concatenate([own_rows, their_rows], axis=0),

time: 380 us -> 380 us (level)
  no operation moved by 1% of the time
where the time goes in v6:
time: 380 us
  starting transfers between devices  228 us (60%)
  waiting for transfers between devices  62.7 us (16%)
  Pallas kernels  53.8 us (14%)
  local copies, waits for them, and re-layouts  26.1 us (7%)
  other arithmetic  7.34 us (2%)
    ppermute x46, starting transfers between devices, shift(): lax.ppermute(value, axis, [(i, (i + steps) % count) for i in range(count)])  213 us
    ppermute x46, waiting for transfers between devices, shift(): lax.ppermute(value, axis, [(i, (i + steps) % count) for i in range(count)])  59.6 us
    pallas_call x2, Pallas kernels, fast_apply(): pl.pallas_call(apply_kernel, name='fast_apply', out_shape=[jax.ShapeDtype...  13.6 us
    pallas_call x2, Pallas kernels, finish(): pl.pallas_call(functools.partial(finish_kernel, j, len(powers)), name='at...  11.8 us
    pallas_call x1, Pallas kernels, compute_grads(): pl.pallas_call(grads_kernel, name='fast_grads', out_shape=[jax.ShapeDtype...  11.7 us
    ppermute x5, starting transfers between devices, with_parts(): return [power] + [lax.ppermute(power, ('heads', 'core'), p) for p in pairs]  8.14 us
    unnamed x66, local copies, waits for them, and re-layouts  7.9 us
    pallas_call x1, Pallas kernels, attend_tail(): pl.pallas_call(tail_kernel, name='attend_tail', out_shape=jax.ShapeDtypeS...  7.87 us
  transfers between devices with their start and end apart: 54, of which 23 were waited for; matrix products, arithmetic and copies ran while one was open for 6% of the time, Pallas kernels for 11%

profile of v6, /device:TPU:1, one launch (start us, length us, event | category | flops | bytes accessed | tf_op | source)
XLA Modules:
  0.0 379.6 jit_solution(6082750209650628516)
XLA Ops:
  1.6 1.5 collective-permute-start
  4.0 3.1 collective-permute-start.1
  7.1 4.7 %collective-permute-done.1 = f32[2,3,16,512]{3,2,1,0:T(8,128)S(1)} collective-permute-done((f32[2,3,16,512]{3,2,1,0:T(8,128)S(1)}, f32[2,3,16,512]{3,2,1,0:T(8,128)S(1)}, u32[]{:S(2)}, u32[]{:S(2)}) %collective-permute-start.1) | collective-permute-done | bytes 196640 | tf_op jit(solution)/shard_map/ppermute | solution.py:24
  11.8 2.7 constant_dynamic-slice_fusion.5
  15.7 1.3 constant_dynamic-slice_fusion.7
  17.2 1.8 collective-permute-start.6
  18.9 3.3 collective-permute-start.5
  23.4 2.7 constant_dynamic-slice_fusion.8
  26.1 1.3 constant_dynamic-slice_fusion.6
  30.6 2.5 collective-permute-start.11
  35.6 2.1 collective-permute-done.11
  40.5 1.6 fusion.15
  42.1 1.7 collective-permute-start.14
  43.8 1.5 fusion.14
  45.3 2.1 collective-permute-done.9.refs_3_
  47.4 1.5 collective-permute-start.13
  49.0 3.4 maximum_select_fusion
  53.2 2.4 collective-permute-done.7.refs_1_
  55.5 2.0 collective-permute-done.14.refs_6_
  58.5 11.7 %fast_grads.1 = (bf16[8,3,16,512]{3,2,1,0:T(8,128)(2,1)S(1)}, bf16[8,3,16,512]{3,2,1,0:T(8,128)(2,1)S(1)}, bf16[8,3,16,512]{3,2,1,0:T(8,128)(2,1)S(1)}, bf16[8,3...) custom-call(s32[6]{0:T(128)S(1)} %stack.78.s_ref, ...), custom_call_target="tpu_custom_call" | custom-call | tf_op jit(solution)/shard_map/fast_grads/pallas_call | solution.py:130
  70.1 2.5 collective-permute-start.19
  72.8 4.0 %collective-permute-start.17 = (bf16[2,384,1024]{2,1,0:T(8,128)(2,1)S(1)}, bf16[2,384,1024]{2,1,0:T(8,128)(2,1)S(1)}, u32[]{:S(2)}, u32[]{:S(2)}) collective-permute-start(bf16[2,384,1024]{2,1,0:T(8,128)(2,1)S(1)} %constant_dynamic-slice_fusion.4), channel_id=1, source_target_pairs={{0,1},{1,0},{2,3},{3,2},{4,5},{5,4},{6,7},{7,6},{8,9},{9,8},{10,11... | collective-permute-start | bytes 4718600 | tf_op jit(solution)/shard_map/ppermute | solution.py:24
  76.8 2.7 collective-permute-start.25
  79.6 2.8 collective-permute-start.20
  82.4 5.4 %collective-permute-done.25 = bf16[8,3,16,512]{3,2,1,0:T(8,128)(2,1)S(1)} collective-permute-done((bf16[8,3,16,512]{3,2,1,0:T(8,128)(2,1)S(1)}, bf16[8,3,16,512]{3,2,1,0:T(8,128)(2,1)S(1)}, u32[]{:S(2)}, u32[]{:S(2)}) %collective-permute-start.25) | collective-permute-done | bytes 393248 | tf_op jit(solution)/shard_map/ppermute | solution.py:24
  88.0 3.5 collective-permute-start.26
  92.1 6.9 %collective-permute-done.26 = bf16[8,3,16,512]{3,2,1,0:T(8,128)(2,1)S(1)} collective-permute-done((bf16[8,3,16,512]{3,2,1,0:T(8,128)(2,1)S(1)}, bf16[8,3,16,512]{3,2,1,0:T(8,128)(2,1)S(1)}, u32[]{:S(2)}, u32[]{:S(2)}) %collective-permute-start.26) | collective-permute-done | bytes 393248 | tf_op jit(solution)/shard_map/ppermute | solution.py:24
  99.1 3.5 collective-permute-start.27
  102.6 6.8 %fast_apply.2 = (f32[2,384,1024]{2,1,0:T(8,128)S(1)}, f32[2,8,384]{2,1,0:T(8,128)S(1)}) custom-call(s32[6]{0:T(128)S(1)} %stack.78.s_ref, bf16[8,3,16,512]{3,2,1,0:T(8,128)(2,1)S(1)} %pad_maximum_fusion.1.refs_0_, bf16[8,3,16,512]{3,2,1,0:T(8,128)(2,1)S(1)} %collective-permute-done.7.refs_1_, bf16[8,3,16,512]{3,2,1,0:T(8,128)(2,1)S(1)} %collective-permute-done.8.refs_2_, ...), custom_call_target="tpu_custom_call" | custom-call | tf_op jit(solution)/shard_map/fast_apply/pallas_call | solution.py:181
  109.4 2.2 collective-permute-start.31
  113.2 3.5 collective-permute-done.22
  116.7 1.5 collective-permute-start.23
  118.6 1.6 collective-permute-done.23
  120.3 2.7 collective-permute-start.24
  123.4 1.3 collective-permute-done.24
  124.7 2.2 collective-permute-done.30
  127.0 3.0 collective-permute-start.32
  130.0 1.7 collective-permute-start.16
  131.6 3.6 collective-permute-start.47
  135.6 2.2 collective-permute-done.33.refs_12_
  137.9 2.4 collective-permute-start.48
  141.1 134.4 %collective-permute-start.35 = (bf16[2,3,16,512]{3,2,1,0:T(8,128)(2,1)S(1)}, bf16[2,3,16,512]{3,2,1,0:T(8,128)(2,1)S(1)}, u32[]{:S(2)}, u32[]{:S(2)}) collective-permute-start(bf16[2,3,16,512]{3,2,1,0:T(8,128)(2,1)S(1)} %get-tuple-element.90), channel_id=1, source_target_pairs={{0,24},{8,0},{16,8},{24,16},{1,25},{9,1},{17,9},{25,17},{2,26},{10... | collective-permute-start | bytes 294920 | tf_op jit(solution)/shard_map/ppermute | solution.py:24
  275.5 1.6 collective-permute-done.35
  277.2 3.0 collective-permute-start.36
  280.2 1.6 collective-permute-done.36
  281.9 3.0 collective-permute-start.37
  284.9 1.6 collective-permute-done.37
  286.7 1.7 collective-permute-done.43
  288.5 1.4 collective-permute-start.44
  290.6 3.9 %collective-permute-done.38.refs_1_ = bf16[8,3,16,512]{3,2,1,0:T(8,128)(2,1)S(1)} collective-permute-done((bf16[8,3,16,512]{3,2,1,0:T(8,128)(2,1)S(1)}, bf16[8,3,16,512]{3,2,1,0:T(8,128)(2,1)S(1)}, u32[]{:S(2)}, u32[]{:S(2)}) %collective-permute-start.38) | collective-permute-done | bytes 393248 | tf_op jit(solution)/shard_map/ppermute | solution.py:24
  296.3 2.6 collective-permute-start.45
  298.9 4.8 %collective-permute-done.39.refs_2_ = bf16[8,3,16,512]{3,2,1,0:T(8,128)(2,1)} collective-permute-done((bf16[8,3,16,512]{3,2,1,0:T(8,128)(2,1)S(1)}, bf16[8,3,16,512]{3,2,1,0:T(8,128)(2,1)}, u32[]{:S(2)}, u32[]{:S(2)}) %collective-permute-start.39) | collective-permute-done | bytes 393248 | tf_op jit(solution)/shard_map/ppermute | solution.py:24
  304.5 5.9 %attend_finish.3 = bf16[384,1024]{1,0:T(8,128)(2,1)} custom-call(s32[6]{0:T(128)S(1)} %stack.78.s_ref, bf16[2,384,1024]{2,1,0:T(8,128)(2,1)S(1)} %collective-permute-done.17.refs_9_.refs_0_.qr.refs_4_, bf16[4,384,1024]{2,1,0:T(8,128)(2,1)S(1)} %collective-permute-done.16.refs_1_.refs_2_.refs_3_.refs_4_, ...), custom_call_target="tpu_custom_call" | custom-call | tf_op jit(solution)/shard_map/attend_finish/pallas_call | solution.py:436
  310.4 8.8 %collective-permute-start.34 = (bf16[384,1024]{1,0:T(8,128)(2,1)}, bf16[384,1024]{1,0:T(8,128)(2,1)}, u32[]{:S(2)}, u32[]{:S(2)}) collective-permute-start(bf16[384,1024]{1,0:T(8,128)(2,1)} %attend_finish.3), channel_id=1, source_target_pairs={{0,1},{1,0},{2,3},{3,2},{4,5},{5,4},{6,7},{7,6},{8,9},{9,8},{10,11... | collective-permute-start | bytes 2359304 | tf_op jit(solution)/shard_map/ppermute | solution.py:24
  319.2 5.1 %collective-permute-start.46 = (bf16[8,3,16,512]{3,2,1,0:T(8,128)(2,1)}, bf16[8,3,16,512]{3,2,1,0:T(8,128)(2,1)}, u32[]{:S(2)}, u32[]{:S(2)}) collective-permute-start(bf16[8,3,16,512]{3,2,1,0:T(8,128)(2,1)} %collective-permute-done.45.refs_6_), channel_id=1, source_target_pairs={{0,24},{8,0},{16,8},{24,16},{1,25},{9,1},{17,9},{25,17},{2,26},{10... | collective-permute-start | bytes 1179656 | tf_op jit(solution)/shard_map/ppermute | solution.py:24
  325.7 7.3 %collective-permute-done.46.refs_7_ = bf16[8,3,16,512]{3,2,1,0:T(8,128)(2,1)} collective-permute-done((bf16[8,3,16,512]{3,2,1,0:T(8,128)(2,1)}, bf16[8,3,16,512]{3,2,1,0:T(8,128)(2,1)}, u32[]{:S(2)}, u32[]{:S(2)}) %collective-permute-start.46) | collective-permute-done | bytes 393248 | tf_op jit(solution)/shard_map/ppermute | solution.py:24
  333.0 1.9 copy-done.3
  334.9 1.4 copy-done.6
  339.3 6.8 %fast_apply.3 = (f32[2,384,1024]{2,1,0:T(8,128)S(1)}, f32[2,8,384]{2,1,0:T(8,128)S(1)}) custom-call(s32[6]{0:T(128)S(1)} %stack.78.s_ref, bf16[8,3,16,512]{3,2,1,0:T(8,128)(2,1)S(1)} %pad_maximum_fusion.3.refs_0_, bf16[8,3,16,512]{3,2,1,0:T(8,128)(2,1)S(1)} %copy-done.18, bf16[8,3,16,512]{3,2,1,0:T(8,128)(2,1)} %collective-permute-done.39.refs_2_, ...), custom_call_target="tpu_custom_call" | custom-call | tf_op jit(solution)/shard_map/fast_apply/pallas_call | solution.py:181
  346.1 5.1 %collective-permute-start.51 = (f32[2,8,384]{2,1,0:T(8,128)S(1)}, f32[2,8,384]{2,1,0:T(8,128)S(1)}, u32[]{:S(2)}, u32[]{:S(2)}) collective-permute-start(f32[2,8,384]{2,1,0:T(8,128)S(1)} %get-tuple-element.73.refs_0_), channel_id=1, source_target_pairs={{0,65},{65,0},{1,64},{64,1},{2,67},{67,2},{3,66},{66,3},{4,69},{69... | collective-permute-start | bytes 73736 | tf_op jit(solution)/shard_map/ppermute | solution.py:497
  351.7 7.1 %attend_local.1 = (f32[2,384,1024]{2,1,0:T(8,128)S(1)}, f32[2,2,384,128]{3,2,1,0:T(8,128)S(1)}) custom-call(s32[6]{0:T(128)S(1)} %stack.78.s_ref, bf16[2,384,2048]{2,1,0:T(8,128)(2,1)S(1)} %copy-done.4, bf16[2,384,1024]{2,1,0:T(8,128)(2,1)S(1)} %copy-done.7, bf16[4,384,1024]{2,1,0:T(8,128)(2,1)} %get-tuple-element.70.kb.k2.vb.v2, ...), custom_call_target="tpu_custom_call" | custom-call | tf_op jit(solution)/shard_map/attend_local/pallas_call | solution.py:242
  358.7 7.9 %attend_tail.1.att_ref = f32[2,384,1024]{2,1,0:T(8,128)S(1)} custom-call(s32[6]{0:T(128)S(1)} %stack.78.s_ref, bf16[4,384,1024]{2,1,0:T(8,128)(2,1)} %collective-permute-done.47.refs_0_, bf16[4,384,1024]{2,1,0:T(8,128)(2,1)} %collective-permute-done.48.refs_1_, bf16[4,384,1024]{2,1,0:T(8,128)(2,1)S(1)} %copy-done.1, bf16[2,384,2048]{2,1,0:T(8,128)(2,1)S(1)} %copy-done.4, ...), custom_call_target="tpu_custom_call" | custom-call | tf_op jit(solution)/shard_map/attend_tail/pallas_call | solution.py:306
  368.8 5.9 %attend_finish.2 = bf16[2,384,2048]{2,1,0:T(8,128)(2,1)} custom-call(s32[6]{0:T(128)S(1)} %stack.78.s_ref, bf16[2,384,2048]{2,1,0:T(8,128)(2,1)S(1)} %copy-done.4, bf16[4,384,1024]{2,1,0:T(8,128)(2,1)S(1)} %copy-done.1, bf16[4,384,1024]{2,1,0:T(8,128)(2,1)S(1)} %copy-done.1, bf16[4,384,1024]{2,1,0:T(8,128)(2,1)S(1)} %copy-done.1, ...), custom_call_target="tpu_custom_call" | custom-call | tf_op jit(solution)/shard_map/attend_finish/pallas_call | solution.py:436
  374.7 2.1 bitcast_dynamic-update-slice_fusion.2
  (169 shorter events, 32.6 us)
Async XLA Ops:
  1.6 2.4 collective-permute-start
  4.0 7.8 %collective-permute-start.1 = (f32[2,3,16,512]{3,2,1,0:T(8,128)S(1)}, f32[2,3,16,512]{3,2,1,0:T(8,128)S(1)}, u32[]{:S(2)}, u32[]{:S(2)}) collective-permute-start(f32[2,3,16,512]{3,2,1,0:T(8,128)S(1)} %maximum_select_fusion.2), channel_id=1, source_target_pairs={{0,32},{32,0},{1,33},{33,1},{2,34},{34,2},{3,35},{35,3},{4,36},{36... | collective-permute-start | bytes 589832 | tf_op jit(solution)/shard_map/ppermute | solution.py:24
  7.1 15.1 %copy-start.31 = (f32[4,2,384]{2,1,0:T(2,128)S(1)}, f32[4,2,384]{2,1,0:T(2,128)}, u32[]{:S(2)}) copy-start(f32[4,2,384]{2,1,0:T(2,128)} %param.11) | copy-start | bytes 36868
  14.5 25.1 %collective-permute-start.3 = (bf16[2,384,1024]{2,1,0:T(8,128)(2,1)}, bf16[2,384,1024]{2,1,0:T(8,128)(2,1)}, u32[]{:S(2)}, u32[]{:S(2)}) collective-permute-start(bf16[2,384,1024]{2,1,0:T(8,128)(2,1)} %constant_dynamic-slice_fusion.5), channel_id=1, source_target_pairs={{0,1},{1,0},{2,3},{3,2},{4,5},{5,4},{6,7},{7,6},{8,9},{9,8},{10,11... | collective-permute-start | bytes 4718600 | tf_op jit(solution)/shard_map/ppermute | solution.py:24
  17.0 25.1 %collective-permute-start.2 = (bf16[2,384,1024]{2,1,0:T(8,128)(2,1)}, bf16[2,384,1024]{2,1,0:T(8,128)(2,1)}, u32[]{:S(2)}, u32[]{:S(2)}) collective-permute-start(bf16[2,384,1024]{2,1,0:T(8,128)(2,1)} %constant_dynamic-slice_fusion.7), channel_id=1, source_target_pairs={{0,1},{1,0},{2,3},{3,2},{4,5},{5,4},{6,7},{7,6},{8,9},{9,8},{10,11... | collective-permute-start | bytes 4718600 | tf_op jit(solution)/shard_map/ppermute | solution.py:24
  17.2 12.2 %collective-permute-start.6 = (bf16[2,3,16,512]{3,2,1,0:T(8,128)(2,1)S(1)}, bf16[2,3,16,512]{3,2,1,0:T(8,128)(2,1)}, u32[]{:S(2)}, u32[]{:S(2)}) collective-permute-start(bf16[2,3,16,512]{3,2,1,0:T(8,128)(2,1)S(1)} %get-tuple-element.92), channel_id=1, source_target_pairs={{0,8},{8,16},{16,24},{24,0},{1,9},{9,17},{17,25},{25,1},{2,10},{10... | collective-permute-start | bytes 294920 | tf_op jit(solution)/shard_map/ppermute | solution.py:24
  18.9 11.6 %collective-permute-start.5 = (bf16[2,3,16,512]{3,2,1,0:T(8,128)(2,1)S(1)}, bf16[2,3,16,512]{3,2,1,0:T(8,128)(2,1)}, u32[]{:S(2)}, u32[]{:S(2)}) collective-permute-start(bf16[2,3,16,512]{3,2,1,0:T(8,128)(2,1)S(1)} %get-tuple-element.92), channel_id=1, source_target_pairs={{0,16},{8,24},{16,0},{24,8},{1,17},{9,25},{17,1},{25,9},{2,18},{10... | collective-permute-start | bytes 294920 | tf_op jit(solution)/shard_map/ppermute | solution.py:24
  22.3 5.2 %collective-permute-start.18 = (f32[2,384]{1,0:T(2,128)S(1)}, f32[2,384]{1,0:T(2,128)S(1)}, u32[]{:S(2)}, u32[]{:S(2)}) collective-permute-start(f32[2,384]{1,0:T(2,128)S(1)} %get-tuple-element.96), channel_id=1, source_target_pairs={{0,1},{1,0},{2,3},{3,2},{4,5},{5,4},{6,7},{7,6},{8,9},{9,8},{10,11... | collective-permute-start | bytes 9224 | tf_op jit(solution)/shard_map/ppermute | solution.py:24
  27.4 5.6 %collective-permute-start.4 = (bf16[2,3,16,512]{3,2,1,0:T(8,128)(2,1)S(1)}, bf16[2,3,16,512]{3,2,1,0:T(8,128)(2,1)S(1)}, u32[]{:S(2)}, u32[]{:S(2)}) collective-permute-start(bf16[2,3,16,512]{3,2,1,0:T(8,128)(2,1)S(1)} %get-tuple-element.92), channel_id=1, source_target_pairs={{0,24},{8,0},{16,8},{24,16},{1,25},{9,1},{17,9},{25,17},{2,26},{10... | collective-permute-start | bytes 294920 | tf_op jit(solution)/shard_map/ppermute | solution.py:24
  29.4 5.9 %collective-permute-start.12 = (bf16[2,3,16,512]{3,2,1,0:T(8,128)(2,1)S(1)}, bf16[2,3,16,512]{3,2,1,0:T(8,128)(2,1)S(1)}, u32[]{:S(2)}, u32[]{:S(2)}) collective-permute-start(bf16[2,3,16,512]{3,2,1,0:T(8,128)(2,1)S(1)} %get-tuple-element.91), channel_id=1, source_target_pairs={{0,2},{2,4},{4,6},{6,0},{1,3},{3,5},{5,7},{7,1},{8,10},{10,12},{12... | collective-permute-start | bytes 294920 | tf_op jit(solution)/shard_map/ppermute | solution.py:24
  30.6 7.1 %collective-permute-start.11 = (bf16[2,3,16,512]{3,2,1,0:T(8,128)(2,1)S(1)}, bf16[2,3,16,512]{3,2,1,0:T(8,128)(2,1)S(1)}, u32[]{:S(2)}, u32[]{:S(2)}) collective-permute-start(bf16[2,3,16,512]{3,2,1,0:T(8,128)(2,1)S(1)} %get-tuple-element.91), channel_id=1, source_target_pairs={{0,4},{2,6},{4,0},{6,2},{1,5},{3,7},{5,1},{7,3},{8,12},{10,14},{12... | collective-permute-start | bytes 294920 | tf_op jit(solution)/shard_map/ppermute | solution.py:24
  33.0 5.3 %collective-permute-start.10 = (bf16[2,3,16,512]{3,2,1,0:T(8,128)(2,1)S(1)}, bf16[2,3,16,512]{3,2,1,0:T(8,128)(2,1)S(1)}, u32[]{:S(2)}, u32[]{:S(2)}) collective-permute-start(bf16[2,3,16,512]{3,2,1,0:T(8,128)(2,1)S(1)} %get-tuple-element.91), channel_id=1, source_target_pairs={{0,6},{2,0},{4,2},{6,4},{1,7},{3,1},{5,3},{7,5},{8,14},{10,8},{12,... | collective-permute-start | bytes 294920 | tf_op jit(solution)/shard_map/ppermute | solution.py:24
  35.2 12.1 %collective-permute-start.9 = (bf16[8,3,16,512]{3,2,1,0:T(8,128)(2,1)S(1)}, bf16[8,3,16,512]{3,2,1,0:T(8,128)(2,1)S(1)}, u32[]{:S(2)}, u32[]{:S(2)}) collective-permute-start(bf16[8,3,16,512]{3,2,1,0:T(8,128)(2,1)S(1)} %pad_maximum_fusion.1.refs_0_), channel_id=1, source_target_pairs={{0,2},{2,4},{4,6},{6,0},{1,3},{3,5},{5,7},{7,1},{8,10},{10,12},{12... | collective-permute-start | bytes 1179656 | tf_op jit(solution)/shard_map/ppermute | solution.py:24
  37.7 15.4 %collective-permute-start.8 = (bf16[8,3,16,512]{3,2,1,0:T(8,128)(2,1)S(1)}, bf16[8,3,16,512]{3,2,1,0:T(8,128)(2,1)S(1)}, u32[]{:S(2)}, u32[]{:S(2)}) collective-permute-start(bf16[8,3,16,512]{3,2,1,0:T(8,128)(2,1)S(1)} %pad_maximum_fusion.1.refs_0_), channel_id=1, source_target_pairs={{0,4},{2,6},{4,0},{6,2},{1,5},{3,7},{5,1},{7,3},{8,12},{10,14},{12... | collective-permute-start | bytes 1179656 | tf_op jit(solution)/shard_map/ppermute | solution.py:24
  38.3 17.2 %collective-permute-start.7 = (bf16[8,3,16,512]{3,2,1,0:T(8,128)(2,1)S(1)}, bf16[8,3,16,512]{3,2,1,0:T(8,128)(2,1)S(1)}, u32[]{:S(2)}, u32[]{:S(2)}) collective-permute-start(bf16[8,3,16,512]{3,2,1,0:T(8,128)(2,1)S(1)} %pad_maximum_fusion.1.refs_0_), channel_id=1, source_target_pairs={{0,6},{2,0},{4,2},{6,4},{1,7},{3,1},{5,3},{7,5},{8,14},{10,8},{12,... | collective-permute-start | bytes 1179656 | tf_op jit(solution)/shard_map/ppermute | solution.py:24
  39.6 15.9 %collective-permute-start.15 = (bf16[8,3,16,512]{3,2,1,0:T(8,128)(2,1)S(1)}, bf16[8,3,16,512]{3,2,1,0:T(8,128)(2,1)S(1)}, u32[]{:S(2)}, u32[]{:S(2)}) collective-permute-start(bf16[8,3,16,512]{3,2,1,0:T(8,128)(2,1)S(1)} %pad_maximum_fusion.2.refs_4_), channel_id=1, source_target_pairs={{0,8},{8,16},{16,24},{24,0},{1,9},{9,17},{17,25},{25,1},{2,10},{10... | collective-permute-start | bytes 1179656 | tf_op jit(solution)/shard_map/ppermute | solution.py:24
  42.1 15.5 %collective-permute-start.14 = (bf16[8,3,16,512]{3,2,1,0:T(8,128)(2,1)S(1)}, bf16[8,3,16,512]{3,2,1,0:T(8,128)(2,1)S(1)}, u32[]{:S(2)}, u32[]{:S(2)}) collective-permute-start(bf16[8,3,16,512]{3,2,1,0:T(8,128)(2,1)S(1)} %pad_maximum_fusion.2.refs_4_), channel_id=1, source_target_pairs={{0,16},{8,24},{16,0},{24,8},{1,17},{9,25},{17,1},{25,9},{2,18},{10... | collective-permute-start | bytes 1179656 | tf_op jit(solution)/shard_map/ppermute | solution.py:24
  47.4 11.1 %collective-permute-start.13 = (bf16[8,3,16,512]{3,2,1,0:T(8,128)(2,1)S(1)}, bf16[8,3,16,512]{3,2,1,0:T(8,128)(2,1)S(1)}, u32[]{:S(2)}, u32[]{:S(2)}) collective-permute-start(bf16[8,3,16,512]{3,2,1,0:T(8,128)(2,1)S(1)} %pad_maximum_fusion.2.refs_4_), channel_id=1, source_target_pairs={{0,24},{8,0},{16,8},{24,16},{1,25},{9,1},{17,9},{25,17},{2,26},{10... | collective-permute-start | bytes 1179656 | tf_op jit(solution)/shard_map/ppermute | solution.py:24
  58.5 14.2 %copy-start.2 = (bf16[2,384,2048]{2,1,0:T(8,128)(2,1)S(1)}, bf16[2,384,2048]{2,1,0:T(8,128)(2,1)}, u32[]{:S(2)}) copy-start(bf16[2,384,2048]{2,1,0:T(8,128)(2,1)} %refs_3_) | copy-start | bytes 9437188
  70.1 9.3 %collective-permute-start.19 = (bf16[8,3,16,512]{3,2,1,0:T(8,128)(2,1)S(1)}, bf16[8,3,16,512]{3,2,1,0:T(8,128)(2,1)S(1)}, u32[]{:S(2)}, u32[]{:S(2)}) collective-permute-start(bf16[8,3,16,512]{3,2,1,0:T(8,128)(2,1)S(1)} %get-tuple-element.54), channel_id=1, source_target_pairs={{0,6},{2,0},{4,2},{6,4},{1,7},{3,1},{5,3},{7,5},{8,14},{10,8},{12,... | collective-permute-start | bytes 1179656 | tf_op jit(solution)/shard_map/ppermute | solution.py:24
  72.8 29.8 %collective-permute-start.17 = (bf16[2,384,1024]{2,1,0:T(8,128)(2,1)S(1)}, bf16[2,384,1024]{2,1,0:T(8,128)(2,1)S(1)}, u32[]{:S(2)}, u32[]{:S(2)}) collective-permute-start(bf16[2,384,1024]{2,1,0:T(8,128)(2,1)S(1)} %constant_dynamic-slice_fusion.4), channel_id=1, source_target_pairs={{0,1},{1,0},{2,3},{3,2},{4,5},{5,4},{6,7},{7,6},{8,9},{9,8},{10,11... | collective-permute-start | bytes 4718600 | tf_op jit(solution)/shard_map/ppermute | solution.py:24
  76.8 11.0 %collective-permute-start.25 = (bf16[8,3,16,512]{3,2,1,0:T(8,128)(2,1)S(1)}, bf16[8,3,16,512]{3,2,1,0:T(8,128)(2,1)S(1)}, u32[]{:S(2)}, u32[]{:S(2)}) collective-permute-start(bf16[8,3,16,512]{3,2,1,0:T(8,128)(2,1)S(1)} %get-tuple-element.58), channel_id=1, source_target_pairs={{0,24},{8,0},{16,8},{24,16},{1,25},{9,1},{17,9},{25,17},{2,26},{10... | collective-permute-start | bytes 1179656 | tf_op jit(solution)/shard_map/ppermute | solution.py:24
  79.6 11.9 %collective-permute-start.20 = (bf16[8,3,16,512]{3,2,1,0:T(8,128)(2,1)S(1)}, bf16[8,3,16,512]{3,2,1,0:T(8,128)(2,1)S(1)}, u32[]{:S(2)}, u32[]{:S(2)}) collective-permute-start(bf16[8,3,16,512]{3,2,1,0:T(8,128)(2,1)S(1)} %add_convert_fusion.3), channel_id=1, source_target_pairs={{0,6},{2,0},{4,2},{6,4},{1,7},{3,1},{5,3},{7,5},{8,14},{10,8},{12,... | collective-permute-start | bytes 1179656 | tf_op jit(solution)/shard_map/ppermute | solution.py:24
  88.0 11.0 %collective-permute-start.26 = (bf16[8,3,16,512]{3,2,1,0:T(8,128)(2,1)S(1)}, bf16[8,3,16,512]{3,2,1,0:T(8,128)(2,1)S(1)}, u32[]{:S(2)}, u32[]{:S(2)}) collective-permute-start(bf16[8,3,16,512]{3,2,1,0:T(8,128)(2,1)S(1)} %add_convert_fusion.1), channel_id=1, source_target_pairs={{0,24},{8,0},{16,8},{24,16},{1,25},{9,1},{17,9},{25,17},{2,26},{10... | collective-permute-start | bytes 1179656 | tf_op jit(solution)/shard_map/ppermute | solution.py:24
  91.6 20.9 %collective-permute-start.21 = (bf16[8,3,16,512]{3,2,1,0:T(8,128)(2,1)S(1)}, bf16[8,3,16,512]{3,2,1,0:T(8,128)(2,1)S(1)}, u32[]{:S(2)}, u32[]{:S(2)}) collective-permute-start(bf16[8,3,16,512]{3,2,1,0:T(8,128)(2,1)S(1)} %add_convert_fusion.2), channel_id=1, source_target_pairs={{0,6},{2,0},{4,2},{6,4},{1,7},{3,1},{5,3},{7,5},{8,14},{10,8},{12,... | collective-permute-start | bytes 1179656 | tf_op jit(solution)/shard_map/ppermute | solution.py:24
  99.1 13.6 %collective-permute-start.27 = (bf16[8,3,16,512]{3,2,1,0:T(8,128)(2,1)S(1)}, bf16[8,3,16,512]{3,2,1,0:T(8,128)(2,1)S(1)}, u32[]{:S(2)}, u32[]{:S(2)}) collective-permute-start(bf16[8,3,16,512]{3,2,1,0:T(8,128)(2,1)S(1)} %add_convert_fusion), channel_id=1, source_target_pairs={{0,24},{8,0},{16,8},{24,16},{1,25},{9,1},{17,9},{25,17},{2,26},{10... | collective-permute-start | bytes 1179656 | tf_op jit(solution)/shard_map/ppermute | solution.py:24
  102.6 201.9 %copy-start.5 = (bf16[2,384,1024]{2,1,0:T(8,128)(2,1)}, bf16[2,384,1024]{2,1,0:T(8,128)(2,1)S(1)}, u32[]{:S(2)}) copy-start(bf16[2,384,1024]{2,1,0:T(8,128)(2,1)S(1)} %collective-permute-done.17.refs_9_.refs_0_.qr.refs_4_) | copy-start | bytes 4718596
  109.4 195.1 %copy-start.12 = (f32[2,384,1024]{2,1,0:T(8,128)}, f32[2,384,1024]{2,1,0:T(8,128)S(1)}, u32[]{:S(2)}) copy-start(f32[2,384,1024]{2,1,0:T(8,128)S(1)} %get-tuple-element.52.refs_9_) | copy-start | bytes 9437188
  109.4 3.0 collective-permute-start.31
  112.4 192.1 %copy-start.21 = (f32[2,8,384]{2,1,0:T(8,128)}, f32[2,8,384]{2,1,0:T(8,128)S(1)}, u32[]{:S(2)}) copy-start(f32[2,8,384]{2,1,0:T(8,128)S(1)} %add.93.refs_11_) | copy-start | bytes 73732
  112.6 27.7 %copy-start.30 = (f32[2,1,3,16,512]{4,3,2,1,0:T(8,128)S(1)}, f32[2,1,3,16,512]{4,3,2,1,0:T(8,128)}, u32[]{:S(2)}) copy-start(f32[2,1,3,16,512]{4,3,2,1,0:T(8,128)} %copy-done.29) | copy-start | bytes 589828
  112.6 4.1 %collective-permute-start.22 = (bf16[2,3,16,512]{3,2,1,0:T(8,128)(2,1)S(1)}, bf16[2,3,16,512]{3,2,1,0:T(8,128)(2,1)S(1)}, u32[]{:S(2)}, u32[]{:S(2)}) collective-permute-start(bf16[2,3,16,512]{3,2,1,0:T(8,128)(2,1)S(1)} %slice.158), channel_id=1, source_target_pairs={{0,24},{8,0},{16,8},{24,16},{1,25},{9,1},{17,9},{25,17},{2,26},{10... | collective-permute-start | bytes 294920 | tf_op jit(solution)/shard_map/ppermute | solution.py:24
  112.8 5.4 %collective-permute-start.28 = (bf16[2,3,16,512]{3,2,1,0:T(8,128)(2,1)S(1)}, bf16[2,3,16,512]{3,2,1,0:T(8,128)(2,1)S(1)}, u32[]{:S(2)}, u32[]{:S(2)}) collective-permute-start(bf16[2,3,16,512]{3,2,1,0:T(8,128)(2,1)S(1)} %slice.157), channel_id=1, source_target_pairs={{0,6},{2,0},{4,2},{6,4},{1,7},{3,1},{5,3},{7,5},{8,14},{10,8},{12,... | collective-permute-start | bytes 294920 | tf_op jit(solution)/shard_map/ppermute | solution.py:24
  116.7 3.5 collective-permute-start.23
  118.3 186.2 %copy-start.32 = (f32[2048]{0:T(1024)S(1)}, f32[2048]{0:T(1024)}, u32[]{:S(2)}) copy-start(f32[2048]{0:T(1024)} %param.15) | copy-start | bytes 24580
  118.3 4.7 %collective-permute-start.29 = (bf16[2,3,16,512]{3,2,1,0:T(8,128)(2,1)S(1)}, bf16[2,3,16,512]{3,2,1,0:T(8,128)(2,1)S(1)}, u32[]{:S(2)}, u32[]{:S(2)}) collective-permute-start(bf16[2,3,16,512]{3,2,1,0:T(8,128)(2,1)S(1)} %fusion.4), channel_id=1, source_target_pairs={{0,6},{2,0},{4,2},{6,4},{1,7},{3,1},{5,3},{7,5},{8,14},{10,8},{12,... | collective-permute-start | bytes 294920 | tf_op jit(solution)/shard_map/ppermute | solution.py:24
  120.3 4.4 %collective-permute-start.24 = (bf16[2,3,16,512]{3,2,1,0:T(8,128)(2,1)S(1)}, bf16[2,3,16,512]{3,2,1,0:T(8,128)(2,1)S(1)}, u32[]{:S(2)}, u32[]{:S(2)}) collective-permute-start(bf16[2,3,16,512]{3,2,1,0:T(8,128)(2,1)S(1)} %fusion.6), channel_id=1, source_target_pairs={{0,24},{8,0},{16,8},{24,16},{1,25},{9,1},{17,9},{25,17},{2,26},{10... | collective-permute-start | bytes 294920 | tf_op jit(solution)/shard_map/ppermute | solution.py:24
  123.0 3.9 %collective-permute-start.30 = (bf16[2,3,16,512]{3,2,1,0:T(8,128)(2,1)S(1)}, bf16[2,3,16,512]{3,2,1,0:T(8,128)(2,1)S(1)}, u32[]{:S(2)}, u32[]{:S(2)}) collective-permute-start(bf16[2,3,16,512]{3,2,1,0:T(8,128)(2,1)S(1)} %fusion.3), channel_id=1, source_target_pairs={{0,6},{2,0},{4,2},{6,4},{1,7},{3,1},{5,3},{7,5},{8,14},{10,8},{12,... | collective-permute-start | bytes 294920 | tf_op jit(solution)/shard_map/ppermute | solution.py:24
  127.0 8.6 %collective-permute-start.32 = (bf16[2,2,3,16,512]{4,3,2,1,0:T(8,128)(2,1)S(1)}, bf16[2,2,3,16,512]{4,3,2,1,0:T(8,128)(2,1)S(1)}, u32[]{:S(2)}, u32[]{:S(2)}) collective-permute-start(bf16[2,2,3,16,512]{4,3,2,1,0:T(8,128)(2,1)S(1)} %pad_maximum_fusion.6), channel_id=1, source_target_pairs={{0,32},{32,0},{1,33},{33,1},{2,34},{34,2},{3,35},{35,3},{4,36},{36... | collective-permute-start | bytes 589832 | tf_op jit(solution)/shard_map/ppermute | solution.py:24
  130.0 174.5 %collective-permute-start.16 = (bf16[4,384,1024]{2,1,0:T(8,128)(2,1)S(1)}, bf16[4,384,1024]{2,1,0:T(8,128)(2,1)S(1)}, u32[]{:S(2)}, u32[]{:S(2)}) collective-permute-start(bf16[4,384,1024]{2,1,0:T(8,128)(2,1)S(1)} %get-tuple-element.43.refs_5_.refs_6_.refs_7_.refs_8_), channel_id=1, source_target_pairs={{0,2},{2,4},{4,6},{6,8},{8,10},{10,12},{12,14},{14,16},{16,18},{18... | collective-permute-start | bytes 9437192 | tf_op jit(solution)/shard_map/ppermute | solution.py:547
  131.6 219.5 %collective-permute-start.47 = (bf16[4,384,1024]{2,1,0:T(8,128)(2,1)}, bf16[4,384,1024]{2,1,0:T(8,128)(2,1)}, u32[]{:S(2)}, u32[]{:S(2)}) collective-permute-start(bf16[4,384,1024]{2,1,0:T(8,128)(2,1)} %get-tuple-element.70.kb.k2.vb.v2), channel_id=1, source_target_pairs={{0,2},{2,4},{4,6},{6,8},{8,10},{10,12},{12,14},{14,16},{16,18},{18... | collective-permute-start | bytes 9437192 | tf_op jit(solution)/shard_map/ppermute | solution.py:548
  135.2 2.7 collective-permute-start.33
  137.9 172.5 %copy-start.23 = (f32[2,8,384]{2,1,0:T(8,128)}, f32[2,8,384]{2,1,0:T(8,128)S(1)}, u32[]{:S(2)}) copy-start(f32[2,8,384]{2,1,0:T(8,128)S(1)} %collective-permute-done.33.refs_12_) | copy-start | bytes 73732
  137.9 213.3 %collective-permute-start.48 = (bf16[4,384,1024]{2,1,0:T(8,128)(2,1)}, bf16[4,384,1024]{2,1,0:T(8,128)(2,1)}, u32[]{:S(2)}, u32[]{:S(2)}) collective-permute-start(bf16[4,384,1024]{2,1,0:T(8,128)(2,1)} %get-tuple-element.70.kb.k2.vb.v2), channel_id=1, source_target_pairs={{30,32},{31,33},{94,96},{95,97}} | collective-permute-start | bytes 9437192 | tf_op jit(solution)/shard_map/ppermute | solution.py:561
  141.1 136.1 %collective-permute-start.35 = (bf16[2,3,16,512]{3,2,1,0:T(8,128)(2,1)S(1)}, bf16[2,3,16,512]{3,2,1,0:T(8,128)(2,1)S(1)}, u32[]{:S(2)}, u32[]{:S(2)}) collective-permute-start(bf16[2,3,16,512]{3,2,1,0:T(8,128)(2,1)S(1)} %get-tuple-element.90), channel_id=1, source_target_pairs={{0,24},{8,0},{16,8},{24,16},{1,25},{9,1},{17,9},{25,17},{2,26},{10... | collective-permute-start | bytes 294920 | tf_op jit(solution)/shard_map/ppermute | solution.py:24
  275.5 4.7 %collective-permute-start.41 = (bf16[2,3,16,512]{3,2,1,0:T(8,128)(2,1)S(1)}, bf16[2,3,16,512]{3,2,1,0:T(8,128)(2,1)S(1)}, u32[]{:S(2)}, u32[]{:S(2)}) collective-permute-start(bf16[2,3,16,512]{3,2,1,0:T(8,128)(2,1)S(1)} %get-tuple-element.89), channel_id=1, source_target_pairs={{0,6},{2,0},{4,2},{6,4},{1,7},{3,1},{5,3},{7,5},{8,14},{10,8},{12,... | collective-permute-start | bytes 294920 | tf_op jit(solution)/shard_map/ppermute | solution.py:24
  277.2 4.7 %collective-permute-start.36 = (bf16[2,3,16,512]{3,2,1,0:T(8,128)(2,1)S(1)}, bf16[2,3,16,512]{3,2,1,0:T(8,128)(2,1)S(1)}, u32[]{:S(2)}, u32[]{:S(2)}) collective-permute-start(bf16[2,3,16,512]{3,2,1,0:T(8,128)(2,1)S(1)} %collective-permute-done.35), channel_id=1, source_target_pairs={{0,24},{8,0},{16,8},{24,16},{1,25},{9,1},{17,9},{25,17},{2,26},{10... | collective-permute-start | bytes 294920 | tf_op jit(solution)/shard_map/ppermute | solution.py:24
  280.2 4.7 %collective-permute-start.42 = (bf16[2,3,16,512]{3,2,1,0:T(8,128)(2,1)S(1)}, bf16[2,3,16,512]{3,2,1,0:T(8,128)(2,1)S(1)}, u32[]{:S(2)}, u32[]{:S(2)}) collective-permute-start(bf16[2,3,16,512]{3,2,1,0:T(8,128)(2,1)S(1)} %collective-permute-done.41), channel_id=1, source_target_pairs={{0,6},{2,0},{4,2},{6,4},{1,7},{3,1},{5,3},{7,5},{8,14},{10,8},{12,... | collective-permute-start | bytes 294920 | tf_op jit(solution)/shard_map/ppermute | solution.py:24
  281.9 4.7 %collective-permute-start.37 = (bf16[2,3,16,512]{3,2,1,0:T(8,128)(2,1)S(1)}, bf16[2,3,16,512]{3,2,1,0:T(8,128)(2,1)S(1)}, u32[]{:S(2)}, u32[]{:S(2)}) collective-permute-start(bf16[2,3,16,512]{3,2,1,0:T(8,128)(2,1)S(1)} %collective-permute-done.36), channel_id=1, source_target_pairs={{0,24},{8,0},{16,8},{24,16},{1,25},{9,1},{17,9},{25,17},{2,26},{10... | collective-permute-start | bytes 294920 | tf_op jit(solution)/shard_map/ppermute | solution.py:24
  284.9 3.5 collective-permute-start.43
  286.6 7.9 %collective-permute-start.38 = (bf16[8,3,16,512]{3,2,1,0:T(8,128)(2,1)S(1)}, bf16[8,3,16,512]{3,2,1,0:T(8,128)(2,1)S(1)}, u32[]{:S(2)}, u32[]{:S(2)}) collective-permute-start(bf16[8,3,16,512]{3,2,1,0:T(8,128)(2,1)S(1)} %pad_maximum_fusion.3.refs_0_), channel_id=1, source_target_pairs={{0,6},{2,0},{4,2},{6,4},{1,7},{3,1},{5,3},{7,5},{8,14},{10,8},{12,... | collective-permute-start | bytes 1179656 | tf_op jit(solution)/shard_map/ppermute | solution.py:24
  288.5 7.9 %collective-permute-start.44 = (bf16[8,3,16,512]{3,2,1,0:T(8,128)(2,1)S(1)}, bf16[8,3,16,512]{3,2,1,0:T(8,128)(2,1)S(1)}, u32[]{:S(2)}, u32[]{:S(2)}) collective-permute-start(bf16[8,3,16,512]{3,2,1,0:T(8,128)(2,1)S(1)} %pad_maximum_fusion.4.refs_4_), channel_id=1, source_target_pairs={{0,24},{8,0},{16,8},{24,16},{1,25},{9,1},{17,9},{25,17},{2,26},{10... | collective-permute-start | bytes 1179656 | tf_op jit(solution)/shard_map/ppermute | solution.py:24
  294.5 9.2 %collective-permute-start.39 = (bf16[8,3,16,512]{3,2,1,0:T(8,128)(2,1)S(1)}, bf16[8,3,16,512]{3,2,1,0:T(8,128)(2,1)}, u32[]{:S(2)}, u32[]{:S(2)}) collective-permute-start(bf16[8,3,16,512]{3,2,1,0:T(8,128)(2,1)S(1)} %collective-permute-done.38.refs_1_), channel_id=1, source_target_pairs={{0,6},{2,0},{4,2},{6,4},{1,7},{3,1},{5,3},{7,5},{8,14},{10,8},{12,... | collective-permute-start | bytes 1179656 | tf_op jit(solution)/shard_map/ppermute | solution.py:24
  296.3 14.1 %copy-start.19 = (bf16[8,3,16,512]{3,2,1,0:T(8,128)(2,1)}, bf16[8,3,16,512]{3,2,1,0:T(8,128)(2,1)S(1)}, u32[]{:S(2)}) copy-start(bf16[8,3,16,512]{3,2,1,0:T(8,128)(2,1)S(1)} %collective-permute-done.44.refs_5_) | copy-start | bytes 1179652
  296.3 22.9 %collective-permute-start.45 = (bf16[8,3,16,512]{3,2,1,0:T(8,128)(2,1)S(1)}, bf16[8,3,16,512]{3,2,1,0:T(8,128)(2,1)}, u32[]{:S(2)}, u32[]{:S(2)}) collective-permute-start(bf16[8,3,16,512]{3,2,1,0:T(8,128)(2,1)S(1)} %collective-permute-done.44.refs_5_), channel_id=1, source_target_pairs={{0,24},{8,0},{16,8},{24,16},{1,25},{9,1},{17,9},{25,17},{2,26},{10... | collective-permute-start | bytes 1179656 | tf_op jit(solution)/shard_map/ppermute | solution.py:24
  303.7 21.5 %collective-permute-start.40 = (bf16[8,3,16,512]{3,2,1,0:T(8,128)(2,1)}, bf16[8,3,16,512]{3,2,1,0:T(8,128)(2,1)}, u32[]{:S(2)}, u32[]{:S(2)}) collective-permute-start(bf16[8,3,16,512]{3,2,1,0:T(8,128)(2,1)} %collective-permute-done.39.refs_2_), channel_id=1, source_target_pairs={{0,6},{2,0},{4,2},{6,4},{1,7},{3,1},{5,3},{7,5},{8,14},{10,8},{12,... | collective-permute-start | bytes 1179656 | tf_op jit(solution)/shard_map/ppermute | solution.py:24
  310.4 64.3 %collective-permute-start.34 = (bf16[384,1024]{1,0:T(8,128)(2,1)}, bf16[384,1024]{1,0:T(8,128)(2,1)}, u32[]{:S(2)}, u32[]{:S(2)}) collective-permute-start(bf16[384,1024]{1,0:T(8,128)(2,1)} %attend_finish.3), channel_id=1, source_target_pairs={{0,1},{1,0},{2,3},{3,2},{4,5},{5,4},{6,7},{7,6},{8,9},{9,8},{10,11... | collective-permute-start | bytes 2359304 | tf_op jit(solution)/shard_map/ppermute | solution.py:24
  319.2 13.8 %collective-permute-start.46 = (bf16[8,3,16,512]{3,2,1,0:T(8,128)(2,1)}, bf16[8,3,16,512]{3,2,1,0:T(8,128)(2,1)}, u32[]{:S(2)}, u32[]{:S(2)}) collective-permute-start(bf16[8,3,16,512]{3,2,1,0:T(8,128)(2,1)} %collective-permute-done.45.refs_6_), channel_id=1, source_target_pairs={{0,24},{8,0},{16,8},{24,16},{1,25},{9,1},{17,9},{25,17},{2,26},{10... | collective-permute-start | bytes 1179656 | tf_op jit(solution)/shard_map/ppermute | solution.py:24
  325.2 42.8 %collective-permute-start.53 = (f32[2,3,8,512]{3,2,1,0:T(8,128)S(1)}, f32[2,3,8,512]{3,2,1,0:T(8,128)S(1)}, u32[]{:S(2)}, u32[]{:S(2)}) collective-permute-start(f32[2,3,8,512]{3,2,1,0:T(8,128)S(1)} %get-tuple-element.85), channel_id=1, source_target_pairs={{0,1},{1,0},{2,3},{3,2},{4,5},{5,4},{6,7},{7,6},{8,9},{9,8},{10,11... | collective-permute-start | bytes 294920 | tf_op jit(solution)/shard_map/ppermute | solution.py:24
  346.1 12.7 %copy-start.1 = (bf16[4,384,1024]{2,1,0:T(8,128)(2,1)S(1)}, bf16[4,384,1024]{2,1,0:T(8,128)(2,1)}, u32[]{:S(2)}) copy-start(bf16[4,384,1024]{2,1,0:T(8,128)(2,1)} %copy-done) | copy-start | bytes 9437188
  346.1 20.5 %collective-permute-start.51 = (f32[2,8,384]{2,1,0:T(8,128)S(1)}, f32[2,8,384]{2,1,0:T(8,128)S(1)}, u32[]{:S(2)}, u32[]{:S(2)}) collective-permute-start(f32[2,8,384]{2,1,0:T(8,128)S(1)} %get-tuple-element.73.refs_0_), channel_id=1, source_target_pairs={{0,65},{65,0},{1,64},{64,1},{2,67},{67,2},{3,66},{66,3},{4,69},{69... | collective-permute-start | bytes 73736 | tf_op jit(solution)/shard_map/ppermute | solution.py:497
  351.2 15.5 %collective-permute-start.50 = (f32[2,8,384]{2,1,0:T(8,128)S(1)}, f32[2,8,384]{2,1,0:T(8,128)S(1)}, u32[]{:S(2)}, u32[]{:S(2)}) collective-permute-start(f32[2,8,384]{2,1,0:T(8,128)S(1)} %get-tuple-element.73.refs_0_), channel_id=1, source_target_pairs={{0,64},{64,0},{1,65},{65,1},{2,66},{66,2},{3,67},{67,3},{4,68},{68... | collective-permute-start | bytes 73736 | tf_op jit(solution)/shard_map/ppermute | solution.py:497
  351.2 15.5 %collective-permute-start.49 = (f32[2,8,384]{2,1,0:T(8,128)S(1)}, f32[2,8,384]{2,1,0:T(8,128)S(1)}, u32[]{:S(2)}, u32[]{:S(2)}) collective-permute-start(f32[2,8,384]{2,1,0:T(8,128)S(1)} %get-tuple-element.73.refs_0_), channel_id=1, source_target_pairs={{0,1},{1,0},{64,65},{65,64},{2,3},{3,2},{66,67},{67,66},{4,5},{5,4... | collective-permute-start | bytes 73736 | tf_op jit(solution)/shard_map/ppermute | solution.py:497
  367.6 11.0 %collective-permute-start.52 = (bf16[384,1024]{1,0:T(8,128)(2,1)S(1)}, bf16[384,1024]{1,0:T(8,128)(2,1)S(1)}, u32[]{:S(2)}, u32[]{:S(2)}) collective-permute-start(bf16[384,1024]{1,0:T(8,128)(2,1)S(1)} %norm_add.3), channel_id=1, source_target_pairs={{0,1},{1,0},{2,3},{3,2},{4,5},{5,4},{6,7},{7,6},{8,9},{9,8},{10,11... | collective-permute-start | bytes 2359304 | tf_op jit(solution)/shard_map/ppermute | solution.py:24
  (23 other events, 141.0 us)
